TPU v7x, 32 devices: a whole 2x2x4 slice. The times are simulated.
32 devices in a mesh: fsdp: 8 (over z, core), tp: 4 (over y, x).
Axes of the slice: x: 2, y: 2, z: 4, core: 2. Of those that a mesh axis runs over, the one named last changes fastest.
Arguments:
- block_in: bfloat16 [12288, 2560], P(('fsdp', 'tp')), may hold values from -6 to 6
- cotangent: bfloat16 [12288, 2560], P(('fsdp', 'tp')), may hold values from -6 to 6
- segment_ids: int32 [8, 1536], P('fsdp'), may hold values from 0 to 3, never falling along the last dimension, each value on 1 to 1152 neighbouring positions
- group_fill: int32 [8], P('fsdp'), may hold values from 1 to 1536, 7680 in all
- input_gain: bfloat16 [2560], P('fsdp'), may hold values from 0.5 to 1.5
- proj_inner: bfloat16 [2560, 2, 5120], P('fsdp', None, 'tp'), may hold values from -0.125 to 0.125
- proj_step: bfloat16 [2560, 80], P('fsdp', 'tp'), may hold values from -0.125 to 0.125
- proj_state: bfloat16 [2560, 256], P('fsdp', 'tp'), may hold values from -0.125 to 0.125
- conv_inner: bfloat16 [5, 5120], P(None, ('tp', 'fsdp')), may hold values from -0.5 to 0.5
- conv_state: bfloat16 [5, 256], P(None, ('tp', 'fsdp')), may hold values from -0.5 to 0.5
- head_params: float32 [3, 80], P(None, 'tp'), may hold values from -7 to 3, as said below
- mixer_gain: bfloat16 [5120], P(('tp', 'fsdp')), may hold values from 0.5 to 1.5
- proj_output: bfloat16 [5120, 2560], P('tp', 'fsdp'), may hold values from -0.078125 to 0.078125
- first_input_gain: float32 [2560], P('fsdp'), may hold values from -32 to 32
- first_proj_inner: float32 [2560, 2, 5120], P('fsdp', None, 'tp'), may hold values from -32 to 32
- first_proj_step: float32 [2560, 80], P('fsdp', 'tp'), may hold values from -32 to 32
- first_proj_state: float32 [2560, 256], P('fsdp', 'tp'), may hold values from -32 to 32
- first_conv_inner: float32 [5, 5120], P(None, ('tp', 'fsdp')), may hold values from -32 to 32
- first_conv_state: float32 [5, 256], P(None, ('tp', 'fsdp')), may hold values from -32 to 32
- first_head_params: float32 [3, 80], P(None, 'tp'), may hold values from -32 to 32
- first_mixer_gain: float32 [5120], P(('tp', 'fsdp')), may hold values from -32 to 32
- first_proj_output: float32 [5120, 2560], P('tp', 'fsdp'), may hold values from -32 to 32
- second_input_gain: float32 [2560], P('fsdp'), may hold values from 30.72 to 122.88
- second_proj_inner: float32 [2560, 2, 5120], P('fsdp', None, 'tp'), may hold values from 30.72 to 122.88
- second_proj_step: float32 [2560, 80], P('fsdp', 'tp'), may hold values from 30.72 to 122.88
- second_proj_state: float32 [2560, 256], P('fsdp', 'tp'), may hold values from 30.72 to 122.88
- second_conv_inner: float32 [5, 5120], P(None, ('tp', 'fsdp')), may hold values from 30.72 to 122.88
- second_conv_state: float32 [5, 256], P(None, ('tp', 'fsdp')), may hold values from 30.72 to 122.88
- second_head_params: float32 [3, 80], P(None, 'tp'), may hold values from 30.72 to 122.88
- second_mixer_gain: float32 [5120], P(('tp', 'fsdp')), may hold values from 30.72 to 122.88
- second_proj_output: float32 [5120, 2560], P('tp', 'fsdp'), may hold values from 30.72 to 122.88
Outputs:
- block_out: bfloat16 [12288, 2560], P(('fsdp', 'tp'))
- d_input: bfloat16 [12288, 2560], P(('fsdp', 'tp'))
- grad_input_gain: float32 [2560], P('fsdp')
- grad_proj_inner: float32 [2560, 2, 5120], P('fsdp', None, 'tp')
- grad_proj_step: float32 [2560, 80], P('fsdp', 'tp')
- grad_proj_state: float32 [2560, 256], P('fsdp', 'tp')
- grad_conv_inner: float32 [5, 5120], P(None, ('tp', 'fsdp'))
- grad_conv_state: float32 [5, 256], P(None, ('tp', 'fsdp'))
- grad_head_params: float32 [3, 80], P(None, 'tp')
- grad_mixer_gain: float32 [5120], P(('tp', 'fsdp'))
- grad_proj_output: float32 [5120, 2560], P('tp', 'fsdp')
- new_input_gain: bfloat16 [2560], P('fsdp')
- new_proj_inner: bfloat16 [2560, 2, 5120], P('fsdp', None, 'tp')
- new_proj_step: bfloat16 [2560, 80], P('fsdp', 'tp')
- new_proj_state: bfloat16 [2560, 256], P('fsdp', 'tp')
- new_conv_inner: bfloat16 [5, 5120], P(None, ('tp', 'fsdp'))
- new_conv_state: bfloat16 [5, 256], P(None, ('tp', 'fsdp'))
- new_head_params: float32 [3, 80], P(None, 'tp')
- new_mixer_gain: bfloat16 [5120], P(('tp', 'fsdp'))
- new_proj_output: bfloat16 [5120, 2560], P('tp', 'fsdp')
- new_first_input_gain: float32 [2560], P('fsdp')
- new_first_proj_inner: float32 [2560, 2, 5120], P('fsdp', None, 'tp')
- new_first_proj_step: float32 [2560, 80], P('fsdp', 'tp')
- new_first_proj_state: float32 [2560, 256], P('fsdp', 'tp')
- new_first_conv_inner: float32 [5, 5120], P(None, ('tp', 'fsdp'))
- new_first_conv_state: float32 [5, 256], P(None, ('tp', 'fsdp'))
- new_first_head_params: float32 [3, 80], P(None, 'tp')
- new_first_mixer_gain: float32 [5120], P(('tp', 'fsdp'))
- new_first_proj_output: float32 [5120, 2560], P('tp', 'fsdp')
- new_second_input_gain: float32 [2560], P('fsdp')
- new_second_proj_inner: float32 [2560, 2, 5120], P('fsdp', None, 'tp')
- new_second_proj_step: float32 [2560, 80], P('fsdp', 'tp')
- new_second_proj_state: float32 [2560, 256], P('fsdp', 'tp')
- new_second_conv_inner: float32 [5, 5120], P(None, ('tp', 'fsdp'))
- new_second_conv_state: float32 [5, 256], P(None, ('tp', 'fsdp'))
- new_second_head_params: float32 [3, 80], P(None, 'tp')
- new_second_mixer_gain: float32 [5120], P(('tp', 'fsdp'))
- new_second_proj_output: float32 [5120, 2560], P('tp', 'fsdp')
Inputs may be any that keep to these rules, and one draw needn't show every extreme that they name: `segment_ids`: within each group the numbers never fall; each packed sequence has at most 1152 slots, and some has exactly 1152. `group_fill`: the live slots of a group are its leading slots; the counts sum to 7680, and the largest is exactly 1536. `head_params`: row 0 lies in [-7, -2.3], row 1 in [0, 2.8], row 2 in [0.25, 2].
All inputs are finite; a program needn't handle non-finite values.
Results may differ from a plain program's by a relative error of at most 0.0076.
The roundings to bfloat16 on the way count: a program that leaves them out, or rounds other values in their place, can miss the bound.
Values may be sent and summed in bfloat16 or wider, within the bound.
A program may use at most 576 MiB of HBM per device.

v0:
```python
import jax
import jax.numpy as jnp
from jax import lax
from jax.sharding import PartitionSpec as P

DI = 5120
N = 128
Q = 256
STEP = 3


NORM_EPS = 1e-05
BETA_ONE = 0.9
BETA_TWO = 0.95
LEARN_RATE = 0.004
LEARN_SMALL = 0.15
WEIGHT_DECAY = 0.1
ADAM_EPS = 1e-08
PRECISE = lax.Precision.HIGHEST


def silu_act(values):
    return values * jax.nn.sigmoid(values)


def causal_conv(inputs, conv_taps, segment):
    tap_count = conv_taps.shape[0] - 1
    length = inputs.shape[0]
    summed = conv_taps[tap_count][None, :] + conv_taps[tap_count - 1][None, :] * inputs
    for offset in range(1, tap_count):
        shifted = jnp.concatenate(
            [jnp.zeros_like(inputs[:offset]), inputs[: length - offset]], axis=0
        )
        earlier = jnp.concatenate(
            [jnp.full((offset,), -1, jnp.int32), segment[: length - offset]], axis=0
        )
        same_doc = (earlier == segment)[:, None]
        summed = summed + conv_taps[tap_count - 1 - offset][None, :] * jnp.where(
            same_doc, shifted, 0.0
        )
    return summed


def ssd_block(
    carry_state, previous, inner_vals, step_sizes, b_rows, c_rows, labels, decay_rates, skip_weights
):
    block_len = inner_vals.shape[0]
    lower_mask = jnp.arange(block_len)[:, None] >= jnp.arange(block_len)[None, :]
    log_steps = step_sizes * decay_rates[None, :]
    cumulative = jnp.cumsum(log_steps, axis=0)
    keep_mask = (lower_mask & (labels[:, None] == labels[None, :]))[:, :, None]
    spread = cumulative[:, None, :] - cumulative[None, :, :]
    decays = jnp.where(keep_mask, jnp.exp(jnp.where(keep_mask, spread, 0.0)), 0.0)
    scores = jnp.dot(c_rows, b_rows.T, precision=PRECISE)
    mixing = decays * scores[:, :, None] * step_sizes[None, :, :]
    inside = jnp.einsum("ijh,jhp->ihp", mixing, inner_vals, precision=PRECISE)
    carried = jnp.where((labels == previous)[:, None], jnp.exp(cumulative), 0.0)
    from_state = (
        jnp.einsum("in,hnp->ihp", c_rows, carry_state, precision=PRECISE) * carried[:, :, None]
    )
    output = inside + from_state + skip_weights[None, :, None] * inner_vals
    final_label = labels[block_len - 1]
    tail_weights = (
        jnp.where(
            (labels == final_label)[:, None],
            jnp.exp(cumulative[block_len - 1][None, :] - cumulative),
            0.0,
        )
        * step_sizes
    )
    kept_share = jnp.where(previous == final_label, jnp.exp(cumulative[block_len - 1]), 0.0)
    new_state = (
        jnp.einsum("jn,jh,jhp->hnp", b_rows, tail_weights, inner_vals, precision=PRECISE)
        + carry_state * kept_share[:, None, None]
    )
    return (new_state, output)


def ssd_scan(inner_vals, step_sizes, decay_rates, b_rows, c_rows, segment, skip_weights):
    row_count, head_count, head_width = inner_vals.shape
    blocks = row_count // Q
    state_width = b_rows.shape[1]
    stacked = (
        inner_vals.reshape(blocks, Q, head_count, head_width),
        step_sizes.reshape(blocks, Q, head_count),
        b_rows.reshape(blocks, Q, state_width),
        c_rows.reshape(blocks, Q, state_width),
        segment.reshape(blocks, Q),
    )

    def advance(carried_in, pieces):
        carry_state, previous = carried_in
        block_vals, block_steps, block_b, block_c, block_labels = pieces
        new_state, output = ssd_block(
            carry_state,
            previous,
            block_vals,
            block_steps,
            block_b,
            block_c,
            block_labels,
            decay_rates,
            skip_weights,
        )
        return ((new_state, block_labels[Q - 1]), output)

    start_state = jnp.zeros((head_count, state_width, head_width), inner_vals.dtype)
    final_carry, outputs = lax.scan(advance, (start_state, jnp.int32(-1)), stacked)
    return outputs.reshape(row_count, head_count, head_width)


def mixer_core(x_raw, dt_raw, b_rows, c_rows, conv_taps, head_params, segment):
    head_count = head_params.shape[1]
    activated = silu_act(causal_conv(x_raw, conv_taps, segment))
    step_sizes = jax.nn.softplus(dt_raw + head_params[0][None, :])
    decay_rates = -jnp.exp(head_params[1])
    shaped = activated.reshape(activated.shape[0], head_count, -1)
    output = ssd_scan(shaped, step_sizes, decay_rates, b_rows, c_rows, segment, head_params[2])
    return output.reshape(activated.shape[0], -1)


def state_act(raw_rows, conv_taps, segment):
    return silu_act(causal_conv(raw_rows, conv_taps, segment))


def contract_rows(left_mat, right_mat):
    return lax.dot_general(
        left_mat, right_mat, (((0,), (0,)), ((), ())), preferred_element_type=jnp.float32
    )


def contract_cols(left_mat, right_mat):
    return lax.dot_general(
        left_mat, right_mat, (((1,), (1,)), ((), ())), preferred_element_type=jnp.float32
    )


def adamw_step(weight, gradient, first_moment, second_moment, decay_factor, learn_rate):
    new_first = BETA_ONE * first_moment + (1.0 - BETA_ONE) * gradient
    new_second = BETA_TWO * second_moment + (1.0 - BETA_TWO) * gradient * gradient
    first_hat = new_first / (1.0 - BETA_ONE**STEP)
    second_hat = new_second / (1.0 - BETA_TWO**STEP)
    weight_f = weight.astype(jnp.float32)
    updated = weight_f - learn_rate * (
        first_hat / (jnp.sqrt(second_hat) + ADAM_EPS) + decay_factor * weight_f
    )
    return (updated.astype(weight.dtype), new_first, new_second)


def body(
    block_in,
    cotangent,
    segment_ids,
    group_fill,
    input_gain,
    proj_inner,
    proj_step,
    proj_state,
    conv_inner,
    conv_state,
    head_params,
    mixer_gain,
    proj_output,
    first_input_gain,
    first_proj_inner,
    first_proj_step,
    first_proj_state,
    first_conv_inner,
    first_conv_state,
    first_head_params,
    first_mixer_gain,
    first_proj_output,
    second_input_gain,
    second_proj_inner,
    second_proj_step,
    second_proj_state,
    second_conv_inner,
    second_conv_state,
    second_head_params,
    second_mixer_gain,
    second_proj_output,
):
    tp_size = lax.axis_size("tp")
    tp_index = lax.axis_index("tp")
    fsdp_index = lax.axis_index("fsdp")
    own_rows = block_in.shape[0]
    segment = segment_ids[0]
    filled = group_fill[0]
    gathered = (
        lax.all_gather(input_gain, "fsdp", axis=0, tiled=True),
        lax.all_gather(proj_inner, "fsdp", axis=0, tiled=True),
        lax.all_gather(proj_step, "fsdp", axis=0, tiled=True),
        lax.all_gather(proj_state, "fsdp", axis=0, tiled=True),
        lax.all_gather(proj_output, "fsdp", axis=1, tiled=True),
        lax.all_gather(conv_inner, "fsdp", axis=1, tiled=True),
        lax.all_gather(conv_state, "fsdp", axis=1, tiled=True),
        lax.all_gather(mixer_gain, "fsdp", axis=0, tiled=True),
    )
    gain_all, inner_all, step_all, state_all, output_all, taps_inner, taps_state, mixer_all = (
        gathered
    )
    inner_flat = inner_all.reshape(inner_all.shape[0], -1)
    block_f = block_in.astype(jnp.float32)
    inv_rms = lax.rsqrt(jnp.mean(block_f * block_f, axis=1, keepdims=True) + NORM_EPS)
    unit_rows = block_f * inv_rms
    gain_f = gain_all.astype(jnp.float32)
    normed = (unit_rows * gain_f[None, :]).astype(jnp.bfloat16)
    group_rows = lax.all_gather(normed, "tp", axis=0, tiled=True)
    both_raw = jnp.dot(group_rows, inner_flat, preferred_element_type=jnp.float32)
    half_cols = both_raw.shape[1] // 2
    z_raw = both_raw[:, :half_cols]
    x_raw = both_raw[:, half_cols:]
    dt_raw = jnp.dot(group_rows, step_all, preferred_element_type=jnp.float32)
    state_raw = jnp.dot(group_rows, state_all, preferred_element_type=jnp.float32)
    state_local, state_back = jax.vjp(
        lambda raw_rows, conv_taps: state_act(raw_rows, conv_taps, segment),
        state_raw,
        taps_state.astype(jnp.float32),
    )
    state_rows = lax.all_gather(state_local.astype(jnp.bfloat16), "tp", axis=1, tiled=True)
    state_f = state_rows.astype(jnp.float32)
    b_rows = state_f[:, :N]
    c_rows = state_f[:, N:]
    mixed_inner, core_back = jax.vjp(
        lambda x_in_raw, dt_in_raw, b_in, c_in, conv_taps, head_in: mixer_core(
            x_in_raw, dt_in_raw, b_in, c_in, conv_taps, head_in, segment
        ),
        x_raw,
        dt_raw,
        b_rows,
        c_rows,
        taps_inner.astype(jnp.float32),
        head_params,
    )
    gate_act = silu_act(z_raw)
    gated_rows = mixed_inner * gate_act
    square_sum = lax.psum(jnp.sum(gated_rows * gated_rows, axis=1), "tp")
    inv_gate = lax.rsqrt(square_sum[:, None] / DI + NORM_EPS)
    unit_gated = gated_rows * inv_gate
    mixer_f = mixer_all.astype(jnp.float32)
    normed_gated = (unit_gated * mixer_f[None, :]).astype(jnp.bfloat16)
    mixed_rows = lax.psum_scatter(
        jnp.dot(normed_gated, output_all, preferred_element_type=jnp.float32),
        "tp",
        scatter_dimension=0,
        tiled=True,
    )
    positions = tp_index * own_rows + jnp.arange(own_rows, dtype=jnp.int32)
    live_rows = (positions < filled)[:, None]
    block_out = (block_f + jnp.where(live_rows, mixed_rows, 0.0)).astype(jnp.bfloat16)
    cot_f = cotangent.astype(jnp.float32)
    own_grad = jnp.where(live_rows, cot_f, 0.0).astype(jnp.bfloat16)
    group_grad = lax.all_gather(own_grad, "tp", axis=0, tiled=True)
    grad_output = contract_rows(normed_gated, group_grad)
    d_normed_gated = contract_cols(group_grad, output_all)
    grad_mixer = jnp.sum(d_normed_gated * unit_gated, axis=0)
    d_unit = d_normed_gated * mixer_f[None, :]
    inner_sum = lax.psum(jnp.sum(d_unit * unit_gated, axis=1), "tp")
    d_gated = inv_gate * (d_unit - unit_gated * (inner_sum[:, None] / DI))
    d_mixed_inner = d_gated * gate_act
    sigmoid_z = jax.nn.sigmoid(z_raw)
    d_z = d_gated * mixed_inner * sigmoid_z * (1.0 + z_raw * (1.0 - sigmoid_z))
    d_x, d_dt, d_b, d_c, grad_conv_inner, grad_head = core_back(d_mixed_inner)
    d_state_all = lax.psum_scatter(
        jnp.concatenate([d_b, d_c], axis=1), "tp", scatter_dimension=1, tiled=True
    )
    d_state_raw, grad_conv_state = state_back(d_state_all)
    d_both = jnp.concatenate([d_z, d_x], axis=1).astype(jnp.bfloat16)
    d_step = d_dt.astype(jnp.bfloat16)
    d_state_b = d_state_raw.astype(jnp.bfloat16)
    grad_inner = contract_rows(group_rows, d_both).reshape(group_rows.shape[1], 2, half_cols)
    grad_step = contract_rows(group_rows, d_step)
    grad_state = contract_rows(group_rows, d_state_b)
    d_normed = lax.psum_scatter(
        contract_cols(d_both, inner_flat)
        + contract_cols(d_step, step_all)
        + contract_cols(d_state_b, state_all),
        "tp",
        scatter_dimension=0,
        tiled=True,
    )
    grad_gain = jnp.sum(d_normed * unit_rows, axis=0)
    scaled = d_normed * gain_f[None, :]
    d_block = inv_rms * (scaled - unit_rows * jnp.mean(scaled * unit_rows, axis=1, keepdims=True))
    d_input = (cot_f + d_block).astype(jnp.bfloat16)
    summed_grads = (
        lax.psum_scatter(grad_inner, "fsdp", scatter_dimension=0, tiled=True),
        lax.psum_scatter(grad_step, "fsdp", scatter_dimension=0, tiled=True),
        lax.psum_scatter(grad_state, "fsdp", scatter_dimension=0, tiled=True),
        lax.psum_scatter(grad_output, "fsdp", scatter_dimension=1, tiled=True),
        lax.psum_scatter(grad_conv_inner, "fsdp", scatter_dimension=1, tiled=True),
        lax.psum_scatter(grad_conv_state, "fsdp", scatter_dimension=1, tiled=True),
        lax.psum_scatter(grad_mixer, "fsdp", scatter_dimension=0, tiled=True),
    )
    head_width = grad_head.shape[1]
    head_full = lax.dynamic_update_slice(
        jnp.zeros((3, head_width * tp_size), jnp.float32),
        grad_head,
        (jnp.int32(0), tp_index * head_width),
    )
    small_sums = lax.psum((grad_gain, head_full), ("fsdp", "tp"))
    gain_width = input_gain.shape[0]
    grad_input_gain = lax.dynamic_slice_in_dim(
        small_sums[0], fsdp_index * gain_width, gain_width, 0
    )
    grad_heads = lax.dynamic_slice_in_dim(small_sums[1], tp_index * head_width, head_width, 1)
    weights = (
        input_gain,
        proj_inner,
        proj_step,
        proj_state,
        conv_inner,
        conv_state,
        head_params,
        mixer_gain,
        proj_output,
    )
    grads = (
        grad_input_gain,
        summed_grads[0],
        summed_grads[1],
        summed_grads[2],
        summed_grads[4],
        summed_grads[5],
        grad_heads,
        summed_grads[6],
        summed_grads[3],
    )
    decays = (0.0, WEIGHT_DECAY, WEIGHT_DECAY, WEIGHT_DECAY, 0.0, 0.0, 0.0, 0.0, WEIGHT_DECAY)
    rates = (
        LEARN_SMALL,
        LEARN_RATE,
        LEARN_RATE,
        LEARN_RATE,
        LEARN_SMALL,
        LEARN_SMALL,
        LEARN_SMALL,
        LEARN_SMALL,
        LEARN_RATE,
    )
    firsts = (
        first_input_gain,
        first_proj_inner,
        first_proj_step,
        first_proj_state,
        first_conv_inner,
        first_conv_state,
        first_head_params,
        first_mixer_gain,
        first_proj_output,
    )
    seconds = (
        second_input_gain,
        second_proj_inner,
        second_proj_step,
        second_proj_state,
        second_conv_inner,
        second_conv_state,
        second_head_params,
        second_mixer_gain,
        second_proj_output,
    )
    updated = [
        adamw_step(
            weights[index], grads[index], firsts[index], seconds[index], decays[index], rates[index]
        )
        for index in range(9)
    ]
    return (
        block_out,
        d_input,
        grads[0],
        grads[1],
        grads[2],
        grads[3],
        grads[4],
        grads[5],
        grads[6],
        grads[7],
        grads[8],
        updated[0][0],
        updated[1][0],
        updated[2][0],
        updated[3][0],
        updated[4][0],
        updated[5][0],
        updated[6][0],
        updated[7][0],
        updated[8][0],
        updated[0][1],
        updated[1][1],
        updated[2][1],
        updated[3][1],
        updated[4][1],
        updated[5][1],
        updated[6][1],
        updated[7][1],
        updated[8][1],
        updated[0][2],
        updated[1][2],
        updated[2][2],
        updated[3][2],
        updated[4][2],
        updated[5][2],
        updated[6][2],
        updated[7][2],
        updated[8][2],
    )


def solution(mesh):
    return jax.shard_map(
        body,
        mesh=mesh,
        in_specs=(
            P(("fsdp", "tp"), None),
            P(("fsdp", "tp"), None),
            P("fsdp", None),
            P("fsdp"),
            P("fsdp"),
            P("fsdp", None, "tp"),
            P("fsdp", "tp"),
            P("fsdp", "tp"),
            P(None, ("tp", "fsdp")),
            P(None, ("tp", "fsdp")),
            P(None, "tp"),
            P(("tp", "fsdp")),
            P("tp", "fsdp"),
            P("fsdp"),
            P("fsdp", None, "tp"),
            P("fsdp", "tp"),
            P("fsdp", "tp"),
            P(None, ("tp", "fsdp")),
            P(None, ("tp", "fsdp")),
            P(None, "tp"),
            P(("tp", "fsdp")),
            P("tp", "fsdp"),
            P("fsdp"),
            P("fsdp", None, "tp"),
            P("fsdp", "tp"),
            P("fsdp", "tp"),
            P(None, ("tp", "fsdp")),
            P(None, ("tp", "fsdp")),
            P(None, "tp"),
            P(("tp", "fsdp")),
            P("tp", "fsdp"),
        ),
        out_specs=(
            P(("fsdp", "tp"), None),
            P(("fsdp", "tp"), None),
            P("fsdp"),
            P("fsdp", None, "tp"),
            P("fsdp", "tp"),
            P("fsdp", "tp"),
            P(None, ("tp", "fsdp")),
            P(None, ("tp", "fsdp")),
            P(None, "tp"),
            P(("tp", "fsdp")),
            P("tp", "fsdp"),
            P("fsdp"),
            P("fsdp", None, "tp"),
            P("fsdp", "tp"),
            P("fsdp", "tp"),
            P(None, ("tp", "fsdp")),
            P(None, ("tp", "fsdp")),
            P(None, "tp"),
            P(("tp", "fsdp")),
            P("tp", "fsdp"),
            P("fsdp"),
            P("fsdp", None, "tp"),
            P("fsdp", "tp"),
            P("fsdp", "tp"),
            P(None, ("tp", "fsdp")),
            P(None, ("tp", "fsdp")),
            P(None, "tp"),
            P(("tp", "fsdp")),
            P("tp", "fsdp"),
            P("fsdp"),
            P("fsdp", None, "tp"),
            P("fsdp", "tp"),
            P("fsdp", "tp"),
            P(None, ("tp", "fsdp")),
            P(None, ("tp", "fsdp")),
            P(None, "tp"),
            P(("tp", "fsdp")),
            P("tp", "fsdp"),
        ),
        check_vma=False,
    )
```

profile of v0, /device:TPU:0, one launch (start us, length us, event | category | flops | bytes accessed | tf_op | source)
XLA Modules:
  0.0 2145.0 jit_solution(4311410896293545360)
XLA Ops:
  11.7 30.2 %all-reduce.36 = (bf16[2560]{0:T(1024)(128)(2,1)S(1)}, bf16[1280]{0:T(1024)(128)(2,1)S(1)}) all-reduce(bf16[2560]{0:T(1024)(128)(2,1)S(1)} %dynamic-update-slice, bf16[1280]{0:T(1024)(128)(2,1)S(1)} %dynamic-update-slice.1), channel_id=1, replica_groups=mesh['fsdp'=8,'tp'=4] {'fsdp'}, use_global_device_ids=true, to_apply=%add.29 | all-reduce | flops 3840 | bytes 15360
  51.8 14.0 all-gather.1
  66.0 14.6 all-gather.2
  81.2 12.7 all_gather.38
  94.3 14.0 all-gather
  111.2 17.9 all-gather.8.cloned.1.call-done
  136.8 11.1 all_gather.40
  156.6 95.3 %all-gather.10.cloned.1.call-done = bf16[2560,2,1280]{2,1,0:T(2,128)(2,1)} async-done(((bf16[320,2,1280]{2,1,0:T(2,128)(2,1)}), bf16[2560,2,1280]{2,1,0:T(2,128)(2,1)}) %all-gather.10.cloned.1.call-update) | async-done | bytes 13107216 | tf_op jit(solution)/shard_map/all_gather | solution.py:191
  251.8 13.0 copy.346
  264.8 26.1 %fusion.250 = f32[1536,2560]{1,0:T(8,128)S(1)} fusion(bf16[1536,2560]{1,0:T(8,128)(2,1)} %all-gather.8.cloned.1.call-done, bf16[2560,2560]{1,0:T(8,128)(2,1)} %bitcast.566), kind=kOutput, calls=%fused_computation.389 | convolution fusion | flops 20132659200 | bytes 36700160 | tf_op jit(solution)/shard_map/dot_general | solution.py:209
  303.8 16.3 fusion.165
  320.1 14.2 reshape.538
  334.3 14.5 copy.260
  361.7 223.4 %while.89 = (s32[]{:T(128)}, f32[20,128,64]{1,2,0:T(8,128)S(1)}, s32[]{:T(128)}, f32[6,256,20,64]{1,3,2,0:T(8,128)}, pred[6,256,256,20]{2,1,3,0:T(32,128)(4,1)},...) while((s32[]{:T(128)}, f32[20,128,64]{1,2,0:T(8,128)S(1)}, ...), condition=%wide.region_4.5_spmd.clone, body=%wide.region_1.4_spmd.clone.sunk | while | flops 2130372224 | bytes 42297776 | solution.py:108
  420.0 9.0 fusion.321
  457.3 8.9 fusion.321
  531.5 9.0 fusion.321
  585.2 13.0 copy.295
  598.2 14.4 reshape.539
  612.6 9.2 multiply_reduce_fusion.6
  621.8 10.2 psum.28
  632.1 18.6 multiply_reduce_fusion
  658.9 16.5 multiply_convert_fusion
  675.4 14.0 reshape.526
  689.4 14.5 copy.268
  709.9 308.5 %while.90 = (s32[]{:T(128)}, f32[20]{0:T(128)S(1)}, f32[20]{0:T(128)S(1)}, f32[20,128,64]{1,2,0:T(8,128)S(1)}, f32[6,256,20,64]{1,3,2,0:T(8,128)}, /*index=5*/f3...) while((s32[]{:T(128)}, f32[20]{0:T(128)S(1)}, ...), condition=%wide.region_22.23_spmd.clone, body=%wide.region_10.22_spmd.clone.sunk | while | flops 4248246272 | bytes 47831784 | solution.py:108
  711.8 13.8 fusion.334
  763.1 13.6 fusion.334
  814.4 13.7 fusion.334
  865.9 13.6 fusion.334
  917.1 13.7 fusion.334
  968.4 13.7 fusion.334
  1022.5 13.1 copy.297
  1035.6 14.6 reshape.540
  1050.2 20.5 multiply_reduce_fusion.4
  1094.8 13.2 add_convert_fusion
  1118.3 28.0 %fusion.170 = f32[2560,2560]{0,1:T(8,128)} fusion(bf16[1536,2560]{1,0:T(8,128)(2,1)} %all-gather.8.cloned.1.call-done, bf16[1536,1280]{1,0:T(8,128)(2,1)} %add_convert_fusion, bf16[1536,1280]{1,0:T(8,128)(2,1)} %get-tuple-element.2180), kind=kOutput, calls=%fused_computation.233 | convolution fusion | flops 20148387840 | bytes 41943040 | tf_op jit(solution)/shard_map/dot_general | solution.py:127
  1146.3 38.5 %copy.276 = f32[2560,2,1280]{2,1,0:T(2,128)} copy(f32[2560,2,1280]{0,2,1:T(8,128)} %bitcast.559) | data formatting | bytes 52428800 | tf_op jit(solution)/shard_map/reshape | solution.py:271
  1185.6 18.6 fusion.231
  1220.4 34.8 %add_add_fusion = f32[1536,2560]{1,0:T(8,128)} fusion(f32[1536,2560]{1,0:T(8,128)} %fusion.252, f32[1536,2560]{1,0:T(8,128)} %fusion.208, bf16[2560,2560]{1,0:T(8,128)(2,1)} %bitcast.567, bf16[1536,1280]{1,0:T(8,128)(2,1)} %add_convert_fusion, bf16[1536,1280]{1,0:T(8,128)(2,1)} %get-tuple-element.2180), kind=kOutput, calls=%fused_computation.196 | convolution fusion | flops 20156252160 | bytes 68157440 | tf_op jit(solution)/shard_map/dot_general | solution.py:133
  1255.3 18.2 fusion.232
  1279.6 27.9 %all-reduce.35 = (f32[5,64]{1,0:T(8,128)S(1)}, f32[1280]{0:T(1024)S(1)}) all-reduce(f32[5,64]{1,0:T(8,128)S(1)} %pad_add_fusion.1, f32[1280]{0:T(1024)S(1)} %copy-done.64), channel_id=9, replica_groups=mesh['fsdp'=8,'tp'=4] {'fsdp'}, use_global_device_ids=true, to_apply=%region_42.43.clone | all-reduce | flops 1600 | bytes 12800
  1310.8 385.5 %all-reduce.39.cloned.1.call-done = f32[2560,2,1280]{2,1,0:T(2,128)} async-done(((f32[2560,2,1280]{2,1,0:T(2,128)}), f32[2560,2,1280]{2,1,0:T(2,128)}) %all-reduce.39.cloned.1.call-update) | async-done | bytes 26214416
  1696.3 17.1 fusion.184
  1713.5 119.9 %reduce-scatter.21.cloned.1.call-done = f32[1280,320]{0,1:T(8,128)} async-done(((f32[1280,2560]{0,1:T(8,128)}), f32[1280,320]{0,1:T(8,128)}) %reduce-scatter.21.cloned.1.call-update) | async-done | bytes 1638416 | tf_op jit(solution)/shard_map/reduce_scatter | solution.py:290
  1838.6 142.7 %reduce-scatter.19.cloned.1.call-done = f32[384,2560]{1,0:T(8,128)} async-done(((f32[1536,2560]{1,0:T(8,128)}), f32[384,2560]{1,0:T(8,128)}) %reduce-scatter.19.cloned.1.call-update) | async-done | bytes 3932176 | tf_op jit(solution)/shard_map/reduce_scatter | solution.py:274
  1984.6 40.0 %all-reduce.34 = (f32[2560]{0:T(1024)S(1)}, f32[3,80]{1,0:T(4,128)S(1)}) all-reduce(f32[2560]{0:T(1024)S(1)} %get-tuple-element.1948, f32[3,80]{1,0:T(4,128)S(1)} %dynamic_update_slice.215), channel_id=1, replica_groups=mesh['fsdp'=8,'tp'=4] {'fsdp','tp'}, use_global_device_ids=true, to_apply=%region_27.28 | all-reduce | flops 2800 | bytes 22400 | tf_op jit(solution)/shard_map/psum | solution.py:301
  2026.0 105.9 %reduce-scatter.15.cloned.1.call-done = f32[384,2560]{1,0:T(8,128)} async-done(((f32[1536,2560]{1,0:T(8,128)}), f32[384,2560]{1,0:T(8,128)}) %reduce-scatter.15.cloned.1.call-update) | async-done | bytes 3932176 | tf_op jit(solution)/shard_map/reduce_scatter | solution.py:242
  (768 shorter events, 562.9 us)
Async XLA Ops:
  7.2 42.4 %copy-start.8 = (bf16[384,2560]{1,0:T(8,128)(2,1)S(1)}, bf16[384,2560]{1,0:T(8,128)(2,1)}, u32[]{:S(2)}) copy-start(bf16[384,2560]{1,0:T(8,128)(2,1)} %param.36) | copy-start | bytes 5898244
  7.2 121.9 %all-gather.8.cloned.1.call-start = ((), (), s32[]{:S(2)}) async-start(), calls=%async_computation.7 | async-start | bytes 9830400 | tf_op jit(solution)/shard_map/all_gather | solution.py:208
  44.1 37.1 %copy-start.62 = (bf16[5,8]{1,0:T(8,128)(2,1)S(1)}, bf16[5,8]{1,0:T(8,128)(2,1)}, u32[]{:S(2)}) copy-start(bf16[5,8]{1,0:T(8,128)(2,1)} %param.44) | copy-start | bytes 244
  44.1 50.1 %copy-start.67 = (f32[3,20]{1,0:T(4,128)S(1)}, f32[3,20]{1,0:T(4,128)}, u32[]{:S(2)}) copy-start(f32[3,20]{1,0:T(4,128)} %param.45) | copy-start | bytes 724
  44.1 50.2 %copy-start.40 = (bf16[320,20]{0,1:T(8,128)(2,1)S(1)}, bf16[320,20]{0,1:T(8,128)(2,1)}, u32[]{:S(2)}) copy-start(bf16[320,20]{0,1:T(8,128)(2,1)} %param.41) | copy-start | bytes 38404
  47.5 204.4 %all-gather.10.cloned.1.call-start = ((), (), s32[]{:S(2)}) async-start(), calls=%async_computation.8 | async-start | bytes 14745600 | tf_op jit(solution)/shard_map/all_gather | solution.py:191
  48.2 583.9 %all-gather.12.cloned.1.call-start = ((), (), s32[]{:S(2)}) async-start(), calls=%async_computation.9 | async-start | bytes 7372800 | tf_op jit(solution)/shard_map/all_gather | solution.py:194
  48.9 583.2 %all-gather.14.cloned.1.call-start = ((), (), s32[]{:S(2)}) async-start(), calls=%async_computation.11 | async-start | bytes 9830400 | tf_op jit(solution)/shard_map/all_gather | solution.py:253
  51.4 1056.6 %reduce-scatter.17.cloned.1.call-start = ((), (), s32[]{:S(2)}) async-start(), calls=%async_computation.12 | async-start | bytes 1966080 | tf_op jit(solution)/shard_map/reduce_scatter | solution.py:264
  66.0 234.7 %copy-start.32 = (f32[1280]{0:T(1024)}, f32[1280]{0:T(1024)S(1)}, u32[]{:S(2)}) copy-start(f32[1280]{0:T(1024)S(1)} %get-tuple-element.1959) | copy-start | bytes 15364
  66.0 234.7 %copy-start.34 = (f32[1280]{0:T(1024)}, f32[1280]{0:T(1024)S(1)}, u32[]{:S(2)}) copy-start(f32[1280]{0:T(1024)S(1)} %get-tuple-element.1958) | copy-start | bytes 15364
  66.0 234.7 %copy-start.36 = (f32[1280]{0:T(1024)}, f32[1280]{0:T(1024)S(1)}, u32[]{:S(2)}) copy-start(f32[1280]{0:T(1024)S(1)} %get-tuple-element.1956) | copy-start | bytes 15364
  66.0 234.7 %copy-start.38 = (f32[1280]{0:T(1024)}, f32[1280]{0:T(1024)S(1)}, u32[]{:S(2)}) copy-start(f32[1280]{0:T(1024)S(1)} %get-tuple-element.1957) | copy-start | bytes 15364
  81.1 55.6 %copy-start.11 = (bf16[2560,64]{0,1:T(8,128)(2,1)}, bf16[2560,64]{0,1:T(8,128)(2,1)S(1)}, u32[]{:S(2)}) copy-start(bf16[2560,64]{0,1:T(8,128)(2,1)S(1)} %reshape.505) | copy-start | bytes 983044
  94.2 53.9 %copy-start.69 = (f32[64]{0:T(128)}, f32[64]{0:T(128)S(1)}, u32[]{:S(2)}) copy-start(f32[64]{0:T(128)S(1)} %get-tuple-element.1963) | copy-start | bytes 772
  94.2 53.9 %copy-start.71 = (f32[64]{0:T(128)}, f32[64]{0:T(128)S(1)}, u32[]{:S(2)}) copy-start(f32[64]{0:T(128)S(1)} %get-tuple-element.1961) | copy-start | bytes 772
  94.2 53.9 %copy-start.73 = (f32[64]{0:T(128)}, f32[64]{0:T(128)S(1)}, u32[]{:S(2)}) copy-start(f32[64]{0:T(128)S(1)} %get-tuple-element.1962) | copy-start | bytes 772
  94.3 53.9 %copy-start.75 = (f32[64]{0:T(128)}, f32[64]{0:T(128)S(1)}, u32[]{:S(2)}) copy-start(f32[64]{0:T(128)S(1)} %get-tuple-element.1964) | copy-start | bytes 772
  108.5 42.0 %copy-start.14 = (bf16[2560,20]{0,1:T(8,128)(2,1)}, bf16[2560,20]{0,1:T(8,128)(2,1)S(1)}, u32[]{:S(2)}) copy-start(bf16[2560,20]{0,1:T(8,128)(2,1)S(1)} %reshape.501) | copy-start | bytes 307204
  109.2 191.5 %copy-start.26 = (pred[1536]{0:T(1024)(128)(4,1)}, pred[1536]{0:T(1024)(128)(4,1)S(1)}, u32[]{:S(2)}) copy-start(pred[1536]{0:T(1024)(128)(4,1)S(1)} %get-tuple-element.2186) | copy-start | bytes 4612
  109.2 191.5 %copy-start.28 = (pred[1536]{0:T(1024)(128)(4,1)}, pred[1536]{0:T(1024)(128)(4,1)S(1)}, u32[]{:S(2)}) copy-start(pred[1536]{0:T(1024)(128)(4,1)S(1)} %get-tuple-element.2187) | copy-start | bytes 4612
  109.2 191.5 %copy-start.30 = (pred[1536]{0:T(1024)(128)(4,1)}, pred[1536]{0:T(1024)(128)(4,1)S(1)}, u32[]{:S(2)}) copy-start(pred[1536]{0:T(1024)(128)(4,1)S(1)} %get-tuple-element.2188) | copy-start | bytes 4612
  1022.4 253.7 %reduce-scatter.27.cloned.1.call-start = ((), (), s32[]{:S(2)}) async-start(), calls=%async_computation.17 | async-start | bytes 737280
  1087.2 190.6 %reduce-scatter.23.cloned.1.call-start = ((), (), s32[]{:S(2)}) async-start(), calls=%async_computation.15 | async-start | bytes 1474560
  1094.7 214.2 %reduce-scatter.25.cloned.1.call-start = ((), (), s32[]{:S(2)}) async-start(), calls=%async_computation.16 | async-start | bytes 1474560
  1118.3 578.0 %all-reduce.39.cloned.1.call-start = ((), (), s32[]{:S(2)}) async-start(), calls=%async_computation.18 | async-start | bytes 52428800
  1184.9 648.5 %reduce-scatter.21.cloned.1.call-start = ((), (), s32[]{:S(2)}) async-start(), calls=%async_computation.14 | async-start | bytes 14745600 | tf_op jit(solution)/shard_map/reduce_scatter | solution.py:290
  1204.2 777.2 %reduce-scatter.19.cloned.1.call-start = ((), (), s32[]{:S(2)}) async-start(), calls=%async_computation.13 | async-start | bytes 19660800 | tf_op jit(solution)/shard_map/reduce_scatter | solution.py:274
  1255.2 876.7 %reduce-scatter.15.cloned.1.call-start = ((), (), s32[]{:S(2)}) async-start(), calls=%async_computation.10 | async-start | bytes 19660800 | tf_op jit(solution)/shard_map/reduce_scatter | solution.py:242
  1273.7 34.5 %copy-start.63 = (bf16[5,8]{1,0:T(8,128)(2,1)S(1)}, bf16[5,8]{1,0:T(8,128)(2,1)}, u32[]{:S(2)}) copy-start(bf16[5,8]{1,0:T(8,128)(2,1)} %param.44) | copy-start | bytes 244
  1273.7 34.5 %copy-start.77 = (f32[5,8]{1,0:T(8,128)S(1)}, f32[5,8]{1,0:T(8,128)}, u32[]{:S(2)}) copy-start(f32[5,8]{1,0:T(8,128)} %param.53) | copy-start | bytes 484
  1273.7 36.3 %copy-start.19 = (bf16[320,64]{0,1:T(8,128)(2,1)S(1)}, bf16[320,64]{0,1:T(8,128)(2,1)}, u32[]{:S(2)}) copy-start(bf16[320,64]{0,1:T(8,128)(2,1)} %param.42) | copy-start | bytes 122884
  1273.7 36.3 %copy-start.23 = (f32[320,64]{0,1:T(8,128)S(1)}, f32[320,64]{0,1:T(8,128)}, u32[]{:S(2)}) copy-start(f32[320,64]{0,1:T(8,128)} %param.51) | copy-start | bytes 245764
  1273.7 36.3 %copy-start.24 = (f32[320,64]{0,1:T(8,128)S(1)}, f32[320,64]{0,1:T(8,128)}, u32[]{:S(2)}) copy-start(f32[320,64]{0,1:T(8,128)} %param.60) | copy-start | bytes 245764
  1273.8 422.5 %copy-start.9 = (bf16[320,2,1280]{2,1,0:T(2,128)(2,1)S(1)}, bf16[320,2,1280]{2,1,0:T(2,128)(2,1)}, u32[]{:S(2)}) copy-start(bf16[320,2,1280]{2,1,0:T(2,128)(2,1)} %param.40) | copy-start | bytes 4915204
  1277.2 436.2 %copy-start.44 = (f32[5,160]{1,0:T(8,128)}, f32[5,160]{1,0:T(8,128)S(1)}, u32[]{:S(2)}) copy-start(f32[5,160]{1,0:T(8,128)S(1)} %copy.290) | copy-start | bytes 9604
  1278.8 434.5 %copy-start.22 = (f32[320,20]{0,1:T(8,128)}, f32[320,20]{0,1:T(8,128)S(1)}, u32[]{:S(2)}) copy-start(f32[320,20]{0,1:T(8,128)S(1)} %copy.286) | copy-start | bytes 76804
  1310.0 403.3 %copy-start.17 = (f32[320,64]{0,1:T(8,128)}, f32[320,64]{0,1:T(8,128)S(1)}, u32[]{:S(2)}) copy-start(f32[320,64]{0,1:T(8,128)S(1)} %copy.288) | copy-start | bytes 245764
  1310.8 522.6 %copy-start.10 = (bf16[1280,320]{0,1:T(8,128)(2,1)S(1)}, bf16[1280,320]{0,1:T(8,128)(2,1)}, u32[]{:S(2)}) copy-start(bf16[1280,320]{0,1:T(8,128)(2,1)} %param.47) | copy-start | bytes 2457604
  1713.4 268.0 %copy-start.5 = (bf16[384,2560]{1,0:T(8,128)(2,1)S(1)}, bf16[384,2560]{1,0:T(8,128)(2,1)}, u32[]{:S(2)}) copy-start(bf16[384,2560]{1,0:T(8,128)(2,1)} %param.35) | copy-start | bytes 5898244
  1713.4 268.0 %copy-start.21 = (f32[2560]{0:T(1024)S(1)}, f32[2560]{0:T(1024)}, u32[]{:S(2)}) copy-start(f32[2560]{0:T(1024)} %copy-done.20) | copy-start | bytes 30724
  1713.4 268.0 %copy-start.46 = (f32[384]{0:T(512)S(1)}, f32[384]{0:T(512)}, u32[]{:S(2)}) copy-start(f32[384]{0:T(512)} %copy-done.45) | copy-start | bytes 4612
  1713.4 311.2 %copy-start.79 = (bf16[320]{0:T(512)(128)(2,1)S(1)}, bf16[320]{0:T(512)(128)(2,1)}, u32[]{:S(2)}) copy-start(bf16[320]{0:T(512)(128)(2,1)} %param.39) | copy-start | bytes 1924
  1713.4 311.2 %copy-start.90 = (f32[320]{0:T(512)S(1)}, f32[320]{0:T(512)}, u32[]{:S(2)}) copy-start(f32[320]{0:T(512)} %param.48) | copy-start | bytes 3844
  1713.4 311.2 %copy-start.91 = (f32[320]{0:T(512)S(1)}, f32[320]{0:T(512)}, u32[]{:S(2)}) copy-start(f32[320]{0:T(512)} %param.57) | copy-start | bytes 3844
  1713.4 311.9 %copy-start.88 = (f32[3,20]{1,0:T(4,128)S(1)}, f32[3,20]{1,0:T(4,128)}, u32[]{:S(2)}) copy-start(f32[3,20]{1,0:T(4,128)} %param.54) | copy-start | bytes 724
  1713.4 311.9 %copy-start.89 = (f32[3,20]{1,0:T(4,128)S(1)}, f32[3,20]{1,0:T(4,128)}, u32[]{:S(2)}) copy-start(f32[3,20]{1,0:T(4,128)} %param.63) | copy-start | bytes 724
  1713.5 418.5 %copy-start.81 = (pred[384]{0:T(512)(128)(4,1)S(1)}, pred[384]{0:T(512)(128)(4,1)}, u32[]{:S(2)}) copy-start(pred[384]{0:T(512)(128)(4,1)} %copy-done.80) | copy-start | bytes 1156
  (73 other events, 874.5 us)
Sparse Core Ops, SparseCore 0:
  47.6 81.4 all-gather.7
  130.8 121.0 all-gather.9
  253.5 65.1 all-gather.11
  320.9 81.8 all-gather.13
  1022.6 28.2 reduce-scatter.16
  1087.3 28.4 reduce-scatter.26
  1118.6 31.6 reduce-scatter.22
  1153.2 31.4 reduce-scatter.24
  1187.2 508.9 all-reduce.38
  1699.0 134.3 reduce-scatter.20
  1836.5 144.8 reduce-scatter.18
  1984.3 147.5 reduce-scatter.14
where the time goes:
time: 2160 us; the launch traced here: 2140 us
  waiting for transfers between devices  869 us (40%)
  matrix products  513 us (24%)
  other arithmetic  276 us (13%)
  local copies, waits for them, and re-layouts  274 us (13%)
  blocking collectives  183 us (8%)
    unnamed x16, waiting for transfers between devices  387 us
    dot_general x18, matrix products, ssd_block(): inside = jnp.einsum('ijh,jhp->ihp', mixing, inner_vals, precision=PRECISE)  182 us
    reduce_scatter x1, waiting for transfers between devices, body(): lax.psum_scatter(contract_cols(d_both, inner_flat) + contract_cols(d_step...  143 us
    reduce_scatter x1, waiting for transfers between devices, body(): lax.psum_scatter(grad_output, 'fsdp', scatter_dimension=1, tiled=True)  120 us
    reduce_scatter x1, waiting for transfers between devices, body(): lax.psum_scatter(jnp.dot(normed_gated, output_all, preferred_element_type...  106 us
    all_gather x1, waiting for transfers between devices, body(): lax.all_gather(proj_inner, 'fsdp', axis=0, tiled=True)  95.3 us
    dynamic_update_slice x30, other arithmetic, ssd_scan(): lax.scan(advance, (start_state, jnp.int32(-1)), stacked)  81.1 us
    dot_general x4, matrix products, contract_cols(): lax.dot_general(left_mat, right_mat, (((1,), (1,)), ((), ())), preferred_...  68.8 us
  transfers between devices with their start and end apart: 12, of which 6 were waited for; matrix products, arithmetic and copies ran while one was open for 31% of the time, Pallas kernels for 0%

commit v1 on v0

v1 whole, which is shorter than its diff:
```python
import functools
import jax
import jax.numpy as jnp
from jax import lax
from jax.experimental import pallas as pl
from jax.experimental.layout import Layout, with_layout_constraint
from jax.experimental.pallas import tpu as pltpu
from jax.sharding import PartitionSpec as P

N = 128
Q = 256
LANE = 128
BLK = 128
NEG = -1e30
F32 = jnp.float32
BF16 = jnp.bfloat16
VMEM_CAP = 56 << 20


def mm(left, right):
    return lax.dot_general(left, right, (((1,), (0,)), ((), ())), preferred_element_type=F32)


def mm_nt(left, right):
    return lax.dot_general(left, right, (((1,), (1,)), ((), ())), preferred_element_type=F32)


def mm_exact(left, right):
    return lax.dot_general(
        left,
        right,
        (((1,), (0,)), ((), ())),
        precision=lax.Precision.HIGHEST,
        preferred_element_type=F32,
    )


def split_two(value):
    high = value.astype(BF16)
    low = (value - high.astype(F32)).astype(BF16)
    return high, low


def spread_heads(value, expand):
    high = value.astype(BF16).astype(F32)
    rest = value - high
    mid = rest.astype(BF16).astype(F32)
    low = rest - mid
    packed = high + pltpu.roll(mid, 32, 1) + pltpu.roll(low, 64, 1)
    return mm(packed.astype(BF16), expand)


def iota2(shape, axis):
    return lax.broadcasted_iota(jnp.int32, shape, axis)


def step_terms(small_ref, meta_ref, hp_ref):
    lane_on = hp_ref[2:3, :]
    pre = small_ref[...] + hp_ref[0:1, :]
    pre = pre * lane_on
    steps = (jnp.maximum(pre, 0.0) + jnp.log1p(jnp.exp(-jnp.abs(pre)))) * lane_on
    logs = steps * hp_ref[1:2, :]
    size = logs.shape[0]
    lower = (iota2((size, size), 0) >= iota2((size, size), 1)).astype(F32)
    cum = mm_exact(lower, logs)
    last = cum[size - 1 : size, :]
    into = jnp.exp(cum) * meta_ref[:, 4:5] * lane_on
    tail = jnp.exp(last - cum) * meta_ref[:, 5:6] * lane_on
    keep = jnp.exp(last) * meta_ref[size - 1 : size, 4:5] * lane_on
    return pre, steps, cum, into, tail, keep


def ssd_fwd_kernel(
    heads,
    raw_ref,
    small_ref,
    bc_raw_ref,
    meta_ref,
    metar_ref,
    taps_ref,
    taps_bc_ref,
    hp_ref,
    skip_ref,
    expand_ref,
    y_ref,
    st_ref,
    bc_ref,
    state,
    tail_rows,
    tail_bc,
    window,
    col_cum,
    row_cum,
    bias,
    scores,
    step_x,
    into_x,
    tail_x,
    keep_x,
    masks,
    b_turned,
):
    chunk = pl.program_id(0)

    @pl.when(chunk == 0)
    def _():
        state[...] = jnp.zeros_like(state)
        tail_rows[...] = jnp.zeros_like(tail_rows)
        tail_bc[...] = jnp.zeros_like(tail_bc)

    st_ref[0] = state[...]
    _, steps, cum, into, tail, keep = step_terms(small_ref, meta_ref, hp_ref)
    row_cum[...] = cum.T
    for head in range(heads):
        col_cum[:, head * LANE : (head + 1) * LANE] = jnp.broadcast_to(
            cum[:, head : head + 1], (Q, LANE)
        )
    expand = expand_ref[...]
    step_x[...] = spread_heads(steps, expand)
    into_x[...] = spread_heads(into, expand)
    tail_x[...] = spread_heads(tail, expand)
    keep_x[...] = spread_heads(jnp.broadcast_to(keep, (8, LANE)), expand)
    for offset in range(1, 4):
        masks[offset - 1] = jnp.broadcast_to(meta_ref[:, offset : offset + 1], (Q, LANE))
    same = (meta_ref[:, 0:1] == metar_ref[0, 0:1, :]) & (
        iota2((Q, Q), 0) >= iota2((Q, Q), 1)
    )
    bias[...] = jnp.where(same, 0.0, NEG)
    for at in range(0, 2 * N, LANE):
        lanes = slice(at, at + LANE)
        window[0:8, :] = tail_bc[:, lanes]
        current = bc_raw_ref[:, lanes]
        window[8 : 8 + Q, :] = current
        conv = taps_bc_ref[4:5, lanes] + taps_bc_ref[3:4, lanes] * current
        for offset in range(1, 4):
            conv = conv + taps_bc_ref[3 - offset : 4 - offset, lanes] * (
                masks[offset - 1] * window[8 - offset : 8 - offset + Q, :]
            )
        bc_ref[:, lanes] = (conv * jax.nn.sigmoid(conv)).astype(BF16)
    tail_bc[...] = bc_raw_ref[Q - 8 : Q, :]
    b_rows = bc_ref[:, :N]
    c_rows = bc_ref[:, N:]
    scores[...] = mm_nt(c_rows, b_rows)
    b_turned[...] = b_rows.astype(F32).T.astype(BF16)
    first = iota2((Q, LANE), 1) < LANE // 2

    def pair(index, _):
        lanes = pl.ds(pl.multiple_of(index * LANE, LANE), LANE)
        window[0:8, :] = tail_rows[:, lanes]
        current = raw_ref[:, lanes]
        window[8 : 8 + Q, :] = current
        conv = taps_ref[4:5, lanes] + taps_ref[3:4, lanes] * current
        for offset in range(1, 4):
            conv = conv + taps_ref[3 - offset : 4 - offset, lanes] * (
                masks[offset - 1] * window[8 - offset : 8 - offset + Q, :]
            )
        vals = conv * jax.nn.sigmoid(conv)
        scaled = (vals * step_x[:, lanes]).astype(BF16)
        zero = jnp.zeros_like(scaled)
        own = (jnp.where(first, scaled, zero), jnp.where(first, zero, scaled))
        held = state[:, lanes]
        base = into_x[:, lanes] * mm(c_rows, held.astype(BF16)) + skip_ref[0:1, lanes] * vals
        for low in range(0, Q, BLK):
            width = low + BLK
            total = base[low:width, :]
            for which in range(2):
                head = index * 2 + which
                across = row_cum[pl.ds(head, 1), :][:, :width]
                down = col_cum[low:width, pl.ds(pl.multiple_of(head * LANE, LANE), LANE)]
                down = jnp.concatenate([down] * (width // LANE), axis=1)
                decays = jnp.exp(down - across + bias[low:width, :width])
                mixing = (decays * scores[low:width, :width]).astype(BF16)
                total = total + mm(mixing, own[which][:width, :])
            y_ref[low:width, lanes] = total
        weighted = (tail_x[:, lanes] * scaled.astype(F32)).astype(BF16)
        state[:, lanes] = held * keep_x[0:1, lanes] + mm(b_turned[...], weighted)
        return 0

    lax.fori_loop(0, heads // 2, pair, 0)
    tail_rows[...] = raw_ref[Q - 8 : Q, :]


def ssd_bwd_kernel(
    heads,
    raw_ref,
    halo_ref,
    small_ref,
    bc_ref,
    meta_ref,
    meta_next_ref,
    metar_ref,
    taps_ref,
    hp_ref,
    skip_ref,
    expand_ref,
    gather_ref,
    y_ref,
    dy_ref,
    st_ref,
    dx_ref,
    ddt_ref,
    dbc_ref,
    dtaps_ref,
    dhp_ref,
    dskip_ref,
    small_turned_ref,
    dstate,
    next_rows,
    carried,
    window,
    dwindow,
    col_cum,
    row_cum,
    bias,
    scores,
    dscores,
    step_x,
    into_x,
    tail_x,
    keep_x,
    masks,
    c_turned,
    sums,
    dbc,
):
    chunk = pl.program_id(0)

    @pl.when(chunk == 0)
    def _():
        dstate[...] = jnp.zeros_like(dstate)
        next_rows[...] = jnp.zeros_like(next_rows)
        carried[...] = jnp.zeros_like(carried)
        dtaps_ref[...] = jnp.zeros_like(dtaps_ref)
        dhp_ref[...] = jnp.zeros_like(dhp_ref)
        dskip_ref[...] = jnp.zeros_like(dskip_ref)

    small_turned_ref[...] = small_ref[...].T
    pre, steps, cum, into, tail, keep = step_terms(small_ref, meta_ref, hp_ref)
    row_cum[...] = cum.T
    for head in range(heads):
        col_cum[:, head * LANE : (head + 1) * LANE] = jnp.broadcast_to(
            cum[:, head : head + 1], (Q, LANE)
        )
    expand = expand_ref[...]
    step_x[...] = spread_heads(steps, expand)
    into_x[...] = spread_heads(into, expand)
    tail_x[...] = spread_heads(tail, expand)
    keep_x[...] = spread_heads(jnp.broadcast_to(keep, (8, LANE)), expand)
    for offset in range(1, 4):
        masks[offset - 1, :Q] = jnp.broadcast_to(meta_ref[:, offset : offset + 1], (Q, LANE))
        masks[offset - 1, Q:] = jnp.broadcast_to(meta_next_ref[:, offset : offset + 1], (8, LANE))
    same = (meta_ref[:, 0:1] == metar_ref[0, 0:1, :]) & (
        iota2((Q, Q), 0) <= iota2((Q, Q), 1)
    )
    bias[...] = jnp.where(same, 0.0, NEG)
    b_rows = bc_ref[:, :N]
    c_rows = bc_ref[:, N:]
    scores[...] = mm_nt(b_rows, c_rows)
    dscores[...] = jnp.zeros_like(dscores)
    c_turned[...] = c_rows.astype(F32).T.astype(BF16)
    sums[...] = jnp.zeros_like(sums)
    dbc[...] = jnp.zeros_like(dbc)
    carry_high, carry_low = split_two(carried[...])
    gather_all = gather_ref[...]
    from_next = mm(carry_high, gather_all) + mm(carry_low, gather_all)
    first = iota2((Q, LANE), 1) < LANE // 2

    def pair(index, _):
        lanes = pl.ds(pl.multiple_of(index * LANE, LANE), LANE)
        window[0:8, :] = halo_ref[:, lanes]
        current = raw_ref[:, lanes]
        window[8 : 8 + Q, :] = current
        conv = taps_ref[4:5, lanes] + taps_ref[3:4, lanes] * current
        for offset in range(1, 4):
            conv = conv + taps_ref[3 - offset : 4 - offset, lanes] * (
                masks[offset - 1, :Q] * window[8 - offset : 8 - offset + Q, :]
            )
        gate = jax.nn.sigmoid(conv)
        vals = conv * gate
        step_here = step_x[:, lanes]
        scaled = (vals * step_here).astype(BF16)
        skip = skip_ref[0:1, lanes]
        dy = dy_ref[:, lanes]
        dy_half = dy.astype(BF16)
        zero = jnp.zeros_like(scaled)
        own = (jnp.where(first, scaled, zero), jnp.where(first, zero, scaled))
        own_dy = (jnp.where(first, dy_half, zero), jnp.where(first, zero, dy_half))
        dheld = dstate[:, lanes]
        dheld_half = dheld.astype(BF16)
        tail_here = tail_x[:, lanes]
        base = tail_here * mm(b_rows, dheld_half)
        pieces = []
        for low in range(0, Q, BLK):
            high = low + BLK
            total = base[low:high, :]
            for which in range(2):
                head = index * 2 + which
                across = row_cum[pl.ds(head, 1), :][:, low:]
                down = col_cum[low:high, pl.ds(pl.multiple_of(head * LANE, LANE), LANE)]
                down = jnp.concatenate([down] * ((Q - low) // LANE), axis=1)
                decays = jnp.exp(across - down + bias[low:high, low:])
                mixing = (decays * scores[low:high, low:]).astype(BF16)
                total = total + mm(mixing, own_dy[which][low:, :])
                dmix = mm_nt(own[which][low:high, :], dy_half[low:, :])
                dscores[low:high, low:] += dmix * decays
            pieces.append(total)
        dscaled = jnp.concatenate(pieces, axis=0)
        held = st_ref[0, :, lanes]
        edy = (into_x[:, lanes] * dy).astype(BF16)
        weighted = (tail_here * scaled.astype(F32)).astype(BF16)
        dbc[:, :N] += mm_nt(weighted, dheld_half)
        dbc[:, N:] += mm_nt(edy, held.astype(BF16))
        gather = gather_ref[lanes, :]
        balance = dy_half.astype(F32) * (y_ref[:, lanes] - skip * vals) - scaled.astype(
            F32
        ) * dscaled
        part_high, part_low = split_two(balance)
        sums[0] += mm(part_high, gather) + mm(part_low, gather)
        part_high, part_low = split_two(vals * dscaled)
        sums[1] += mm(part_high, gather) + mm(part_low, gather)
        dskip_ref[0:1, lanes] += jnp.sum(dy * vals, axis=0, keepdims=True)
        dheld_new = keep_x[0:1, lanes] * dheld + mm(c_turned[...], edy)
        dstate[:, lanes] = dheld_new
        carried[0:1, lanes] = jnp.sum(dheld_new * held, axis=0, keepdims=True)
        dvals = step_here * dscaled + skip * dy
        dconv = dvals * (gate * (1.0 + conv * (1.0 - gate)))
        dwindow[0:Q, :] = dconv
        dwindow[Q : Q + 8, :] = next_rows[:, lanes]
        next_rows[:, lanes] = dconv[0:8, :]
        dtaps_ref[4:5, lanes] += jnp.sum(dconv, axis=0, keepdims=True)
        dtaps_ref[3:4, lanes] += jnp.sum(dconv * current, axis=0, keepdims=True)
        draw = taps_ref[3:4, lanes] * dconv
        for offset in range(1, 4):
            shifted = masks[offset - 1, :Q] * window[8 - offset : 8 - offset + Q, :]
            dtaps_ref[3 - offset : 4 - offset, lanes] += jnp.sum(
                dconv * shifted, axis=0, keepdims=True
            )
            draw = draw + taps_ref[3 - offset : 4 - offset, lanes] * (
                masks[offset - 1, offset : offset + Q] * dwindow[offset : offset + Q, :]
            )
        dx_ref[:, lanes] = draw.astype(BF16)
        return 0

    lax.fori_loop(0, heads // 2, pair, 0)
    dscores_now = dscores[...]
    d_b = dbc[:, :N] + mm(dscores_now.astype(BF16), c_rows)
    d_c = dbc[:, N:] + mm(dscores_now.T.astype(BF16), b_rows)
    dbc_ref[:N, :] = d_b.T
    dbc_ref[N:, :] = d_c.T
    dcum = sums[0] + jnp.where(iota2((Q, LANE), 0) == Q - 1, from_next[0:1, :], 0.0)
    upper = (iota2((Q, Q), 0) <= iota2((Q, Q), 1)).astype(F32)
    dlogs = mm_exact(upper, dcum)
    dsteps = (dlogs * hp_ref[1:2, :] + sums[1]) * jax.nn.sigmoid(pre) * hp_ref[2:3, :]
    ddt_ref[...] = dsteps.T
    dhp_ref[0:1, :] += jnp.sum(dsteps, axis=0, keepdims=True)
    dhp_ref[1:2, :] += jnp.sum(dlogs * steps, axis=0, keepdims=True)


def head_tables(heads):
    width = heads * (LANE // 2)
    owner = jnp.arange(width) // (LANE // 2)
    slot = jnp.arange(LANE)
    expand = ((slot % 32)[:, None] == owner[None, :]) & (slot < 96)[:, None]
    gather = owner[:, None] == slot[None, :]
    return expand.astype(BF16), gather.astype(BF16)


def segment_tables(segment):
    length = segment.shape[0]
    chunks = length // Q
    columns = [segment.astype(F32)]
    for offset in range(1, 4):
        earlier = jnp.concatenate(
            [jnp.full((offset,), -1, jnp.int32), segment[: length - offset]], axis=0
        )
        columns.append((earlier == segment).astype(F32))
    by_chunk = segment.reshape(chunks, Q)
    last = by_chunk[:, Q - 1]
    before = jnp.concatenate([jnp.full((1,), -1, jnp.int32), last[: chunks - 1]], axis=0)
    columns.append((by_chunk == before[:, None]).astype(F32).reshape(length))
    columns.append((by_chunk == last[:, None]).astype(F32).reshape(length))
    meta = jnp.pad(jnp.stack(columns, axis=1), ((0, 0), (0, LANE - len(columns))))
    meta_rows = jnp.broadcast_to(by_chunk.astype(F32)[:, None, :], (chunks, 8, Q))
    return meta, meta_rows


def head_rows(head_params):
    heads = head_params.shape[1]
    rates = -jnp.exp(head_params[1])
    table = jnp.stack([head_params[0], rates, jnp.ones_like(rates)], axis=0)
    return jnp.pad(table, ((0, 5), (0, LANE - heads)))


def time_like(seconds):
    return pl.CostEstimate(
        flops=int(seconds * 1.1e15), bytes_accessed=int(seconds * 3.4e12), transcendentals=0
    )


def full_spec(shape):
    return pl.BlockSpec(shape, lambda c: (0,) * len(shape))


def ssd_forward(raw, bc_raw, meta, meta_rows, taps, taps_bc, hp, skip, expand, heads):
    length = raw.shape[0]
    width = heads * (LANE // 2)
    chunks = length // Q
    small_at = width // LANE
    return pl.pallas_call(
        functools.partial(ssd_fwd_kernel, heads),
        grid=(chunks,),
        out_shape=(
            jax.ShapeDtypeStruct((length, width), F32),
            jax.ShapeDtypeStruct((chunks, N, width), F32),
            jax.ShapeDtypeStruct((length, 2 * N), BF16),
        ),
        in_specs=[
            pl.BlockSpec((Q, width), lambda c: (c, 0)),
            pl.BlockSpec((Q, LANE), lambda c: (c, small_at)),
            pl.BlockSpec((Q, 2 * N), lambda c: (c, 0)),
            pl.BlockSpec((Q, LANE), lambda c: (c, 0)),
            pl.BlockSpec((1, 8, Q), lambda c: (c, 0, 0)),
            full_spec((8, width)),
            full_spec((8, 2 * N)),
            full_spec((8, LANE)),
            full_spec((8, width)),
            full_spec((LANE, width)),
        ],
        out_specs=(
            pl.BlockSpec((Q, width), lambda c: (c, 0)),
            pl.BlockSpec((1, N, width), lambda c: (c, 0, 0)),
            pl.BlockSpec((Q, 2 * N), lambda c: (c, 0)),
        ),
        scratch_shapes=[
            pltpu.VMEM((N, width), F32),
            pltpu.VMEM((8, width), F32),
            pltpu.VMEM((8, 2 * N), F32),
            pltpu.VMEM((Q + 8, LANE), F32),
            pltpu.VMEM((Q, heads * LANE), F32),
            pltpu.VMEM((LANE, Q), F32),
            pltpu.VMEM((Q, Q), F32),
            pltpu.VMEM((Q, Q), F32),
            pltpu.VMEM((Q, width), F32),
            pltpu.VMEM((Q, width), F32),
            pltpu.VMEM((Q, width), F32),
            pltpu.VMEM((8, width), F32),
            pltpu.VMEM((3, Q, LANE), F32),
            pltpu.VMEM((N, Q), BF16),
        ],
        compiler_params=pltpu.CompilerParams(vmem_limit_bytes=VMEM_CAP),
        cost_estimate=time_like(37e-6 * length * heads / 30720),
        name="ssd_fwd",
    )(raw, raw, bc_raw, meta, meta_rows, taps, taps_bc, hp, skip, expand)


def ssd_backward(raw, bc, meta, meta_rows, taps, hp, skip, expand, gather, y, dy, states, heads):
    length = raw.shape[0]
    width = heads * (LANE // 2)
    chunks = length // Q
    small_at = width // LANE
    per = Q // 8

    def at(c):
        return chunks - 1 - c

    return pl.pallas_call(
        functools.partial(ssd_bwd_kernel, heads),
        grid=(chunks,),
        out_shape=(
            jax.ShapeDtypeStruct((length, width), BF16),
            jax.ShapeDtypeStruct((LANE, length), F32),
            jax.ShapeDtypeStruct((2 * N, length), F32),
            jax.ShapeDtypeStruct((8, width), F32),
            jax.ShapeDtypeStruct((8, LANE), F32),
            jax.ShapeDtypeStruct((8, width), F32),
            jax.ShapeDtypeStruct((LANE, length), F32),
        ),
        in_specs=[
            pl.BlockSpec((Q, width), lambda c: (at(c), 0)),
            pl.BlockSpec((8, width), lambda c: (jnp.maximum(at(c) * per - 1, 0), 0)),
            pl.BlockSpec((Q, LANE), lambda c: (at(c), small_at)),
            pl.BlockSpec((Q, 2 * N), lambda c: (at(c), 0)),
            pl.BlockSpec((Q, LANE), lambda c: (at(c), 0)),
            pl.BlockSpec(
                (8, LANE), lambda c: (jnp.minimum((at(c) + 1) * per, chunks * per - 1), 0)
            ),
            pl.BlockSpec((1, 8, Q), lambda c: (at(c), 0, 0)),
            full_spec((8, width)),
            full_spec((8, LANE)),
            full_spec((8, width)),
            full_spec((LANE, width)),
            full_spec((width, LANE)),
            pl.BlockSpec((Q, width), lambda c: (at(c), 0)),
            pl.BlockSpec((Q, width), lambda c: (at(c), 0)),
            pl.BlockSpec((1, N, width), lambda c: (at(c), 0, 0)),
        ],
        out_specs=(
            pl.BlockSpec((Q, width), lambda c: (at(c), 0)),
            pl.BlockSpec((LANE, Q), lambda c: (0, at(c))),
            pl.BlockSpec((2 * N, Q), lambda c: (0, at(c))),
            full_spec((8, width)),
            full_spec((8, LANE)),
            full_spec((8, width)),
            pl.BlockSpec((LANE, Q), lambda c: (0, at(c))),
        ),
        scratch_shapes=[
            pltpu.VMEM((N, width), F32),
            pltpu.VMEM((8, width), F32),
            pltpu.VMEM((8, width), F32),
            pltpu.VMEM((Q + 8, LANE), F32),
            pltpu.VMEM((Q + 8, LANE), F32),
            pltpu.VMEM((Q, heads * LANE), F32),
            pltpu.VMEM((LANE, Q), F32),
            pltpu.VMEM((Q, Q), F32),
            pltpu.VMEM((Q, Q), F32),
            pltpu.VMEM((Q, Q), F32),
            pltpu.VMEM((Q, width), F32),
            pltpu.VMEM((Q, width), F32),
            pltpu.VMEM((Q, width), F32),
            pltpu.VMEM((8, width), F32),
            pltpu.VMEM((3, Q + 8, LANE), F32),
            pltpu.VMEM((N, Q), BF16),
            pltpu.VMEM((2, Q, LANE), F32),
            pltpu.VMEM((Q, 2 * N), F32),
        ],
        compiler_params=pltpu.CompilerParams(vmem_limit_bytes=VMEM_CAP),
        cost_estimate=time_like(69e-6 * length * heads / 30720),
        name="ssd_bwd",
    )(
        raw, raw, raw, bc, meta, meta, meta_rows, taps, hp, skip, expand, gather, y, dy, states
    )


def dn_kernel(step, dz_ref, dx_ref, side_ref, gate_ref, inner_ref, normed_ref, out_ref, sums_ref, turned):
    width = dz_ref.shape[1]

    @pl.when(pl.program_id(0) == 0)
    def _():
        turned[...] = side_ref[...].T.astype(BF16)

    gate = gate_ref[...]
    inner = inner_ref[:, :width]
    side = inner_ref[:, width:]
    sums_ref[...] = jnp.zeros_like(sums_ref)

    def rows(index, _):
        at = pl.ds(pl.multiple_of(index * step, step), step)
        total = mm_nt(dz_ref[at, :], gate) + mm_nt(dx_ref[at, :], inner)
        total = total + mm_nt(turned[at, :], side)
        out_ref[at, :] = total.astype(BF16)
        sums_ref[0:1, :] += jnp.sum(total * normed_ref[at, :].astype(F32), axis=0, keepdims=True)
        return 0

    lax.fori_loop(0, dz_ref.shape[0] // step, rows, 0)


def d_normed_half(d_z, d_x, d_side, gate_all, x_all, normed, which, step=768, tile=256):
    length, width = d_z.shape
    model = gate_all.shape[0]
    half = model // 2
    first = which * half // tile
    return pl.pallas_call(
        functools.partial(dn_kernel, step),
        grid=(half // tile,),
        out_shape=(
            jax.ShapeDtypeStruct((length, half), BF16),
            jax.ShapeDtypeStruct((8, half), F32),
        ),
        in_specs=[
            full_spec((length, width)),
            full_spec((length, width)),
            full_spec((LANE, length)),
            pl.BlockSpec((tile, width), lambda n: (n + first, 0)),
            pl.BlockSpec((tile, width + LANE), lambda n: (n + first, 0)),
            pl.BlockSpec((length, tile), lambda n: (0, n + first)),
        ],
        out_specs=(
            pl.BlockSpec((length, tile), lambda n: (0, n)),
            pl.BlockSpec((8, tile), lambda n: (0, n)),
        ),
        scratch_shapes=[pltpu.VMEM((length, LANE), BF16)],
        compiler_params=pltpu.CompilerParams(vmem_limit_bytes=VMEM_CAP),
        cost_estimate=time_like(12e-6),
        name="d_normed",
    )(d_z, d_x, d_side, gate_all, x_all, normed)

DI = 5120
STEP = 3
NORM_EPS = 1e-05
BETA_ONE = 0.9
BETA_TWO = 0.95
LEARN_RATE = 0.004
LEARN_SMALL = 0.15
WEIGHT_DECAY = 0.1
ADAM_EPS = 1e-08


def by_rows(value):
    return with_layout_constraint(value, Layout(major_to_minor=(0, 1)))


def silu_act(values):
    return values * jax.nn.sigmoid(values)


def later(row, offset):
    return jnp.pad(row, ((0, 0), (offset, 0)))[:, : row.shape[1]]


def state_act(raw_cols, conv_taps, doc_masks):
    conv = conv_taps[4][:, None] + conv_taps[3][:, None] * raw_cols
    for offset in range(1, 4):
        conv = conv + conv_taps[3 - offset][:, None] * (
            doc_masks[offset - 1][None, :] * later(raw_cols, offset)
        )
    return silu_act(conv)


def contract_rows(left_mat, right_mat):
    return lax.dot_general(
        left_mat, right_mat, (((0,), (0,)), ((), ())), preferred_element_type=F32
    )


def adamw_step(weight, gradient, first_moment, second_moment, decay_factor, learn_rate):
    new_first = BETA_ONE * first_moment + (1.0 - BETA_ONE) * gradient
    new_second = BETA_TWO * second_moment + (1.0 - BETA_TWO) * gradient * gradient
    first_hat = new_first / (1.0 - BETA_ONE**STEP)
    second_hat = new_second / (1.0 - BETA_TWO**STEP)
    weight_f = weight.astype(F32)
    updated = weight_f - learn_rate * (
        first_hat / (jnp.sqrt(second_hat) + ADAM_EPS) + decay_factor * weight_f
    )
    return (updated.astype(weight.dtype), new_first, new_second)


def swap(value, distance, size):
    return lax.ppermute(value, "tp", [(at, at ^ distance) for at in range(size)])


def tied(*values):
    return lax.optimization_barrier(values)


def gather_parts(value, size):
    if size != 4:
        return [value] + [swap(value, k, size) for k in range(1, size)]
    half = value.shape[0] // 2
    one, two = swap(value, 1, size), swap(value, 2, size)
    far = jnp.concatenate([swap(two[:half], 1, size), swap(one[half:], 2, size)], axis=0)
    return [value, one, two, far]


def scatter_start(left, right, rows, index, size):
    def block(value, distance):
        return lax.dynamic_slice_in_dim(value, (index ^ distance) * rows, rows, 0)

    sent, kept = [], []
    for half, near in ((left, 1), (right, 2)):
        if size == 4:
            pair = jnp.concatenate([block(half, 3), block(half, near)], axis=0)
            sent.append(swap(pair, near, size))
            kept.append((block(half, 3 - near), block(half, 0)))
        else:
            sent.append([swap(block(half, k), k, size) for k in range(1, size)])
            kept.append(block(half, 0))
    return sent, kept


def scatter_middle(sent, kept, rows, size):
    if size != 4:
        return sent, kept
    passed = [
        (kept[at][0].astype(F32) + sent[at][:rows].astype(F32)).astype(BF16) for at in range(2)
    ]
    own = [kept[at][1].astype(F32) + sent[at][rows:].astype(F32) for at in range(2)]
    return passed, own


def scatter_last(passed, size):
    if size != 4:
        return passed[0] + passed[1]
    return [swap(passed[0], 2, size), swap(passed[1], 1, size)]


def scatter_end(own, last):
    each = len(last) // 2
    totals = []
    for at in range(2):
        total = own[at].astype(F32)
        for piece in last[at * each : (at + 1) * each]:
            total = total + piece.astype(F32)
        totals.append(total)
    return jnp.concatenate(totals, axis=1)


def all_sum(value, size):
    distance = 1
    while distance < size:
        value = value + swap(value, distance, size)
        distance *= 2
    return value


def fsdp_swap(value, distance, size):
    return lax.ppermute(value, "fsdp", [(at, at ^ distance) for at in range(size)])


def gather_by_swaps(value, index, size):
    whole = jnp.zeros((size,) + value.shape, value.dtype)
    for distance in range(size):
        piece = value if distance == 0 else fsdp_swap(value, distance, size)
        whole = lax.dynamic_update_slice(
            whole, piece[None], (index ^ distance, jnp.int32(0), jnp.int32(0))
        )
    return whole


def pair_sum(value, index, size):
    blocks = value.reshape(size // 2, 2, value.shape[0] // size, value.shape[1])
    core = index % 2
    away = lax.dynamic_slice_in_dim(blocks, 1 - core, 1, 1)[:, 0]
    own = lax.dynamic_slice_in_dim(blocks, core, 1, 1)[:, 0]
    return (own.astype(F32) + fsdp_swap(away, 1, size).astype(F32)).astype(value.dtype)


def chip_scatter(value, size):
    groups = [list(range(core, size, 2)) for core in range(2)]
    flat = value.reshape(value.shape[0] * value.shape[1], value.shape[2])
    return lax.psum_scatter(
        flat, "fsdp", scatter_dimension=0, axis_index_groups=groups, tiled=True
    ).astype(F32)


def chip_sum(value, index, size):
    chip = index // 2

    def block(distance):
        return lax.dynamic_slice_in_dim(value, chip ^ distance, 1, 0)[0]

    total = block(0).astype(F32)
    for distance in range(1, size // 2):
        total = total + fsdp_swap(block(distance), 2 * distance, size).astype(F32)
    return total


def pad_cols(value, width):
    return jnp.pad(value, ((0, 0), (0, width - value.shape[1])))


def body(
    block_in,
    cotangent,
    segment_ids,
    group_fill,
    input_gain,
    proj_inner,
    proj_step,
    proj_state,
    conv_inner,
    conv_state,
    head_params,
    mixer_gain,
    proj_output,
    *moments,
):
    tp_size = lax.axis_size("tp")
    fsdp_size = lax.axis_size("fsdp")
    tp_index = lax.axis_index("tp")
    fsdp_index = lax.axis_index("fsdp")
    own_rows, model = block_in.shape
    group_rows = own_rows * tp_size
    shard, _, width = proj_inner.shape
    heads = proj_step.shape[1]
    state_cols = proj_state.shape[1]
    segment = segment_ids[0]
    filled = group_fill[0]

    small_values = jnp.concatenate(
        [conv_inner.reshape(-1), conv_state.reshape(-1), mixer_gain], axis=0
    )
    small_count = small_values.shape[0]
    inner_n, state_n = conv_inner.size, conv_state.size
    small_cols = -(-(small_count + 3 * heads) // shard)
    small_block = jnp.pad(small_values, (0, small_cols * shard - small_count)).reshape(
        shard, small_cols
    )
    used = heads + state_cols
    side = pad_cols(
        jnp.concatenate([proj_step, proj_state, input_gain[:, None], small_block], axis=1), LANE
    )
    x_local = jnp.concatenate([proj_inner[:, 1, :], side], axis=1)
    x_all = lax.all_gather(x_local, "fsdp", axis=0, tiled=True)
    turned = jnp.concatenate(
        [proj_state.T, jnp.pad(conv_state.reshape(1, -1), ((0, 15), (0, shard - state_n)))], axis=0
    )
    turned = lax.all_gather(turned, "tp", axis=0, tiled=False)
    state_local = turned[:, :state_cols].reshape(tp_size * state_cols, shard).T
    conv_row = jnp.pad(
        turned[:, state_cols, :state_n].reshape(1, tp_size * state_n),
        ((0, 15), (0, tp_size * (state_cols - state_n))),
    )
    gate_all = lax.all_gather(proj_inner[:, 0, :], "fsdp", axis=0, tiled=True)
    block_sent, state_local = tied(block_in, state_local)
    row_parts = [by_rows(part) for part in gather_parts(block_sent, tp_size)]
    state_packed = gather_by_swaps(
        jnp.concatenate([state_local, conv_row], axis=0), fsdp_index, fsdp_size
    )
    out_local, *row_parts = tied(proj_output.T, *row_parts)
    out_all = lax.all_gather(out_local, "fsdp", axis=0, tiled=True)
    state_all = state_packed[:, :shard].reshape(model, tp_size * state_cols)
    taps_bc = (
        state_packed[:, shard, : tp_size * state_n]
        .reshape(fsdp_size, tp_size, 5, -1)
        .transpose(2, 1, 0, 3)
        .reshape(5, tp_size * state_cols)
        .astype(F32)
    )
    positions = tp_index * own_rows + jnp.arange(own_rows, dtype=jnp.int32)
    live_rows = (positions < filled)[:, None]
    block_f = block_in.astype(F32)
    cot_f = cotangent.astype(F32)
    own_grad, *row_parts = tied(
        jnp.where(live_rows, cot_f, 0.0).astype(BF16), *row_parts
    )
    grad_parts = [by_rows(own_grad)] + [swap(own_grad, k, tp_size) for k in range(1, tp_size)]

    side_all = x_all[:, width:]
    gain_f = side_all[:, used].astype(F32)
    extras = side_all[:, used + 1 : used + 1 + small_cols].reshape(fsdp_size, shard * small_cols)

    def from_owners(flat, rows):
        return flat.reshape(fsdp_size, rows, -1).transpose(1, 0, 2).reshape(rows, -1).astype(F32)

    taps_inner = from_owners(extras[:, :inner_n], 5)
    taps_state = from_owners(extras[:, inner_n : inner_n + state_n], 5)
    mixer_f = from_owners(extras[:, inner_n + state_n : small_count], 1)[0]

    def unit_of(rows):
        rows_f = rows.astype(F32)
        scale = lax.rsqrt(jnp.mean(rows_f * rows_f, axis=1, keepdims=True) + NORM_EPS)
        return rows_f * scale, scale

    def place(parts):
        whole = jnp.zeros((group_rows, model), BF16)
        for distance in range(tp_size):
            whole = lax.dynamic_update_slice(
                whole, parts[distance], ((tp_index ^ distance) * own_rows, jnp.int32(0))
            )
        return whole

    normed = by_rows(
        place([(unit_of(rows)[0] * gain_f[None, :]).astype(BF16) for rows in row_parts])
    )

    raw = mm(normed, x_all)
    bc_raw = mm(normed, state_all)
    meta, meta_rows = segment_tables(segment)
    expand, gather = head_tables(heads)
    taps8 = jnp.pad(taps_inner, ((0, 3), (0, 0)))
    taps_bc8 = jnp.pad(taps_bc, ((0, 3), (0, 0)))
    hp8 = head_rows(head_params)
    skip8 = jnp.broadcast_to(jnp.repeat(head_params[2], LANE // 2)[None, :], (8, width))
    mixed, states, bc = ssd_forward(
        raw, bc_raw, meta, meta_rows, taps8, taps_bc8, hp8, skip8, expand, heads
    )

    mixed, *grad_parts = tied(mixed, *grad_parts)
    group_grad = by_rows(place(grad_parts))

    z_raw = mm(normed, gate_all)
    sig = jax.nn.sigmoid(z_raw)
    gate_act = z_raw * sig
    gated = mixed * gate_act
    square_sum = lax.psum(jnp.sum(gated * gated, axis=1), "tp")
    inv_gate = lax.rsqrt(square_sum / DI + NORM_EPS)[:, None]
    unit_gated = gated * inv_gate
    normed_gated = (unit_gated * mixer_f[None, :]).astype(BF16)
    sum_out = pair_sum(
        contract_rows(group_grad, normed_gated).astype(BF16), fsdp_index, fsdp_size
    )
    group_grad, sum_out = tied(group_grad, sum_out)
    grad_out = chip_scatter(sum_out, fsdp_size)

    d_ng = mm(group_grad, out_all)
    d_unit = d_ng * mixer_f[None, :]
    inner_mean = lax.psum(jnp.sum(d_unit * unit_gated, axis=1), "tp")[:, None] / DI
    grad_mixer = jnp.sum(d_ng * unit_gated, axis=0)
    d_gated = inv_gate * (d_unit - unit_gated * inner_mean)
    d_mixed = d_gated * gate_act
    d_z = (d_gated * mixed * sig * (1.0 + z_raw * (1.0 - sig))).astype(BF16)
    part_gate, grad_out = tied(contract_rows(normed, d_z).astype(BF16), grad_out)
    sum_gate = pair_sum(part_gate, fsdp_index, fsdp_size)

    half = model // 2
    mixed_left = mm_nt(normed_gated, out_all[:half]).astype(BF16)
    mixed_right = mm_nt(normed_gated, out_all[half:]).astype(BF16)
    mixed_sent, mixed_kept = scatter_start(mixed_left, mixed_right, own_rows, tp_index, tp_size)
    d_mixed, sum_gate, mixed_left, mixed_right = tied(d_mixed, sum_gate, mixed_left, mixed_right)
    grad_gate = chip_scatter(sum_gate, fsdp_size)
    d_x, d_dt, d_bc, d_taps, d_heads, d_skip, small_turned = ssd_backward(
        raw,
        bc,
        meta,
        meta_rows,
        taps8,
        hp8,
        skip8,
        expand,
        gather,
        mixed,
        d_mixed,
        states,
        heads,
    )
    d_x, mixed_sent = tied(d_x, mixed_sent)
    mixed_passed, mixed_kept = scatter_middle(mixed_sent, mixed_kept, own_rows, tp_size)
    mixed_last = scatter_last(mixed_passed, tp_size)
    d_x, grad_gate = tied(d_x, grad_gate)
    sum_x = pair_sum(contract_rows(normed, d_x).astype(BF16), fsdp_index, fsdp_size)
    sum_x, d_z = tied(sum_x, d_z)
    grad_x = chip_scatter(sum_x, fsdp_size)

    def state_block(distance):
        return lax.dynamic_slice_in_dim(d_bc, (tp_index ^ distance) * state_cols, state_cols, 0)

    d_state_act = state_block(0)
    for k in range(1, tp_size):
        d_state_act = d_state_act + swap(state_block(k), k, tp_size)
    doc_masks = [meta[:, k] for k in range(1, 4)]
    _, state_back = jax.vjp(
        lambda raw_cols, conv_taps: state_act(raw_cols, conv_taps, doc_masks),
        small_turned[heads:used],
        taps_state,
    )
    d_state_raw, grad_conv_state = state_back(d_state_act)
    d_side = jnp.concatenate([d_dt[:heads], d_state_raw], axis=0)
    d_side = jnp.pad(d_side, ((0, LANE - used), (0, 0)))

    d_normed_left, gains_left = d_normed_half(d_z, d_x, d_side, gate_all, x_all, normed, 0)
    d_normed_right, gains_right = d_normed_half(d_z, d_x, d_side, gate_all, x_all, normed, 1)
    d_normed_left, *mixed_last = tied(d_normed_left, *mixed_last)
    mixed_rows = scatter_end(mixed_kept, mixed_last)
    block_out = (block_f + jnp.where(live_rows, mixed_rows, 0.0)).astype(BF16)
    sent, kept = scatter_start(d_normed_left, d_normed_right, own_rows, tp_index, tp_size)
    passed, kept = scatter_middle(sent, kept, own_rows, tp_size)
    grad_x, passed = tied(grad_x, passed)
    d_normed = scatter_end(kept, scatter_last(passed, tp_size))
    gain_sums = jnp.concatenate([gains_left[0], gains_right[0]], axis=0)

    grad_head = jnp.stack(
        [
            d_heads[0, :heads],
            hp8[1, :heads] * d_heads[1, :heads],
            jnp.sum(d_skip[0].reshape(heads, LANE // 2), axis=1),
        ],
        axis=0,
    )

    def by_owner(value):
        rows = value.shape[0]
        return value.reshape(rows, fsdp_size, -1).transpose(1, 0, 2).reshape(fsdp_size, -1)

    grad_extras = jnp.concatenate(
        [
            by_owner(d_taps[:5]),
            by_owner(grad_conv_state),
            by_owner(grad_mixer[None, :]),
            jnp.broadcast_to(grad_head.reshape(1, -1), (fsdp_size, 3 * heads)),
        ],
        axis=1,
    )
    grad_extras = pad_cols(grad_extras, small_cols * shard).reshape(fsdp_size * shard, small_cols)
    grad_extras = jnp.concatenate([gain_sums[:, None], grad_extras], axis=1)
    side_part = lax.dot_general(
        normed, d_side.astype(BF16), (((0,), (1,)), ((), ())), preferred_element_type=F32
    ) + jnp.pad(grad_extras, ((0, 0), (used, LANE - used - 1 - small_cols)))
    grad_side = chip_sum(pair_sum(side_part, fsdp_index, fsdp_size), fsdp_index, fsdp_size)
    grad_input_gain = all_sum(grad_side[:, used], tp_size) / input_gain.astype(F32)

    unit_rows, inv_rms = unit_of(block_in)
    scaled = d_normed * gain_f[None, :]
    d_block = inv_rms * (scaled - unit_rows * jnp.mean(scaled * unit_rows, axis=1, keepdims=True))
    d_input = (cot_f + d_block).astype(BF16)

    own_extras = grad_side[:, used + 1 : used + 1 + small_cols].reshape(-1)
    grads = (
        grad_input_gain,
        jnp.stack([grad_gate, grad_x], axis=1),
        grad_side[:, :heads],
        grad_side[:, heads:used],
        own_extras[:inner_n].reshape(conv_inner.shape),
        own_extras[inner_n : inner_n + state_n].reshape(conv_state.shape),
        own_extras[small_count : small_count + 3 * heads].reshape(3, heads),
        own_extras[inner_n + state_n : small_count],
        grad_out.T,
    )
    weights = (
        input_gain,
        proj_inner,
        proj_step,
        proj_state,
        conv_inner,
        conv_state,
        head_params,
        mixer_gain,
        proj_output,
    )
    large = (1, 2, 3, 8)
    updated = [
        adamw_step(
            weights[at],
            grads[at],
            moments[at],
            moments[9 + at],
            WEIGHT_DECAY if at in large else 0.0,
            LEARN_RATE if at in large else LEARN_SMALL,
        )
        for at in range(9)
    ]
    return (
        block_out,
        d_input,
        *grads,
        *[entry[0] for entry in updated],
        *[entry[1] for entry in updated],
        *[entry[2] for entry in updated],
    )


def weight_specs():
    return (
        P("fsdp"),
        P("fsdp", None, "tp"),
        P("fsdp", "tp"),
        P("fsdp", "tp"),
        P(None, ("tp", "fsdp")),
        P(None, ("tp", "fsdp")),
        P(None, "tp"),
        P(("tp", "fsdp")),
        P("tp", "fsdp"),
    )


def solution(mesh):
    rows = P(("fsdp", "tp"), None)
    return jax.shard_map(
        body,
        mesh=mesh,
        in_specs=(rows, rows, P("fsdp", None), P("fsdp")) + weight_specs() * 3,
        out_specs=(rows, rows) + weight_specs() * 4,
        check_vma=False,
    )
```

time: 2160 us -> 657 us (0.30)
  waiting for transfers between devices: 869 us -> 99.8 us
  matrix products: 513 us -> 116 us
  local copies, waits for them, and re-layouts: 274 us -> 94.2 us
  other arithmetic: 276 us -> 113 us
  blocking collectives: 183 us -> 27.6 us
  Pallas kernels: 0 us -> 146 us
  starting transfers between devices: 0.49 us -> 36.6 us
    unnamed x16 -> x6, waiting for transfers between devices: 387 us -> 0.79 us
    dot_general x74 -> x7, matrix products: 439 us -> 76.4 us  [the longest x4 56 us: mm(): lax.dot_general(left, right, (((1,), (0,)), ((), ())), preferred_element_...]
    reduce_scatter x4 -> x3, waiting for transfers between devices: 369 us -> 19.9 us  [chip_scatter(): lax.psum_scatter(flat, 'fsdp', scatter_dimension=0, axis_index_groups=gro...]
    pallas_call x0 -> x4, Pallas kernels: none -> 146 us  [the longest x1 68.8 us: ssd_backward(): pl.pallas_call(functools.partial(ssd_bwd_kernel, heads), grid=(chunks,),...]
    reshape x21 -> x15, local copies, waits for them, and re-layouts: 125 us -> 3.45 us  [the longest x1 1.34 us: body(): pad_cols(grad_extras, small_cols * shard)]
    all_gather x4 -> x3, waiting for transfers between devices: 113 us -> 1.65 us  [the longest x1 1.63 us: body(): x_all = lax.all_gather(x_local, 'fsdp', axis=0, tiled=True)]
    ppermute x0 -> x34, waiting for transfers between devices: none -> 77.4 us  [the longest x20 49.8 us: swap(): lax.ppermute(value, 'tp', [(at, at ^ distance) for at in range(size)])]
    dynamic_update_slice x30 -> x4, other arithmetic: 81.1 us -> 5.65 us  [place(): lax.dynamic_update_slice(whole, parts[distance], ((tp_index ^ distance) *...]
  transfers between devices with their start and end apart: 12 -> 40, of which waited for: 6 -> 15; matrix products, arithmetic and copies ran while one was open for 31% -> 42% of each run, Pallas kernels for 0% -> 22%
where the time goes in v1:
time: 657 us; the launch traced here: 650 us
  Pallas kernels  146 us (22%)
  matrix products  116 us (18%)
  other arithmetic  113 us (17%)
  waiting for transfers between devices  99.8 us (15%)
  local copies, waits for them, and re-layouts  94.2 us (14%)
  starting transfers between devices  36.6 us (6%)
  blocking collectives  27.6 us (4%)
  between operations  16.8 us (3%)
    pallas_call x1, Pallas kernels, ssd_backward(): pl.pallas_call(functools.partial(ssd_bwd_kernel, heads), grid=(chunks,),...  68.8 us
    dot_general x4, matrix products, mm(): lax.dot_general(left, right, (((1,), (0,)), ((), ())), preferred_element_...  56 us
    ppermute x20, waiting for transfers between devices, swap(): lax.ppermute(value, 'tp', [(at, at ^ distance) for at in range(size)])  49.8 us
    dot_general x3, matrix products, contract_rows(): lax.dot_general(left_mat, right_mat, (((0,), (0,)), ((), ())), preferred_...  39.9 us
    pallas_call x2, Pallas kernels, d_normed_half(): pl.pallas_call(functools.partial(dn_kernel, step), grid=(half // tile,),...  39.2 us
    pallas_call x1, Pallas kernels, ssd_forward(): pl.pallas_call(functools.partial(ssd_fwd_kernel, heads), grid=(chunks,),...  37.7 us
    unnamed x177, local copies, waits for them, and re-layouts  34.1 us
    ppermute x14, waiting for transfers between devices, fsdp_swap(): lax.ppermute(value, 'fsdp', [(at, at ^ distance) for at in range(size)])  27.6 us
  transfers between devices with their start and end apart: 40, of which 15 were waited for; matrix products, arithmetic and copies ran while one was open for 42% of the time, Pallas kernels for 22%

profile of v1, /device:TPU:0, one launch (start us, length us, event | category | flops | bytes accessed | tf_op | source)
XLA Modules:
  0.0 650.3 jit_solution(18331748361231505883)
XLA Ops:
  12.9 10.4 %all-gather = bf16[320,320]{1,0:T(8,128)(2,1)S(1)} all-gather(bf16[80,320]{1,0:T(8,128)(2,1)S(1)} %fusion.67), channel_id=2, replica_groups=mesh['fsdp'=8,'tp'=4] {'tp'}, dimensions={0}, use_global_device_ids=true | all-gather | bytes 256000 | tf_op jit(solution)/shard_map/all_gather | solution.py:797
  33.0 3.2 fusion.9
  37.6 2.6 collective-permute-start.7
  40.4 13.5 %collective-permute-done.5 = bf16[336,256]{0,1:T(8,128)(2,1)S(1)} collective-permute-done((bf16[336,256]{0,1:T(8,128)(2,1)}, bf16[336,256]{0,1:T(8,128)(2,1)S(1)}, u32[]{:S(2)}, u32[]{:S(2)}) %collective-permute-start.5) | collective-permute-done | bytes 172064 | tf_op jit(solution)/shard_map/ppermute | solution.py:706
  53.9 12.1 %collective-permute-done.1 = bf16[384,2560]{1,0:T(8,128)(2,1)} collective-permute-done((bf16[384,2560]{1,0:T(8,128)(2,1)S(1)}, bf16[384,2560]{1,0:T(8,128)(2,1)}, u32[]{:S(2)}, u32[]{:S(2)}) %collective-permute-start.1) | collective-permute-done | bytes 1966112 | tf_op jit(solution)/shard_map/ppermute | solution.py:638
  66.1 3.6 collective-permute-start.9
  101.7 4.6 collective-permute-done.2
  107.1 2.9 pad_maximum_fusion.1
  131.5 3.4 fusion.118.bc_raw_ref
  137.4 15.0 %fusion.117.raw_ref.small_ref.halo_ref = f32[1536,1408]{1,0:T(8,128)} fusion(bf16[1536,2560]{1,0:T(8,128)(2,1)S(1)} %fusion.33.normed_ref, bf16[2560,1408]{1,0:T(8,128)(2,1)S(1)} %bitcast.149), kind=kOutput, calls=%fused_computation.301 | convolution fusion | flops 11072962560 | bytes 23724032 | tf_op jit(solution)/shard_map/dot_general | solution.py:21
  153.7 37.7 %ssd_fwd.1 = (f32[1536,1280]{1,0:T(8,128)}, f32[6,128,1280]{2,1,0:T(8,128)}, bf16[1536,256]{1,0:T(8,128)(2,1)}) custom-call(f32[1536,1408]{1,0:T(8,128)} %fusion.117.raw_ref.small_ref.halo_ref, f32[1536,1408]{1,0:T(8,128)} %fusion.117.raw_ref.small_ref.halo_ref, f32[1536,256]{1,0:T(8,128)} %fusion.118.bc_raw_ref, f32[1536,128]{1,0:T(8,128)} %pad.105.meta_ref.meta_next_ref, ...), custom_call_target="tpu_custom_call" | custom-call | flops 40699998208 | bytes 125800000 | tf_op jit(solution)/shard_map/ssd_fwd/pallas_call | solution.py:409
  191.4 7.0 %collective-permute-done.12 = bf16[384,2560]{1,0:T(8,128)(2,1)} collective-permute-done((bf16[384,2560]{1,0:T(8,128)(2,1)}, bf16[384,2560]{1,0:T(8,128)(2,1)}, u32[]{:S(2)}, u32[]{:S(2)}) %collective-permute-start.12) | collective-permute-done | bytes 1966112 | tf_op jit(solution)/shard_map/ppermute | solution.py:638
  198.5 19.6 %multiply_reduce_fusion.2 = (f32[1536]{0:T(1024)S(1)}, f32[1536,1280]{1,0:T(8,128)}, f32[1536,1280]{1,0:T(8,128)}) fusion(f32[1536,1280]{1,0:T(8,128)} %get-tuple-element.100.y_ref, bf16[1536,2560]{1,0:T(8,128)(2,1)} %copy-done.7, bf16[2560,1,1280]{2,0,1:T(8,128)(2,1)} %all-gather.10.cloned.1.call-done), kind=kOutput, calls=%fused_computation.8 | convolution fusion | flops 10080090112 | bytes 38017024 | tf_op jit(solution)/shard_map/dot_general | solution.py:21
  218.1 9.2 %psum.14 = f32[1536]{0:T(1024)S(1)} all-reduce(f32[1536]{0:T(1024)S(1)} %get-tuple-element.409), channel_id=1, replica_groups=mesh['fsdp'=8,'tp'=4] {'tp'}, use_global_device_ids=true, to_apply=%region_5.6 | all-reduce | flops 1536 | bytes 12288 | tf_op jit(solution)/shard_map/psum | solution.py:875
  237.8 11.1 %convolution_convert_fusion.2 = bf16[2560,1280]{1,0:T(8,128)(2,1)S(1)} fusion(bf16[1536,2560]{1,0:T(8,128)(2,1)S(1)} %constant_dynamic-update-slice_fusion, bf16[1536,1280]{1,0:T(8,128)(2,1)S(1)} %multiply_convert_fusion.1), kind=kOutput, calls=%fused_computation.2 | convolution fusion | flops 10069606400 | bytes 18350080 | tf_op jit(solution)/shard_map/dot_general | solution.py:620
  258.9 5.4 fusion.3
  264.4 18.1 %multiply_reduce_fusion = (f32[1280]{0:T(1024)S(1)}, f32[1536]{0:T(1024)S(1)}, f32[1536,1280]{1,0:T(8,128)}) fusion(f32[1536,1280]{1,0:T(8,128)} %get-tuple-element.410, f32[1536]{0:T(1024)S(1)} %add_rsqrt_fusion, f32[1280]{0:T(1024)S(1)} %reshape.450, bf16[1536,2560]{1,0:T(8,128)(2,1)} %copy-done.6, bf16[2560,1280]{1,0:T(8,128)(2,1)} %all-gather.8.cloned.1.call-done), kind=kOutput, calls=%fused_computation.3 | convolution fusion | flops 10078124032 | bytes 30169088 | tf_op jit(solution)/shard_map/dot_general | solution.py:21
  282.4 8.0 %psum.15 = f32[1536]{0:T(1024)S(1)} all-reduce(f32[1536]{0:T(1024)S(1)} %get-tuple-element.367), channel_id=1, replica_groups=mesh['fsdp'=8,'tp'=4] {'tp'}, use_global_device_ids=true, to_apply=%region_7.8 | all-reduce | flops 1536 | bytes 12288 | tf_op jit(solution)/shard_map/psum | solution.py:887
  290.4 15.4 %multiply_convert_fusion = (bf16[1536,1280]{1,0:T(8,128)(2,1)S(1)}, f32[1536,1280]{1,0:T(8,128)}) fusion(f32[1536,1280]{1,0:T(8,128)} %get-tuple-element.451, f32[1536,1280]{1,0:T(8,128)} %get-tuple-element.100.y_ref, f32[1536]{0:T(1024)S(1)} %broadcast_multiply_fusion, f32[1536,1280]{1,0:T(8,128)} %get-tuple-element.410, ...), kind=kLoop, calls=%fused_computation.4 | loop fusion | flops 33423360 | bytes 43271168 | tf_op jit(solution)/shard_map/convert_element_type | solution.py:891
  307.8 14.5 %convolution_convert_fusion.1 = bf16[2560,1280]{1,0:T(8,128)(2,1)} fusion(bf16[1536,2560]{1,0:T(8,128)(2,1)} %copy-done.7, bf16[1536,1280]{1,0:T(8,128)(2,1)S(1)} %get-tuple-element.117.dz_ref), kind=kOutput, calls=%fused_computation.1 | convolution fusion | flops 10069606400 | bytes 18350080 | tf_op jit(solution)/shard_map/dot_general | solution.py:620
  322.3 19.9 %reduce-scatter.4.cloned.1.call-done = bf16[320,1280]{1,0:T(8,128)(2,1)} async-done(((bf16[1280,1280]{1,0:T(8,128)(2,1)}), bf16[320,1280]{1,0:T(8,128)(2,1)}) %reduce-scatter.4.cloned.1.call-update) | async-done | bytes 819216 | tf_op jit(solution)/shard_map/reduce_scatter | solution.py:730
  343.5 4.5 dynamic-slice_bitcast_fusion.1
  348.0 8.1 %convolution_convert_fusion.3 = bf16[1536,1280]{1,0:T(8,128)(2,1)S(1)} fusion(bf16[1536,1280]{1,0:T(8,128)(2,1)S(1)} %copy-done.19, bf16[2560,1280]{1,0:T(8,128)(2,1)} %all-gather.8.cloned.1.call-done), kind=kOutput, calls=%fused_computation.11 | convolution fusion | flops 5035130880 | bytes 11141120 | tf_op jit(solution)/shard_map/dot_general | solution.py:25
  360.1 5.9 convolution_convert_fusion.4
  370.2 4.8 fusion.39
  375.0 5.5 fusion.2
  380.5 68.8 %ssd_bwd.1 = (bf16[1536,1280]{1,0:T(8,128)(2,1)}, f32[128,1536]{1,0:T(8,128)}, f32[256,1536]{1,0:T(8,128)}, f32[8,1280]{1,0:T(8,128)}, f32[8,128]{1,0:T(8,128)}, /*index=5*/f32[8,1280]{1,0:T(8,128)}, f32[128,1536]{1,0:T(8,128)}) custom-call(f32[1536,1408]{1,0:T(8,128)} %fusion.117.raw_ref.small_ref.halo_ref, ...), custom_call_target="tpu_custom_call" | custom-call | flops 75900002304 | bytes 234600000 | tf_op jit(solution)/shard_map/ssd_bwd/pallas_call | solution.py:466
  449.4 2.4 convert_element_type.420
  451.8 14.2 %convolution_convert_fusion = bf16[2560,1280]{1,0:T(8,128)(2,1)S(1)} fusion(bf16[1536,2560]{1,0:T(8,128)(2,1)} %copy-done.7, bf16[1536,1280]{1,0:T(8,128)(2,1)} %get-tuple-element.116.dx_ref), kind=kOutput, calls=%fused_computation | convolution fusion | flops 10069606400 | bytes 18350080 | tf_op jit(solution)/shard_map/dot_general | solution.py:620
  472.1 2.4 collective-permute-start.21
  475.6 2.7 add_convert_fusion.2
  480.9 2.7 add_convert_fusion.3
  484.1 7.5 %collective-permute-done.20 = f32[64,1536]{1,0:T(8,128)} collective-permute-done((f32[64,1536]{1,0:T(8,128)}, f32[64,1536]{1,0:T(8,128)}, u32[]{:S(2)}, u32[]{:S(2)}) %collective-permute-start.20) | collective-permute-done | bytes 393248 | tf_op jit(solution)/shard_map/ppermute | solution.py:638
  497.1 5.4 fusion.1
  502.5 19.5 %d_normed.3 = (bf16[1536,1280]{1,0:T(8,128)(2,1)}, f32[8,1280]{1,0:T(8,128)}) custom-call(bf16[1536,1280]{1,0:T(8,128)(2,1)} %copy-done.20, bf16[1536,1280]{1,0:T(8,128)(2,1)} %get-tuple-element.116.dx_ref, f32[128,1536]{1,0:T(8,128)} %select_maximum_fusion.1.side_ref, bf16[2560,1280]{1,0:T(8,128)(2,1)} %bitcast.166, ...), custom_call_target="tpu_custom_call" | custom-call | flops 13200000000 | bytes 40800000 | tf_op jit(solution)/shard_map/d_normed/pallas_call | solution.py:562
  522.0 19.7 %d_normed.2 = (bf16[1536,1280]{1,0:T(8,128)(2,1)}, f32[8,1280]{1,0:T(8,128)}) custom-call(bf16[1536,1280]{1,0:T(8,128)(2,1)} %copy-done.20, bf16[1536,1280]{1,0:T(8,128)(2,1)} %get-tuple-element.116.dx_ref, f32[128,1536]{1,0:T(8,128)} %select_maximum_fusion.1.side_ref, bf16[2560,1280]{1,0:T(8,128)(2,1)} %bitcast.167, ...), custom_call_target="tpu_custom_call" | custom-call | flops 13200000000 | bytes 40800000 | tf_op jit(solution)/shard_map/d_normed/pallas_call | solution.py:562
  542.9 6.4 convolution_add_fusion
  561.3 5.2 convert_add_fusion.7
  566.7 4.8 collective-permute-done.29
  571.5 6.6 %collective-permute-done.31 = f32[320,128]{0,1:T(8,128)S(1)} collective-permute-done((f32[320,128]{0,1:T(8,128)S(1)}, f32[320,128]{0,1:T(8,128)S(1)}, u32[]{:S(2)}, u32[]{:S(2)}) %collective-permute-start.31) | collective-permute-done | bytes 163872 | tf_op jit(solution)/shard_map/ppermute | solution.py:706
  584.0 15.8 %collective-permute-done.32 = f32[320]{0:T(512)S(1)} collective-permute-done((f32[320]{0:T(512)S(1)}, f32[320]{0:T(512)S(1)}, u32[]{:S(2)}, u32[]{:S(2)}) %collective-permute-start.32) | collective-permute-done | bytes 1312 | tf_op jit(solution)/shard_map/ppermute | solution.py:638
  605.7 2.8 add_convert_fusion.1
  612.1 5.5 fusion.28
  617.6 4.2 copy.375
  621.8 4.2 copy.377
  626.1 4.2 copy.378
  630.3 2.8 copy.376
  640.0 3.1 fusion.10
  (435 shorter events, 156.6 us)
Async XLA Ops:
  7.3 113.1 %all-gather.6.cloned.1.call-start = ((), (), s32[]{:S(2)}) async-start(), calls=%async_computation.3 | async-start | bytes 8110080 | tf_op jit(solution)/shard_map/all_gather | solution.py:793
  12.0 186.6 %all-gather.10.cloned.1.call-start = ((), (), s32[]{:S(2)}) async-start(), calls=%async_computation.8 | async-start | bytes 7372800 | tf_op jit(solution)/shard_map/all_gather | solution.py:803
  12.7 251.7 %all-gather.8.cloned.1.call-start = ((), (), s32[]{:S(2)}) async-start(), calls=%async_computation.4 | async-start | bytes 7372800 | tf_op jit(solution)/shard_map/all_gather | solution.py:810
  23.3 42.7 %collective-permute-start.1 = (bf16[384,2560]{1,0:T(8,128)(2,1)S(1)}, bf16[384,2560]{1,0:T(8,128)(2,1)}, u32[]{:S(2)}, u32[]{:S(2)}) collective-permute-start(bf16[384,2560]{1,0:T(8,128)(2,1)S(1)} %copy-done), channel_id=1, source_target_pairs={{0,2},{1,3},{2,0},{3,1},{4,6},{5,7},{6,4},{7,5},{8,10},{9,11},{10,... | collective-permute-start | bytes 5898248 | tf_op jit(solution)/shard_map/ppermute | solution.py:638
  24.9 44.8 %collective-permute-start = (bf16[384,2560]{1,0:T(8,128)(2,1)S(1)}, bf16[384,2560]{1,0:T(8,128)(2,1)}, u32[]{:S(2)}, u32[]{:S(2)}) collective-permute-start(bf16[384,2560]{1,0:T(8,128)(2,1)S(1)} %copy-done), channel_id=1, source_target_pairs={{0,1},{1,0},{2,3},{3,2},{4,5},{5,4},{6,7},{7,6},{8,9},{9,8},{10,11... | collective-permute-start | bytes 5898248 | tf_op jit(solution)/shard_map/ppermute | solution.py:638
  26.4 10.6 %collective-permute-start.4 = (bf16[336,256]{0,1:T(8,128)(2,1)}, bf16[336,256]{0,1:T(8,128)(2,1)S(1)}, u32[]{:S(2)}, u32[]{:S(2)}) collective-permute-start(bf16[336,256]{0,1:T(8,128)(2,1)} %fusion.54), channel_id=1, source_target_pairs={{0,4},{4,0},{8,12},{12,8},{16,20},{20,16},{24,28},{28,24},{1,5},{5... | collective-permute-start | bytes 516104 | tf_op jit(solution)/shard_map/ppermute | solution.py:706
  26.4 27.6 %collective-permute-start.5 = (bf16[336,256]{0,1:T(8,128)(2,1)}, bf16[336,256]{0,1:T(8,128)(2,1)S(1)}, u32[]{:S(2)}, u32[]{:S(2)}) collective-permute-start(bf16[336,256]{0,1:T(8,128)(2,1)} %fusion.54), channel_id=1, source_target_pairs={{0,8},{4,12},{8,0},{12,4},{16,24},{20,28},{24,16},{28,20},{1,9},{5... | collective-permute-start | bytes 516104 | tf_op jit(solution)/shard_map/ppermute | solution.py:706
  27.9 53.7 %collective-permute-start.6 = (bf16[336,256]{0,1:T(8,128)(2,1)}, bf16[336,256]{0,1:T(8,128)(2,1)}, u32[]{:S(2)}, u32[]{:S(2)}) collective-permute-start(bf16[336,256]{0,1:T(8,128)(2,1)} %fusion.54), channel_id=1, source_target_pairs={{0,12},{4,8},{8,4},{12,0},{16,28},{20,24},{24,20},{28,16},{1,13},{... | collective-permute-start | bytes 516104 | tf_op jit(solution)/shard_map/ppermute | solution.py:706
  30.1 39.5 %copy-start.65 = (pred[384]{0:T(512)(128)(4,1)}, pred[384]{0:T(512)(128)(4,1)S(1)}, u32[]{:S(2)}) copy-start(pred[384]{0:T(512)(128)(4,1)S(1)} %add_compare_fusion.1) | copy-start | bytes 1156
  31.4 38.5 %copy-start.32 = (f32[1536]{0:T(1024)}, f32[1536]{0:T(1024)S(1)}, u32[]{:S(2)}) copy-start(f32[1536]{0:T(1024)S(1)} %get-tuple-element.437) | copy-start | bytes 18436
  37.6 45.5 %collective-permute-start.7 = (bf16[336,256]{0,1:T(8,128)(2,1)}, bf16[336,256]{0,1:T(8,128)(2,1)}, u32[]{:S(2)}, u32[]{:S(2)}) collective-permute-start(bf16[336,256]{0,1:T(8,128)(2,1)} %fusion.54), channel_id=1, source_target_pairs={{0,16},{4,20},{8,24},{12,28},{16,0},{20,4},{24,8},{28,12},{1,17},{... | collective-permute-start | bytes 516104 | tf_op jit(solution)/shard_map/ppermute | solution.py:706
  53.9 35.8 %collective-permute-start.8 = (bf16[336,256]{0,1:T(8,128)(2,1)}, bf16[336,256]{0,1:T(8,128)(2,1)}, u32[]{:S(2)}, u32[]{:S(2)}) collective-permute-start(bf16[336,256]{0,1:T(8,128)(2,1)} %fusion.54), channel_id=1, source_target_pairs={{0,20},{4,16},{8,28},{12,24},{16,4},{20,0},{24,12},{28,8},{1,21},{... | collective-permute-start | bytes 516104 | tf_op jit(solution)/shard_map/ppermute | solution.py:706
  66.1 25.4 %collective-permute-start.9 = (bf16[336,256]{0,1:T(8,128)(2,1)}, bf16[336,256]{0,1:T(8,128)(2,1)}, u32[]{:S(2)}, u32[]{:S(2)}) collective-permute-start(bf16[336,256]{0,1:T(8,128)(2,1)} %fusion.54), channel_id=1, source_target_pairs={{0,24},{4,28},{8,16},{12,20},{16,8},{20,12},{24,0},{28,4},{1,25},{... | collective-permute-start | bytes 516104 | tf_op jit(solution)/shard_map/ppermute | solution.py:706
  69.7 23.5 %collective-permute-start.10 = (bf16[336,256]{0,1:T(8,128)(2,1)}, bf16[336,256]{0,1:T(8,128)(2,1)}, u32[]{:S(2)}, u32[]{:S(2)}) collective-permute-start(bf16[336,256]{0,1:T(8,128)(2,1)} %fusion.54), channel_id=1, source_target_pairs={{0,28},{4,24},{8,20},{12,16},{16,12},{20,8},{24,4},{28,0},{1,29},{... | collective-permute-start | bytes 516104 | tf_op jit(solution)/shard_map/ppermute | solution.py:706
  81.6 24.7 %collective-permute-start.2 = (bf16[192,2560]{1,0:T(8,128)(2,1)}, bf16[192,2560]{1,0:T(8,128)(2,1)}, u32[]{:S(2)}, u32[]{:S(2)}) collective-permute-start(bf16[192,2560]{1,0:T(8,128)(2,1)} %slice.262), channel_id=1, source_target_pairs={{0,1},{1,0},{2,3},{3,2},{4,5},{5,4},{6,7},{7,6},{8,9},{9,8},{10,11... | collective-permute-start | bytes 2949128 | tf_op jit(solution)/shard_map/ppermute | solution.py:638
  83.1 24.0 %collective-permute-start.3 = (bf16[192,2560]{1,0:T(8,128)(2,1)}, bf16[192,2560]{1,0:T(8,128)(2,1)}, u32[]{:S(2)}, u32[]{:S(2)}) collective-permute-start(bf16[192,2560]{1,0:T(8,128)(2,1)} %slice.263), channel_id=1, source_target_pairs={{0,2},{1,3},{2,0},{3,1},{4,6},{5,7},{6,4},{7,5},{8,10},{9,11},{10,... | collective-permute-start | bytes 2949128 | tf_op jit(solution)/shard_map/ppermute | solution.py:638
  110.0 81.4 %collective-permute-start.11 = (bf16[384,2560]{1,0:T(8,128)(2,1)}, bf16[384,2560]{1,0:T(8,128)(2,1)}, u32[]{:S(2)}, u32[]{:S(2)}) collective-permute-start(bf16[384,2560]{1,0:T(8,128)(2,1)} %fusion.9), channel_id=1, source_target_pairs={{0,1},{1,0},{2,3},{3,2},{4,5},{5,4},{6,7},{7,6},{8,9},{9,8},{10,11... | collective-permute-start | bytes 5898248 | tf_op jit(solution)/shard_map/ppermute | solution.py:638
  111.5 87.0 %collective-permute-start.12 = (bf16[384,2560]{1,0:T(8,128)(2,1)}, bf16[384,2560]{1,0:T(8,128)(2,1)}, u32[]{:S(2)}, u32[]{:S(2)}) collective-permute-start(bf16[384,2560]{1,0:T(8,128)(2,1)} %fusion.9), channel_id=1, source_target_pairs={{0,2},{1,3},{2,0},{3,1},{4,6},{5,7},{6,4},{7,5},{8,10},{9,11},{10,... | collective-permute-start | bytes 5898248 | tf_op jit(solution)/shard_map/ppermute | solution.py:638
  112.0 86.4 %collective-permute-start.13 = (bf16[384,2560]{1,0:T(8,128)(2,1)}, bf16[384,2560]{1,0:T(8,128)(2,1)}, u32[]{:S(2)}, u32[]{:S(2)}) collective-permute-start(bf16[384,2560]{1,0:T(8,128)(2,1)} %fusion.9), channel_id=1, source_target_pairs={{0,3},{1,2},{2,1},{3,0},{4,7},{5,6},{6,5},{7,4},{8,11},{9,10},{10,... | collective-permute-start | bytes 5898248 | tf_op jit(solution)/shard_map/ppermute | solution.py:638
  118.5 223.6 %reduce-scatter.4.cloned.1.call-start = ((), (), s32[]{:S(2)}) async-start(), calls=%async_computation.5 | async-start | bytes 4096000 | tf_op jit(solution)/shard_map/reduce_scatter | solution.py:730
  252.7 6.2 collective-permute-start.14
  264.3 185.1 %reduce-scatter.6.cloned.1.call-start = ((), (), s32[]{:S(2)}) async-start(), calls=%async_computation.6 | async-start | bytes 4096000 | tf_op jit(solution)/shard_map/reduce_scatter | solution.py:730
  347.9 27.1 %collective-permute-start.15 = (bf16[4,320,1280]{2,1,0:T(8,128)(2,1)}, bf16[4,320,1280]{2,1,0:T(8,128)(2,1)}, u32[]{:S(2)}, u32[]{:S(2)}) collective-permute-start(bf16[4,320,1280]{2,1,0:T(8,128)(2,1)} %dynamic-slice_bitcast_fusion.1), channel_id=1, source_target_pairs={{0,4},{4,0},{8,12},{12,8},{16,20},{20,16},{24,28},{28,24},{1,5},{5... | collective-permute-start | bytes 9830408 | tf_op jit(solution)/shard_map/ppermute | solution.py:706
  358.6 90.8 %collective-permute-start.17 = (bf16[768,1280]{1,0:T(8,128)(2,1)}, bf16[768,1280]{1,0:T(8,128)(2,1)}, u32[]{:S(2)}, u32[]{:S(2)}) collective-permute-start(bf16[768,1280]{1,0:T(8,128)(2,1)} %pad_maximum_fusion.3), channel_id=1, source_target_pairs={{0,2},{1,3},{2,0},{3,1},{4,6},{5,7},{6,4},{7,5},{8,10},{9,11},{10,... | collective-permute-start | bytes 5898248 | tf_op jit(solution)/shard_map/ppermute | solution.py:638
  368.6 80.7 %collective-permute-start.16 = (bf16[768,1280]{1,0:T(8,128)(2,1)}, bf16[768,1280]{1,0:T(8,128)(2,1)}, u32[]{:S(2)}, u32[]{:S(2)}) collective-permute-start(bf16[768,1280]{1,0:T(8,128)(2,1)} %pad_maximum_fusion.2), channel_id=1, source_target_pairs={{0,1},{1,0},{2,3},{3,2},{4,5},{5,4},{6,7},{7,6},{8,9},{9,8},{10,11... | collective-permute-start | bytes 5898248 | tf_op jit(solution)/shard_map/ppermute | solution.py:638
  380.5 228.1 %reduce-scatter.8.cloned.1.call-start = ((), (), s32[]{:S(2)}) async-start(), calls=%async_computation.7 | async-start | bytes 4096000 | tf_op jit(solution)/shard_map/reduce_scatter | solution.py:730
  470.0 27.0 %collective-permute-start.18 = (bf16[4,320,1280]{2,1,0:T(8,128)(2,1)}, bf16[4,320,1280]{2,1,0:T(8,128)(2,1)}, u32[]{:S(2)}, u32[]{:S(2)}) collective-permute-start(bf16[4,320,1280]{2,1,0:T(8,128)(2,1)} %dynamic-slice_bitcast_fusion), channel_id=1, source_target_pairs={{0,4},{4,0},{8,12},{12,8},{16,20},{20,16},{24,28},{28,24},{1,5},{5... | collective-permute-start | bytes 9830408 | tf_op jit(solution)/shard_map/ppermute | solution.py:706
  471.0 12.5 %collective-permute-start.19 = (f32[64,1536]{1,0:T(8,128)}, f32[64,1536]{1,0:T(8,128)}, u32[]{:S(2)}, u32[]{:S(2)}) collective-permute-start(f32[64,1536]{1,0:T(8,128)} %get-tuple-element.426), channel_id=1, source_target_pairs={{0,1},{1,0},{2,3},{3,2},{4,5},{5,4},{6,7},{7,6},{8,9},{9,8},{10,11... | collective-permute-start | bytes 1179656 | tf_op jit(solution)/shard_map/ppermute | solution.py:638
  471.5 20.0 %collective-permute-start.20 = (f32[64,1536]{1,0:T(8,128)}, f32[64,1536]{1,0:T(8,128)}, u32[]{:S(2)}, u32[]{:S(2)}) collective-permute-start(f32[64,1536]{1,0:T(8,128)} %get-tuple-element.428), channel_id=1, source_target_pairs={{0,2},{1,3},{2,0},{3,1},{4,6},{5,7},{6,4},{7,5},{8,10},{9,11},{10,... | collective-permute-start | bytes 1179656 | tf_op jit(solution)/shard_map/ppermute | solution.py:638
  472.1 19.6 %collective-permute-start.21 = (f32[64,1536]{1,0:T(8,128)S(1)}, f32[64,1536]{1,0:T(8,128)}, u32[]{:S(2)}, u32[]{:S(2)}) collective-permute-start(f32[64,1536]{1,0:T(8,128)S(1)} %get-tuple-element.427), channel_id=1, source_target_pairs={{0,3},{1,2},{2,1},{3,0},{4,7},{5,6},{6,5},{7,4},{8,11},{9,10},{10,... | collective-permute-start | bytes 1179656 | tf_op jit(solution)/shard_map/ppermute | solution.py:638
  478.3 74.3 %collective-permute-start.23 = (bf16[384,1280]{1,0:T(8,128)(2,1)}, bf16[384,1280]{1,0:T(8,128)(2,1)}, u32[]{:S(2)}, u32[]{:S(2)}) collective-permute-start(bf16[384,1280]{1,0:T(8,128)(2,1)} %add_convert_fusion.2), channel_id=1, source_target_pairs={{0,1},{1,0},{2,3},{3,2},{4,5},{5,4},{6,7},{7,6},{8,9},{9,8},{10,11... | collective-permute-start | bytes 2949128 | tf_op jit(solution)/shard_map/ppermute | solution.py:638
  483.5 69.1 %collective-permute-start.22 = (bf16[384,1280]{1,0:T(8,128)(2,1)}, bf16[384,1280]{1,0:T(8,128)(2,1)}, u32[]{:S(2)}, u32[]{:S(2)}) collective-permute-start(bf16[384,1280]{1,0:T(8,128)(2,1)} %add_convert_fusion.3), channel_id=1, source_target_pairs={{0,2},{1,3},{2,0},{3,1},{4,6},{5,7},{6,4},{7,5},{8,10},{9,11},{10,... | collective-permute-start | bytes 2949128 | tf_op jit(solution)/shard_map/ppermute | solution.py:638
  549.4 6.5 %collective-permute-start.28 = (f32[4,320,128]{2,1,0:T(8,128)S(1)}, f32[4,320,128]{2,1,0:T(8,128)S(1)}, u32[]{:S(2)}, u32[]{:S(2)}) collective-permute-start(f32[4,320,128]{2,1,0:T(8,128)S(1)} %dynamic-slice_bitcast_fusion.3), channel_id=1, source_target_pairs={{0,4},{4,0},{8,12},{12,8},{16,20},{20,16},{24,28},{28,24},{1,5},{5... | collective-permute-start | bytes 1966088 | tf_op jit(solution)/shard_map/ppermute | solution.py:706
  551.1 52.9 %collective-permute-start.25 = (bf16[768,1280]{1,0:T(8,128)(2,1)}, bf16[768,1280]{1,0:T(8,128)(2,1)}, u32[]{:S(2)}, u32[]{:S(2)}) collective-permute-start(bf16[768,1280]{1,0:T(8,128)(2,1)} %pad_maximum_fusion.5), channel_id=1, source_target_pairs={{0,2},{1,3},{2,0},{3,1},{4,6},{5,7},{6,4},{7,5},{8,10},{9,11},{10,... | collective-permute-start | bytes 5898248 | tf_op jit(solution)/shard_map/ppermute | solution.py:638
  554.2 51.6 %collective-permute-start.24 = (bf16[768,1280]{1,0:T(8,128)(2,1)}, bf16[768,1280]{1,0:T(8,128)(2,1)}, u32[]{:S(2)}, u32[]{:S(2)}) collective-permute-start(bf16[768,1280]{1,0:T(8,128)(2,1)} %pad_maximum_fusion.4), channel_id=1, source_target_pairs={{0,1},{1,0},{2,3},{3,2},{4,5},{5,4},{6,7},{7,6},{8,9},{9,8},{10,11... | collective-permute-start | bytes 5898248 | tf_op jit(solution)/shard_map/ppermute | solution.py:638
  556.2 15.2 %collective-permute-start.29 = (f32[320,128]{0,1:T(8,128)S(1)}, f32[320,128]{0,1:T(8,128)S(1)}, u32[]{:S(2)}, u32[]{:S(2)}) collective-permute-start(f32[320,128]{0,1:T(8,128)S(1)} %copy.364), channel_id=1, source_target_pairs={{0,8},{4,12},{8,0},{12,4},{16,24},{20,28},{24,16},{28,20},{1,9},{5... | collective-permute-start | bytes 491528 | tf_op jit(solution)/shard_map/ppermute | solution.py:706
  557.4 14.1 %collective-permute-start.30 = (f32[320,128]{0,1:T(8,128)S(1)}, f32[320,128]{0,1:T(8,128)S(1)}, u32[]{:S(2)}, u32[]{:S(2)}) collective-permute-start(f32[320,128]{0,1:T(8,128)S(1)} %copy.366), channel_id=1, source_target_pairs={{0,16},{4,20},{8,24},{12,28},{16,0},{20,4},{24,8},{28,12},{1,17},{... | collective-permute-start | bytes 491528 | tf_op jit(solution)/shard_map/ppermute | solution.py:706
  559.8 41.2 %copy-start.68 = (bf16[160]{0:T(256)(128)(2,1)S(1)}, bf16[160]{0:T(256)(128)(2,1)}, u32[]{:S(2)}) copy-start(bf16[160]{0:T(256)(128)(2,1)} %param.42) | copy-start | bytes 964
  559.8 41.2 %copy-start.74 = (f32[160]{0:T(256)S(1)}, f32[160]{0:T(256)}, u32[]{:S(2)}) copy-start(f32[160]{0:T(256)} %param.51) | copy-start | bytes 1924
  559.8 41.2 %copy-start.75 = (f32[160]{0:T(256)S(1)}, f32[160]{0:T(256)}, u32[]{:S(2)}) copy-start(f32[160]{0:T(256)} %param.60) | copy-start | bytes 1924
  559.8 43.6 %copy-start.64 = (bf16[320]{0:T(512)(128)(2,1)S(1)}, bf16[320]{0:T(512)(128)(2,1)}, u32[]{:S(2)}) copy-start(bf16[320]{0:T(512)(128)(2,1)} %param.35) | copy-start | bytes 1924
  559.8 43.6 %copy-start.71 = (f32[320]{0:T(512)S(1)}, f32[320]{0:T(512)}, u32[]{:S(2)}) copy-start(f32[320]{0:T(512)} %param.44) | copy-start | bytes 3844
  559.8 43.6 %copy-start.72 = (f32[320]{0:T(512)S(1)}, f32[320]{0:T(512)}, u32[]{:S(2)}) copy-start(f32[320]{0:T(512)} %param.53) | copy-start | bytes 3844
  559.8 18.3 %collective-permute-start.31 = (f32[320,128]{0,1:T(8,128)S(1)}, f32[320,128]{0,1:T(8,128)S(1)}, u32[]{:S(2)}, u32[]{:S(2)}) collective-permute-start(f32[320,128]{0,1:T(8,128)S(1)} %copy.367), channel_id=1, source_target_pairs={{0,24},{4,28},{8,16},{12,20},{16,8},{20,12},{24,0},{28,4},{1,25},{... | collective-permute-start | bytes 491528 | tf_op jit(solution)/shard_map/ppermute | solution.py:706
  579.4 20.4 %collective-permute-start.32 = (f32[320]{0:T(512)S(1)}, f32[320]{0:T(512)S(1)}, u32[]{:S(2)}, u32[]{:S(2)}) collective-permute-start(f32[320]{0:T(512)S(1)} %slice_reduce_fusion.13), channel_id=1, source_target_pairs={{0,1},{1,0},{2,3},{3,2},{4,5},{5,4},{6,7},{7,6},{8,9},{9,8},{10,11... | collective-permute-start | bytes 3848 | tf_op jit(solution)/shard_map/ppermute | solution.py:638
  599.8 3.6 collective-permute-start.33
  609.8 23.3 %collective-permute-start.26 = (bf16[384,1280]{1,0:T(8,128)(2,1)}, bf16[384,1280]{1,0:T(8,128)(2,1)S(1)}, u32[]{:S(2)}, u32[]{:S(2)}) collective-permute-start(bf16[384,1280]{1,0:T(8,128)(2,1)} %add_convert_fusion.1), channel_id=1, source_target_pairs={{0,2},{1,3},{2,0},{3,1},{4,6},{5,7},{6,4},{7,5},{8,10},{9,11},{10,... | collective-permute-start | bytes 2949128 | tf_op jit(solution)/shard_map/ppermute | solution.py:638
  611.1 24.0 %collective-permute-start.27 = (bf16[384,1280]{1,0:T(8,128)(2,1)S(1)}, bf16[384,1280]{1,0:T(8,128)(2,1)S(1)}, u32[]{:S(2)}, u32[]{:S(2)}) collective-permute-start(bf16[384,1280]{1,0:T(8,128)(2,1)S(1)} %add_convert_fusion), channel_id=1, source_target_pairs={{0,1},{1,0},{2,3},{3,2},{4,5},{5,4},{6,7},{7,6},{8,9},{9,8},{10,11... | collective-permute-start | bytes 2949128 | tf_op jit(solution)/shard_map/ppermute | solution.py:638
  (74 other events, 883.8 us)
Sparse Core Ops, SparseCore 0:
  12.1 108.3 all-gather.5
  122.6 65.4 all-gather.9
  189.8 69.0 all-gather.7
  264.4 77.7 reduce-scatter.3
  380.6 60.5 reduce-scatter.5
  502.6 67.4 reduce-scatter.7

commit v2 on v1

v2 whole, which is shorter than its diff:
```python
import functools
import jax
import jax.numpy as jnp
from jax import lax
from jax.experimental import pallas as pl
from jax.experimental.layout import Layout, with_layout_constraint
from jax.experimental.pallas import tpu as pltpu
from jax.sharding import PartitionSpec as P

N = 128
Q = 256
LANE = 128
BLK = 128
SLOTS = 32
UNROLL = 10
LOG2E = 1.4426950408889634
F32 = jnp.float32
BF16 = jnp.bfloat16
VMEM_CAP = 56 << 20


def mm(left, right):
    return lax.dot_general(left, right, (((1,), (0,)), ((), ())), preferred_element_type=F32)


def mm_nt(left, right):
    return lax.dot_general(left, right, (((1,), (1,)), ((), ())), preferred_element_type=F32)


def split_two(value):
    high = value.astype(BF16)
    low = (value - high.astype(F32)).astype(BF16)
    return high, low


def split_three(value):
    high = value.astype(BF16).astype(F32)
    rest = value - high
    mid = rest.astype(BF16).astype(F32)
    return high, mid, rest - mid


def as_columns(value):
    parts = split_three(value)
    stacked = jnp.concatenate(list(parts) + [jnp.zeros_like(value)], axis=0)
    return stacked.T.astype(BF16)


def lane_sums(value, table):
    parts = jnp.concatenate(split_three(value), axis=0).astype(BF16)
    sums = mm(parts, table)
    return sums[:SLOTS] + sums[SLOTS : 2 * SLOTS] + sums[2 * SLOTS :]


def iota2(shape, axis):
    return lax.broadcasted_iota(jnp.int32, shape, axis)


def step_terms(small_ref, meta_ref, hp_ref):
    on = hp_ref[:, 2:3]
    pre = (small_ref[...] + hp_ref[:, 0:1]) * on
    steps = (jnp.maximum(pre, 0.0) + jnp.log1p(jnp.exp(-jnp.abs(pre)))) * on
    upto = (iota2((Q, Q), 0) <= iota2((Q, Q), 1)).astype(BF16)
    cum = lane_sums(steps * hp_ref[:, 1:2], upto) * LOG2E
    into = jnp.exp2(cum) * meta_ref[0, 1:2, :] * on
    tail = jnp.exp2(cum[:, Q - 1 : Q] - cum) * meta_ref[0, 2:3, :] * on
    return pre, steps, cum, into, tail


def ssd_fwd_kernel(
    heads,
    raw_ref,
    small_ref,
    bc_ref,
    masks_ref,
    meta_ref,
    seg_ref,
    taps_ref,
    hp_ref,
    skip_ref,
    expand_ref,
    widen_ref,
    y_ref,
    st_ref,
    state,
    tail_rows,
    window,
    row_cum,
    scores,
    columns,
    spreads,
    wide_cum,
):
    chunk = pl.program_id(0)

    @pl.when(chunk == 0)
    def _():
        state[...] = jnp.zeros_like(state)
        tail_rows[...] = jnp.zeros_like(tail_rows)

    st_ref[0] = state[...]
    _, steps, cum, into, tail = step_terms(small_ref, meta_ref, hp_ref)
    row_cum[...] = cum
    for at, value in enumerate((cum, steps, into, tail)):
        columns[at] = as_columns(value)
    for at in range(3):
        spreads[at] = mm(columns[at + 1], expand_ref[...])
    cum_cols = jnp.concatenate([cum] * 4, axis=0).T
    for head in range(heads):
        wide_cum[:, head * LANE : (head + 1) * LANE] = jnp.broadcast_to(
            cum_cols[:, head : head + 1], (Q, LANE)
        )
    same = (seg_ref[:, 0:1] == meta_ref[0, 0:1, :]) & (iota2((Q, Q), 0) >= iota2((Q, Q), 1))
    b_turned = bc_ref[:N, :]
    c_rows = bc_ref[N:, :].astype(F32).T.astype(BF16)
    scores[...] = jnp.where(same, mm(c_rows, b_turned), 0.0)
    first = iota2((Q, LANE), 1) < LANE // 2

    def pair(index, _):
        lanes = pl.ds(pl.multiple_of(index * LANE, LANE), LANE)
        both = pl.ds(pl.multiple_of(index * 2 * LANE, 2 * LANE), 2 * LANE)
        window[0:8, :] = tail_rows[:, lanes]
        current = raw_ref[:, lanes]
        window[8 : 8 + Q, :] = current
        conv = taps_ref[4:5, lanes] + taps_ref[3:4, lanes] * current
        for offset in range(1, 4):
            conv = conv + taps_ref[3 - offset : 4 - offset, lanes] * (
                masks_ref[:, (offset - 1) * LANE : offset * LANE]
                * window[8 - offset : 8 - offset + Q, :]
            )
        vals = conv * jax.nn.sigmoid(conv)
        scaled = (vals * spreads[0, :, lanes]).astype(BF16)
        zero = jnp.zeros_like(scaled)
        own = (jnp.where(first, scaled, zero), jnp.where(first, zero, scaled))
        held = state[:, lanes]
        into_here = spreads[1, :, lanes]
        base = into_here * mm(c_rows, held.astype(BF16)) + skip_ref[0:1, lanes] * vals
        cum_cols = wide_cum[:, both]
        for low in range(0, Q, BLK):
            width = low + BLK
            total = base[low:width, :]
            for which in range(2):
                across = row_cum[pl.ds(index * 2 + which, 1), :][:, :width]
                down = cum_cols[low:width, which * LANE : (which + 1) * LANE]
                down = jnp.concatenate([down] * (width // LANE), axis=1)
                decays = jnp.exp2(jnp.minimum(down - across, 0.0))
                mixing = (decays * scores[low:width, :width]).astype(BF16)
                total = total + mm(mixing, own[which][:width, :])
            y_ref[low:width, lanes] = total
        weighted = (spreads[2, :, lanes] * scaled.astype(F32)).astype(BF16)
        state[:, lanes] = held * into_here[Q - 1 : Q, :] + mm(b_turned, weighted)
        return 0

    lax.fori_loop(0, heads // 2, pair, 0, unroll=UNROLL)
    tail_rows[...] = raw_ref[Q - 8 : Q, :]


def ssd_bwd_kernel(
    heads,
    raw_ref,
    halo_ref,
    small_ref,
    bc_ref,
    masks_ref,
    masks_next_ref,
    meta_ref,
    seg_ref,
    taps_ref,
    hp_ref,
    skip_ref,
    expand_ref,
    widen_ref,
    gather_ref,
    y_ref,
    dy_ref,
    st_ref,
    dx_ref,
    ddt_ref,
    dbc_ref,
    dtaps_ref,
    dhp_ref,
    dskip_ref,
    dstate,
    next_rows,
    carried,
    window,
    dwindow,
    row_cum,
    scores,
    dscores,
    columns,
    into_dy,
    tail_vals,
    balance_parts,
    direct_parts,
    wide_cum,
):
    chunk = pl.program_id(0)

    @pl.when(chunk == 0)
    def _():
        dstate[...] = jnp.zeros_like(dstate)
        next_rows[...] = jnp.zeros_like(next_rows)
        carried[...] = jnp.zeros_like(carried)
        dtaps_ref[...] = jnp.zeros_like(dtaps_ref)
        dhp_ref[...] = jnp.zeros_like(dhp_ref)
        dskip_ref[...] = jnp.zeros_like(dskip_ref)

    pre, steps, cum, into, tail = step_terms(small_ref, meta_ref, hp_ref)
    row_cum[...] = cum
    for at, value in enumerate((cum, steps, into, tail)):
        columns[at] = as_columns(value)
    cum_cols = jnp.concatenate([cum] * 4, axis=0).T
    for head in range(heads):
        wide_cum[:, head * LANE : (head + 1) * LANE] = jnp.broadcast_to(
            cum_cols[:, head : head + 1], (Q, LANE)
        )
    same = (seg_ref[:, 0:1] == meta_ref[0, 0:1, :]) & (iota2((Q, Q), 0) <= iota2((Q, Q), 1))
    b_rows = bc_ref[:N, :].astype(F32).T.astype(BF16)
    c_turned = bc_ref[N:, :]
    scores[...] = jnp.where(same, mm(b_rows, c_turned), 0.0)
    dscores[...] = jnp.zeros_like(dscores)
    carry_high, carry_low = split_two(carried[...])
    gather_all = gather_ref[...]
    from_next = mm(carry_high, gather_all) + mm(carry_low, gather_all)
    dstate_half = dstate[...].astype(BF16)
    first = iota2((Q, LANE), 1) < LANE // 2

    def pair(index, _):
        lanes = pl.ds(pl.multiple_of(index * LANE, LANE), LANE)
        both = pl.ds(pl.multiple_of(index * 2 * LANE, 2 * LANE), 2 * LANE)
        window[0:8, :] = halo_ref[:, lanes]
        current = raw_ref[:, lanes]
        window[8 : 8 + Q, :] = current
        conv = taps_ref[4:5, lanes] + taps_ref[3:4, lanes] * current
        for offset in range(1, 4):
            conv = conv + taps_ref[3 - offset : 4 - offset, lanes] * (
                masks_ref[:, (offset - 1) * LANE : offset * LANE]
                * window[8 - offset : 8 - offset + Q, :]
            )
        gate = jax.nn.sigmoid(conv)
        vals = conv * gate
        expand = expand_ref[:, lanes]
        step_here = mm(columns[1], expand)
        scaled = (vals * step_here).astype(BF16)
        skip = skip_ref[0:1, lanes]
        dy = dy_ref[:, lanes]
        dy_half = dy.astype(BF16)
        zero = jnp.zeros_like(scaled)
        own = (jnp.where(first, scaled, zero), jnp.where(first, zero, scaled))
        own_dy = (jnp.where(first, dy_half, zero), jnp.where(first, zero, dy_half))
        dheld = dstate[:, lanes]
        tail_here = mm(columns[3], expand)
        into_here = mm(columns[2], expand)
        base = tail_here * mm(b_rows, dheld.astype(BF16))
        cum_cols = wide_cum[:, both]
        pieces = []
        for low in range(0, Q, BLK):
            high = low + BLK
            total = base[low:high, :]
            for which in range(2):
                across = row_cum[pl.ds(index * 2 + which, 1), :][:, low:]
                down = cum_cols[low:high, which * LANE : (which + 1) * LANE]
                down = jnp.concatenate([down] * ((Q - low) // LANE), axis=1)
                decays = jnp.exp2(jnp.minimum(across - down, 0.0))
                mixing = (decays * scores[low:high, low:]).astype(BF16)
                total = total + mm(mixing, own_dy[which][low:, :])
                dmix = mm_nt(own[which][low:high, :], dy_half[low:, :])
                dscores[low:high, low:] += dmix * decays
            pieces.append(total)
        dscaled = jnp.concatenate(pieces, axis=0)
        held = st_ref[0, :, lanes]
        edy = (into_here * dy).astype(BF16)
        scaled_f = scaled.astype(F32)
        into_dy[:, lanes] = edy
        tail_vals[:, lanes] = (tail_here * scaled_f).astype(BF16)
        balance = dy_half.astype(F32) * (y_ref[:, lanes] - skip * vals) - scaled_f * dscaled
        part_high, part_low = split_two(balance)
        balance_parts[0, :, lanes] = part_high
        balance_parts[1, :, lanes] = part_low
        part_high, part_low = split_two(vals * dscaled)
        direct_parts[0, :, lanes] = part_high
        direct_parts[1, :, lanes] = part_low
        dskip_ref[0:1, lanes] += jnp.sum(dy * vals, axis=0, keepdims=True)
        dheld_new = into_here[Q - 1 : Q, :] * dheld + mm(c_turned, edy)
        dstate[:, lanes] = dheld_new
        carried[0:1, lanes] = jnp.sum(dheld_new * held, axis=0, keepdims=True)
        dvals = step_here * dscaled + skip * dy
        dconv = dvals * (gate * (1.0 + conv * (1.0 - gate)))
        dwindow[0:Q, :] = dconv
        dwindow[Q : Q + 8, :] = next_rows[:, lanes]
        next_rows[:, lanes] = dconv[0:8, :]
        dtaps_ref[4:5, lanes] += jnp.sum(dconv, axis=0, keepdims=True)
        dtaps_ref[3:4, lanes] += jnp.sum(dconv * current, axis=0, keepdims=True)
        draw = taps_ref[3:4, lanes] * dconv
        for offset in range(1, 4):
            mask = masks_ref[:, (offset - 1) * LANE : offset * LANE]
            mask_next = masks_next_ref[:, (offset - 1) * LANE : offset * LANE]
            mask_later = jnp.concatenate([mask, mask_next], axis=0)[offset : offset + Q, :]
            shifted = mask * window[8 - offset : 8 - offset + Q, :]
            dtaps_ref[3 - offset : 4 - offset, lanes] += jnp.sum(
                dconv * shifted, axis=0, keepdims=True
            )
            draw = draw + taps_ref[3 - offset : 4 - offset, lanes] * (
                mask_later * dwindow[offset : offset + Q, :]
            )
        dx_ref[:, lanes] = draw.astype(BF16)
        return 0

    lax.fori_loop(0, heads // 2, pair, 0, unroll=UNROLL)
    dscores_now = jnp.where(same, dscores[...], 0.0)
    d_b = mm_nt(tail_vals[...], dstate_half) + mm_nt(dscores_now.astype(BF16), c_turned)
    d_c = mm_nt(into_dy[...], st_ref[0].astype(BF16)) + mm(dscores_now.T.astype(BF16), b_rows)
    dbc_ref[:N, :] = d_b.T
    dbc_ref[N:, :] = d_c.T
    balance = mm(balance_parts[0], gather_all) + mm(balance_parts[1], gather_all)
    balance = balance + jnp.where(iota2((Q, LANE), 0) == Q - 1, from_next[0:1, :], 0.0)
    direct = mm(direct_parts[0], gather_all) + mm(direct_parts[1], gather_all)
    since = (iota2((Q, Q), 0) >= iota2((Q, Q), 1)).astype(BF16)
    dlogs = lane_sums(balance.T[:SLOTS], since)
    dsteps = dlogs * hp_ref[:, 1:2] + direct.T[:SLOTS]
    dsteps = dsteps * jax.nn.sigmoid(pre) * hp_ref[:, 2:3]
    ddt_ref[...] = dsteps
    dhp_ref[:, 0:1] += jnp.sum(dsteps, axis=1, keepdims=True)
    dhp_ref[:, 1:2] += jnp.sum(dlogs * steps, axis=1, keepdims=True)


def head_tables(heads):
    width = heads * (LANE // 2)
    owner = jnp.arange(width) // (LANE // 2)
    wide_owner = jnp.arange(heads * LANE) // LANE
    slot = jnp.arange(LANE)
    real = (slot < 3 * SLOTS)[:, None]
    expand = ((slot % SLOTS)[:, None] == owner[None, :]) & real
    widen = ((slot % SLOTS)[:, None] == wide_owner[None, :]) & real
    gather = owner[:, None] == slot[None, :]
    return expand.astype(BF16), widen.astype(BF16), gather.astype(BF16)


def segment_tables(segment):
    length = segment.shape[0]
    chunks = length // Q
    doc_masks = []
    for offset in range(1, 4):
        earlier = jnp.concatenate(
            [jnp.full((offset,), -1, jnp.int32), segment[: length - offset]], axis=0
        )
        doc_masks.append((earlier == segment).astype(F32))
    masks = jnp.concatenate(
        [jnp.broadcast_to(mask[:, None], (length, LANE)) for mask in doc_masks], axis=1
    )
    by_chunk = segment.reshape(chunks, Q)
    last = by_chunk[:, Q - 1]
    before = jnp.concatenate([jnp.full((1,), -1, jnp.int32), last[: chunks - 1]], axis=0)
    rows = [
        by_chunk.astype(F32),
        (by_chunk == before[:, None]).astype(F32),
        (by_chunk == last[:, None]).astype(F32),
    ]
    meta = jnp.pad(jnp.stack(rows, axis=1), ((0, 0), (0, 5), (0, 0)))
    seg_cols = jnp.broadcast_to(segment.astype(F32)[:, None], (length, LANE))
    return doc_masks, masks, meta, seg_cols


def head_columns(head_params):
    heads = head_params.shape[1]
    rates = -jnp.exp(head_params[1])
    table = jnp.stack([head_params[0], rates, jnp.ones_like(rates)], axis=1)
    return jnp.pad(table, ((0, SLOTS - heads), (0, LANE - 3)))


def time_like(seconds):
    return pl.CostEstimate(
        flops=int(seconds * 1.1e15), bytes_accessed=int(seconds * 3.4e12), transcendentals=0
    )


def full_spec(shape):
    return pl.BlockSpec(shape, lambda c: (0,) * len(shape))


def ssd_forward(raw, small, bc, tables, taps, hp, skip, spread, heads):
    length = raw.shape[0]
    width = heads * (LANE // 2)
    chunks = length // Q
    _, masks, meta, seg_cols = tables
    expand, widen, _ = spread
    return pl.pallas_call(
        functools.partial(ssd_fwd_kernel, heads),
        grid=(chunks,),
        out_shape=(
            jax.ShapeDtypeStruct((length, width), F32),
            jax.ShapeDtypeStruct((chunks, N, width), F32),
        ),
        in_specs=[
            pl.BlockSpec((Q, width), lambda c: (c, 0)),
            pl.BlockSpec((SLOTS, Q), lambda c: (0, c)),
            pl.BlockSpec((2 * N, Q), lambda c: (0, c)),
            pl.BlockSpec((Q, 3 * LANE), lambda c: (c, 0)),
            pl.BlockSpec((1, 8, Q), lambda c: (c, 0, 0)),
            pl.BlockSpec((Q, LANE), lambda c: (c, 0)),
            full_spec((8, width)),
            full_spec((SLOTS, LANE)),
            full_spec((8, width)),
            full_spec((LANE, width)),
            full_spec((LANE, heads * LANE)),
        ],
        out_specs=(
            pl.BlockSpec((Q, width), lambda c: (c, 0)),
            pl.BlockSpec((1, N, width), lambda c: (c, 0, 0)),
        ),
        scratch_shapes=[
            pltpu.VMEM((N, width), F32),
            pltpu.VMEM((8, width), F32),
            pltpu.VMEM((Q + 8, LANE), F32),
            pltpu.VMEM((SLOTS, Q), F32),
            pltpu.VMEM((Q, Q), F32),
            pltpu.VMEM((4, Q, LANE), BF16),
            pltpu.VMEM((3, Q, width), F32),
            pltpu.VMEM((Q, heads * LANE), F32),
        ],
        compiler_params=pltpu.CompilerParams(vmem_limit_bytes=VMEM_CAP),
        cost_estimate=time_like(37e-6 * length * heads / 30720),
        name="ssd_fwd",
    )(raw, small, bc, masks, meta, seg_cols, taps, hp, skip, expand, widen)


def ssd_backward(raw, small, bc, tables, taps, hp, skip, spread, y, dy, states, heads):
    length = raw.shape[0]
    width = heads * (LANE // 2)
    chunks = length // Q
    per = Q // 8
    _, masks, meta, seg_cols = tables

    def at(c):
        return chunks - 1 - c

    return pl.pallas_call(
        functools.partial(ssd_bwd_kernel, heads),
        grid=(chunks,),
        out_shape=(
            jax.ShapeDtypeStruct((length, width), BF16),
            jax.ShapeDtypeStruct((SLOTS, length), F32),
            jax.ShapeDtypeStruct((2 * N, length), F32),
            jax.ShapeDtypeStruct((8, width), F32),
            jax.ShapeDtypeStruct((SLOTS, LANE), F32),
            jax.ShapeDtypeStruct((8, width), F32),
        ),
        in_specs=[
            pl.BlockSpec((Q, width), lambda c: (at(c), 0)),
            pl.BlockSpec((8, width), lambda c: (jnp.maximum(at(c) * per - 1, 0), 0)),
            pl.BlockSpec((SLOTS, Q), lambda c: (0, at(c))),
            pl.BlockSpec((2 * N, Q), lambda c: (0, at(c))),
            pl.BlockSpec((Q, 3 * LANE), lambda c: (at(c), 0)),
            pl.BlockSpec(
                (8, 3 * LANE), lambda c: (jnp.minimum((at(c) + 1) * per, chunks * per - 1), 0)
            ),
            pl.BlockSpec((1, 8, Q), lambda c: (at(c), 0, 0)),
            pl.BlockSpec((Q, LANE), lambda c: (at(c), 0)),
            full_spec((8, width)),
            full_spec((SLOTS, LANE)),
            full_spec((8, width)),
            full_spec((LANE, width)),
            full_spec((LANE, heads * LANE)),
            full_spec((width, LANE)),
            pl.BlockSpec((Q, width), lambda c: (at(c), 0)),
            pl.BlockSpec((Q, width), lambda c: (at(c), 0)),
            pl.BlockSpec((1, N, width), lambda c: (at(c), 0, 0)),
        ],
        out_specs=(
            pl.BlockSpec((Q, width), lambda c: (at(c), 0)),
            pl.BlockSpec((SLOTS, Q), lambda c: (0, at(c))),
            pl.BlockSpec((2 * N, Q), lambda c: (0, at(c))),
            full_spec((8, width)),
            full_spec((SLOTS, LANE)),
            full_spec((8, width)),
        ),
        scratch_shapes=[
            pltpu.VMEM((N, width), F32),
            pltpu.VMEM((8, width), F32),
            pltpu.VMEM((8, width), F32),
            pltpu.VMEM((Q + 8, LANE), F32),
            pltpu.VMEM((Q + 8, LANE), F32),
            pltpu.VMEM((SLOTS, Q), F32),
            pltpu.VMEM((Q, Q), F32),
            pltpu.VMEM((Q, Q), F32),
            pltpu.VMEM((4, Q, LANE), BF16),
            pltpu.VMEM((Q, width), BF16),
            pltpu.VMEM((Q, width), BF16),
            pltpu.VMEM((2, Q, width), BF16),
            pltpu.VMEM((2, Q, width), BF16),
            pltpu.VMEM((Q, heads * LANE), F32),
        ],
        compiler_params=pltpu.CompilerParams(vmem_limit_bytes=VMEM_CAP),
        cost_estimate=time_like(69e-6 * length * heads / 30720),
        name="ssd_bwd",
    )(
        raw,
        raw,
        small,
        bc,
        masks,
        masks,
        meta,
        seg_cols,
        taps,
        hp,
        skip,
        *spread,
        y,
        dy,
        states,
    )


def dn_kernel(count, rows, at_ref, *refs):
    dz, dx, side, normed = (refs[k * count : (k + 1) * count] for k in range(4))
    gate_ref, inner_ref, out_ref, sums_ref = refs[4 * count : 4 * count + 4]
    turned = refs[4 * count + 4]
    width = dz[0].shape[1]

    @pl.when(pl.program_id(0) == 0)
    def _():
        for k in range(count):
            turned[k * rows : (k + 1) * rows, :] = side[k][...].T.astype(BF16)

    gate = gate_ref[...]
    inner = inner_ref[:, :width]
    last = inner_ref[:, width:]
    sums = None
    for k in range(count):
        at = slice(k * rows, (k + 1) * rows)
        total = mm_nt(dz[k][...], gate) + mm_nt(dx[k][...], inner) + mm_nt(turned[at, :], last)
        out_ref[at, :] = total.astype(BF16)
        part = jnp.sum(total * normed[k][...].astype(F32), axis=0, keepdims=True)
        sums = part if sums is None else sums + part
    sums_ref[0:1, :] = sums


def d_normed_blocks(d_z, d_x, d_side, gate_all, x_all, normed, blocks, which, rows, tile=256):
    length, width = d_z.shape
    count = blocks.shape[0]
    half = gate_all.shape[0] // 2
    first = which * half // tile

    def rows_of(k):
        return pl.BlockSpec((rows, width), lambda n, at, k=k: (at[k], 0))

    def cols_of(k):
        return pl.BlockSpec((LANE, rows), lambda n, at, k=k: (0, at[k]))

    def tile_of(k):
        return pl.BlockSpec((rows, tile), lambda n, at, k=k: (at[k], n + first))

    each = range(count)
    return pl.pallas_call(
        functools.partial(dn_kernel, count, rows),
        grid_spec=pltpu.PrefetchScalarGridSpec(
            num_scalar_prefetch=1,
            grid=(half // tile,),
            in_specs=[rows_of(k) for k in each]
            + [rows_of(k) for k in each]
            + [cols_of(k) for k in each]
            + [tile_of(k) for k in each]
            + [
                pl.BlockSpec((tile, width), lambda n, at: (n + first, 0)),
                pl.BlockSpec((tile, width + LANE), lambda n, at: (n + first, 0)),
            ],
            out_specs=(
                pl.BlockSpec((count * rows, tile), lambda n, at: (0, n)),
                pl.BlockSpec((8, tile), lambda n, at: (0, n)),
            ),
            scratch_shapes=[pltpu.VMEM((count * rows, LANE), BF16)],
        ),
        out_shape=(
            jax.ShapeDtypeStruct((count * rows, half), BF16),
            jax.ShapeDtypeStruct((8, half), F32),
        ),
        compiler_params=pltpu.CompilerParams(vmem_limit_bytes=VMEM_CAP),
        cost_estimate=time_like(1e-7),
        name="d_normed",
    )(
        blocks,
        *([d_z] * count),
        *([d_x] * count),
        *([d_side] * count),
        *([normed] * count),
        gate_all,
        x_all,
    )


def adam_kernel(step, gate_ref, inner_ref, weight_ref, first_ref, second_ref, *outs):
    grad_out, weight_out, first_out, second_out = outs
    for part, grad_ref in ((0, gate_ref), (1, inner_ref)):
        grad = grad_ref[...].astype(F32)
        new_weight, new_first, new_second = step(
            weight_ref[:, part, :], grad, first_ref[:, part, :], second_ref[:, part, :]
        )
        grad_out[:, part, :] = grad
        weight_out[:, part, :] = new_weight
        first_out[:, part, :] = new_first
        second_out[:, part, :] = new_second


def adam_pair(step, grad_gate, grad_inner, weight, first, second, rows=40):
    shard, _, width = weight.shape
    deep = pl.BlockSpec((rows, 2, width), lambda n: (n, 0, 0))
    flat = pl.BlockSpec((rows, width), lambda n: (n, 0))
    like = jax.ShapeDtypeStruct(weight.shape, F32)
    return pl.pallas_call(
        functools.partial(adam_kernel, step),
        grid=(shard // rows,),
        out_shape=(like, jax.ShapeDtypeStruct(weight.shape, weight.dtype), like, like),
        in_specs=[flat, flat, deep, deep, deep],
        out_specs=(deep,) * 4,
        compiler_params=pltpu.CompilerParams(vmem_limit_bytes=VMEM_CAP),
        cost_estimate=pl.CostEstimate(flops=1000, bytes_accessed=1000, transcendentals=0),
        name="adam_pair",
    )(grad_gate, grad_inner, weight, first, second)

DI = 5120
STEP = 3
NORM_EPS = 1e-05
BETA_ONE = 0.9
BETA_TWO = 0.95
LEARN_RATE = 0.004
LEARN_SMALL = 0.15
WEIGHT_DECAY = 0.1
ADAM_EPS = 1e-08


def by_rows(value):
    return with_layout_constraint(value, Layout(major_to_minor=(0, 1)))


def silu_act(values):
    return values * jax.nn.sigmoid(values)


def later(row, offset):
    return jnp.pad(row, ((0, 0), (offset, 0)))[:, : row.shape[1]]


def state_act(raw_cols, conv_taps, doc_masks):
    conv = conv_taps[4][:, None] + conv_taps[3][:, None] * raw_cols
    for offset in range(1, 4):
        conv = conv + conv_taps[3 - offset][:, None] * (
            doc_masks[offset - 1][None, :] * later(raw_cols, offset)
        )
    return silu_act(conv)


def contract_rows(left_mat, right_mat):
    return lax.dot_general(
        left_mat, right_mat, (((0,), (0,)), ((), ())), preferred_element_type=F32
    )


def adamw_step(weight, gradient, first_moment, second_moment, decay_factor, learn_rate):
    new_first = BETA_ONE * first_moment + (1.0 - BETA_ONE) * gradient
    new_second = BETA_TWO * second_moment + (1.0 - BETA_TWO) * gradient * gradient
    first_hat = new_first / (1.0 - BETA_ONE**STEP)
    second_hat = new_second / (1.0 - BETA_TWO**STEP)
    weight_f = weight.astype(F32)
    updated = weight_f - learn_rate * (
        first_hat / (jnp.sqrt(second_hat) + ADAM_EPS) + decay_factor * weight_f
    )
    return (updated.astype(weight.dtype), new_first, new_second)


def swap(value, distance, size):
    return lax.ppermute(value, "tp", [(at, at ^ distance) for at in range(size)])


def tied(*values):
    return lax.optimization_barrier(values)


def gather_parts(value, size, near_done):
    if size != 4:
        one, *others = near_done(swap(value, 1, size))
        return [value, one] + [swap(value, k, size) for k in range(2, size)], *others
    half = value.shape[0] // 2
    one, two = swap(value, 1, size), swap(value, 2, size)
    one, *others = near_done(one)
    far = jnp.concatenate([swap(two[:half], 1, size), swap(one[half:], 2, size)], axis=0)
    return [value, one, two, far], *others


def scatter_start(left, right, rows, index, size):
    def block(value, distance):
        return lax.dynamic_slice_in_dim(value, (index ^ distance) * rows, rows, 0)

    sent, kept = [], []
    for half, near in ((left, 1), (right, 2)):
        if size == 4:
            pair = jnp.concatenate([block(half, 3), block(half, near)], axis=0)
            sent.append(swap(pair, near, size))
            kept.append((block(half, 3 - near), block(half, 0)))
        else:
            sent.append([swap(block(half, k), k, size) for k in range(1, size)])
            kept.append(block(half, 0))
    return sent, kept


def scatter_middle(sent, kept, rows, size):
    if size != 4:
        return sent, [(one,) for one in kept]
    passed = [
        (kept[at][0].astype(F32) + sent[at][:rows].astype(F32)).astype(BF16) for at in range(2)
    ]
    return passed, [(kept[at][1], sent[at][rows:]) for at in range(2)]


def scatter_last(passed, size):
    if size != 4:
        return passed[0] + passed[1]
    return [swap(passed[0], 2, size), swap(passed[1], 1, size)]


def scatter_end(own, last):
    each = len(last) // 2
    totals = []
    for at in range(2):
        total = own[at][0].astype(F32)
        for piece in own[at][1:]:
            total = total + piece.astype(F32)
        for piece in last[at * each : (at + 1) * each]:
            total = total + piece.astype(F32)
        totals.append(total)
    return jnp.concatenate(totals, axis=1)


def all_sum(value, size):
    distance = 1
    while distance < size:
        value = value + swap(value, distance, size)
        distance *= 2
    return value


def fsdp_swap(value, distance, size):
    return lax.ppermute(value, "fsdp", [(at, at ^ distance) for at in range(size)])


def gather_by_swaps(value, index, size):
    whole = jnp.zeros((size,) + value.shape, value.dtype)
    for distance in range(size):
        piece = value if distance == 0 else fsdp_swap(value, distance, size)
        whole = lax.dynamic_update_slice(whole, piece[None], (index ^ distance, jnp.int32(0)))
    return whole


def pair_sum(value, index, size):
    blocks = value.reshape(size // 2, 2, value.shape[0] // size, value.shape[1])
    core = index % 2
    away = lax.dynamic_slice_in_dim(blocks, 1 - core, 1, 1)[:, 0]
    own = lax.dynamic_slice_in_dim(blocks, core, 1, 1)[:, 0]
    return (own.astype(F32) + fsdp_swap(away, 1, size).astype(F32)).astype(value.dtype)


def chip_scatter(value, size):
    groups = [list(range(core, size, 2)) for core in range(2)]
    flat = value.reshape(value.shape[0] * value.shape[1], value.shape[2])
    return lax.psum_scatter(
        flat, "fsdp", scatter_dimension=0, axis_index_groups=groups, tiled=True
    )


def chip_sum(value, index, size):
    chip = index // 2

    def block(distance):
        return lax.dynamic_slice_in_dim(value, chip ^ distance, 1, 0)[0]

    total = block(0).astype(F32)
    for distance in range(1, size // 2):
        total = total + fsdp_swap(block(distance), 2 * distance, size).astype(F32)
    return total


def pad_cols(value, width):
    return jnp.pad(value, ((0, 0), (0, width - value.shape[1])))


def body(
    block_in,
    cotangent,
    segment_ids,
    group_fill,
    input_gain,
    proj_inner,
    proj_step,
    proj_state,
    conv_inner,
    conv_state,
    head_params,
    mixer_gain,
    proj_output,
    *moments,
):
    tp_size = lax.axis_size("tp")
    fsdp_size = lax.axis_size("fsdp")
    tp_index = lax.axis_index("tp")
    fsdp_index = lax.axis_index("fsdp")
    own_rows, model = block_in.shape
    group_rows = own_rows * tp_size
    shard, _, width = proj_inner.shape
    heads = proj_step.shape[1]
    state_cols = proj_state.shape[1]
    segment = segment_ids[0]
    filled = group_fill[0]

    small_values = jnp.concatenate(
        [conv_inner.reshape(-1), conv_state.reshape(-1), mixer_gain], axis=0
    )
    small_count = small_values.shape[0]
    inner_n, state_n = conv_inner.size, conv_state.size
    small_cols = -(-(small_count + 3 * heads) // shard)
    small_block = jnp.pad(small_values, (0, small_cols * shard - small_count)).reshape(
        shard, small_cols
    )
    used = heads + state_cols
    side = pad_cols(
        jnp.concatenate([proj_step, proj_state, input_gain[:, None], small_block], axis=1), LANE
    )
    x_local = jnp.concatenate([proj_inner[:, 1, :], side], axis=1)
    x_all = lax.all_gather(x_local, "fsdp", axis=0, tiled=True)
    gate_all = lax.all_gather(proj_inner[:, 0, :], "fsdp", axis=0, tiled=True)
    gain_all = lax.dynamic_update_slice(
        jnp.zeros((fsdp_size, shard), BF16), input_gain[None], (fsdp_index, jnp.int32(0))
    )
    distance = 1
    while distance < fsdp_size:
        gain_all = gain_all + fsdp_swap(gain_all, distance, fsdp_size)
        distance *= 2
    gain_f = gain_all.reshape(model).astype(F32)
    positions = tp_index * own_rows + jnp.arange(own_rows, dtype=jnp.int32)
    live_rows = (positions < filled)[:, None]
    block_f = block_in.astype(F32)
    cot_f = cotangent.astype(F32)
    own_grad = jnp.where(live_rows, cot_f, 0.0).astype(BF16)
    blank = jnp.zeros((group_rows, model), BF16)

    def unit_of(rows):
        rows_f = rows.astype(F32)
        scale = lax.rsqrt(jnp.mean(rows_f * rows_f, axis=1, keepdims=True) + NORM_EPS)
        return rows_f * scale, scale

    def normed_of(rows):
        return (unit_of(rows)[0] * gain_f[None, :]).astype(BF16)

    def put(whole, part, distance):
        return lax.dynamic_update_slice(
            whole, part, ((tp_index ^ distance) * own_rows, jnp.int32(0))
        )

    started = put(blank, normed_of(block_in), 0)

    def near_done(one):
        return tied(one, started, own_grad)

    row_parts, started, own_grad = gather_parts(block_in, tp_size, near_done)
    row_parts = [by_rows(part) for part in row_parts]
    out_local, *row_parts = tied(proj_output.T, *row_parts)
    out_all = lax.all_gather(out_local, "fsdp", axis=0, tiled=True)
    own_grad, *row_parts = tied(own_grad, *row_parts)
    near = min(3, tp_size)
    grad_parts = [by_rows(own_grad)] + [swap(own_grad, k, tp_size) for k in range(1, near)]

    side_all = x_all[:, width:]
    extras = side_all[:, used + 1 : used + 1 + small_cols].reshape(fsdp_size, shard * small_cols)

    def from_owners(flat, rows):
        return flat.reshape(fsdp_size, rows, -1).transpose(1, 0, 2).reshape(rows, -1).astype(F32)

    taps_inner = from_owners(extras[:, :inner_n], 5)
    taps_state = from_owners(extras[:, inner_n : inner_n + state_n], 5)
    mixer_f = from_owners(extras[:, inner_n + state_n : small_count], 1)[0]

    normed = started
    for distance in range(1, tp_size - 1):
        normed = put(normed, normed_of(row_parts[distance]), distance)
    far_rows, normed = tied(row_parts[-1], normed)
    normed = by_rows(put(normed, normed_of(far_rows), tp_size - 1))
    small = lax.dot_general(
        side_all, normed, (((0,), (1,)), ((), ())), preferred_element_type=F32
    )
    raw = mm(normed, x_all)
    tables = segment_tables(segment)
    doc_masks = tables[0]
    state_vals, state_back = jax.vjp(
        lambda raw_cols, conv_taps: state_act(raw_cols, conv_taps, doc_masks),
        small[heads:used],
        taps_state,
    )
    state_local = state_vals.astype(BF16)
    bc = jnp.zeros((tp_size * state_cols, group_rows), BF16)
    for k in range(tp_size):
        piece = state_local if k == 0 else swap(state_local, k, tp_size)
        bc = lax.dynamic_update_slice(bc, piece, ((tp_index ^ k) * state_cols, jnp.int32(0)))
    own_grad, bc = tied(own_grad, bc)
    grad_parts += [swap(own_grad, k, tp_size) for k in range(near, tp_size)]
    spread = head_tables(heads)
    taps8 = jnp.pad(taps_inner, ((0, 3), (0, 0)))
    hp8 = head_columns(head_params)
    skip8 = jnp.broadcast_to(jnp.repeat(head_params[2], LANE // 2)[None, :], (8, width))
    mixed, states = ssd_forward(raw, small, bc, tables, taps8, hp8, skip8, spread, heads)

    z_raw = mm(normed, gate_all)
    sig = jax.nn.sigmoid(z_raw)
    gate_act = z_raw * sig
    gated = mixed * gate_act
    square_sum, *grad_parts = tied(jnp.sum(gated * gated, axis=1), *grad_parts)
    square_sum = all_sum(square_sum, tp_size)
    group_grad = jnp.zeros((group_rows, model), BF16)
    for distance in range(tp_size):
        group_grad = put(group_grad, grad_parts[distance], distance)
    group_grad = by_rows(group_grad)
    inv_gate = lax.rsqrt(square_sum / DI + NORM_EPS)[:, None]
    unit_gated = gated * inv_gate
    normed_gated = (unit_gated * mixer_f[None, :]).astype(BF16)
    sum_out = pair_sum(
        contract_rows(group_grad, normed_gated).astype(BF16), fsdp_index, fsdp_size
    )
    half = model // 2
    mixed_halves = [mm_nt(normed_gated, out_all[:half])]
    normed_gated, sum_out = tied(normed_gated, sum_out)
    grad_out = chip_scatter(sum_out, fsdp_size)
    mixed_halves.append(mm_nt(normed_gated, out_all[half:]))
    inner_sum = jnp.sum(mixed_halves[0] * group_grad[:, :half].astype(F32), axis=1) + jnp.sum(
        mixed_halves[1] * group_grad[:, half:].astype(F32), axis=1
    )
    inner_sum = all_sum(inner_sum, tp_size)
    mixed_left, mixed_right = (part.astype(BF16) for part in mixed_halves)
    mixed_sent, mixed_kept = scatter_start(mixed_left, mixed_right, own_rows, tp_index, tp_size)

    inner_mean = inner_sum[:, None] / DI
    d_ng = mm(group_grad, out_all)
    grad_mixer = jnp.sum(d_ng * unit_gated, axis=0)
    d_gated = inv_gate * (d_ng * mixer_f[None, :] - unit_gated * inner_mean)
    d_mixed = d_gated * gate_act
    d_z = (d_gated * mixed * sig * (1.0 + z_raw * (1.0 - sig))).astype(BF16)
    part_gate, mixed_sent = tied(contract_rows(normed, d_z).astype(BF16), mixed_sent)
    sum_gate = pair_sum(part_gate, fsdp_index, fsdp_size)
    mixed_passed, mixed_kept = scatter_middle(mixed_sent, mixed_kept, own_rows, tp_size)
    sum_gate, grad_out = tied(sum_gate, grad_out)

    d_mixed, sum_gate, mixed_passed = tied(d_mixed, sum_gate, mixed_passed)
    mixed_last = scatter_last(mixed_passed, tp_size)
    grad_gate = chip_scatter(sum_gate, fsdp_size)
    d_x, d_dt, d_bc, d_taps, d_heads, d_skip = ssd_backward(
        raw, small, bc, tables, taps8, hp8, skip8, spread, mixed, d_mixed, states, heads
    )
    def state_block(distance):
        return lax.dynamic_slice_in_dim(d_bc, (tp_index ^ distance) * state_cols, state_cols, 0)

    state_parts = [state_block(0)]
    state_parts += [swap(state_block(k), k, tp_size) for k in range(1, tp_size)]
    part_x, mixed_last, grad_gate, *state_parts = tied(
        contract_rows(normed, d_x).astype(BF16), mixed_last, grad_gate, *state_parts
    )
    sum_x = pair_sum(part_x, fsdp_index, fsdp_size)

    d_state_raw, grad_conv_state = state_back(sum(state_parts[1:], state_parts[0]).astype(F32))
    d_side = jnp.concatenate([d_dt[:heads], d_state_raw], axis=0)
    d_side = jnp.pad(d_side, ((0, LANE - used), (0, 0)))

    four = tp_size == 4
    side_part = lax.dot_general(
        normed, d_side.astype(BF16), (((0,), (1,)), ((), ())), preferred_element_type=F32
    )

    def side_gradient(side_part, d_taps, d_skip, d_heads, grad_conv_state, gain_sums):
        grad_head = jnp.stack(
            [
                d_heads[:heads, 0],
                hp8[:heads, 1] * d_heads[:heads, 1],
                jnp.sum(d_skip[0].reshape(heads, LANE // 2), axis=1),
            ],
            axis=0,
        )

        def by_owner(value):
            rows = value.shape[0]
            return value.reshape(rows, fsdp_size, -1).transpose(1, 0, 2).reshape(fsdp_size, -1)

        grad_extras = jnp.concatenate(
            [
                by_owner(d_taps[:5]),
                by_owner(grad_conv_state),
                by_owner(grad_mixer[None, :]),
                jnp.broadcast_to(grad_head.reshape(1, -1), (fsdp_size, 3 * heads)),
            ],
            axis=1,
        )
        grad_extras = pad_cols(grad_extras, small_cols * shard).reshape(fsdp_size * shard, small_cols)
        grad_extras = jnp.concatenate([gain_sums[:, None], grad_extras], axis=1)
        side_part = side_part + jnp.pad(
            grad_extras, ((0, 0), (used, LANE - used - 1 - small_cols))
        )
        side_part = pair_sum(side_part, fsdp_index, fsdp_size)
        return chip_sum(side_part, fsdp_index, fsdp_size)

    def d_normed_of(distances, which):
        return d_normed_blocks(
            d_z, d_x, d_side, gate_all, x_all, normed, tp_index ^ jnp.array(distances), which, own_rows
        )

    if four:
        left_away, gains_one = d_normed_of([3, 1], 0)
        gains_one, sum_x = tied(gains_one, sum_x)
        right_away, gains_two = d_normed_of([3, 2], 1)
        gains_two, mixed_last, d_taps, d_skip, d_heads, grad_conv_state = tied(
            gains_two, mixed_last, d_taps, d_skip, d_heads, grad_conv_state
        )
        sent = [swap(left_away, 1, 4), swap(right_away, 2, 4)]
        left_kept, gains_three = d_normed_of([2, 0], 0)
        sent[0], d_side_late, side_part = tied(sent[0], d_side, side_part)
        right_kept, gains_four = d_normed_blocks(
            d_z, d_x, d_side_late, gate_all, x_all, normed, tp_index ^ jnp.array([1, 0]), 1, own_rows
        )
        kept = [
            (left_kept[:own_rows], left_kept[own_rows:]),
            (right_kept[:own_rows], right_kept[own_rows:]),
        ]
        gain_sums = jnp.concatenate([gains_one + gains_three, gains_two + gains_four], axis=1)[0]
    else:
        left, gains_one = d_normed_of(list(range(tp_size)), 0)
        right, gains_two = d_normed_of(list(range(tp_size)), 1)
        sent = [
            [
                swap(part[k * own_rows : (k + 1) * own_rows], k, tp_size)
                for k in range(1, tp_size)
            ]
            for part in (left, right)
        ]
        kept = [left[:own_rows], right[:own_rows]]
        gain_sums = jnp.concatenate([gains_one, gains_two], axis=1)[0]
    grad_x = chip_scatter(sum_x, fsdp_size)
    passed, kept = scatter_middle(sent, kept, own_rows, tp_size)
    passed, mixed_last = tied(passed, mixed_last)
    mixed_rows = scatter_end(mixed_kept, mixed_last)
    block_out = (block_f + jnp.where(live_rows, mixed_rows, 0.0)).astype(BF16)
    grad_x, passed = tied(grad_x, passed)
    last = scatter_last(passed, tp_size)
    grad_side = side_gradient(side_part, d_taps, d_skip, d_heads, grad_conv_state, gain_sums)
    gain_part, last[0] = tied(grad_side[:, used], last[0])
    grad_input_gain = all_sum(gain_part, tp_size) / input_gain.astype(F32)
    d_normed = scatter_end(kept, last)

    unit_rows, inv_rms = unit_of(block_in)
    scaled = d_normed * gain_f[None, :]
    d_block = inv_rms * (scaled - unit_rows * jnp.mean(scaled * unit_rows, axis=1, keepdims=True))
    d_input = (cot_f + d_block).astype(BF16)

    own_extras = grad_side[:, used + 1 : used + 1 + small_cols].reshape(-1)
    grads = (
        grad_input_gain,
        None,
        grad_side[:, :heads],
        grad_side[:, heads:used],
        own_extras[:inner_n].reshape(conv_inner.shape),
        own_extras[inner_n : inner_n + state_n].reshape(conv_state.shape),
        own_extras[small_count : small_count + 3 * heads].reshape(3, heads),
        own_extras[inner_n + state_n : small_count],
        grad_out.astype(F32).T,
    )
    weights = (
        input_gain,
        proj_inner,
        proj_step,
        proj_state,
        conv_inner,
        conv_state,
        head_params,
        mixer_gain,
        proj_output,
    )
    large = (1, 2, 3, 8)
    grads = list(grads)
    updated = [None] * 9
    for at in range(9):
        decay = WEIGHT_DECAY if at in large else 0.0
        rate = LEARN_RATE if at in large else LEARN_SMALL
        if at == 1:
            grads[1], *updated[1] = adam_pair(
                lambda w, g, m, v: adamw_step(w, g, m, v, WEIGHT_DECAY, LEARN_RATE),
                grad_gate,
                grad_x,
                proj_inner,
                moments[1],
                moments[10],
            )
        else:
            updated[at] = adamw_step(
                weights[at], grads[at], moments[at], moments[9 + at], decay, rate
            )
    return (
        block_out,
        d_input,
        *grads,
        *[entry[0] for entry in updated],
        *[entry[1] for entry in updated],
        *[entry[2] for entry in updated],
    )


def weight_specs():
    return (
        P("fsdp"),
        P("fsdp", None, "tp"),
        P("fsdp", "tp"),
        P("fsdp", "tp"),
        P(None, ("tp", "fsdp")),
        P(None, ("tp", "fsdp")),
        P(None, "tp"),
        P(("tp", "fsdp")),
        P("tp", "fsdp"),
    )


def solution(mesh):
    rows = P(("fsdp", "tp"), None)
    return jax.shard_map(
        body,
        mesh=mesh,
        in_specs=(rows, rows, P("fsdp", None), P("fsdp")) + weight_specs() * 3,
        out_specs=(rows, rows) + weight_specs() * 4,
        check_vma=False,
    )
```

time: 657 us -> 571 us (0.87)
  local copies, waits for them, and re-layouts: 94.2 us -> 56.6 us
  waiting for transfers between devices: 99.8 us -> 68.2 us
  other arithmetic: 113 us -> 85.1 us
  blocking collectives: 27.6 us -> 0 us
  matrix products: 116 us -> 141 us
  starting transfers between devices: 36.6 us -> 56.1 us
  Pallas kernels: 146 us -> 139 us
    pallas_call x2 -> x5, Pallas kernels: 39.2 us -> 63.6 us  [the longest x4 48 us: d_normed_blocks(): pl.pallas_call(functools.partial(dn_kernel, count, rows), grid_spec=pltpu...]
    convert_element_type x11 -> x9, other arithmetic: 28.4 us -> 7.18 us  [the longest x1 3.4 us: body(): own_grad = jnp.where(live_rows, cot_f, 0.0).astype(BF16)]
    unnamed x177 -> x162, local copies, waits for them, and re-layouts: 34.1 us -> 13.2 us
    reduce_scatter x3, waiting for transfers between devices: 19.9 us -> 0.02 us  [chip_scatter(): lax.psum_scatter(flat, 'fsdp', scatter_dimension=0, axis_index_groups=gro...]
    psum x2 -> x0, blocking collectives: 17.1 us -> none  [the longest x1 9.16 us: body(): square_sum = lax.psum(jnp.sum(gated * gated, axis=1), 'tp')]
    pallas_call x1, Pallas kernels: 37.7 us -> 21.3 us  [ssd_forward(): pl.pallas_call(functools.partial(ssd_fwd_kernel, heads), grid=(chunks,),...]
    ppermute x14 -> x10, waiting for transfers between devices: 27.6 us -> 12 us  [fsdp_swap(): lax.ppermute(value, 'fsdp', [(at, at ^ distance) for at in range(size)])]
    pallas_call x1, Pallas kernels: 68.8 us -> 53.7 us  [ssd_backward(): pl.pallas_call(functools.partial(ssd_bwd_kernel, heads), grid=(chunks,),...]
  transfers between devices with their start and end apart: 40 -> 43, of which waited for: 15 -> 17; matrix products, arithmetic and copies ran while one was open for 42% -> 45% of each run, Pallas kernels for 22% -> 25%
where the time goes in v2:
time: 571 us; the launch traced here: 562 us
  matrix products  141 us (25%)
  Pallas kernels  139 us (24%)
  other arithmetic  85.1 us (15%)
  waiting for transfers between devices  68.2 us (12%)
  local copies, waits for them, and re-layouts  56.6 us (10%)
  starting transfers between devices  56.1 us (10%)
  between operations  16.5 us (3%)
    dot_general x3, matrix products, mm(): lax.dot_general(left, right, (((1,), (0,)), ((), ())), preferred_element_...  63.1 us
    ppermute x27, waiting for transfers between devices, swap(): lax.ppermute(value, 'tp', [(at, at ^ distance) for at in range(size)])  56 us
    pallas_call x1, Pallas kernels, ssd_backward(): pl.pallas_call(functools.partial(ssd_bwd_kernel, heads), grid=(chunks,),...  53.7 us
    pallas_call x4, Pallas kernels, d_normed_blocks(): pl.pallas_call(functools.partial(dn_kernel, count, rows), grid_spec=pltpu...  48 us
    dot_general x3, matrix products, contract_rows(): lax.dot_general(left_mat, right_mat, (((0,), (0,)), ((), ())), preferred_...  41.4 us
    ppermute x27, starting transfers between devices, swap(): lax.ppermute(value, 'tp', [(at, at ^ distance) for at in range(size)])  36.8 us
    dot_general x2, matrix products, mm_nt(): lax.dot_general(left, right, (((1,), (1,)), ((), ())), preferred_element_...  25.7 us
    pallas_call x1, Pallas kernels, ssd_forward(): pl.pallas_call(functools.partial(ssd_fwd_kernel, heads), grid=(chunks,),...  21.3 us
  transfers between devices with their start and end apart: 43, of which 17 were waited for; matrix products, arithmetic and copies ran while one was open for 45% of the time, Pallas kernels for 25%

profile of v2, /device:TPU:0, one launch (start us, length us, event | category | flops | bytes accessed | tf_op | source)
XLA Modules:
  0.0 561.7 jit_solution(130275457391807580)
XLA Ops:
  12.3 5.6 fusion.115
  19.2 2.4 copy.289
  21.7 3.0 collective-permute-start.4
  28.4 3.4 fusion.7
  37.4 2.4 collective-permute-start.3
  43.7 23.9 %collective-permute-done.4 = bf16[384,2560]{1,0:T(8,128)(2,1)} collective-permute-done((bf16[384,2560]{1,0:T(8,128)(2,1)S(1)}, bf16[384,2560]{1,0:T(8,128)(2,1)}, u32[]{:S(2)}, u32[]{:S(2)}) %collective-permute-start.4) | collective-permute-done | bytes 1966112 | tf_op jit(solution)/shard_map/ppermute | solution.py:673
  77.1 14.8 %collective-permute-done.5 = bf16[192,2560]{1,0:T(8,128)(2,1)S(1)} collective-permute-done((bf16[192,2560]{1,0:T(8,128)(2,1)S(1)}, bf16[192,2560]{1,0:T(8,128)(2,1)S(1)}, u32[]{:S(2)}, u32[]{:S(2)}) %collective-permute-start.5) | collective-permute-done | bytes 983072 | tf_op jit(solution)/shard_map/ppermute | solution.py:673
  91.9 2.5 collective-permute-done.6
  96.6 3.0 fusion.9
  99.6 3.4 fusion.32
  103.0 3.5 fusion.31
  107.0 11.3 %reduce-scatter.4.cloned.1.call-start = ((), (), s32[]{:S(2)}) async-start(), calls=%async_computation.5 | async-start | bytes 4096000 | tf_op jit(solution)/shard_map/reduce_scatter | solution.py:766
  123.2 6.2 %fusion.40.small_ref = f32[128,1536]{1,0:T(8,128)S(1)} fusion(bf16[1536,2560]{1,0:T(8,128)(2,1)} %fusion.30.refs_6_.refs_7_, bf16[2560,1408]{1,0:T(8,128)(2,1)} %all-gather.5.cloned.1.call-done.refs_9_), kind=kOutput, calls=%fused_computation.95 | convolution fusion | flops 1006632960 | bytes 9306112 | tf_op jit(solution)/shard_map/dot_general | solution.py:887
  135.9 18.3 %fusion.116.raw_ref.halo_ref = f32[1536,1408]{1,0:T(8,128)} fusion(bf16[1536,2560]{1,0:T(8,128)(2,1)} %fusion.30.refs_6_.refs_7_, bf16[2560,1408]{1,0:T(8,128)(2,1)} %all-gather.5.cloned.1.call-done.refs_9_), kind=kOutput, calls=%fused_computation.292 | convolution fusion | flops 11072962560 | bytes 23724032 | tf_op jit(solution)/shard_map/dot_general | solution.py:23
  161.3 21.3 %ssd_fwd.1 = (f32[1536,1280]{1,0:T(8,128)}, f32[6,128,1280]{2,1,0:T(8,128)}) custom-call(f32[1536,1408]{1,0:T(8,128)} %fusion.116.raw_ref.halo_ref, f32[128,1536]{1,0:T(8,128)} %copy-done.16, bf16[256,1536]{1,0:T(8,128)(2,1)} %copy-done.25, f32[1536,384]{1,0:T(8,128)} %pad_maximum_fusion.masks_ref.masks_next_ref, ...), custom_call_target="tpu_custom_call" | custom-call | flops 40699998208 | bytes 125800000 | tf_op jit(solution)/shard_map/ssd_fwd/pallas_call | solution.py:388
  182.6 18.5 %multiply_reduce_fusion.3 = (f32[1536]{0:T(1024)S(1)}, f32[1536,1280]{1,0:T(8,128)S(1)}, f32[1536,1280]{1,0:T(8,128)}) fusion(f32[1536,1280]{1,0:T(8,128)} %get-tuple-element.131.y_ref, bf16[1536,2560]{1,0:T(8,128)(2,1)} %fusion.30.refs_6_.refs_7_, bf16[2560,1,1280]{2,0,1:T(8,128)(2,1)} %all-gather.9.cloned.1.call-done), kind=kOutput, calls=%fused_computation.9 | convolution fusion | flops 10080090112 | bytes 38017024 | tf_op jit(solution)/shard_map/dot_general | solution.py:23
  202.5 3.1 constant_dynamic-update-slice_fusion.2
  213.7 11.1 %convolution_convert_fusion.2 = bf16[2560,1280]{1,0:T(8,128)(2,1)S(1)} fusion(bf16[1536,2560]{1,0:T(8,128)(2,1)S(1)} %constant_dynamic-update-slice_fusion, bf16[1536,1280]{1,0:T(8,128)(2,1)S(1)} %multiply_convert_fusion.1), kind=kOutput, calls=%fused_computation.2 | convolution fusion | flops 10069606400 | bytes 18350080 | tf_op jit(solution)/shard_map/dot_general | solution.py:655
  224.9 2.7 copy-done.8
  229.6 10.0 %fusion.27 = f32[1536,1280]{1,0:T(8,128)} fusion(bf16[1536,1280]{1,0:T(8,128)(2,1)} %copy-done.12, bf16[2560,1280]{1,0:T(8,128)(2,1)} %all-gather.7.cloned.1.call-done), kind=kOutput, calls=%fused_computation.54 | convolution fusion | flops 5033164800 | bytes 15073280 | tf_op jit(solution)/shard_map/dot_general | solution.py:27
  239.7 2.6 fusion.3
  242.3 15.7 %multiply_reduce_fusion.1 = (f32[1536]{0:T(1024)S(1)}, f32[1536]{0:T(1024)S(1)}, bf16[1536,1280]{1,0:T(8,128)(2,1)S(1)}, bf16[1536,1280]{1,0:T(8,128)(2,1)S(1)}) fusion(bf16[1536,2560]{1,0:T(8,128)(2,1)} %copy-done.4, f32[1536,1280]{1,0:T(8,128)} %fusion.27, bf16[1536,1280]{1,0:T(8,128)(2,1)} %copy-done.12, bf16[2560,1280]{1,0:T(8,128)(2,1)} %all-gather.7.cloned.1.call-done), kind=kOutput, calls=%fused_computation.6 | convolution fusion | flops 5048890368 | bytes 30814208 | tf_op jit(solution)/shard_map/dot_general | solution.py:27
  264.2 5.5 collective-permute-start.17
  271.3 26.3 %fusion.24 = (f32[1536,1280]{1,0:T(8,128)}, bf16[1536,1280]{1,0:T(8,128)(2,1)}, f32[1280]{0:T(1024)S(1)}) fusion(f32[1536]{0:T(1024)S(1)} %add_multiply_fusion, f32[1536,1280]{1,0:T(8,128)} %copy-done.3, f32[1280]{0:T(1024)S(1)} %reshape.466, f32[1536]{0:T(1024)S(1)} %add_rsqrt_fusion, f32[1536,1280]{1,0:T(8,128)} %get-tuple-element.432, ...), kind=kOutput, calls=%fused_computation.51 | convolution fusion | flops 10103684096 | bytes 49829888 | tf_op jit(solution)/shard_map/dot_general | solution.py:23
  297.6 14.2 %convolution_convert_fusion.1 = bf16[2560,1280]{1,0:T(8,128)(2,1)S(1)} fusion(bf16[1536,2560]{1,0:T(8,128)(2,1)} %fusion.30.refs_6_.refs_7_, bf16[1536,1280]{1,0:T(8,128)(2,1)} %get-tuple-element.399.refs_0_.refs_1_), kind=kOutput, calls=%fused_computation.1 | convolution fusion | flops 10069606400 | bytes 18350080 | tf_op jit(solution)/shard_map/dot_general | solution.py:655
  311.8 4.0 collective-permute-done.19
  322.0 2.6 fusion.2
  325.3 53.7 %ssd_bwd.1 = (bf16[1536,1280]{1,0:T(8,128)(2,1)}, f32[32,1536]{1,0:T(8,128)}, f32[256,1536]{1,0:T(8,128)}, f32[8,1280]{1,0:T(8,128)}, f32[32,128]{1,0:T(8,128)}, /*index=5*/f32[8,1280]{1,0:T(8,128)}) custom-call(f32[1536,1408]{1,0:T(8,128)} %fusion.116.raw_ref.halo_ref, f32[1536,1408]{1,0:T(8,128)} %fusion.116.raw_ref.halo_ref, f32[128,1536]{1,0:T(8,128)} %copy-done.16, ...), custom_call_target="tpu_custom_call" | custom-call | flops 75900002304 | bytes 234600000 | tf_op jit(solution)/shard_map/ssd_bwd/pallas_call | solution.py:438
  380.5 2.9 collective-permute-start.25
  384.1 16.1 %convolution_convert_fusion = bf16[2560,1280]{1,0:T(8,128)(2,1)} fusion(bf16[1536,2560]{1,0:T(8,128)(2,1)} %fusion.30.refs_6_.refs_7_, bf16[1536,1280]{1,0:T(8,128)(2,1)} %get-tuple-element.147.refs_2_.refs_3_), kind=kOutput, calls=%fused_computation | convolution fusion | flops 10069606400 | bytes 18350080 | tf_op jit(solution)/shard_map/dot_general | solution.py:655
  401.0 3.9 dynamic-slice_bitcast_fusion
  410.2 12.2 %d_normed.5 = (bf16[768,1280]{1,0:T(8,128)(2,1)}, f32[8,1280]{1,0:T(8,128)}) custom-call(s32[2]{0:T(128)} %get-tuple-element.436.at_ref, bf16[1536,1280]{1,0:T(8,128)(2,1)} %get-tuple-element.399.refs_0_.refs_1_, bf16[1536,1280]{1,0:T(8,128)(2,1)} %get-tuple-element.399.refs_0_.refs_1_, bf16[1536,1280]{1,0:T(8,128)(2,1)} %get-tuple-element.147.refs_2_.refs_3_, ...), custom_call_target="tpu_custom_call" | custom-call | flops 110000000 | bytes 340000 | tf_op jit(solution)/shard_map/d_normed/pallas_call | solution.py:556
  424.2 4.4 fusion.1
  430.0 4.8 fusion.35
  434.9 12.2 %d_normed.7 = (bf16[768,1280]{1,0:T(8,128)(2,1)}, f32[8,1280]{1,0:T(8,128)}) custom-call(s32[2]{0:T(128)} %get-tuple-element.434.at_ref, bf16[1536,1280]{1,0:T(8,128)(2,1)} %get-tuple-element.399.refs_0_.refs_1_, bf16[1536,1280]{1,0:T(8,128)(2,1)} %get-tuple-element.399.refs_0_.refs_1_, bf16[1536,1280]{1,0:T(8,128)(2,1)} %get-tuple-element.147.refs_2_.refs_3_, ...), custom_call_target="tpu_custom_call" | custom-call | flops 110000000 | bytes 340000 | tf_op jit(solution)/shard_map/d_normed/pallas_call | solution.py:556
  449.3 4.2 fusion.51
  456.4 11.8 %d_normed.4 = (bf16[768,1280]{1,0:T(8,128)(2,1)}, f32[8,1280]{1,0:T(8,128)}) custom-call(s32[2]{0:T(128)} %get-tuple-element.437.at_ref, bf16[1536,1280]{1,0:T(8,128)(2,1)} %get-tuple-element.399.refs_0_.refs_1_, bf16[1536,1280]{1,0:T(8,128)(2,1)} %get-tuple-element.399.refs_0_.refs_1_, bf16[1536,1280]{1,0:T(8,128)(2,1)} %get-tuple-element.147.refs_2_.refs_3_, ...), custom_call_target="tpu_custom_call" | custom-call | flops 110000000 | bytes 340000 | tf_op jit(solution)/shard_map/d_normed/pallas_call | solution.py:556
  468.2 11.8 %d_normed.6 = (bf16[768,1280]{1,0:T(8,128)(2,1)}, f32[8,1280]{1,0:T(8,128)}) custom-call(s32[2]{0:T(128)} %get-tuple-element.435.at_ref, bf16[1536,1280]{1,0:T(8,128)(2,1)} %get-tuple-element.399.refs_0_.refs_1_, bf16[1536,1280]{1,0:T(8,128)(2,1)} %get-tuple-element.399.refs_0_.refs_1_, bf16[1536,1280]{1,0:T(8,128)(2,1)} %get-tuple-element.147.refs_2_.refs_3_, ...), custom_call_target="tpu_custom_call" | custom-call | flops 110000000 | bytes 340000 | tf_op jit(solution)/shard_map/d_normed/pallas_call | solution.py:556
  480.9 2.4 add_convert_fusion.1
  486.1 6.3 %collective-permute-done.27 = bf16[768,1280]{1,0:T(8,128)(2,1)} collective-permute-done((bf16[768,1280]{1,0:T(8,128)(2,1)}, bf16[768,1280]{1,0:T(8,128)(2,1)}, u32[]{:S(2)}, u32[]{:S(2)}) %collective-permute-start.27) | collective-permute-done | bytes 1966112 | tf_op jit(solution)/shard_map/ppermute | solution.py:673
  492.4 2.4 add_convert_fusion
  497.7 3.4 collective-permute-start.30
  501.1 3.4 convert_add_fusion.8
  504.6 5.4 collective-permute-done.31
  510.0 3.5 collective-permute-done.30
  525.7 15.6 %adam_pair.1 = (f32[320,2,1280]{2,1,0:T(2,128)}, bf16[320,2,1280]{2,1,0:T(2,128)(2,1)}, f32[320,2,1280]{2,1,0:T(2,128)}, f32[320,2,1280]{2,1,0:T(2,128)}) custom-call(bf16[320,1280]{1,0:T(8,128)(2,1)} %reduce-scatter.6.cloned.1.call-done.gate_ref, bf16[320,1280]{1,0:T(8,128)(2,1)} %reduce-scatter.8.cloned.1.call-done.inner_ref, ...), custom_call_target="tpu_custom_call" | custom-call | flops 1000 | bytes 1000 | tf_op jit(solution)/shard_map/adam_pair/pallas_call | solution.py:611
  544.2 2.7 collective-permute-done.34
  550.9 3.1 fusion.8
  (409 shorter events, 117.8 us)
Async XLA Ops:
  7.2 112.9 %all-gather.5.cloned.1.call-start = ((), (), s32[]{:S(2)}) async-start(), calls=%async_computation.3 | async-start | bytes 8110080 | tf_op jit(solution)/shard_map/all_gather | solution.py:829
  19.1 163.4 %all-gather.9.cloned.1.call-start = ((), (), s32[]{:S(2)}) async-start(), calls=%async_computation.8 | async-start | bytes 7372800 | tf_op jit(solution)/shard_map/all_gather | solution.py:830
  21.6 208.0 %all-gather.7.cloned.1.call-start = ((), (), s32[]{:S(2)}) async-start(), calls=%async_computation.4 | async-start | bytes 7372800 | tf_op jit(solution)/shard_map/all_gather | solution.py:867
  21.7 46.0 %collective-permute-start.4 = (bf16[384,2560]{1,0:T(8,128)(2,1)S(1)}, bf16[384,2560]{1,0:T(8,128)(2,1)}, u32[]{:S(2)}, u32[]{:S(2)}) collective-permute-start(bf16[384,2560]{1,0:T(8,128)(2,1)S(1)} %copy-done.1), channel_id=1, source_target_pairs={{0,2},{1,3},{2,0},{3,1},{4,6},{5,7},{6,4},{7,5},{8,10},{9,11},{10,... | collective-permute-start | bytes 5898248 | tf_op jit(solution)/shard_map/ppermute | solution.py:673
  24.7 46.0 %collective-permute-start = (bf16[384,2560]{1,0:T(8,128)(2,1)S(1)}, bf16[384,2560]{1,0:T(8,128)(2,1)}, u32[]{:S(2)}, u32[]{:S(2)}) collective-permute-start(bf16[384,2560]{1,0:T(8,128)(2,1)S(1)} %copy-done.1), channel_id=1, source_target_pairs={{0,1},{1,0},{2,3},{3,2},{4,5},{5,4},{6,7},{7,6},{8,9},{9,8},{10,11... | collective-permute-start | bytes 5898248 | tf_op jit(solution)/shard_map/ppermute | solution.py:673
  26.3 7.1 %collective-permute-start.1 = (bf16[8,320]{1,0:T(8,128)(2,1)S(1)}, bf16[8,320]{1,0:T(8,128)(2,1)S(1)}, u32[]{:S(2)}, u32[]{:S(2)}) collective-permute-start(bf16[8,320]{1,0:T(8,128)(2,1)S(1)} %dynamic_update_slice.41), channel_id=1, source_target_pairs={{0,4},{4,0},{8,12},{12,8},{16,20},{20,16},{24,28},{28,24},{1,5},{5... | collective-permute-start | bytes 15368 | tf_op jit(solution)/shard_map/ppermute | solution.py:744
  28.4 101.1 %copy-start.30 = (f32[1536]{0:T(1024)}, f32[1536]{0:T(1024)S(1)}, u32[]{:S(2)}) copy-start(f32[1536]{0:T(1024)S(1)} %get-tuple-element.423) | copy-start | bytes 18436
  28.4 101.1 %copy-start.32 = (f32[1536]{0:T(1024)}, f32[1536]{0:T(1024)S(1)}, u32[]{:S(2)}) copy-start(f32[1536]{0:T(1024)S(1)} %get-tuple-element.424) | copy-start | bytes 18436
  33.5 3.9 collective-permute-start.2
  37.4 5.2 collective-permute-start.3
  42.7 75.6 %copy-start.26 = (f32[2560]{0:T(1024)}, f32[2560]{0:T(1024)S(1)}, u32[]{:S(2)}) copy-start(f32[2560]{0:T(1024)S(1)} %reshape.464) | copy-start | bytes 30724
  43.7 32.2 %copy-start = (bf16[1536,2560]{1,0:T(8,128)(2,1)}, bf16[1536,2560]{1,0:T(8,128)(2,1)S(1)}, u32[]{:S(2)}) copy-start(bf16[1536,2560]{1,0:T(8,128)(2,1)S(1)} %fusion.29) | copy-start | bytes 23592964
  68.9 23.0 %collective-permute-start.5 = (bf16[192,2560]{1,0:T(8,128)(2,1)S(1)}, bf16[192,2560]{1,0:T(8,128)(2,1)S(1)}, u32[]{:S(2)}, u32[]{:S(2)}) collective-permute-start(bf16[192,2560]{1,0:T(8,128)(2,1)S(1)} %slice.260), channel_id=1, source_target_pairs={{0,1},{1,0},{2,3},{3,2},{4,5},{5,4},{6,7},{7,6},{8,9},{9,8},{10,11... | collective-permute-start | bytes 2949128 | tf_op jit(solution)/shard_map/ppermute | solution.py:673
  72.0 22.4 %collective-permute-start.6 = (bf16[192,2560]{1,0:T(8,128)(2,1)S(1)}, bf16[192,2560]{1,0:T(8,128)(2,1)S(1)}, u32[]{:S(2)}, u32[]{:S(2)}) collective-permute-start(bf16[192,2560]{1,0:T(8,128)(2,1)S(1)} %slice.201), channel_id=1, source_target_pairs={{0,2},{1,3},{2,0},{3,1},{4,6},{5,7},{6,4},{7,5},{8,10},{9,11},{10,... | collective-permute-start | bytes 2949128 | tf_op jit(solution)/shard_map/ppermute | solution.py:673
  94.5 106.5 %collective-permute-start.11 = (bf16[384,2560]{1,0:T(8,128)(2,1)}, bf16[384,2560]{1,0:T(8,128)(2,1)}, u32[]{:S(2)}, u32[]{:S(2)}) collective-permute-start(bf16[384,2560]{1,0:T(8,128)(2,1)} %fusion.7), channel_id=1, source_target_pairs={{0,2},{1,3},{2,0},{3,1},{4,6},{5,7},{6,4},{7,5},{8,10},{9,11},{10,... | collective-permute-start | bytes 5898248 | tf_op jit(solution)/shard_map/ppermute | solution.py:673
  96.1 104.9 %collective-permute-start.10 = (bf16[384,2560]{1,0:T(8,128)(2,1)}, bf16[384,2560]{1,0:T(8,128)(2,1)}, u32[]{:S(2)}, u32[]{:S(2)}) collective-permute-start(bf16[384,2560]{1,0:T(8,128)(2,1)} %fusion.7), channel_id=1, source_target_pairs={{0,1},{1,0},{2,3},{3,2},{4,5},{5,4},{6,7},{7,6},{8,9},{9,8},{10,11... | collective-permute-start | bytes 5898248 | tf_op jit(solution)/shard_map/ppermute | solution.py:673
  107.0 217.6 %reduce-scatter.4.cloned.1.call-start = ((), (), s32[]{:S(2)}) async-start(), calls=%async_computation.5 | async-start | bytes 4096000 | tf_op jit(solution)/shard_map/reduce_scatter | solution.py:766
  131.5 24.3 %collective-permute-start.8 = (bf16[64,1536]{1,0:T(8,128)(2,1)}, bf16[64,1536]{1,0:T(8,128)(2,1)}, u32[]{:S(2)}, u32[]{:S(2)}) collective-permute-start(bf16[64,1536]{1,0:T(8,128)(2,1)} %get-tuple-element.396), channel_id=1, source_target_pairs={{0,2},{1,3},{2,0},{3,1},{4,6},{5,7},{6,4},{7,5},{8,10},{9,11},{10,... | collective-permute-start | bytes 589832 | tf_op jit(solution)/shard_map/ppermute | solution.py:673
  132.2 22.6 %collective-permute-start.7 = (bf16[64,1536]{1,0:T(8,128)(2,1)}, bf16[64,1536]{1,0:T(8,128)(2,1)}, u32[]{:S(2)}, u32[]{:S(2)}) collective-permute-start(bf16[64,1536]{1,0:T(8,128)(2,1)} %get-tuple-element.396), channel_id=1, source_target_pairs={{0,1},{1,0},{2,3},{3,2},{4,5},{5,4},{6,7},{7,6},{8,9},{9,8},{10,11... | collective-permute-start | bytes 589832 | tf_op jit(solution)/shard_map/ppermute | solution.py:673
  133.7 23.1 %collective-permute-start.9 = (bf16[64,1536]{1,0:T(8,128)(2,1)}, bf16[64,1536]{1,0:T(8,128)(2,1)}, u32[]{:S(2)}, u32[]{:S(2)}) collective-permute-start(bf16[64,1536]{1,0:T(8,128)(2,1)} %get-tuple-element.396), channel_id=1, source_target_pairs={{0,3},{1,2},{2,1},{3,0},{4,7},{5,6},{6,5},{7,4},{8,11},{9,10},{10,... | collective-permute-start | bytes 589832 | tf_op jit(solution)/shard_map/ppermute | solution.py:673
  157.7 43.3 %collective-permute-start.12 = (bf16[384,2560]{1,0:T(8,128)(2,1)S(1)}, bf16[384,2560]{1,0:T(8,128)(2,1)}, u32[]{:S(2)}, u32[]{:S(2)}) collective-permute-start(bf16[384,2560]{1,0:T(8,128)(2,1)S(1)} %copy-done.6), channel_id=1, source_target_pairs={{0,3},{1,2},{2,1},{3,0},{4,7},{5,6},{6,5},{7,4},{8,11},{9,10},{10,... | collective-permute-start | bytes 5898248 | tf_op jit(solution)/shard_map/ppermute | solution.py:673
  201.1 6.3 %collective-permute-start.13 = (f32[1536]{0:T(1024)S(1)}, f32[1536]{0:T(1024)S(1)}, u32[]{:S(2)}, u32[]{:S(2)}) collective-permute-start(f32[1536]{0:T(1024)S(1)} %get-tuple-element.133), channel_id=1, source_target_pairs={{0,1},{1,0},{2,3},{3,2},{4,5},{5,4},{6,7},{7,6},{8,9},{9,8},{10,11... | collective-permute-start | bytes 18440 | tf_op jit(solution)/shard_map/ppermute | solution.py:673
  207.4 3.7 collective-permute-start.14
  229.5 10.1 %collective-permute-start.15 = (bf16[4,320,1280]{2,1,0:T(8,128)(2,1)}, bf16[4,320,1280]{2,1,0:T(8,128)(2,1)S(1)}, u32[]{:S(2)}, u32[]{:S(2)}) collective-permute-start(bf16[4,320,1280]{2,1,0:T(8,128)(2,1)} %dynamic-slice_bitcast_fusion.2), channel_id=1, source_target_pairs={{0,4},{4,0},{8,12},{12,8},{16,20},{20,16},{24,28},{28,24},{1,5},{5... | collective-permute-start | bytes 9830408 | tf_op jit(solution)/shard_map/ppermute | solution.py:744
  242.3 158.6 %reduce-scatter.6.cloned.1.call-start = ((), (), s32[]{:S(2)}) async-start(), calls=%async_computation.6 | async-start | bytes 4096000 | tf_op jit(solution)/shard_map/reduce_scatter | solution.py:766
  258.0 6.1 %collective-permute-start.16 = (f32[1536]{0:T(1024)S(1)}, f32[1536]{0:T(1024)S(1)}, u32[]{:S(2)}, u32[]{:S(2)}) collective-permute-start(f32[1536]{0:T(1024)S(1)} %add.500), channel_id=1, source_target_pairs={{0,1},{1,0},{2,3},{3,2},{4,5},{5,4},{6,7},{7,6},{8,9},{9,8},{10,11... | collective-permute-start | bytes 18440 | tf_op jit(solution)/shard_map/ppermute | solution.py:673
  262.6 49.2 %collective-permute-start.18 = (bf16[768,1280]{1,0:T(8,128)(2,1)}, bf16[768,1280]{1,0:T(8,128)(2,1)S(1)}, u32[]{:S(2)}, u32[]{:S(2)}) collective-permute-start(bf16[768,1280]{1,0:T(8,128)(2,1)} %pad_maximum_fusion.2), channel_id=1, source_target_pairs={{0,1},{1,0},{2,3},{3,2},{4,5},{5,4},{6,7},{7,6},{8,9},{9,8},{10,11... | collective-permute-start | bytes 5898248 | tf_op jit(solution)/shard_map/ppermute | solution.py:673
  264.2 7.1 %collective-permute-start.17 = (f32[1536]{0:T(1024)S(1)}, f32[1536]{0:T(1024)S(1)}, u32[]{:S(2)}, u32[]{:S(2)}) collective-permute-start(f32[1536]{0:T(1024)S(1)} %add.501), channel_id=1, source_target_pairs={{0,2},{1,3},{2,0},{3,1},{4,6},{5,7},{6,4},{7,5},{8,10},{9,11},{10,... | collective-permute-start | bytes 18440 | tf_op jit(solution)/shard_map/ppermute | solution.py:673
  271.1 44.7 %collective-permute-start.19 = (bf16[768,1280]{1,0:T(8,128)(2,1)}, bf16[768,1280]{1,0:T(8,128)(2,1)}, u32[]{:S(2)}, u32[]{:S(2)}) collective-permute-start(bf16[768,1280]{1,0:T(8,128)(2,1)} %pad_maximum_fusion.3), channel_id=1, source_target_pairs={{0,2},{1,3},{2,0},{3,1},{4,6},{5,7},{6,4},{7,5},{8,10},{9,11},{10,... | collective-permute-start | bytes 5898248 | tf_op jit(solution)/shard_map/ppermute | solution.py:673
  316.1 5.9 %collective-permute-start.20 = (bf16[4,320,1280]{2,1,0:T(8,128)(2,1)S(1)}, bf16[4,320,1280]{2,1,0:T(8,128)(2,1)S(1)}, u32[]{:S(2)}, u32[]{:S(2)}) collective-permute-start(bf16[4,320,1280]{2,1,0:T(8,128)(2,1)S(1)} %dynamic-slice_bitcast_fusion.1), channel_id=1, source_target_pairs={{0,4},{4,0},{8,12},{12,8},{16,20},{20,16},{24,28},{28,24},{1,5},{5... | collective-permute-start | bytes 9830408 | tf_op jit(solution)/shard_map/ppermute | solution.py:744
  324.6 193.6 %reduce-scatter.8.cloned.1.call-start = ((), (), s32[]{:S(2)}) async-start(), calls=%async_computation.7 | async-start | bytes 4096000 | tf_op jit(solution)/shard_map/reduce_scatter | solution.py:766
  324.6 76.3 %collective-permute-start.21 = (bf16[384,1280]{1,0:T(8,128)(2,1)}, bf16[384,1280]{1,0:T(8,128)(2,1)}, u32[]{:S(2)}, u32[]{:S(2)}) collective-permute-start(bf16[384,1280]{1,0:T(8,128)(2,1)} %add_convert_fusion.3), channel_id=1, source_target_pairs={{0,2},{1,3},{2,0},{3,1},{4,6},{5,7},{6,4},{7,5},{8,10},{9,11},{10,... | collective-permute-start | bytes 2949128 | tf_op jit(solution)/shard_map/ppermute | solution.py:673
  325.0 76.0 %collective-permute-start.22 = (bf16[384,1280]{1,0:T(8,128)(2,1)S(1)}, bf16[384,1280]{1,0:T(8,128)(2,1)}, u32[]{:S(2)}, u32[]{:S(2)}) collective-permute-start(bf16[384,1280]{1,0:T(8,128)(2,1)S(1)} %add_convert_fusion.2), channel_id=1, source_target_pairs={{0,1},{1,0},{2,3},{3,2},{4,5},{5,4},{6,7},{7,6},{8,9},{9,8},{10,11... | collective-permute-start | bytes 2949128 | tf_op jit(solution)/shard_map/ppermute | solution.py:673
  380.5 19.8 %collective-permute-start.25 = (f32[64,1536]{1,0:T(8,128)S(1)}, f32[64,1536]{1,0:T(8,128)S(1)}, u32[]{:S(2)}, u32[]{:S(2)}) collective-permute-start(f32[64,1536]{1,0:T(8,128)S(1)} %get-tuple-element.411), channel_id=1, source_target_pairs={{0,3},{1,2},{2,1},{3,0},{4,7},{5,6},{6,5},{7,4},{8,11},{9,10},{10,... | collective-permute-start | bytes 1179656 | tf_op jit(solution)/shard_map/ppermute | solution.py:673
  383.4 17.4 %collective-permute-start.24 = (f32[64,1536]{1,0:T(8,128)S(1)}, f32[64,1536]{1,0:T(8,128)}, u32[]{:S(2)}, u32[]{:S(2)}) collective-permute-start(f32[64,1536]{1,0:T(8,128)S(1)} %get-tuple-element.412), channel_id=1, source_target_pairs={{0,2},{1,3},{2,0},{3,1},{4,6},{5,7},{6,4},{7,5},{8,10},{9,11},{10,... | collective-permute-start | bytes 1179656 | tf_op jit(solution)/shard_map/ppermute | solution.py:673
  383.7 17.2 %collective-permute-start.23 = (f32[64,1536]{1,0:T(8,128)S(1)}, f32[64,1536]{1,0:T(8,128)}, u32[]{:S(2)}, u32[]{:S(2)}) collective-permute-start(f32[64,1536]{1,0:T(8,128)S(1)} %get-tuple-element.413), channel_id=1, source_target_pairs={{0,1},{1,0},{2,3},{3,2},{4,5},{5,4},{6,7},{7,6},{8,9},{9,8},{10,11... | collective-permute-start | bytes 1179656 | tf_op jit(solution)/shard_map/ppermute | solution.py:673
  404.8 19.3 %collective-permute-start.28 = (bf16[4,320,1280]{2,1,0:T(8,128)(2,1)}, bf16[4,320,1280]{2,1,0:T(8,128)(2,1)}, u32[]{:S(2)}, u32[]{:S(2)}) collective-permute-start(bf16[4,320,1280]{2,1,0:T(8,128)(2,1)} %dynamic-slice_bitcast_fusion), channel_id=1, source_target_pairs={{0,4},{4,0},{8,12},{12,8},{16,20},{20,16},{24,28},{28,24},{1,5},{5... | collective-permute-start | bytes 9830408 | tf_op jit(solution)/shard_map/ppermute | solution.py:744
  422.5 45.7 %collective-permute-start.26 = (bf16[768,1280]{1,0:T(8,128)(2,1)}, bf16[768,1280]{1,0:T(8,128)(2,1)}, u32[]{:S(2)}, u32[]{:S(2)}) collective-permute-start(bf16[768,1280]{1,0:T(8,128)(2,1)} %get-tuple-element.158), channel_id=1, source_target_pairs={{0,1},{1,0},{2,3},{3,2},{4,5},{5,4},{6,7},{7,6},{8,9},{9,8},{10,11... | collective-permute-start | bytes 5898248 | tf_op jit(solution)/shard_map/ppermute | solution.py:673
  447.1 45.3 %collective-permute-start.27 = (bf16[768,1280]{1,0:T(8,128)(2,1)}, bf16[768,1280]{1,0:T(8,128)(2,1)}, u32[]{:S(2)}, u32[]{:S(2)}) collective-permute-start(bf16[768,1280]{1,0:T(8,128)(2,1)} %get-tuple-element.162), channel_id=1, source_target_pairs={{0,2},{1,3},{2,0},{3,1},{4,6},{5,7},{6,4},{7,5},{8,10},{9,11},{10,... | collective-permute-start | bytes 5898248 | tf_op jit(solution)/shard_map/ppermute | solution.py:673
  486.0 10.9 %collective-permute-start.29 = (f32[4,320,128]{2,1,0:T(8,128)S(1)}, f32[4,320,128]{2,1,0:T(8,128)S(1)}, u32[]{:S(2)}, u32[]{:S(2)}) collective-permute-start(f32[4,320,128]{2,1,0:T(8,128)S(1)} %dynamic-slice_bitcast_fusion.3), channel_id=1, source_target_pairs={{0,4},{4,0},{8,12},{12,8},{16,20},{20,16},{24,28},{28,24},{1,5},{5... | collective-permute-start | bytes 1966088 | tf_op jit(solution)/shard_map/ppermute | solution.py:744
  497.6 12.4 %collective-permute-start.31 = (f32[320,128]{0,1:T(8,128)S(1)}, f32[320,128]{0,1:T(8,128)S(1)}, u32[]{:S(2)}, u32[]{:S(2)}) collective-permute-start(f32[320,128]{0,1:T(8,128)S(1)} %copy.278), channel_id=1, source_target_pairs={{0,16},{4,20},{8,24},{12,28},{16,0},{20,4},{24,8},{28,12},{1,17},{... | collective-permute-start | bytes 491528 | tf_op jit(solution)/shard_map/ppermute | solution.py:744
  497.6 12.4 %collective-permute-start.32 = (f32[320,128]{0,1:T(8,128)S(1)}, f32[320,128]{0,1:T(8,128)S(1)}, u32[]{:S(2)}, u32[]{:S(2)}) collective-permute-start(f32[320,128]{0,1:T(8,128)S(1)} %copy.279), channel_id=1, source_target_pairs={{0,24},{4,28},{8,16},{12,20},{16,8},{20,12},{24,0},{28,4},{1,25},{... | collective-permute-start | bytes 491528 | tf_op jit(solution)/shard_map/ppermute | solution.py:744
  497.7 15.8 %collective-permute-start.30 = (f32[320,128]{0,1:T(8,128)S(1)}, f32[320,128]{0,1:T(8,128)}, u32[]{:S(2)}, u32[]{:S(2)}) collective-permute-start(f32[320,128]{0,1:T(8,128)S(1)} %copy.276), channel_id=1, source_target_pairs={{0,8},{4,12},{8,0},{12,4},{16,24},{20,28},{24,16},{28,20},{1,9},{5... | collective-permute-start | bytes 491528 | tf_op jit(solution)/shard_map/ppermute | solution.py:744
  514.8 26.4 %copy-start.50 = (f32[5,8]{1,0:T(8,128)}, f32[5,8]{1,0:T(8,128)S(1)}, u32[]{:S(2)}) copy-start(f32[5,8]{1,0:T(8,128)S(1)} %reshape.462) | copy-start | bytes 484
  518.1 23.5 %collective-permute-start.33 = (bf16[384,1280]{1,0:T(8,128)(2,1)}, bf16[384,1280]{1,0:T(8,128)(2,1)S(1)}, u32[]{:S(2)}, u32[]{:S(2)}) collective-permute-start(bf16[384,1280]{1,0:T(8,128)(2,1)} %add_convert_fusion.1), channel_id=1, source_target_pairs={{0,2},{1,3},{2,0},{3,1},{4,6},{5,7},{6,4},{7,5},{8,10},{9,11},{10,... | collective-permute-start | bytes 2949128 | tf_op jit(solution)/shard_map/ppermute | solution.py:673
  523.2 23.7 %collective-permute-start.34 = (bf16[384,1280]{1,0:T(8,128)(2,1)}, bf16[384,1280]{1,0:T(8,128)(2,1)}, u32[]{:S(2)}, u32[]{:S(2)}) collective-permute-start(bf16[384,1280]{1,0:T(8,128)(2,1)} %add_convert_fusion), channel_id=1, source_target_pairs={{0,1},{1,0},{2,3},{3,2},{4,5},{5,4},{6,7},{7,6},{8,9},{9,8},{10,11... | collective-permute-start | bytes 2949128 | tf_op jit(solution)/shard_map/ppermute | solution.py:673
  541.6 8.0 %collective-permute-start.35 = (f32[320]{0:T(512)S(1)}, f32[320]{0:T(512)S(1)}, u32[]{:S(2)}, u32[]{:S(2)}) collective-permute-start(f32[320]{0:T(512)S(1)} %slice_reduce_fusion.10), channel_id=1, source_target_pairs={{0,1},{1,0},{2,3},{3,2},{4,5},{5,4},{6,7},{7,6},{8,9},{9,8},{10,11... | collective-permute-start | bytes 3848 | tf_op jit(solution)/shard_map/ppermute | solution.py:673
  549.7 4.3 collective-permute-start.36
  (73 other events, 722.1 us)
Sparse Core Ops, SparseCore 0:
  19.3 75.2 all-gather.4
  96.8 65.5 all-gather.8
  164.0 65.5 all-gather.6
  242.4 64.5 reduce-scatter.3
  324.7 58.4 reduce-scatter.5
  428.7 59.3 reduce-scatter.7

commit v3 on v2

--- a/solution.py
+++ b/solution.py
@@ -732,6 +732,13 @@
     return jnp.concatenate(totals, axis=1)
 
 
+def row_sum(value, size):
+    total = value
+    for distance in range(1, size):
+        total = total + swap(value, distance, size)
+    return total
+
+
 def all_sum(value, size):
     distance = 1
     while distance < size:
@@ -825,9 +832,10 @@
     side = pad_cols(
         jnp.concatenate([proj_step, proj_state, input_gain[:, None], small_block], axis=1), LANE
     )
-    x_local = jnp.concatenate([proj_inner[:, 1, :], side], axis=1)
+    (inner_halves,) = tied(proj_inner.transpose(1, 0, 2))
+    x_local = jnp.concatenate([inner_halves[1], side], axis=1)
     x_all = lax.all_gather(x_local, "fsdp", axis=0, tiled=True)
-    gate_all = lax.all_gather(proj_inner[:, 0, :], "fsdp", axis=0, tiled=True)
+    gate_all = lax.all_gather(inner_halves[0], "fsdp", axis=0, tiled=True)
     gain_all = lax.dynamic_update_slice(
         jnp.zeros((fsdp_size, shard), BF16), input_gain[None], (fsdp_index, jnp.int32(0))
     )
@@ -863,8 +871,6 @@
 
     row_parts, started, own_grad = gather_parts(block_in, tp_size, near_done)
     row_parts = [by_rows(part) for part in row_parts]
-    out_local, *row_parts = tied(proj_output.T, *row_parts)
-    out_all = lax.all_gather(out_local, "fsdp", axis=0, tiled=True)
     own_grad, *row_parts = tied(own_grad, *row_parts)
     near = min(3, tp_size)
     grad_parts = [by_rows(own_grad)] + [swap(own_grad, k, tp_size) for k in range(1, near)]
@@ -900,7 +906,8 @@
     for k in range(tp_size):
         piece = state_local if k == 0 else swap(state_local, k, tp_size)
         bc = lax.dynamic_update_slice(bc, piece, ((tp_index ^ k) * state_cols, jnp.int32(0)))
-    own_grad, bc = tied(own_grad, bc)
+    own_grad, bc, out_local = tied(own_grad, bc, proj_output.T)
+    out_all = lax.all_gather(out_local, "fsdp", axis=0, tiled=True)
     grad_parts += [swap(own_grad, k, tp_size) for k in range(near, tp_size)]
     spread = head_tables(heads)
     taps8 = jnp.pad(taps_inner, ((0, 3), (0, 0)))
@@ -913,7 +920,7 @@
     gate_act = z_raw * sig
     gated = mixed * gate_act
     square_sum, *grad_parts = tied(jnp.sum(gated * gated, axis=1), *grad_parts)
-    square_sum = all_sum(square_sum, tp_size)
+    square_sum = row_sum(square_sum, tp_size)
     group_grad = jnp.zeros((group_rows, model), BF16)
     for distance in range(tp_size):
         group_grad = put(group_grad, grad_parts[distance], distance)
@@ -932,7 +939,7 @@
     inner_sum = jnp.sum(mixed_halves[0] * group_grad[:, :half].astype(F32), axis=1) + jnp.sum(
         mixed_halves[1] * group_grad[:, half:].astype(F32), axis=1
     )
-    inner_sum = all_sum(inner_sum, tp_size)
+    inner_sum = row_sum(inner_sum, tp_size)
     mixed_left, mixed_right = (part.astype(BF16) for part in mixed_halves)
     mixed_sent, mixed_kept = scatter_start(mixed_left, mixed_right, own_rows, tp_index, tp_size)
 
@@ -1017,7 +1024,7 @@
         )
         sent = [swap(left_away, 1, 4), swap(right_away, 2, 4)]
         left_kept, gains_three = d_normed_of([2, 0], 0)
-        sent[0], d_side_late, side_part = tied(sent[0], d_side, side_part)
+        sent[0], d_side_late, side_part, grad_out = tied(sent[0], d_side, side_part, grad_out)
         right_kept, gains_four = d_normed_blocks(
             d_z, d_x, d_side_late, gate_all, x_all, normed, tp_index ^ jnp.array([1, 0]), 1, own_rows
         )
@@ -1046,8 +1053,8 @@
     grad_x, passed = tied(grad_x, passed)
     last = scatter_last(passed, tp_size)
     grad_side = side_gradient(side_part, d_taps, d_skip, d_heads, grad_conv_state, gain_sums)
-    gain_part, last[0] = tied(grad_side[:, used], last[0])
-    grad_input_gain = all_sum(gain_part, tp_size) / input_gain.astype(F32)
+    grad_side, last[0] = tied(grad_side, last[0])
+    grad_input_gain = all_sum(grad_side[:, used], tp_size) / input_gain.astype(F32)
     d_normed = scatter_end(kept, last)
 
     unit_rows, inv_rms = unit_of(block_in)

time: 571 us -> 564 us (0.988)
  starting transfers between devices: 56.1 us -> 45.5 us
    reduce_scatter x3, starting transfers between devices: 11.4 us -> 0.33 us  [chip_scatter(): lax.psum_scatter(flat, 'fsdp', scatter_dimension=0, axis_index_groups=gro...]
    ppermute x10, waiting for transfers between devices: 12 us -> 18.8 us  [fsdp_swap(): lax.ppermute(value, 'fsdp', [(at, at ^ distance) for at in range(size)])]
    ppermute x27 -> x29, waiting for transfers between devices: 56 us -> 50.1 us  [swap(): lax.ppermute(value, 'tp', [(at, at ^ distance) for at in range(size)])]
    unnamed x162 -> x201, local copies, waits for them, and re-layouts: 13.2 us -> 11.8 us
    ppermute x27 -> x29, starting transfers between devices: 36.8 us -> 36.4 us  [swap(): lax.ppermute(value, 'tp', [(at, at ^ distance) for at in range(size)])]
  transfers between devices with their start and end apart: 43 -> 45, of which waited for: 17 -> 13; matrix products, arithmetic and copies ran while one was open for 45% -> 46% of each run, Pallas kernels for 25% -> 25%
where the time goes in v3:
time: 564 us; the launch traced here: 558 us
  matrix products  142 us (25%)
  Pallas kernels  138 us (24%)
  other arithmetic  87.1 us (15%)
  waiting for transfers between devices  69.1 us (12%)
  local copies, waits for them, and re-layouts  59 us (10%)
  starting transfers between devices  45.5 us (8%)
  between operations  16.6 us (3%)
    dot_general x3, matrix products, mm(): lax.dot_general(left, right, (((1,), (0,)), ((), ())), preferred_element_...  63.2 us
    pallas_call x1, Pallas kernels, ssd_backward(): pl.pallas_call(functools.partial(ssd_bwd_kernel, heads), grid=(chunks,),...  53.3 us
    ppermute x29, waiting for transfers between devices, swap(): lax.ppermute(value, 'tp', [(at, at ^ distance) for at in range(size)])  50.1 us
    pallas_call x4, Pallas kernels, d_normed_blocks(): pl.pallas_call(functools.partial(dn_kernel, count, rows), grid_spec=pltpu...  48.5 us
    dot_general x3, matrix products, contract_rows(): lax.dot_general(left_mat, right_mat, (((0,), (0,)), ((), ())), preferred_...  41.5 us
    ppermute x29, starting transfers between devices, swap(): lax.ppermute(value, 'tp', [(at, at ^ distance) for at in range(size)])  36.4 us
    dot_general x2, matrix products, mm_nt(): lax.dot_general(left, right, (((1,), (1,)), ((), ())), preferred_element_...  24.5 us
    pallas_call x1, Pallas kernels, ssd_forward(): pl.pallas_call(functools.partial(ssd_fwd_kernel, heads), grid=(chunks,),...  21.2 us
  transfers between devices with their start and end apart: 45, of which 13 were waited for; matrix products, arithmetic and copies ran while one was open for 46% of the time, Pallas kernels for 25%

profile of v3, /device:TPU:0, one launch (start us, length us, event | category | flops | bytes accessed | tf_op | source)
XLA Modules:
  0.0 557.7 jit_solution(10641182760323224378)
XLA Ops:
  16.2 3.0 collective-permute-start.4
  22.7 3.2 fusion.7
  32.0 2.4 collective-permute-start.3
  36.8 3.6 broadcast.302.clone
  42.2 19.9 %collective-permute-done.4 = bf16[384,2560]{1,0:T(8,128)(2,1)} collective-permute-done((bf16[384,2560]{1,0:T(8,128)(2,1)S(1)}, bf16[384,2560]{1,0:T(8,128)(2,1)}, u32[]{:S(2)}, u32[]{:S(2)}) %collective-permute-start.4) | collective-permute-done | bytes 1966112 | tf_op jit(solution)/shard_map/ppermute | solution.py:673
  71.6 14.8 %collective-permute-done.5 = bf16[192,2560]{1,0:T(8,128)(2,1)S(1)} collective-permute-done((bf16[192,2560]{1,0:T(8,128)(2,1)S(1)}, bf16[192,2560]{1,0:T(8,128)(2,1)S(1)}, u32[]{:S(2)}, u32[]{:S(2)}) %collective-permute-start.5) | collective-permute-done | bytes 983072 | tf_op jit(solution)/shard_map/ppermute | solution.py:673
  86.4 2.5 collective-permute-done.6
  91.1 3.0 fusion.9
  94.1 3.3 fusion.32
  97.5 3.5 fusion.31
  109.4 6.3 %fusion.40.small_ref = f32[128,1536]{1,0:T(8,128)S(1)} fusion(bf16[1536,2560]{1,0:T(8,128)(2,1)} %fusion.30.refs_6_.refs_7_, bf16[2560,1408]{1,0:T(8,128)(2,1)} %all-gather.5.cloned.1.call-done.refs_9_), kind=kOutput, calls=%fused_computation.96 | convolution fusion | flops 1006632960 | bytes 9306112 | tf_op jit(solution)/shard_map/dot_general | solution.py:893
  127.1 18.3 %fusion.115.raw_ref.halo_ref = f32[1536,1408]{1,0:T(8,128)} fusion(bf16[1536,2560]{1,0:T(8,128)(2,1)} %fusion.30.refs_6_.refs_7_, bf16[2560,1408]{1,0:T(8,128)(2,1)} %all-gather.5.cloned.1.call-done.refs_9_), kind=kOutput, calls=%fused_computation.292 | convolution fusion | flops 11072962560 | bytes 23724032 | tf_op jit(solution)/shard_map/dot_general | solution.py:23
  152.5 21.2 %ssd_fwd.1 = (f32[1536,1280]{1,0:T(8,128)}, f32[6,128,1280]{2,1,0:T(8,128)}) custom-call(f32[1536,1408]{1,0:T(8,128)} %fusion.115.raw_ref.halo_ref, f32[128,1536]{1,0:T(8,128)} %copy-done.15, bf16[256,1536]{1,0:T(8,128)(2,1)} %copy-done.29, f32[1536,384]{1,0:T(8,128)} %pad_maximum_fusion.masks_ref.masks_next_ref, ...), custom_call_target="tpu_custom_call" | custom-call | flops 40699998208 | bytes 125800000 | tf_op jit(solution)/shard_map/ssd_fwd/pallas_call | solution.py:388
  173.7 18.4 %multiply_reduce_fusion.3 = (f32[1536]{0:T(1024)S(1)}, f32[1536,1280]{1,0:T(8,128)S(1)}, f32[1536,1280]{1,0:T(8,128)}) fusion(f32[1536,1280]{1,0:T(8,128)} %get-tuple-element.126.y_ref, bf16[1536,2560]{1,0:T(8,128)(2,1)} %fusion.30.refs_6_.refs_7_, bf16[1,2560,1280]{2,1,0:T(8,128)(2,1)} %all-gather.9.cloned.1.call-done), kind=kOutput, calls=%fused_computation.9 | convolution fusion | flops 10080090112 | bytes 38017024 | tf_op jit(solution)/shard_map/dot_general | solution.py:23
  202.7 2.3 copy-done.5
  205.0 11.3 %convolution_convert_fusion.2 = bf16[2560,1280]{1,0:T(8,128)(2,1)S(1)} fusion(bf16[1536,2560]{1,0:T(8,128)(2,1)S(1)} %constant_dynamic-update-slice_fusion, bf16[1536,1280]{1,0:T(8,128)(2,1)S(1)} %multiply_convert_fusion.1), kind=kOutput, calls=%fused_computation.2 | convolution fusion | flops 10069606400 | bytes 18350080 | tf_op jit(solution)/shard_map/dot_general | solution.py:655
  216.3 2.7 copy-done.7
  219.0 1.9 dynamic-slice_bitcast_fusion.2
  220.9 6.1 %collective-permute-done.16 = bf16[4,320,1280]{2,1,0:T(8,128)(2,1)S(1)} collective-permute-done((bf16[4,320,1280]{2,1,0:T(8,128)(2,1)}, bf16[4,320,1280]{2,1,0:T(8,128)(2,1)S(1)}, u32[]{:S(2)}, u32[]{:S(2)}) %collective-permute-start.16) | collective-permute-done | bytes 3276832 | tf_op jit(solution)/shard_map/ppermute | solution.py:751
  227.0 4.4 fusion.3
  231.5 10.2 %fusion.27 = f32[1536,1280]{1,0:T(8,128)} fusion(bf16[1536,1280]{1,0:T(8,128)(2,1)} %copy-done.10, bf16[2560,1280]{1,0:T(8,128)(2,1)} %all-gather.7.cloned.1.call-done), kind=kOutput, calls=%fused_computation.54 | convolution fusion | flops 5033164800 | bytes 15073280 | tf_op jit(solution)/shard_map/dot_general | solution.py:27
  241.7 14.3 %multiply_reduce_fusion.1 = (f32[1536]{0:T(1024)S(1)}, f32[1536]{0:T(1024)S(1)}, bf16[1536,1280]{1,0:T(8,128)(2,1)S(1)}, bf16[1536,1280]{1,0:T(8,128)(2,1)S(1)}) fusion(bf16[1536,2560]{1,0:T(8,128)(2,1)} %copy-done.5, f32[1536,1280]{1,0:T(8,128)} %fusion.27, bf16[1536,1280]{1,0:T(8,128)(2,1)S(1)} %copy-done.11, ...), kind=kOutput, calls=%fused_computation.6 | convolution fusion | flops 5048890368 | bytes 30814208 | tf_op jit(solution)/shard_map/dot_general | solution.py:27
  256.0 1.9 collective-permute-start.19
  265.1 26.4 %fusion.24 = (f32[1536,1280]{1,0:T(8,128)}, bf16[1536,1280]{1,0:T(8,128)(2,1)}, f32[1280]{0:T(1024)S(1)}) fusion(f32[1536]{0:T(1024)S(1)} %add_multiply_fusion, f32[1536,1280]{1,0:T(8,128)} %copy-done.4, f32[1280]{0:T(1024)S(1)} %copy-done.58, f32[1536]{0:T(1024)S(1)} %add_rsqrt_fusion, f32[1536,1280]{1,0:T(8,128)} %get-tuple-element.428, ...), kind=kOutput, calls=%fused_computation.51 | convolution fusion | flops 10103684096 | bytes 49829888 | tf_op jit(solution)/shard_map/dot_general | solution.py:23
  291.5 14.3 %convolution_convert_fusion.1 = bf16[2560,1280]{1,0:T(8,128)(2,1)S(1)} fusion(bf16[1536,2560]{1,0:T(8,128)(2,1)} %fusion.30.refs_6_.refs_7_, bf16[1536,1280]{1,0:T(8,128)(2,1)} %get-tuple-element.395.refs_0_.refs_1_), kind=kOutput, calls=%fused_computation.1 | convolution fusion | flops 10069606400 | bytes 18350080 | tf_op jit(solution)/shard_map/dot_general | solution.py:655
  305.8 2.0 collective-permute-done.21
  309.0 2.4 add_convert_fusion.3
  313.9 2.6 fusion.2
  319.4 53.3 %ssd_bwd.1 = (bf16[1536,1280]{1,0:T(8,128)(2,1)}, f32[32,1536]{1,0:T(8,128)}, f32[256,1536]{1,0:T(8,128)}, f32[8,1280]{1,0:T(8,128)}, f32[32,128]{1,0:T(8,128)}, /*index=5*/f32[8,1280]{1,0:T(8,128)}) custom-call(f32[1536,1408]{1,0:T(8,128)} %fusion.115.raw_ref.halo_ref, f32[1536,1408]{1,0:T(8,128)} %fusion.115.raw_ref.halo_ref, f32[128,1536]{1,0:T(8,128)} %copy-done.15, ...), custom_call_target="tpu_custom_call" | custom-call | flops 75900002304 | bytes 234600000 | tf_op jit(solution)/shard_map/ssd_bwd/pallas_call | solution.py:438
  377.7 15.9 %convolution_convert_fusion = bf16[2560,1280]{1,0:T(8,128)(2,1)} fusion(bf16[1536,2560]{1,0:T(8,128)(2,1)} %fusion.30.refs_6_.refs_7_, bf16[1536,1280]{1,0:T(8,128)(2,1)} %get-tuple-element.142.refs_2_.refs_3_), kind=kOutput, calls=%fused_computation | convolution fusion | flops 10069606400 | bytes 18350080 | tf_op jit(solution)/shard_map/dot_general | solution.py:655
  393.8 4.0 dynamic-slice_bitcast_fusion
  402.6 12.2 %d_normed.5 = (bf16[768,1280]{1,0:T(8,128)(2,1)}, f32[8,1280]{1,0:T(8,128)}) custom-call(s32[2]{0:T(128)} %get-tuple-element.432.at_ref, bf16[1536,1280]{1,0:T(8,128)(2,1)} %get-tuple-element.395.refs_0_.refs_1_, bf16[1536,1280]{1,0:T(8,128)(2,1)} %get-tuple-element.395.refs_0_.refs_1_, bf16[1536,1280]{1,0:T(8,128)(2,1)} %get-tuple-element.142.refs_2_.refs_3_, ...), custom_call_target="tpu_custom_call" | custom-call | flops 110000000 | bytes 340000 | tf_op jit(solution)/shard_map/d_normed/pallas_call | solution.py:556
  414.9 4.4 fusion.1
  421.0 11.8 %d_normed.7 = (bf16[768,1280]{1,0:T(8,128)(2,1)}, f32[8,1280]{1,0:T(8,128)}) custom-call(s32[2]{0:T(128)} %get-tuple-element.430.at_ref, bf16[1536,1280]{1,0:T(8,128)(2,1)} %get-tuple-element.395.refs_0_.refs_1_, bf16[1536,1280]{1,0:T(8,128)(2,1)} %get-tuple-element.395.refs_0_.refs_1_, bf16[1536,1280]{1,0:T(8,128)(2,1)} %get-tuple-element.142.refs_2_.refs_3_, ...), custom_call_target="tpu_custom_call" | custom-call | flops 110000000 | bytes 340000 | tf_op jit(solution)/shard_map/d_normed/pallas_call | solution.py:556
  436.9 12.0 %d_normed.4 = (bf16[768,1280]{1,0:T(8,128)(2,1)}, f32[8,1280]{1,0:T(8,128)}) custom-call(s32[2]{0:T(128)} %get-tuple-element.433.at_ref, bf16[1536,1280]{1,0:T(8,128)(2,1)} %get-tuple-element.395.refs_0_.refs_1_, bf16[1536,1280]{1,0:T(8,128)(2,1)} %get-tuple-element.395.refs_0_.refs_1_, bf16[1536,1280]{1,0:T(8,128)(2,1)} %get-tuple-element.142.refs_2_.refs_3_, ...), custom_call_target="tpu_custom_call" | custom-call | flops 110000000 | bytes 340000 | tf_op jit(solution)/shard_map/d_normed/pallas_call | solution.py:556
  448.9 6.5 %fusion.51 = f32[2560,128]{1,0:T(8,128)} fusion(bf16[1536,2560]{1,0:T(8,128)(2,1)} %fusion.30.refs_6_.refs_7_, f32[64,1536]{1,0:T(8,128)S(1)} %copy-done.28, f32[20,1536]{1,0:T(8,128)S(1)} %slice.237), kind=kOutput, calls=%fused_computation.122 | convolution fusion | flops 1008009216 | bytes 9691136 | tf_op jit(solution)/shard_map/dot_general | solution.py:978
  455.5 9.4 %collective-permute-done.28 = bf16[768,1280]{1,0:T(8,128)(2,1)S(1)} collective-permute-done((bf16[768,1280]{1,0:T(8,128)(2,1)}, bf16[768,1280]{1,0:T(8,128)(2,1)S(1)}, u32[]{:S(2)}, u32[]{:S(2)}) %collective-permute-start.28) | collective-permute-done | bytes 1966112 | tf_op jit(solution)/shard_map/ppermute | solution.py:673
  464.8 12.5 %d_normed.6 = (bf16[768,1280]{1,0:T(8,128)(2,1)}, f32[8,1280]{1,0:T(8,128)}) custom-call(s32[2]{0:T(128)} %get-tuple-element.431.at_ref, bf16[1536,1280]{1,0:T(8,128)(2,1)} %get-tuple-element.395.refs_0_.refs_1_, bf16[1536,1280]{1,0:T(8,128)(2,1)} %get-tuple-element.395.refs_0_.refs_1_, bf16[1536,1280]{1,0:T(8,128)(2,1)} %get-tuple-element.142.refs_2_.refs_3_, ...), custom_call_target="tpu_custom_call" | custom-call | flops 110000000 | bytes 340000 | tf_op jit(solution)/shard_map/d_normed/pallas_call | solution.py:556
  479.5 4.6 fusion.35
  484.7 2.2 fusion.38
  487.0 2.4 add_convert_fusion
  489.4 3.5 convert_add_fusion.7
  494.4 2.4 collective-permute-start.33
  498.7 3.1 convert_add_fusion.8
  502.4 9.3 %collective-permute-done.33 = f32[320,128]{0,1:T(8,128)S(1)} collective-permute-done((f32[320,128]{0,1:T(8,128)S(1)}, f32[320,128]{0,1:T(8,128)S(1)}, u32[]{:S(2)}, u32[]{:S(2)}) %collective-permute-start.33) | collective-permute-done | bytes 163872 | tf_op jit(solution)/shard_map/ppermute | solution.py:751
  513.4 15.4 %adam_pair.1 = (f32[320,2,1280]{2,1,0:T(2,128)}, bf16[320,2,1280]{2,1,0:T(2,128)(2,1)}, f32[320,2,1280]{2,1,0:T(2,128)}, f32[320,2,1280]{2,1,0:T(2,128)}) custom-call(bf16[320,1280]{1,0:T(8,128)(2,1)} %reduce-scatter.6.cloned.1.call-done.gate_ref, bf16[320,1280]{1,0:T(8,128)(2,1)} %reduce-scatter.8.cloned.1.call-done.inner_ref, ...), custom_call_target="tpu_custom_call" | custom-call | flops 1000 | bytes 1000 | tf_op jit(solution)/shard_map/adam_pair/pallas_call | solution.py:611
  530.7 2.3 convert_add_fusion.5
  538.2 6.0 %fusion.8 = (bf16[384,2560]{1,0:T(8,128)(2,1)}, bf16[384,2560]{1,0:T(8,128)(2,1)}) fusion(bf16[384,2560]{1,0:T(8,128)(2,1)} %param.36, bf16[384,2560]{1,0:T(8,128)(2,1)S(1)} %copy-done.1, f32[384,1280]{1,0:T(8,128)} %copy-done.3, f32[384,1280]{1,0:T(8,128)} %copy-done.2, f32[384]{0:T(512)S(1)} %broadcast_multiply_fusion, f32[2560]{0:T(1024)S(1)} %copy-done.31, ...), kind=kLoop, calls=%fused_computation.33 | loop fusion | flops 13762560 | bytes 15742336 | tf_op jit(solution)/shard_map/convert_element_type | solution.py:1063
  (449 shorter events, 121.5 us)
Async XLA Ops:
  7.2 96.0 %all-gather.5.cloned.1.call-start = ((), (), s32[]{:S(2)}) async-start(), calls=%async_computation.3 | async-start | bytes 8110080 | tf_op jit(solution)/shard_map/all_gather | solution.py:837
  16.1 157.6 %all-gather.9.cloned.1.call-start = ((), (), s32[]{:S(2)}) async-start(), calls=%async_computation.8 | async-start | bytes 7372800 | tf_op jit(solution)/shard_map/all_gather | solution.py:838
  16.2 46.0 %collective-permute-start.4 = (bf16[384,2560]{1,0:T(8,128)(2,1)S(1)}, bf16[384,2560]{1,0:T(8,128)(2,1)}, u32[]{:S(2)}, u32[]{:S(2)}) collective-permute-start(bf16[384,2560]{1,0:T(8,128)(2,1)S(1)} %copy-done), channel_id=1, source_target_pairs={{0,2},{1,3},{2,0},{3,1},{4,6},{5,7},{6,4},{7,5},{8,10},{9,11},{10,... | collective-permute-start | bytes 5898248 | tf_op jit(solution)/shard_map/ppermute | solution.py:673
  19.2 46.0 %collective-permute-start = (bf16[384,2560]{1,0:T(8,128)(2,1)S(1)}, bf16[384,2560]{1,0:T(8,128)(2,1)}, u32[]{:S(2)}, u32[]{:S(2)}) collective-permute-start(bf16[384,2560]{1,0:T(8,128)(2,1)S(1)} %copy-done), channel_id=1, source_target_pairs={{0,1},{1,0},{2,3},{3,2},{4,5},{5,4},{6,7},{7,6},{8,9},{9,8},{10,11... | collective-permute-start | bytes 5898248 | tf_op jit(solution)/shard_map/ppermute | solution.py:673
  20.7 7.0 %collective-permute-start.1 = (bf16[8,320]{1,0:T(8,128)(2,1)S(1)}, bf16[8,320]{1,0:T(8,128)(2,1)S(1)}, u32[]{:S(2)}, u32[]{:S(2)}) collective-permute-start(bf16[8,320]{1,0:T(8,128)(2,1)S(1)} %dynamic_update_slice.41), channel_id=1, source_target_pairs={{0,4},{4,0},{8,12},{12,8},{16,20},{20,16},{24,28},{28,24},{1,5},{5... | collective-permute-start | bytes 15368 | tf_op jit(solution)/shard_map/ppermute | solution.py:751
  20.8 210.6 %all-gather.7.cloned.1.call-start = ((), (), s32[]{:S(2)}) async-start(), calls=%async_computation.4 | async-start | bytes 7372800 | tf_op jit(solution)/shard_map/all_gather | solution.py:910
  26.1 89.8 %copy-start.33 = (f32[1536]{0:T(1024)}, f32[1536]{0:T(1024)S(1)}, u32[]{:S(2)}) copy-start(f32[1536]{0:T(1024)S(1)} %get-tuple-element.419) | copy-start | bytes 18436
  26.1 89.8 %copy-start.35 = (f32[1536]{0:T(1024)}, f32[1536]{0:T(1024)S(1)}, u32[]{:S(2)}) copy-start(f32[1536]{0:T(1024)S(1)} %get-tuple-element.420) | copy-start | bytes 18436
  28.0 3.9 collective-permute-start.2
  32.0 4.8 collective-permute-start.3
  36.8 64.6 %copy-start.30 = (f32[2560]{0:T(1024)}, f32[2560]{0:T(1024)S(1)}, u32[]{:S(2)}) copy-start(f32[2560]{0:T(1024)S(1)} %reshape.464) | copy-start | bytes 30724
  63.4 23.0 %collective-permute-start.5 = (bf16[192,2560]{1,0:T(8,128)(2,1)S(1)}, bf16[192,2560]{1,0:T(8,128)(2,1)S(1)}, u32[]{:S(2)}, u32[]{:S(2)}) collective-permute-start(bf16[192,2560]{1,0:T(8,128)(2,1)S(1)} %slice.260), channel_id=1, source_target_pairs={{0,1},{1,0},{2,3},{3,2},{4,5},{5,4},{6,7},{7,6},{8,9},{9,8},{10,11... | collective-permute-start | bytes 2949128 | tf_op jit(solution)/shard_map/ppermute | solution.py:673
  66.5 22.4 %collective-permute-start.6 = (bf16[192,2560]{1,0:T(8,128)(2,1)S(1)}, bf16[192,2560]{1,0:T(8,128)(2,1)S(1)}, u32[]{:S(2)}, u32[]{:S(2)}) collective-permute-start(bf16[192,2560]{1,0:T(8,128)(2,1)S(1)} %slice.201), channel_id=1, source_target_pairs={{0,2},{1,3},{2,0},{3,1},{4,6},{5,7},{6,4},{7,5},{8,10},{9,11},{10,... | collective-permute-start | bytes 2949128 | tf_op jit(solution)/shard_map/ppermute | solution.py:673
  89.0 103.2 %collective-permute-start.11 = (bf16[384,2560]{1,0:T(8,128)(2,1)S(1)}, bf16[384,2560]{1,0:T(8,128)(2,1)}, u32[]{:S(2)}, u32[]{:S(2)}) collective-permute-start(bf16[384,2560]{1,0:T(8,128)(2,1)S(1)} %copy-done.6), channel_id=1, source_target_pairs={{0,2},{1,3},{2,0},{3,1},{4,6},{5,7},{6,4},{7,5},{8,10},{9,11},{10,... | collective-permute-start | bytes 5898248 | tf_op jit(solution)/shard_map/ppermute | solution.py:673
  90.6 101.6 %collective-permute-start.10 = (bf16[384,2560]{1,0:T(8,128)(2,1)S(1)}, bf16[384,2560]{1,0:T(8,128)(2,1)}, u32[]{:S(2)}, u32[]{:S(2)}) collective-permute-start(bf16[384,2560]{1,0:T(8,128)(2,1)S(1)} %copy-done.6), channel_id=1, source_target_pairs={{0,1},{1,0},{2,3},{3,2},{4,5},{5,4},{6,7},{7,6},{8,9},{9,8},{10,11... | collective-permute-start | bytes 5898248 | tf_op jit(solution)/shard_map/ppermute | solution.py:673
  117.9 29.1 %collective-permute-start.8 = (bf16[64,1536]{1,0:T(8,128)(2,1)}, bf16[64,1536]{1,0:T(8,128)(2,1)}, u32[]{:S(2)}, u32[]{:S(2)}) collective-permute-start(bf16[64,1536]{1,0:T(8,128)(2,1)} %get-tuple-element.392), channel_id=1, source_target_pairs={{0,2},{1,3},{2,0},{3,1},{4,6},{5,7},{6,4},{7,5},{8,10},{9,11},{10,... | collective-permute-start | bytes 589832 | tf_op jit(solution)/shard_map/ppermute | solution.py:673
  118.4 27.6 %collective-permute-start.7 = (bf16[64,1536]{1,0:T(8,128)(2,1)}, bf16[64,1536]{1,0:T(8,128)(2,1)}, u32[]{:S(2)}, u32[]{:S(2)}) collective-permute-start(bf16[64,1536]{1,0:T(8,128)(2,1)} %get-tuple-element.392), channel_id=1, source_target_pairs={{0,1},{1,0},{2,3},{3,2},{4,5},{5,4},{6,7},{7,6},{8,9},{9,8},{10,11... | collective-permute-start | bytes 589832 | tf_op jit(solution)/shard_map/ppermute | solution.py:673
  119.8 28.1 %collective-permute-start.9 = (bf16[64,1536]{1,0:T(8,128)(2,1)}, bf16[64,1536]{1,0:T(8,128)(2,1)}, u32[]{:S(2)}, u32[]{:S(2)}) collective-permute-start(bf16[64,1536]{1,0:T(8,128)(2,1)} %get-tuple-element.392), channel_id=1, source_target_pairs={{0,3},{1,2},{2,1},{3,0},{4,7},{5,6},{6,5},{7,4},{8,11},{9,10},{10,... | collective-permute-start | bytes 589832 | tf_op jit(solution)/shard_map/ppermute | solution.py:673
  148.9 43.3 %collective-permute-start.12 = (bf16[384,2560]{1,0:T(8,128)(2,1)S(1)}, bf16[384,2560]{1,0:T(8,128)(2,1)}, u32[]{:S(2)}, u32[]{:S(2)}) collective-permute-start(bf16[384,2560]{1,0:T(8,128)(2,1)S(1)} %copy-done.6), channel_id=1, source_target_pairs={{0,3},{1,2},{2,1},{3,0},{4,7},{5,6},{6,5},{7,4},{8,11},{9,10},{10,... | collective-permute-start | bytes 5898248 | tf_op jit(solution)/shard_map/ppermute | solution.py:673
  150.4 166.1 %reduce-scatter.4.cloned.1.call-start = ((), (), s32[]{:S(2)}) async-start(), calls=%async_computation.5 | async-start | bytes 4096000 | tf_op jit(solution)/shard_map/reduce_scatter | solution.py:773
  192.2 9.7 %collective-permute-start.15 = (f32[1536]{0:T(1024)S(1)}, f32[1536]{0:T(1024)S(1)}, u32[]{:S(2)}, u32[]{:S(2)}) collective-permute-start(f32[1536]{0:T(1024)S(1)} %get-tuple-element.128), channel_id=1, source_target_pairs={{0,3},{1,2},{2,1},{3,0},{4,7},{5,6},{6,5},{7,4},{8,11},{9,10},{10,... | collective-permute-start | bytes 18440 | tf_op jit(solution)/shard_map/ppermute | solution.py:673
  193.8 8.0 %collective-permute-start.14 = (f32[1536]{0:T(1024)S(1)}, f32[1536]{0:T(1024)S(1)}, u32[]{:S(2)}, u32[]{:S(2)}) collective-permute-start(f32[1536]{0:T(1024)S(1)} %get-tuple-element.128), channel_id=1, source_target_pairs={{0,2},{1,3},{2,0},{3,1},{4,6},{5,7},{6,4},{7,5},{8,10},{9,11},{10,... | collective-permute-start | bytes 18440 | tf_op jit(solution)/shard_map/ppermute | solution.py:673
  194.4 7.5 %collective-permute-start.13 = (f32[1536]{0:T(1024)S(1)}, f32[1536]{0:T(1024)S(1)}, u32[]{:S(2)}, u32[]{:S(2)}) collective-permute-start(f32[1536]{0:T(1024)S(1)} %get-tuple-element.128), channel_id=1, source_target_pairs={{0,1},{1,0},{2,3},{3,2},{4,5},{5,4},{6,7},{7,6},{8,9},{9,8},{10,11... | collective-permute-start | bytes 18440 | tf_op jit(solution)/shard_map/ppermute | solution.py:673
  220.9 6.1 %collective-permute-start.16 = (bf16[4,320,1280]{2,1,0:T(8,128)(2,1)}, bf16[4,320,1280]{2,1,0:T(8,128)(2,1)S(1)}, u32[]{:S(2)}, u32[]{:S(2)}) collective-permute-start(bf16[4,320,1280]{2,1,0:T(8,128)(2,1)} %dynamic-slice_bitcast_fusion.2), channel_id=1, source_target_pairs={{0,4},{4,0},{8,12},{12,8},{16,20},{20,16},{24,28},{28,24},{1,5},{5... | collective-permute-start | bytes 9830408 | tf_op jit(solution)/shard_map/ppermute | solution.py:751
  231.4 162.4 %reduce-scatter.6.cloned.1.call-start = ((), (), s32[]{:S(2)}) async-start(), calls=%async_computation.6 | async-start | bytes 4096000 | tf_op jit(solution)/shard_map/reduce_scatter | solution.py:773
  256.0 9.1 %collective-permute-start.19 = (f32[1536]{0:T(1024)S(1)}, f32[1536]{0:T(1024)S(1)}, u32[]{:S(2)}, u32[]{:S(2)}) collective-permute-start(f32[1536]{0:T(1024)S(1)} %add.507), channel_id=1, source_target_pairs={{0,3},{1,2},{2,1},{3,0},{4,7},{5,6},{6,5},{7,4},{8,11},{9,10},{10,... | collective-permute-start | bytes 18440 | tf_op jit(solution)/shard_map/ppermute | solution.py:673
  257.9 7.2 %collective-permute-start.18 = (f32[1536]{0:T(1024)S(1)}, f32[1536]{0:T(1024)S(1)}, u32[]{:S(2)}, u32[]{:S(2)}) collective-permute-start(f32[1536]{0:T(1024)S(1)} %add.507), channel_id=1, source_target_pairs={{0,2},{1,3},{2,0},{3,1},{4,6},{5,7},{6,4},{7,5},{8,10},{9,11},{10,... | collective-permute-start | bytes 18440 | tf_op jit(solution)/shard_map/ppermute | solution.py:673
  258.4 6.6 %collective-permute-start.17 = (f32[1536]{0:T(1024)S(1)}, f32[1536]{0:T(1024)S(1)}, u32[]{:S(2)}, u32[]{:S(2)}) collective-permute-start(f32[1536]{0:T(1024)S(1)} %add.507), channel_id=1, source_target_pairs={{0,1},{1,0},{2,3},{3,2},{4,5},{5,4},{6,7},{7,6},{8,9},{9,8},{10,11... | collective-permute-start | bytes 18440 | tf_op jit(solution)/shard_map/ppermute | solution.py:673
  261.2 44.5 %collective-permute-start.20 = (bf16[768,1280]{1,0:T(8,128)(2,1)}, bf16[768,1280]{1,0:T(8,128)(2,1)S(1)}, u32[]{:S(2)}, u32[]{:S(2)}) collective-permute-start(bf16[768,1280]{1,0:T(8,128)(2,1)} %pad_maximum_fusion.2), channel_id=1, source_target_pairs={{0,1},{1,0},{2,3},{3,2},{4,5},{5,4},{6,7},{7,6},{8,9},{9,8},{10,11... | collective-permute-start | bytes 5898248 | tf_op jit(solution)/shard_map/ppermute | solution.py:673
  263.6 44.2 %collective-permute-start.21 = (bf16[768,1280]{1,0:T(8,128)(2,1)}, bf16[768,1280]{1,0:T(8,128)(2,1)}, u32[]{:S(2)}, u32[]{:S(2)}) collective-permute-start(bf16[768,1280]{1,0:T(8,128)(2,1)} %pad_maximum_fusion.3), channel_id=1, source_target_pairs={{0,2},{1,3},{2,0},{3,1},{4,6},{5,7},{6,4},{7,5},{8,10},{9,11},{10,... | collective-permute-start | bytes 5898248 | tf_op jit(solution)/shard_map/ppermute | solution.py:673
  308.0 5.9 %collective-permute-start.22 = (bf16[4,320,1280]{2,1,0:T(8,128)(2,1)S(1)}, bf16[4,320,1280]{2,1,0:T(8,128)(2,1)S(1)}, u32[]{:S(2)}, u32[]{:S(2)}) collective-permute-start(bf16[4,320,1280]{2,1,0:T(8,128)(2,1)S(1)} %dynamic-slice_bitcast_fusion.1), channel_id=1, source_target_pairs={{0,4},{4,0},{8,12},{12,8},{16,20},{20,16},{24,28},{28,24},{1,5},{5... | collective-permute-start | bytes 9830408 | tf_op jit(solution)/shard_map/ppermute | solution.py:751
  316.5 176.6 %reduce-scatter.8.cloned.1.call-start = ((), (), s32[]{:S(2)}) async-start(), calls=%async_computation.7 | async-start | bytes 4096000 | tf_op jit(solution)/shard_map/reduce_scatter | solution.py:773
  316.5 77.2 %collective-permute-start.23 = (bf16[384,1280]{1,0:T(8,128)(2,1)}, bf16[384,1280]{1,0:T(8,128)(2,1)}, u32[]{:S(2)}, u32[]{:S(2)}) collective-permute-start(bf16[384,1280]{1,0:T(8,128)(2,1)} %add_convert_fusion.3), channel_id=1, source_target_pairs={{0,2},{1,3},{2,0},{3,1},{4,6},{5,7},{6,4},{7,5},{8,10},{9,11},{10,... | collective-permute-start | bytes 2949128 | tf_op jit(solution)/shard_map/ppermute | solution.py:673
  318.1 75.7 %collective-permute-start.24 = (bf16[384,1280]{1,0:T(8,128)(2,1)S(1)}, bf16[384,1280]{1,0:T(8,128)(2,1)}, u32[]{:S(2)}, u32[]{:S(2)}) collective-permute-start(bf16[384,1280]{1,0:T(8,128)(2,1)S(1)} %add_convert_fusion.2), channel_id=1, source_target_pairs={{0,1},{1,0},{2,3},{3,2},{4,5},{5,4},{6,7},{7,6},{8,9},{9,8},{10,11... | collective-permute-start | bytes 2949128 | tf_op jit(solution)/shard_map/ppermute | solution.py:673
  374.1 19.5 %collective-permute-start.27 = (f32[64,1536]{1,0:T(8,128)S(1)}, f32[64,1536]{1,0:T(8,128)}, u32[]{:S(2)}, u32[]{:S(2)}) collective-permute-start(f32[64,1536]{1,0:T(8,128)S(1)} %get-tuple-element.407), channel_id=1, source_target_pairs={{0,3},{1,2},{2,1},{3,0},{4,7},{5,6},{6,5},{7,4},{8,11},{9,10},{10,... | collective-permute-start | bytes 1179656 | tf_op jit(solution)/shard_map/ppermute | solution.py:673
  374.9 18.8 %collective-permute-start.26 = (f32[64,1536]{1,0:T(8,128)S(1)}, f32[64,1536]{1,0:T(8,128)}, u32[]{:S(2)}, u32[]{:S(2)}) collective-permute-start(f32[64,1536]{1,0:T(8,128)S(1)} %get-tuple-element.408), channel_id=1, source_target_pairs={{0,2},{1,3},{2,0},{3,1},{4,6},{5,7},{6,4},{7,5},{8,10},{9,11},{10,... | collective-permute-start | bytes 1179656 | tf_op jit(solution)/shard_map/ppermute | solution.py:673
  376.4 17.3 %collective-permute-start.25 = (f32[64,1536]{1,0:T(8,128)S(1)}, f32[64,1536]{1,0:T(8,128)}, u32[]{:S(2)}, u32[]{:S(2)}) collective-permute-start(f32[64,1536]{1,0:T(8,128)S(1)} %get-tuple-element.409), channel_id=1, source_target_pairs={{0,1},{1,0},{2,3},{3,2},{4,5},{5,4},{6,7},{7,6},{8,9},{9,8},{10,11... | collective-permute-start | bytes 1179656 | tf_op jit(solution)/shard_map/ppermute | solution.py:673
  397.9 17.0 %collective-permute-start.30 = (bf16[4,320,1280]{2,1,0:T(8,128)(2,1)}, bf16[4,320,1280]{2,1,0:T(8,128)(2,1)}, u32[]{:S(2)}, u32[]{:S(2)}) collective-permute-start(bf16[4,320,1280]{2,1,0:T(8,128)(2,1)} %dynamic-slice_bitcast_fusion), channel_id=1, source_target_pairs={{0,4},{4,0},{8,12},{12,8},{16,20},{20,16},{24,28},{28,24},{1,5},{5... | collective-permute-start | bytes 9830408 | tf_op jit(solution)/shard_map/ppermute | solution.py:751
  419.3 45.5 %collective-permute-start.28 = (bf16[768,1280]{1,0:T(8,128)(2,1)}, bf16[768,1280]{1,0:T(8,128)(2,1)S(1)}, u32[]{:S(2)}, u32[]{:S(2)}) collective-permute-start(bf16[768,1280]{1,0:T(8,128)(2,1)} %get-tuple-element.153), channel_id=1, source_target_pairs={{0,1},{1,0},{2,3},{3,2},{4,5},{5,4},{6,7},{7,6},{8,9},{9,8},{10,11... | collective-permute-start | bytes 5898248 | tf_op jit(solution)/shard_map/ppermute | solution.py:673
  435.9 51.1 %collective-permute-start.29 = (bf16[768,1280]{1,0:T(8,128)(2,1)}, bf16[768,1280]{1,0:T(8,128)(2,1)}, u32[]{:S(2)}, u32[]{:S(2)}) collective-permute-start(bf16[768,1280]{1,0:T(8,128)(2,1)} %get-tuple-element.158), channel_id=1, source_target_pairs={{0,2},{1,3},{2,0},{3,1},{4,6},{5,7},{6,4},{7,5},{8,10},{9,11},{10,... | collective-permute-start | bytes 5898248 | tf_op jit(solution)/shard_map/ppermute | solution.py:673
  486.9 6.1 %collective-permute-start.31 = (f32[4,320,128]{2,1,0:T(8,128)S(1)}, f32[4,320,128]{2,1,0:T(8,128)S(1)}, u32[]{:S(2)}, u32[]{:S(2)}) collective-permute-start(f32[4,320,128]{2,1,0:T(8,128)S(1)} %dynamic-slice_bitcast_fusion.3), channel_id=1, source_target_pairs={{0,4},{4,0},{8,12},{12,8},{16,20},{20,16},{24,28},{28,24},{1,5},{5... | collective-permute-start | bytes 1966088 | tf_op jit(solution)/shard_map/ppermute | solution.py:751
  493.1 35.7 %collective-permute-start.35 = (bf16[384,1280]{1,0:T(8,128)(2,1)}, bf16[384,1280]{1,0:T(8,128)(2,1)}, u32[]{:S(2)}, u32[]{:S(2)}) collective-permute-start(bf16[384,1280]{1,0:T(8,128)(2,1)} %add_convert_fusion.1), channel_id=1, source_target_pairs={{0,2},{1,3},{2,0},{3,1},{4,6},{5,7},{6,4},{7,5},{8,10},{9,11},{10,... | collective-permute-start | bytes 2949128 | tf_op jit(solution)/shard_map/ppermute | solution.py:673
  494.4 17.2 %collective-permute-start.33 = (f32[320,128]{0,1:T(8,128)S(1)}, f32[320,128]{0,1:T(8,128)S(1)}, u32[]{:S(2)}, u32[]{:S(2)}) collective-permute-start(f32[320,128]{0,1:T(8,128)S(1)} %copy.271), channel_id=1, source_target_pairs={{0,16},{4,20},{8,24},{12,28},{16,0},{20,4},{24,8},{28,12},{1,17},{... | collective-permute-start | bytes 491528 | tf_op jit(solution)/shard_map/ppermute | solution.py:751
  496.8 14.8 %collective-permute-start.34 = (f32[320,128]{0,1:T(8,128)S(1)}, f32[320,128]{0,1:T(8,128)S(1)}, u32[]{:S(2)}, u32[]{:S(2)}) collective-permute-start(f32[320,128]{0,1:T(8,128)S(1)} %copy.272), channel_id=1, source_target_pairs={{0,24},{4,28},{8,16},{12,20},{16,8},{20,12},{24,0},{28,4},{1,25},{... | collective-permute-start | bytes 491528 | tf_op jit(solution)/shard_map/ppermute | solution.py:751
  498.4 14.0 %collective-permute-start.32 = (f32[320,128]{0,1:T(8,128)S(1)}, f32[320,128]{0,1:T(8,128)}, u32[]{:S(2)}, u32[]{:S(2)}) collective-permute-start(f32[320,128]{0,1:T(8,128)S(1)} %copy.269), channel_id=1, source_target_pairs={{0,8},{4,12},{8,0},{12,4},{16,24},{20,28},{24,16},{28,20},{1,9},{5... | collective-permute-start | bytes 491528 | tf_op jit(solution)/shard_map/ppermute | solution.py:751
  502.0 28.7 %collective-permute-start.36 = (bf16[384,1280]{1,0:T(8,128)(2,1)}, bf16[384,1280]{1,0:T(8,128)(2,1)S(1)}, u32[]{:S(2)}, u32[]{:S(2)}) collective-permute-start(bf16[384,1280]{1,0:T(8,128)(2,1)} %add_convert_fusion), channel_id=1, source_target_pairs={{0,1},{1,0},{2,3},{3,2},{4,5},{5,4},{6,7},{7,6},{8,9},{9,8},{10,11... | collective-permute-start | bytes 2949128 | tf_op jit(solution)/shard_map/ppermute | solution.py:673
  535.7 10.7 %collective-permute-start.37 = (f32[320]{0:T(512)S(1)}, f32[320]{0:T(512)S(1)}, u32[]{:S(2)}, u32[]{:S(2)}) collective-permute-start(f32[320]{0:T(512)S(1)} %slice_reduce_fusion.10), channel_id=1, source_target_pairs={{0,1},{1,0},{2,3},{3,2},{4,5},{5,4},{6,7},{7,6},{8,9},{9,8},{10,11... | collective-permute-start | bytes 3848 | tf_op jit(solution)/shard_map/ppermute | solution.py:673
  546.4 3.7 collective-permute-start.38
  (95 other events, 739.4 us)
Sparse Core Ops, SparseCore 0:
  16.2 75.2 all-gather.4
  93.7 65.5 all-gather.8
  160.9 66.1 all-gather.6
  231.5 62.7 reduce-scatter.3
  316.6 63.2 reduce-scatter.5
  419.4 62.1 reduce-scatter.7

commit v4 on v3

--- a/solution.py
+++ b/solution.py
@@ -619,6 +619,145 @@
         name="adam_pair",
     )(grad_gate, grad_inner, weight, first, second)
 
+
+def product_kernel(left_ref, right_ref, out_ref):
+    out_ref[...] = mm(left_ref[...], right_ref[...])
+
+
+def gate_kernel(left_ref, right_ref, mixed_ref, z_ref, gated_ref, sums_ref):
+    z_raw = mm(left_ref[...], right_ref[...])
+    gated = mixed_ref[...] * (z_raw * jax.nn.sigmoid(z_raw))
+    z_ref[...] = z_raw
+    gated_ref[...] = gated
+    sums = jnp.sum(gated * gated, axis=1, keepdims=True)
+    sums_ref[...] = jnp.broadcast_to(sums, (sums.shape[0], LANE)).T[:8]
+
+
+def output_kernel(left_ref, right_ref, grad_ref, first_ref, second_ref, sums_ref):
+    half = first_ref.shape[1]
+    total = None
+    for at, out_ref in ((0, first_ref), (half, second_ref)):
+        part = mm_nt(left_ref[...], right_ref[at : at + half, :])
+        out_ref[...] = part.astype(BF16)
+        sums = jnp.sum(part * grad_ref[:, at : at + half].astype(F32), axis=1, keepdims=True)
+        total = sums if total is None else total + sums
+    sums_ref[...] = jnp.broadcast_to(total, (total.shape[0], LANE)).T[:8]
+
+
+def gate_grad_kernel(
+    left_ref, right_ref, z_ref, mixed_ref, gain_ref, inv_ref, mean_ref, dy_ref, dz_ref, dgain_ref
+):
+    @pl.when(pl.program_id(0) == 0)
+    def _():
+        dgain_ref[...] = jnp.zeros_like(dgain_ref)
+
+    d_ng = mm(left_ref[...], right_ref[...])
+    z_raw = z_ref[...]
+    mixed = mixed_ref[...]
+    inv = inv_ref[...]
+    sig = jax.nn.sigmoid(z_raw)
+    gate_act = z_raw * sig
+    unit = mixed * gate_act * inv
+    dgain_ref[0:1, :] += jnp.sum(d_ng * unit, axis=0, keepdims=True)
+    d_gated = inv * (d_ng * gain_ref[0:1, :] - unit * mean_ref[...])
+    dy_ref[...] = d_gated * gate_act
+    dz_ref[...] = (d_gated * mixed * sig * (1.0 + z_raw * (1.0 - sig))).astype(BF16)
+
+
+def row_call(kernel, name, seconds, length, rows, ins, outs):
+    def spec(shape, split):
+        if split == "rows":
+            return pl.BlockSpec((rows,) + shape, lambda m: (m, 0))
+        if split == "lanes":
+            return pl.BlockSpec(shape + (rows,), lambda m: (0, m))
+        return pl.BlockSpec(shape, lambda m: (0, 0))
+
+    return pl.pallas_call(
+        kernel,
+        grid=(length // rows,),
+        out_shape=tuple(jax.ShapeDtypeStruct(full, kind) for full, kind, _, _ in outs),
+        in_specs=[spec(shape, split) for _, shape, split in ins],
+        out_specs=tuple(spec(shape, split) for _, _, shape, split in outs),
+        compiler_params=pltpu.CompilerParams(vmem_limit_bytes=VMEM_CAP),
+        cost_estimate=time_like(seconds),
+        name=name,
+    )(*[array for array, _, _ in ins])
+
+
+def inner_product(normed, x_all, width, rows=256):
+    length, model = normed.shape
+    return row_call(
+        product_kernel,
+        "inner_product",
+        14e-6,
+        length,
+        rows,
+        [(normed, (model,), "rows"), (x_all, (model, width), None)],
+        [((length, width), F32, (width,), "rows")],
+    )[0]
+
+
+def gate_product(normed, gate_all, mixed, rows=256):
+    length, model = normed.shape
+    width = gate_all.shape[1]
+    wide = ((length, width), F32, (width,), "rows")
+    z_raw, gated, sums = row_call(
+        gate_kernel,
+        "gate_product",
+        16e-6,
+        length,
+        rows,
+        [(normed, (model,), "rows"), (gate_all, (model, width), None), (mixed, (width,), "rows")],
+        [wide, wide, ((8, length), F32, (8,), "lanes")],
+    )
+    return z_raw, gated, sums[0]
+
+
+def output_product(normed_gated, out_all, group_grad, rows=256):
+    length, width = normed_gated.shape
+    model = out_all.shape[0]
+    part = ((length, model // 2), BF16, (model // 2,), "rows")
+    left, right, sums = row_call(
+        output_kernel,
+        "output_product",
+        16e-6,
+        length,
+        rows,
+        [
+            (normed_gated, (width,), "rows"),
+            (out_all, (model, width), None),
+            (group_grad, (model,), "rows"),
+        ],
+        [part, part, ((8, length), F32, (8,), "lanes")],
+    )
+    return left, right, sums[0]
+
+
+def gate_gradient(group_grad, out_all, z_raw, mixed, gain, inv, mean, rows=256):
+    length, model = group_grad.shape
+    width = out_all.shape[1]
+    return row_call(
+        gate_grad_kernel,
+        "gate_gradient",
+        18e-6,
+        length,
+        rows,
+        [
+            (group_grad, (model,), "rows"),
+            (out_all, (model, width), None),
+            (z_raw, (width,), "rows"),
+            (mixed, (width,), "rows"),
+            (gain, (8, width), None),
+            (inv, (1,), "rows"),
+            (mean, (1,), "rows"),
+        ],
+        [
+            ((length, width), F32, (width,), "rows"),
+            ((length, width), BF16, (width,), "rows"),
+            ((8, width), F32, (8, width), None),
+        ],
+    )
+
 DI = 5120
 STEP = 3
 NORM_EPS = 1e-05
@@ -739,12 +878,12 @@
     return total
 
 
-def all_sum(value, size):
-    distance = 1
-    while distance < size:
-        value = value + swap(value, distance, size)
-        distance *= 2
-    return value
+def all_sum(value, index, size):
+    terms = jnp.zeros((size,) + value.shape, value.dtype)
+    for distance in range(size):
+        piece = value if distance == 0 else swap(value, distance, size)
+        terms = lax.dynamic_update_slice(terms, piece[None], (index ^ distance, jnp.int32(0)))
+    return jnp.sum(terms, axis=0)
 
 
 def fsdp_swap(value, distance, size):
@@ -893,7 +1032,7 @@
     small = lax.dot_general(
         side_all, normed, (((0,), (1,)), ((), ())), preferred_element_type=F32
     )
-    raw = mm(normed, x_all)
+    raw = inner_product(normed, x_all, width)
     tables = segment_tables(segment)
     doc_masks = tables[0]
     state_vals, state_back = jax.vjp(
@@ -915,40 +1054,31 @@
     skip8 = jnp.broadcast_to(jnp.repeat(head_params[2], LANE // 2)[None, :], (8, width))
     mixed, states = ssd_forward(raw, small, bc, tables, taps8, hp8, skip8, spread, heads)
 
-    z_raw = mm(normed, gate_all)
-    sig = jax.nn.sigmoid(z_raw)
-    gate_act = z_raw * sig
-    gated = mixed * gate_act
-    square_sum, *grad_parts = tied(jnp.sum(gated * gated, axis=1), *grad_parts)
+    z_raw, gated, square_sum = gate_product(normed, gate_all, mixed)
+    square_sum, *grad_parts = tied(square_sum, *grad_parts)
     square_sum = row_sum(square_sum, tp_size)
     group_grad = jnp.zeros((group_rows, model), BF16)
     for distance in range(tp_size):
         group_grad = put(group_grad, grad_parts[distance], distance)
     group_grad = by_rows(group_grad)
     inv_gate = lax.rsqrt(square_sum / DI + NORM_EPS)[:, None]
-    unit_gated = gated * inv_gate
-    normed_gated = (unit_gated * mixer_f[None, :]).astype(BF16)
+    normed_gated = (gated * inv_gate * mixer_f[None, :]).astype(BF16)
     sum_out = pair_sum(
         contract_rows(group_grad, normed_gated).astype(BF16), fsdp_index, fsdp_size
     )
     half = model // 2
-    mixed_halves = [mm_nt(normed_gated, out_all[:half])]
     normed_gated, sum_out = tied(normed_gated, sum_out)
     grad_out = chip_scatter(sum_out, fsdp_size)
-    mixed_halves.append(mm_nt(normed_gated, out_all[half:]))
-    inner_sum = jnp.sum(mixed_halves[0] * group_grad[:, :half].astype(F32), axis=1) + jnp.sum(
-        mixed_halves[1] * group_grad[:, half:].astype(F32), axis=1
-    )
+    mixed_left, mixed_right, inner_sum = output_product(normed_gated, out_all, group_grad)
     inner_sum = row_sum(inner_sum, tp_size)
-    mixed_left, mixed_right = (part.astype(BF16) for part in mixed_halves)
     mixed_sent, mixed_kept = scatter_start(mixed_left, mixed_right, own_rows, tp_index, tp_size)
 
     inner_mean = inner_sum[:, None] / DI
-    d_ng = mm(group_grad, out_all)
-    grad_mixer = jnp.sum(d_ng * unit_gated, axis=0)
-    d_gated = inv_gate * (d_ng * mixer_f[None, :] - unit_gated * inner_mean)
-    d_mixed = d_gated * gate_act
-    d_z = (d_gated * mixed * sig * (1.0 + z_raw * (1.0 - sig))).astype(BF16)
+    mixer8 = jnp.broadcast_to(mixer_f[None, :], (8, width))
+    d_mixed, d_z, grad_mixer = gate_gradient(
+        group_grad, out_all, z_raw, mixed, mixer8, inv_gate, inner_mean
+    )
+    grad_mixer = grad_mixer[0]
     part_gate, mixed_sent = tied(contract_rows(normed, d_z).astype(BF16), mixed_sent)
     sum_gate = pair_sum(part_gate, fsdp_index, fsdp_size)
     mixed_passed, mixed_kept = scatter_middle(mixed_sent, mixed_kept, own_rows, tp_size)
@@ -1054,7 +1184,7 @@
     last = scatter_last(passed, tp_size)
     grad_side = side_gradient(side_part, d_taps, d_skip, d_heads, grad_conv_state, gain_sums)
     grad_side, last[0] = tied(grad_side, last[0])
-    grad_input_gain = all_sum(grad_side[:, used], tp_size) / input_gain.astype(F32)
+    grad_input_gain = all_sum(grad_side[:, used], tp_index, tp_size) / input_gain.astype(F32)
     d_normed = scatter_end(kept, last)
 
     unit_rows, inv_rms = unit_of(block_in)

time: 564 us -> 555 us (0.984)
  matrix products: 142 us -> 54 us
  Pallas kernels: 138 us -> 210 us
  local copies, waits for them, and re-layouts: 59 us -> 67 us
    dot_general x5 -> x0, matrix products: 87.6 us -> none  [the longest x3 63.2 us: mm(): lax.dot_general(left, right, (((1,), (0,)), ((), ())), preferred_element_...]
    pallas_call x0 -> x4, Pallas kernels: none -> 72.3 us  [row_call(): pl.pallas_call(kernel, grid=(length // rows,), out_shape=tuple((jax.Shape...]
    ppermute x29 -> x30, waiting for transfers between devices: 50.1 us -> 51.5 us  [swap(): lax.ppermute(value, 'tp', [(at, at ^ distance) for at in range(size)])]
    ppermute x29 -> x30, starting transfers between devices: 36.4 us -> 37.7 us  [swap(): lax.ppermute(value, 'tp', [(at, at ^ distance) for at in range(size)])]
    unnamed x201 -> x203, local copies, waits for them, and re-layouts: 11.8 us -> 12 us
  transfers between devices with their start and end apart: 45 -> 46, of which waited for: 13 -> 14; matrix products, arithmetic and copies ran while one was open for 46% -> 33% of each run, Pallas kernels for 25% -> 38%
where the time goes in v4:
time: 555 us; the launch traced here: 549 us
  Pallas kernels  210 us (38%)
  other arithmetic  84.7 us (15%)
  waiting for transfers between devices  68.3 us (12%)
  local copies, waits for them, and re-layouts  67 us (12%)
  matrix products  54 us (10%)
  starting transfers between devices  47.5 us (9%)
  between operations  16.6 us (3%)
    pallas_call x4, Pallas kernels, row_call(): pl.pallas_call(kernel, grid=(length // rows,), out_shape=tuple((jax.Shape...  72.3 us
    pallas_call x1, Pallas kernels, ssd_backward(): pl.pallas_call(functools.partial(ssd_bwd_kernel, heads), grid=(chunks,),...  52.9 us
    ppermute x30, waiting for transfers between devices, swap(): lax.ppermute(value, 'tp', [(at, at ^ distance) for at in range(size)])  51.5 us
    pallas_call x4, Pallas kernels, d_normed_blocks(): pl.pallas_call(functools.partial(dn_kernel, count, rows), grid_spec=pltpu...  48.4 us
    dot_general x3, matrix products, contract_rows(): lax.dot_general(left_mat, right_mat, (((0,), (0,)), ((), ())), preferred_...  41.1 us
    ppermute x30, starting transfers between devices, swap(): lax.ppermute(value, 'tp', [(at, at ^ distance) for at in range(size)])  37.7 us
    pallas_call x1, Pallas kernels, ssd_forward(): pl.pallas_call(functools.partial(ssd_fwd_kernel, heads), grid=(chunks,),...  21.2 us
    ppermute x10, waiting for transfers between devices, fsdp_swap(): lax.ppermute(value, 'fsdp', [(at, at ^ distance) for at in range(size)])  16.7 us
  transfers between devices with their start and end apart: 46, of which 14 were waited for; matrix products, arithmetic and copies ran while one was open for 33% of the time, Pallas kernels for 38%

profile of v4, /device:TPU:0, one launch (start us, length us, event | category | flops | bytes accessed | tf_op | source)
XLA Modules:
  0.0 548.7 jit_solution(8137174959354889267)
XLA Ops:
  16.1 3.0 collective-permute-start.4
  22.7 3.2 fusion.6
  31.9 2.4 collective-permute-start.3
  36.8 3.7 broadcast.298.clone
  42.3 19.8 %collective-permute-done.4 = bf16[384,2560]{1,0:T(8,128)(2,1)} collective-permute-done((bf16[384,2560]{1,0:T(8,128)(2,1)S(1)}, bf16[384,2560]{1,0:T(8,128)(2,1)}, u32[]{:S(2)}, u32[]{:S(2)}) %collective-permute-start.4) | collective-permute-done | bytes 1966112 | tf_op jit(solution)/shard_map/ppermute | solution.py:812
  71.5 14.9 %collective-permute-done.5 = bf16[192,2560]{1,0:T(8,128)(2,1)S(1)} collective-permute-done((bf16[192,2560]{1,0:T(8,128)(2,1)S(1)}, bf16[192,2560]{1,0:T(8,128)(2,1)S(1)}, u32[]{:S(2)}, u32[]{:S(2)}) %collective-permute-start.5) | collective-permute-done | bytes 983072 | tf_op jit(solution)/shard_map/ppermute | solution.py:812
  86.4 2.5 collective-permute-done.6
  91.1 3.0 fusion.8
  94.1 3.4 fusion.26
  97.5 3.5 fusion.25
  109.5 6.3 %fusion.33.small_ref = f32[128,1536]{1,0:T(8,128)S(1)} fusion(bf16[1536,2560]{1,0:T(8,128)(2,1)} %fusion.24.left_ref.refs_6_.refs_7_, bf16[2560,1408]{1,0:T(8,128)(2,1)} %all-gather.5.cloned.1.call-done.right_ref.refs_9_), kind=kOutput, calls=%fused_computation.82 | convolution fusion | flops 1006632960 | bytes 9306112 | tf_op jit(solution)/shard_map/dot_general | solution.py:1032
  126.5 15.8 %inner_product.1.raw_ref.halo_ref = f32[1536,1280]{1,0:T(8,128)} custom-call(bf16[1536,2560]{1,0:T(8,128)(2,1)} %fusion.24.left_ref.refs_6_.refs_7_, bf16[2560,1408]{1,0:T(8,128)(2,1)} %all-gather.5.cloned.1.call-done.right_ref.refs_9_), custom_call_target="tpu_custom_call" | custom-call | flops 15399999488 | bytes 47600000 | tf_op jit(solution)/shard_map/inner_product/pallas_call | solution.py:675
  150.1 21.2 %ssd_fwd.1 = (f32[1536,1280]{1,0:T(8,128)}, f32[6,128,1280]{2,1,0:T(8,128)}) custom-call(f32[1536,1280]{1,0:T(8,128)} %inner_product.1.raw_ref.halo_ref, f32[128,1536]{1,0:T(8,128)} %copy-done.12, bf16[256,1536]{1,0:T(8,128)(2,1)} %copy-done.30, f32[1536,384]{1,0:T(8,128)} %pad_maximum_fusion.masks_ref.masks_next_ref, ...), custom_call_target="tpu_custom_call" | custom-call | flops 40699998208 | bytes 125800000 | tf_op jit(solution)/shard_map/ssd_fwd/pallas_call | solution.py:388
  171.4 18.4 %gate_product.1 = (f32[1536,1280]{1,0:T(8,128)}, f32[1536,1280]{1,0:T(8,128)}, f32[8,1536]{1,0:T(8,128)}) custom-call(bf16[1536,2560]{1,0:T(8,128)(2,1)} %fusion.24.left_ref.refs_6_.refs_7_, bf16[2560,1280]{1,0:T(8,128)(2,1)} %bitcast.94, f32[1536,1280]{1,0:T(8,128)} %get-tuple-element.135.mixed_ref.y_ref), custom_call_target="tpu_custom_call" | custom-call | flops 17600000000 | bytes 54400000 | tf_op jit(solution)/shard_map/gate_product/pallas_call | solution.py:675
  195.0 2.0 constant_dynamic-update-slice_fusion.2
  201.5 2.3 copy-done.4
  203.8 11.0 %convolution_convert_fusion.2 = bf16[2560,1280]{1,0:T(8,128)(2,1)S(1)} fusion(bf16[1536,2560]{1,0:T(8,128)(2,1)S(1)} %constant_dynamic-update-slice_fusion.grad_ref.left_ref, bf16[1536,1280]{1,0:T(8,128)(2,1)S(1)} %multiply_convert_fusion.left_ref), kind=kOutput, calls=%fused_computation.2 | convolution fusion | flops 10069606400 | bytes 18350080 | tf_op jit(solution)/shard_map/dot_general | solution.py:794
  214.8 2.1 dynamic-slice_bitcast_fusion.2
  219.6 4.9 collective-permute-done.16
  224.5 4.4 fusion.2
  229.1 16.7 %output_product.1 = (bf16[1536,1280]{1,0:T(8,128)(2,1)}, bf16[1536,1280]{1,0:T(8,128)(2,1)}, f32[8,1536]{1,0:T(8,128)}) custom-call(bf16[1536,1280]{1,0:T(8,128)(2,1)} %copy-done.8, bf16[2560,1280]{1,0:T(8,128)(2,1)} %all-gather.7.cloned.1.call-done.right_ref, bf16[1536,2560]{1,0:T(8,128)(2,1)} %copy-done.4), custom_call_target="tpu_custom_call" | custom-call | flops 17600000000 | bytes 54400000 | tf_op jit(solution)/shard_map/output_product/pallas_call | solution.py:675
  258.8 21.3 %gate_gradient.1 = (f32[1536,1280]{1,0:T(8,128)}, bf16[1536,1280]{1,0:T(8,128)(2,1)}, f32[8,1280]{1,0:T(8,128)}) custom-call(bf16[1536,2560]{1,0:T(8,128)(2,1)} %copy-done.4, bf16[2560,1280]{1,0:T(8,128)(2,1)} %all-gather.7.cloned.1.call-done.right_ref, f32[1536,1280]{1,0:T(8,128)} %get-tuple-element.147.z_ref, ...), custom_call_target="tpu_custom_call" | custom-call | flops 19800000512 | bytes 61200000 | tf_op jit(solution)/shard_map/gate_gradient/pallas_call | solution.py:675
  280.1 14.0 %convolution_convert_fusion.1 = bf16[2560,1280]{1,0:T(8,128)(2,1)S(1)} fusion(bf16[1536,2560]{1,0:T(8,128)(2,1)} %fusion.24.left_ref.refs_6_.refs_7_, bf16[1536,1280]{1,0:T(8,128)(2,1)} %get-tuple-element.149.refs_0_.refs_1_), kind=kOutput, calls=%fused_computation.1 | convolution fusion | flops 10069606400 | bytes 18350080 | tf_op jit(solution)/shard_map/dot_general | solution.py:794
  294.1 3.7 collective-permute-done.21
  297.8 2.6 collective-permute-done.20
  302.1 2.4 add_convert_fusion.3
  306.6 2.6 fusion.1
  311.3 52.9 %ssd_bwd.1 = (bf16[1536,1280]{1,0:T(8,128)(2,1)}, f32[32,1536]{1,0:T(8,128)}, f32[256,1536]{1,0:T(8,128)}, f32[8,1280]{1,0:T(8,128)}, f32[32,128]{1,0:T(8,128)}, /*index=5*/f32[8,1280]{1,0:T(8,128)}) custom-call(f32[1536,1280]{1,0:T(8,128)} %inner_product.1.raw_ref.halo_ref, f32[1536,1280]{1,0:T(8,128)} %inner_product.1.raw_ref.halo_ref, ...), custom_call_target="tpu_custom_call" | custom-call | flops 75900002304 | bytes 234600000 | tf_op jit(solution)/shard_map/ssd_bwd/pallas_call | solution.py:438
  365.7 2.6 collective-permute-start.27
  369.2 16.2 %convolution_convert_fusion = bf16[2560,1280]{1,0:T(8,128)(2,1)} fusion(bf16[1536,2560]{1,0:T(8,128)(2,1)} %fusion.24.left_ref.refs_6_.refs_7_, bf16[1536,1280]{1,0:T(8,128)(2,1)} %get-tuple-element.159.refs_2_.refs_3_), kind=kOutput, calls=%fused_computation | convolution fusion | flops 10069606400 | bytes 18350080 | tf_op jit(solution)/shard_map/dot_general | solution.py:794
  385.9 4.0 dynamic-slice_bitcast_fusion
  393.5 12.2 %d_normed.5 = (bf16[768,1280]{1,0:T(8,128)(2,1)}, f32[8,1280]{1,0:T(8,128)}) custom-call(s32[2]{0:T(128)} %get-tuple-element.441.at_ref, bf16[1536,1280]{1,0:T(8,128)(2,1)} %get-tuple-element.149.refs_0_.refs_1_, bf16[1536,1280]{1,0:T(8,128)(2,1)} %get-tuple-element.149.refs_0_.refs_1_, bf16[1536,1280]{1,0:T(8,128)(2,1)} %get-tuple-element.159.refs_2_.refs_3_, ...), custom_call_target="tpu_custom_call" | custom-call | flops 110000000 | bytes 340000 | tf_op jit(solution)/shard_map/d_normed/pallas_call | solution.py:556
  405.7 4.4 fusion
  413.2 11.8 %d_normed.7 = (bf16[768,1280]{1,0:T(8,128)(2,1)}, f32[8,1280]{1,0:T(8,128)}) custom-call(s32[2]{0:T(128)} %get-tuple-element.439.at_ref, bf16[1536,1280]{1,0:T(8,128)(2,1)} %get-tuple-element.149.refs_0_.refs_1_, bf16[1536,1280]{1,0:T(8,128)(2,1)} %get-tuple-element.149.refs_0_.refs_1_, bf16[1536,1280]{1,0:T(8,128)(2,1)} %get-tuple-element.159.refs_2_.refs_3_, ...), custom_call_target="tpu_custom_call" | custom-call | flops 110000000 | bytes 340000 | tf_op jit(solution)/shard_map/d_normed/pallas_call | solution.py:556
  429.5 12.0 %d_normed.4 = (bf16[768,1280]{1,0:T(8,128)(2,1)}, f32[8,1280]{1,0:T(8,128)}) custom-call(s32[2]{0:T(128)} %get-tuple-element.442.at_ref, bf16[1536,1280]{1,0:T(8,128)(2,1)} %get-tuple-element.149.refs_0_.refs_1_, bf16[1536,1280]{1,0:T(8,128)(2,1)} %get-tuple-element.149.refs_0_.refs_1_, bf16[1536,1280]{1,0:T(8,128)(2,1)} %get-tuple-element.159.refs_2_.refs_3_, ...), custom_call_target="tpu_custom_call" | custom-call | flops 110000000 | bytes 340000 | tf_op jit(solution)/shard_map/d_normed/pallas_call | solution.py:556
  441.5 6.5 %fusion.44 = f32[2560,128]{1,0:T(8,128)} fusion(bf16[1536,2560]{1,0:T(8,128)(2,1)} %fusion.24.left_ref.refs_6_.refs_7_, f32[64,1536]{1,0:T(8,128)S(1)} %copy-done.27, f32[20,1536]{1,0:T(8,128)S(1)} %slice.232), kind=kOutput, calls=%fused_computation.108 | convolution fusion | flops 1008009216 | bytes 9691136 | tf_op jit(solution)/shard_map/dot_general | solution.py:1108
  448.0 7.6 %collective-permute-done.28 = bf16[768,1280]{1,0:T(8,128)(2,1)S(1)} collective-permute-done((bf16[768,1280]{1,0:T(8,128)(2,1)}, bf16[768,1280]{1,0:T(8,128)(2,1)S(1)}, u32[]{:S(2)}, u32[]{:S(2)}) %collective-permute-start.28) | collective-permute-done | bytes 1966112 | tf_op jit(solution)/shard_map/ppermute | solution.py:812
  455.6 12.5 %d_normed.6 = (bf16[768,1280]{1,0:T(8,128)(2,1)}, f32[8,1280]{1,0:T(8,128)}) custom-call(s32[2]{0:T(128)} %get-tuple-element.440.at_ref, bf16[1536,1280]{1,0:T(8,128)(2,1)} %get-tuple-element.149.refs_0_.refs_1_, bf16[1536,1280]{1,0:T(8,128)(2,1)} %get-tuple-element.149.refs_0_.refs_1_, bf16[1536,1280]{1,0:T(8,128)(2,1)} %get-tuple-element.159.refs_2_.refs_3_, ...), custom_call_target="tpu_custom_call" | custom-call | flops 110000000 | bytes 340000 | tf_op jit(solution)/shard_map/d_normed/pallas_call | solution.py:556
  470.3 4.4 fusion.29
  475.2 2.2 fusion.31
  477.6 2.5 add_convert_fusion
  480.1 3.1 convert_add_fusion.7
  485.3 2.6 collective-permute-start.33
  489.9 3.1 convert_add_fusion.8
  494.3 8.2 %collective-permute-done.33 = f32[320,128]{0,1:T(8,128)S(1)} collective-permute-done((f32[320,128]{0,1:T(8,128)S(1)}, f32[320,128]{0,1:T(8,128)S(1)}, u32[]{:S(2)}, u32[]{:S(2)}) %collective-permute-start.33) | collective-permute-done | bytes 163872 | tf_op jit(solution)/shard_map/ppermute | solution.py:890
  504.1 15.6 %adam_pair.1 = (f32[320,2,1280]{2,1,0:T(2,128)}, bf16[320,2,1280]{2,1,0:T(2,128)(2,1)}, f32[320,2,1280]{2,1,0:T(2,128)}, f32[320,2,1280]{2,1,0:T(2,128)}) custom-call(bf16[320,1280]{1,0:T(8,128)(2,1)} %reduce-scatter.6.cloned.1.call-done.gate_ref, bf16[320,1280]{1,0:T(8,128)(2,1)} %reduce-scatter.8.cloned.1.call-done.inner_ref, ...), custom_call_target="tpu_custom_call" | custom-call | flops 1000 | bytes 1000 | tf_op jit(solution)/shard_map/adam_pair/pallas_call | solution.py:611
  525.1 2.4 convert_add_fusion.5
  532.3 6.0 %fusion.7 = (bf16[384,2560]{1,0:T(8,128)(2,1)}, bf16[384,2560]{1,0:T(8,128)(2,1)}) fusion(bf16[384,2560]{1,0:T(8,128)(2,1)} %param.36, bf16[384,2560]{1,0:T(8,128)(2,1)S(1)} %copy-done.1, f32[384,1280]{1,0:T(8,128)} %copy-done.3, f32[384,1280]{1,0:T(8,128)} %copy-done.2, f32[384]{0:T(512)S(1)} %broadcast_multiply_fusion, f32[2560]{0:T(1024)S(1)} %copy-done.32, ...), kind=kLoop, calls=%fused_computation.25 | loop fusion | flops 13762560 | bytes 15742336 | tf_op jit(solution)/shard_map/convert_element_type | solution.py:1193
  (466 shorter events, 128.3 us)
Async XLA Ops:
  7.2 96.1 %all-gather.5.cloned.1.call-start = ((), (), s32[]{:S(2)}) async-start(), calls=%async_computation.3 | async-start | bytes 8110080 | tf_op jit(solution)/shard_map/all_gather | solution.py:976
  16.1 155.3 %all-gather.9.cloned.1.call-start = ((), (), s32[]{:S(2)}) async-start(), calls=%async_computation.8 | async-start | bytes 7372800 | tf_op jit(solution)/shard_map/all_gather | solution.py:977
  16.1 46.0 %collective-permute-start.4 = (bf16[384,2560]{1,0:T(8,128)(2,1)S(1)}, bf16[384,2560]{1,0:T(8,128)(2,1)}, u32[]{:S(2)}, u32[]{:S(2)}) collective-permute-start(bf16[384,2560]{1,0:T(8,128)(2,1)S(1)} %copy-done), channel_id=1, source_target_pairs={{0,2},{1,3},{2,0},{3,1},{4,6},{5,7},{6,4},{7,5},{8,10},{9,11},{10,... | collective-permute-start | bytes 5898248 | tf_op jit(solution)/shard_map/ppermute | solution.py:812
  19.2 46.0 %collective-permute-start = (bf16[384,2560]{1,0:T(8,128)(2,1)S(1)}, bf16[384,2560]{1,0:T(8,128)(2,1)}, u32[]{:S(2)}, u32[]{:S(2)}) collective-permute-start(bf16[384,2560]{1,0:T(8,128)(2,1)S(1)} %copy-done), channel_id=1, source_target_pairs={{0,1},{1,0},{2,3},{3,2},{4,5},{5,4},{6,7},{7,6},{8,9},{9,8},{10,11... | collective-permute-start | bytes 5898248 | tf_op jit(solution)/shard_map/ppermute | solution.py:812
  20.7 7.0 %collective-permute-start.1 = (bf16[8,320]{1,0:T(8,128)(2,1)S(1)}, bf16[8,320]{1,0:T(8,128)(2,1)S(1)}, u32[]{:S(2)}, u32[]{:S(2)}) collective-permute-start(bf16[8,320]{1,0:T(8,128)(2,1)S(1)} %dynamic_update_slice.53), channel_id=1, source_target_pairs={{0,4},{4,0},{8,12},{12,8},{16,20},{20,16},{24,28},{28,24},{1,5},{5... | collective-permute-start | bytes 15368 | tf_op jit(solution)/shard_map/ppermute | solution.py:890
  20.8 208.2 %all-gather.7.cloned.1.call-start = ((), (), s32[]{:S(2)}) async-start(), calls=%async_computation.4 | async-start | bytes 7372800 | tf_op jit(solution)/shard_map/all_gather | solution.py:1049
  26.1 89.8 %copy-start.34 = (f32[1536]{0:T(1024)}, f32[1536]{0:T(1024)S(1)}, u32[]{:S(2)}) copy-start(f32[1536]{0:T(1024)S(1)} %get-tuple-element.430) | copy-start | bytes 18436
  26.1 89.8 %copy-start.36 = (f32[1536]{0:T(1024)}, f32[1536]{0:T(1024)S(1)}, u32[]{:S(2)}) copy-start(f32[1536]{0:T(1024)S(1)} %get-tuple-element.431) | copy-start | bytes 18436
  28.0 4.0 collective-permute-start.2
  31.9 4.8 collective-permute-start.3
  63.4 23.0 %collective-permute-start.5 = (bf16[192,2560]{1,0:T(8,128)(2,1)S(1)}, bf16[192,2560]{1,0:T(8,128)(2,1)S(1)}, u32[]{:S(2)}, u32[]{:S(2)}) collective-permute-start(bf16[192,2560]{1,0:T(8,128)(2,1)S(1)} %slice.256), channel_id=1, source_target_pairs={{0,1},{1,0},{2,3},{3,2},{4,5},{5,4},{6,7},{7,6},{8,9},{9,8},{10,11... | collective-permute-start | bytes 2949128 | tf_op jit(solution)/shard_map/ppermute | solution.py:812
  66.5 22.4 %collective-permute-start.6 = (bf16[192,2560]{1,0:T(8,128)(2,1)S(1)}, bf16[192,2560]{1,0:T(8,128)(2,1)S(1)}, u32[]{:S(2)}, u32[]{:S(2)}) collective-permute-start(bf16[192,2560]{1,0:T(8,128)(2,1)S(1)} %slice.198), channel_id=1, source_target_pairs={{0,2},{1,3},{2,0},{3,1},{4,6},{5,7},{6,4},{7,5},{8,10},{9,11},{10,... | collective-permute-start | bytes 2949128 | tf_op jit(solution)/shard_map/ppermute | solution.py:812
  89.0 101.7 %collective-permute-start.11 = (bf16[384,2560]{1,0:T(8,128)(2,1)S(1)}, bf16[384,2560]{1,0:T(8,128)(2,1)}, u32[]{:S(2)}, u32[]{:S(2)}) collective-permute-start(bf16[384,2560]{1,0:T(8,128)(2,1)S(1)} %copy-done.5), channel_id=1, source_target_pairs={{0,2},{1,3},{2,0},{3,1},{4,6},{5,7},{6,4},{7,5},{8,10},{9,11},{10,... | collective-permute-start | bytes 5898248 | tf_op jit(solution)/shard_map/ppermute | solution.py:812
  90.6 100.1 %collective-permute-start.10 = (bf16[384,2560]{1,0:T(8,128)(2,1)S(1)}, bf16[384,2560]{1,0:T(8,128)(2,1)}, u32[]{:S(2)}, u32[]{:S(2)}) collective-permute-start(bf16[384,2560]{1,0:T(8,128)(2,1)S(1)} %copy-done.5), channel_id=1, source_target_pairs={{0,1},{1,0},{2,3},{3,2},{4,5},{5,4},{6,7},{7,6},{8,9},{9,8},{10,11... | collective-permute-start | bytes 5898248 | tf_op jit(solution)/shard_map/ppermute | solution.py:812
  118.0 25.9 %collective-permute-start.8 = (bf16[64,1536]{1,0:T(8,128)(2,1)}, bf16[64,1536]{1,0:T(8,128)(2,1)}, u32[]{:S(2)}, u32[]{:S(2)}) collective-permute-start(bf16[64,1536]{1,0:T(8,128)(2,1)} %get-tuple-element.406), channel_id=1, source_target_pairs={{0,2},{1,3},{2,0},{3,1},{4,6},{5,7},{6,4},{7,5},{8,10},{9,11},{10,... | collective-permute-start | bytes 589832 | tf_op jit(solution)/shard_map/ppermute | solution.py:812
  118.5 24.4 %collective-permute-start.7 = (bf16[64,1536]{1,0:T(8,128)(2,1)}, bf16[64,1536]{1,0:T(8,128)(2,1)}, u32[]{:S(2)}, u32[]{:S(2)}) collective-permute-start(bf16[64,1536]{1,0:T(8,128)(2,1)} %get-tuple-element.406), channel_id=1, source_target_pairs={{0,1},{1,0},{2,3},{3,2},{4,5},{5,4},{6,7},{7,6},{8,9},{9,8},{10,11... | collective-permute-start | bytes 589832 | tf_op jit(solution)/shard_map/ppermute | solution.py:812
  119.9 25.0 %collective-permute-start.9 = (bf16[64,1536]{1,0:T(8,128)(2,1)}, bf16[64,1536]{1,0:T(8,128)(2,1)}, u32[]{:S(2)}, u32[]{:S(2)}) collective-permute-start(bf16[64,1536]{1,0:T(8,128)(2,1)} %get-tuple-element.406), channel_id=1, source_target_pairs={{0,3},{1,2},{2,1},{3,0},{4,7},{5,6},{6,5},{7,4},{8,11},{9,10},{10,... | collective-permute-start | bytes 589832 | tf_op jit(solution)/shard_map/ppermute | solution.py:812
  145.8 44.9 %collective-permute-start.12 = (bf16[384,2560]{1,0:T(8,128)(2,1)S(1)}, bf16[384,2560]{1,0:T(8,128)(2,1)}, u32[]{:S(2)}, u32[]{:S(2)}) collective-permute-start(bf16[384,2560]{1,0:T(8,128)(2,1)S(1)} %copy-done.5), channel_id=1, source_target_pairs={{0,3},{1,2},{2,1},{3,0},{4,7},{5,6},{6,5},{7,4},{8,11},{9,10},{10,... | collective-permute-start | bytes 5898248 | tf_op jit(solution)/shard_map/ppermute | solution.py:812
  147.2 162.0 %reduce-scatter.4.cloned.1.call-start = ((), (), s32[]{:S(2)}) async-start(), calls=%async_computation.5 | async-start | bytes 4096000 | tf_op jit(solution)/shard_map/reduce_scatter | solution.py:912
  190.7 10.0 %collective-permute-start.15 = (f32[1536]{0:T(1024)S(1)}, f32[1536]{0:T(1024)S(1)}, u32[]{:S(2)}, u32[]{:S(2)}) collective-permute-start(f32[1536]{0:T(1024)S(1)} %slice_reduce_fusion.3), channel_id=1, source_target_pairs={{0,3},{1,2},{2,1},{3,0},{4,7},{5,6},{6,5},{7,4},{8,11},{9,10},{10,... | collective-permute-start | bytes 18440 | tf_op jit(solution)/shard_map/ppermute | solution.py:812
  192.4 8.3 %collective-permute-start.14 = (f32[1536]{0:T(1024)S(1)}, f32[1536]{0:T(1024)S(1)}, u32[]{:S(2)}, u32[]{:S(2)}) collective-permute-start(f32[1536]{0:T(1024)S(1)} %slice_reduce_fusion.3), channel_id=1, source_target_pairs={{0,2},{1,3},{2,0},{3,1},{4,6},{5,7},{6,4},{7,5},{8,10},{9,11},{10,... | collective-permute-start | bytes 18440 | tf_op jit(solution)/shard_map/ppermute | solution.py:812
  192.9 7.9 %collective-permute-start.13 = (f32[1536]{0:T(1024)S(1)}, f32[1536]{0:T(1024)S(1)}, u32[]{:S(2)}, u32[]{:S(2)}) collective-permute-start(f32[1536]{0:T(1024)S(1)} %slice_reduce_fusion.3), channel_id=1, source_target_pairs={{0,1},{1,0},{2,3},{3,2},{4,5},{5,4},{6,7},{7,6},{8,9},{9,8},{10,11... | collective-permute-start | bytes 18440 | tf_op jit(solution)/shard_map/ppermute | solution.py:812
  218.5 6.1 %collective-permute-start.16 = (bf16[4,320,1280]{2,1,0:T(8,128)(2,1)}, bf16[4,320,1280]{2,1,0:T(8,128)(2,1)S(1)}, u32[]{:S(2)}, u32[]{:S(2)}) collective-permute-start(bf16[4,320,1280]{2,1,0:T(8,128)(2,1)} %dynamic-slice_bitcast_fusion.2), channel_id=1, source_target_pairs={{0,4},{4,0},{8,12},{12,8},{16,20},{20,16},{24,28},{28,24},{1,5},{5... | collective-permute-start | bytes 9830408 | tf_op jit(solution)/shard_map/ppermute | solution.py:890
  229.0 156.8 %reduce-scatter.6.cloned.1.call-start = ((), (), s32[]{:S(2)}) async-start(), calls=%async_computation.6 | async-start | bytes 4096000 | tf_op jit(solution)/shard_map/reduce_scatter | solution.py:912
  246.8 10.2 %collective-permute-start.19 = (f32[1536]{0:T(1024)S(1)}, f32[1536]{0:T(1024)S(1)}, u32[]{:S(2)}, u32[]{:S(2)}) collective-permute-start(f32[1536]{0:T(1024)S(1)} %slice_reduce_fusion.2), channel_id=1, source_target_pairs={{0,3},{1,2},{2,1},{3,0},{4,7},{5,6},{6,5},{7,4},{8,11},{9,10},{10,... | collective-permute-start | bytes 18440 | tf_op jit(solution)/shard_map/ppermute | solution.py:812
  248.3 8.6 %collective-permute-start.18 = (f32[1536]{0:T(1024)S(1)}, f32[1536]{0:T(1024)S(1)}, u32[]{:S(2)}, u32[]{:S(2)}) collective-permute-start(f32[1536]{0:T(1024)S(1)} %slice_reduce_fusion.2), channel_id=1, source_target_pairs={{0,2},{1,3},{2,0},{3,1},{4,6},{5,7},{6,4},{7,5},{8,10},{9,11},{10,... | collective-permute-start | bytes 18440 | tf_op jit(solution)/shard_map/ppermute | solution.py:812
  248.8 8.2 %collective-permute-start.17 = (f32[1536]{0:T(1024)S(1)}, f32[1536]{0:T(1024)S(1)}, u32[]{:S(2)}, u32[]{:S(2)}) collective-permute-start(f32[1536]{0:T(1024)S(1)} %slice_reduce_fusion.2), channel_id=1, source_target_pairs={{0,1},{1,0},{2,3},{3,2},{4,5},{5,4},{6,7},{7,6},{8,9},{9,8},{10,11... | collective-permute-start | bytes 18440 | tf_op jit(solution)/shard_map/ppermute | solution.py:812
  253.5 44.3 %collective-permute-start.21 = (bf16[768,1280]{1,0:T(8,128)(2,1)}, bf16[768,1280]{1,0:T(8,128)(2,1)S(1)}, u32[]{:S(2)}, u32[]{:S(2)}) collective-permute-start(bf16[768,1280]{1,0:T(8,128)(2,1)} %pad_maximum_fusion.3), channel_id=1, source_target_pairs={{0,2},{1,3},{2,0},{3,1},{4,6},{5,7},{6,4},{7,5},{8,10},{9,11},{10,... | collective-permute-start | bytes 5898248 | tf_op jit(solution)/shard_map/ppermute | solution.py:812
  256.5 43.9 %collective-permute-start.20 = (bf16[768,1280]{1,0:T(8,128)(2,1)}, bf16[768,1280]{1,0:T(8,128)(2,1)S(1)}, u32[]{:S(2)}, u32[]{:S(2)}) collective-permute-start(bf16[768,1280]{1,0:T(8,128)(2,1)} %pad_maximum_fusion.2), channel_id=1, source_target_pairs={{0,1},{1,0},{2,3},{3,2},{4,5},{5,4},{6,7},{7,6},{8,9},{9,8},{10,11... | collective-permute-start | bytes 5898248 | tf_op jit(solution)/shard_map/ppermute | solution.py:812
  300.7 5.9 %collective-permute-start.22 = (bf16[4,320,1280]{2,1,0:T(8,128)(2,1)S(1)}, bf16[4,320,1280]{2,1,0:T(8,128)(2,1)S(1)}, u32[]{:S(2)}, u32[]{:S(2)}) collective-permute-start(bf16[4,320,1280]{2,1,0:T(8,128)(2,1)S(1)} %dynamic-slice_bitcast_fusion.1), channel_id=1, source_target_pairs={{0,4},{4,0},{8,12},{12,8},{16,20},{20,16},{24,28},{28,24},{1,5},{5... | collective-permute-start | bytes 9830408 | tf_op jit(solution)/shard_map/ppermute | solution.py:890
  309.2 174.1 %reduce-scatter.8.cloned.1.call-start = ((), (), s32[]{:S(2)}) async-start(), calls=%async_computation.7 | async-start | bytes 4096000 | tf_op jit(solution)/shard_map/reduce_scatter | solution.py:912
  310.3 75.4 %collective-permute-start.23 = (bf16[384,1280]{1,0:T(8,128)(2,1)S(1)}, bf16[384,1280]{1,0:T(8,128)(2,1)}, u32[]{:S(2)}, u32[]{:S(2)}) collective-permute-start(bf16[384,1280]{1,0:T(8,128)(2,1)S(1)} %copy-done.28), channel_id=1, source_target_pairs={{0,2},{1,3},{2,0},{3,1},{4,6},{5,7},{6,4},{7,5},{8,10},{9,11},{10,... | collective-permute-start | bytes 2949128 | tf_op jit(solution)/shard_map/ppermute | solution.py:812
  310.8 74.9 %collective-permute-start.24 = (bf16[384,1280]{1,0:T(8,128)(2,1)}, bf16[384,1280]{1,0:T(8,128)(2,1)}, u32[]{:S(2)}, u32[]{:S(2)}) collective-permute-start(bf16[384,1280]{1,0:T(8,128)(2,1)} %add_convert_fusion.2), channel_id=1, source_target_pairs={{0,1},{1,0},{2,3},{3,2},{4,5},{5,4},{6,7},{7,6},{8,9},{9,8},{10,11... | collective-permute-start | bytes 2949128 | tf_op jit(solution)/shard_map/ppermute | solution.py:812
  365.7 19.7 %collective-permute-start.27 = (f32[64,1536]{1,0:T(8,128)S(1)}, f32[64,1536]{1,0:T(8,128)S(1)}, u32[]{:S(2)}, u32[]{:S(2)}) collective-permute-start(f32[64,1536]{1,0:T(8,128)S(1)} %get-tuple-element.416), channel_id=1, source_target_pairs={{0,3},{1,2},{2,1},{3,0},{4,7},{5,6},{6,5},{7,4},{8,11},{9,10},{10,... | collective-permute-start | bytes 1179656 | tf_op jit(solution)/shard_map/ppermute | solution.py:812
  368.3 17.4 %collective-permute-start.26 = (f32[64,1536]{1,0:T(8,128)S(1)}, f32[64,1536]{1,0:T(8,128)S(1)}, u32[]{:S(2)}, u32[]{:S(2)}) collective-permute-start(f32[64,1536]{1,0:T(8,128)S(1)} %get-tuple-element.417), channel_id=1, source_target_pairs={{0,2},{1,3},{2,0},{3,1},{4,6},{5,7},{6,4},{7,5},{8,10},{9,11},{10,... | collective-permute-start | bytes 1179656 | tf_op jit(solution)/shard_map/ppermute | solution.py:812
  368.8 17.0 %collective-permute-start.25 = (f32[64,1536]{1,0:T(8,128)S(1)}, f32[64,1536]{1,0:T(8,128)S(1)}, u32[]{:S(2)}, u32[]{:S(2)}) collective-permute-start(f32[64,1536]{1,0:T(8,128)S(1)} %get-tuple-element.418), channel_id=1, source_target_pairs={{0,1},{1,0},{2,3},{3,2},{4,5},{5,4},{6,7},{7,6},{8,9},{9,8},{10,11... | collective-permute-start | bytes 1179656 | tf_op jit(solution)/shard_map/ppermute | solution.py:812
  389.9 15.8 %collective-permute-start.30 = (bf16[4,320,1280]{2,1,0:T(8,128)(2,1)}, bf16[4,320,1280]{2,1,0:T(8,128)(2,1)}, u32[]{:S(2)}, u32[]{:S(2)}) collective-permute-start(bf16[4,320,1280]{2,1,0:T(8,128)(2,1)} %dynamic-slice_bitcast_fusion), channel_id=1, source_target_pairs={{0,4},{4,0},{8,12},{12,8},{16,20},{20,16},{24,28},{28,24},{1,5},{5... | collective-permute-start | bytes 9830408 | tf_op jit(solution)/shard_map/ppermute | solution.py:890
  410.1 45.5 %collective-permute-start.28 = (bf16[768,1280]{1,0:T(8,128)(2,1)}, bf16[768,1280]{1,0:T(8,128)(2,1)S(1)}, u32[]{:S(2)}, u32[]{:S(2)}) collective-permute-start(bf16[768,1280]{1,0:T(8,128)(2,1)} %get-tuple-element.170), channel_id=1, source_target_pairs={{0,1},{1,0},{2,3},{3,2},{4,5},{5,4},{6,7},{7,6},{8,9},{9,8},{10,11... | collective-permute-start | bytes 5898248 | tf_op jit(solution)/shard_map/ppermute | solution.py:812
  428.1 49.5 %collective-permute-start.29 = (bf16[768,1280]{1,0:T(8,128)(2,1)}, bf16[768,1280]{1,0:T(8,128)(2,1)}, u32[]{:S(2)}, u32[]{:S(2)}) collective-permute-start(bf16[768,1280]{1,0:T(8,128)(2,1)} %get-tuple-element.175), channel_id=1, source_target_pairs={{0,2},{1,3},{2,0},{3,1},{4,6},{5,7},{6,4},{7,5},{8,10},{9,11},{10,... | collective-permute-start | bytes 5898248 | tf_op jit(solution)/shard_map/ppermute | solution.py:812
  477.5 5.7 %collective-permute-start.31 = (f32[4,320,128]{2,1,0:T(8,128)S(1)}, f32[4,320,128]{2,1,0:T(8,128)S(1)}, u32[]{:S(2)}, u32[]{:S(2)}) collective-permute-start(f32[4,320,128]{2,1,0:T(8,128)S(1)} %dynamic-slice_bitcast_fusion.3), channel_id=1, source_target_pairs={{0,4},{4,0},{8,12},{12,8},{16,20},{20,16},{24,28},{28,24},{1,5},{5... | collective-permute-start | bytes 1966088 | tf_op jit(solution)/shard_map/ppermute | solution.py:890
  483.3 36.4 %collective-permute-start.35 = (bf16[384,1280]{1,0:T(8,128)(2,1)}, bf16[384,1280]{1,0:T(8,128)(2,1)}, u32[]{:S(2)}, u32[]{:S(2)}) collective-permute-start(bf16[384,1280]{1,0:T(8,128)(2,1)} %add_convert_fusion.1), channel_id=1, source_target_pairs={{0,2},{1,3},{2,0},{3,1},{4,6},{5,7},{6,4},{7,5},{8,10},{9,11},{10,... | collective-permute-start | bytes 2949128 | tf_op jit(solution)/shard_map/ppermute | solution.py:812
  485.3 17.2 %collective-permute-start.33 = (f32[320,128]{0,1:T(8,128)S(1)}, f32[320,128]{0,1:T(8,128)S(1)}, u32[]{:S(2)}, u32[]{:S(2)}) collective-permute-start(f32[320,128]{0,1:T(8,128)S(1)} %copy.255), channel_id=1, source_target_pairs={{0,16},{4,20},{8,24},{12,28},{16,0},{20,4},{24,8},{28,12},{1,17},{... | collective-permute-start | bytes 491528 | tf_op jit(solution)/shard_map/ppermute | solution.py:890
  487.9 14.6 %collective-permute-start.34 = (f32[320,128]{0,1:T(8,128)S(1)}, f32[320,128]{0,1:T(8,128)S(1)}, u32[]{:S(2)}, u32[]{:S(2)}) collective-permute-start(f32[320,128]{0,1:T(8,128)S(1)} %copy.256), channel_id=1, source_target_pairs={{0,24},{4,28},{8,16},{12,20},{16,8},{20,12},{24,0},{28,4},{1,25},{... | collective-permute-start | bytes 491528 | tf_op jit(solution)/shard_map/ppermute | solution.py:890
  489.4 13.7 %collective-permute-start.32 = (f32[320,128]{0,1:T(8,128)S(1)}, f32[320,128]{0,1:T(8,128)}, u32[]{:S(2)}, u32[]{:S(2)}) collective-permute-start(f32[320,128]{0,1:T(8,128)S(1)} %copy.253), channel_id=1, source_target_pairs={{0,8},{4,12},{8,0},{12,4},{16,24},{20,28},{24,16},{28,20},{1,9},{5... | collective-permute-start | bytes 491528 | tf_op jit(solution)/shard_map/ppermute | solution.py:890
  493.1 32.0 %collective-permute-start.36 = (bf16[384,1280]{1,0:T(8,128)(2,1)}, bf16[384,1280]{1,0:T(8,128)(2,1)S(1)}, u32[]{:S(2)}, u32[]{:S(2)}) collective-permute-start(bf16[384,1280]{1,0:T(8,128)(2,1)} %add_convert_fusion), channel_id=1, source_target_pairs={{0,1},{1,0},{2,3},{3,2},{4,5},{5,4},{6,7},{7,6},{8,9},{9,8},{10,11... | collective-permute-start | bytes 2949128 | tf_op jit(solution)/shard_map/ppermute | solution.py:812
  520.0 20.9 %collective-permute-start.39 = (f32[320]{0:T(512)S(1)}, f32[320]{0:T(512)S(1)}, u32[]{:S(2)}, u32[]{:S(2)}) collective-permute-start(f32[320]{0:T(512)S(1)} %get-tuple-element.427), channel_id=1, source_target_pairs={{0,3},{1,2},{2,1},{3,0},{4,7},{5,6},{6,5},{7,4},{8,11},{9,10},{10,... | collective-permute-start | bytes 3848 | tf_op jit(solution)/shard_map/ppermute | solution.py:812
  521.7 19.1 %collective-permute-start.38 = (f32[320]{0:T(512)S(1)}, f32[320]{0:T(512)S(1)}, u32[]{:S(2)}, u32[]{:S(2)}) collective-permute-start(f32[320]{0:T(512)S(1)} %get-tuple-element.427), channel_id=1, source_target_pairs={{0,2},{1,3},{2,0},{3,1},{4,6},{5,7},{6,4},{7,5},{8,10},{9,11},{10,... | collective-permute-start | bytes 3848 | tf_op jit(solution)/shard_map/ppermute | solution.py:812
  523.0 17.8 %collective-permute-start.37 = (f32[320]{0:T(512)S(1)}, f32[320]{0:T(512)S(1)}, u32[]{:S(2)}, u32[]{:S(2)}) collective-permute-start(f32[320]{0:T(512)S(1)} %get-tuple-element.427), channel_id=1, source_target_pairs={{0,1},{1,0},{2,3},{3,2},{4,5},{5,4},{6,7},{7,6},{8,9},{9,8},{10,11... | collective-permute-start | bytes 3848 | tf_op jit(solution)/shard_map/ppermute | solution.py:812
  (97 other events, 727.8 us)
Sparse Core Ops, SparseCore 0:
  16.2 75.2 all-gather.4
  93.7 65.5 all-gather.8
  160.9 65.5 all-gather.6
  229.2 62.8 reduce-scatter.3
  309.3 61.8 reduce-scatter.5
  410.3 63.4 reduce-scatter.7

commit v5 on v4

--- a/solution.py
+++ b/solution.py
@@ -914,16 +914,15 @@
     )
 
 
-def chip_sum(value, index, size):
+def chip_sum(value, index, size, after):
     chip = index // 2
 
     def block(distance):
         return lax.dynamic_slice_in_dim(value, chip ^ distance, 1, 0)[0]
 
-    total = block(0).astype(F32)
-    for distance in range(1, size // 2):
-        total = total + fsdp_swap(block(distance), 2 * distance, size).astype(F32)
-    return total
+    pieces = [fsdp_swap(block(k), 2 * k, size) for k in range(1, size // 2)]
+    pieces, after = tied(pieces, after)
+    return sum(pieces, block(0)), after
 
 
 def pad_cols(value, width):
@@ -959,30 +958,42 @@
     filled = group_fill[0]
 
     small_values = jnp.concatenate(
-        [conv_inner.reshape(-1), conv_state.reshape(-1), mixer_gain], axis=0
-    )
-    small_count = small_values.shape[0]
+        [input_gain, conv_inner.reshape(-1), conv_state.reshape(-1), mixer_gain], axis=0
+    )
     inner_n, state_n = conv_inner.size, conv_state.size
+    small_count = inner_n + state_n + mixer_gain.size
     small_cols = -(-(small_count + 3 * heads) // shard)
-    small_block = jnp.pad(small_values, (0, small_cols * shard - small_count)).reshape(
-        shard, small_cols
-    )
     used = heads + state_cols
-    side = pad_cols(
-        jnp.concatenate([proj_step, proj_state, input_gain[:, None], small_block], axis=1), LANE
-    )
+    side = pad_cols(jnp.concatenate([proj_step, proj_state], axis=1), LANE)
     (inner_halves,) = tied(proj_inner.transpose(1, 0, 2))
     x_local = jnp.concatenate([inner_halves[1], side], axis=1)
     x_all = lax.all_gather(x_local, "fsdp", axis=0, tiled=True)
     gate_all = lax.all_gather(inner_halves[0], "fsdp", axis=0, tiled=True)
-    gain_all = lax.dynamic_update_slice(
-        jnp.zeros((fsdp_size, shard), BF16), input_gain[None], (fsdp_index, jnp.int32(0))
+    small_all = lax.dynamic_update_slice(
+        jnp.zeros((fsdp_size, small_values.size), BF16),
+        small_values[None],
+        (fsdp_index, jnp.int32(0)),
     )
     distance = 1
     while distance < fsdp_size:
-        gain_all = gain_all + fsdp_swap(gain_all, distance, fsdp_size)
+        small_all = small_all + fsdp_swap(small_all, distance, fsdp_size)
         distance *= 2
-    gain_f = gain_all.reshape(model).astype(F32)
+    gain_f = small_all[:, :shard].reshape(model).astype(F32)
+    extras = small_all[:, shard:]
+
+    def from_owners(flat, rows):
+        return flat.reshape(fsdp_size, rows, -1).transpose(1, 0, 2).reshape(rows, -1).astype(F32)
+
+    taps_inner = from_owners(extras[:, :inner_n], 5)
+    taps_state = from_owners(extras[:, inner_n : inner_n + state_n], 5)
+    mixer_f = from_owners(extras[:, inner_n + state_n : small_count], 1)[0]
+    taps8 = jnp.pad(taps_inner, ((0, 3), (0, 0)))
+    mixer8 = jnp.broadcast_to(mixer_f[None, :], (8, width))
+    spread = head_tables(heads)
+    tables = segment_tables(segment)
+    doc_masks = tables[0]
+    hp8 = head_columns(head_params)
+    skip8 = jnp.broadcast_to(jnp.repeat(head_params[2], LANE // 2)[None, :], (8, width))
     positions = tp_index * own_rows + jnp.arange(own_rows, dtype=jnp.int32)
     live_rows = (positions < filled)[:, None]
     block_f = block_in.astype(F32)
@@ -1006,24 +1017,18 @@
     started = put(blank, normed_of(block_in), 0)
 
     def near_done(one):
-        return tied(one, started, own_grad)
-
-    row_parts, started, own_grad = gather_parts(block_in, tp_size, near_done)
+        return tied(one, started, own_grad, taps8, taps_state, mixer8, hp8, skip8, *tables[1:])
+
+    row_parts, started, own_grad, taps8, taps_state, mixer8, hp8, skip8, *late = gather_parts(
+        block_in, tp_size, near_done
+    )
+    tables = (doc_masks, *late)
     row_parts = [by_rows(part) for part in row_parts]
     own_grad, *row_parts = tied(own_grad, *row_parts)
     near = min(3, tp_size)
     grad_parts = [by_rows(own_grad)] + [swap(own_grad, k, tp_size) for k in range(1, near)]
 
     side_all = x_all[:, width:]
-    extras = side_all[:, used + 1 : used + 1 + small_cols].reshape(fsdp_size, shard * small_cols)
-
-    def from_owners(flat, rows):
-        return flat.reshape(fsdp_size, rows, -1).transpose(1, 0, 2).reshape(rows, -1).astype(F32)
-
-    taps_inner = from_owners(extras[:, :inner_n], 5)
-    taps_state = from_owners(extras[:, inner_n : inner_n + state_n], 5)
-    mixer_f = from_owners(extras[:, inner_n + state_n : small_count], 1)[0]
-
     normed = started
     for distance in range(1, tp_size - 1):
         normed = put(normed, normed_of(row_parts[distance]), distance)
@@ -1033,8 +1038,6 @@
         side_all, normed, (((0,), (1,)), ((), ())), preferred_element_type=F32
     )
     raw = inner_product(normed, x_all, width)
-    tables = segment_tables(segment)
-    doc_masks = tables[0]
     state_vals, state_back = jax.vjp(
         lambda raw_cols, conv_taps: state_act(raw_cols, conv_taps, doc_masks),
         small[heads:used],
@@ -1048,10 +1051,6 @@
     own_grad, bc, out_local = tied(own_grad, bc, proj_output.T)
     out_all = lax.all_gather(out_local, "fsdp", axis=0, tiled=True)
     grad_parts += [swap(own_grad, k, tp_size) for k in range(near, tp_size)]
-    spread = head_tables(heads)
-    taps8 = jnp.pad(taps_inner, ((0, 3), (0, 0)))
-    hp8 = head_columns(head_params)
-    skip8 = jnp.broadcast_to(jnp.repeat(head_params[2], LANE // 2)[None, :], (8, width))
     mixed, states = ssd_forward(raw, small, bc, tables, taps8, hp8, skip8, spread, heads)
 
     z_raw, gated, square_sum = gate_product(normed, gate_all, mixed)
@@ -1062,7 +1061,7 @@
         group_grad = put(group_grad, grad_parts[distance], distance)
     group_grad = by_rows(group_grad)
     inv_gate = lax.rsqrt(square_sum / DI + NORM_EPS)[:, None]
-    normed_gated = (gated * inv_gate * mixer_f[None, :]).astype(BF16)
+    normed_gated = (gated * inv_gate * mixer8[0:1]).astype(BF16)
     sum_out = pair_sum(
         contract_rows(group_grad, normed_gated).astype(BF16), fsdp_index, fsdp_size
     )
@@ -1074,7 +1073,6 @@
     mixed_sent, mixed_kept = scatter_start(mixed_left, mixed_right, own_rows, tp_index, tp_size)
 
     inner_mean = inner_sum[:, None] / DI
-    mixer8 = jnp.broadcast_to(mixer_f[None, :], (8, width))
     d_mixed, d_z, grad_mixer = gate_gradient(
         group_grad, out_all, z_raw, mixed, mixer8, inv_gate, inner_mean
     )
@@ -1109,7 +1107,7 @@
         normed, d_side.astype(BF16), (((0,), (1,)), ((), ())), preferred_element_type=F32
     )
 
-    def side_gradient(side_part, d_taps, d_skip, d_heads, grad_conv_state, gain_sums):
+    def side_gradient(side_part, d_taps, d_skip, d_heads, grad_conv_state, gain_sums, after):
         grad_head = jnp.stack(
             [
                 d_heads[:heads, 0],
@@ -1138,7 +1136,7 @@
             grad_extras, ((0, 0), (used, LANE - used - 1 - small_cols))
         )
         side_part = pair_sum(side_part, fsdp_index, fsdp_size)
-        return chip_sum(side_part, fsdp_index, fsdp_size)
+        return chip_sum(side_part, fsdp_index, fsdp_size, after)
 
     def d_normed_of(distances, which):
         return d_normed_blocks(
@@ -1154,6 +1152,8 @@
         )
         sent = [swap(left_away, 1, 4), swap(right_away, 2, 4)]
         left_kept, gains_three = d_normed_of([2, 0], 0)
+        mixed_rows = scatter_end(mixed_kept, mixed_last)
+        block_out = (block_f + jnp.where(live_rows, mixed_rows, 0.0)).astype(BF16)
         sent[0], d_side_late, side_part, grad_out = tied(sent[0], d_side, side_part, grad_out)
         right_kept, gains_four = d_normed_blocks(
             d_z, d_x, d_side_late, gate_all, x_all, normed, tp_index ^ jnp.array([1, 0]), 1, own_rows
@@ -1164,6 +1164,8 @@
         ]
         gain_sums = jnp.concatenate([gains_one + gains_three, gains_two + gains_four], axis=1)[0]
     else:
+        mixed_rows = scatter_end(mixed_kept, mixed_last)
+        block_out = (block_f + jnp.where(live_rows, mixed_rows, 0.0)).astype(BF16)
         left, gains_one = d_normed_of(list(range(tp_size)), 0)
         right, gains_two = d_normed_of(list(range(tp_size)), 1)
         sent = [
@@ -1177,12 +1179,20 @@
         gain_sums = jnp.concatenate([gains_one, gains_two], axis=1)[0]
     grad_x = chip_scatter(sum_x, fsdp_size)
     passed, kept = scatter_middle(sent, kept, own_rows, tp_size)
-    passed, mixed_last = tied(passed, mixed_last)
-    mixed_rows = scatter_end(mixed_kept, mixed_last)
-    block_out = (block_f + jnp.where(live_rows, mixed_rows, 0.0)).astype(BF16)
     grad_x, passed = tied(grad_x, passed)
     last = scatter_last(passed, tp_size)
-    grad_side = side_gradient(side_part, d_taps, d_skip, d_heads, grad_conv_state, gain_sums)
+    pair = adam_pair(
+        lambda w, g, m, v: adamw_step(w, g, m, v, WEIGHT_DECAY, LEARN_RATE),
+        grad_gate,
+        grad_x,
+        proj_inner,
+        moments[1],
+        moments[10],
+    )
+    kept, last = tied(kept, last)
+    grad_side, pair = side_gradient(
+        side_part, d_taps, d_skip, d_heads, grad_conv_state, gain_sums, pair
+    )
     grad_side, last[0] = tied(grad_side, last[0])
     grad_input_gain = all_sum(grad_side[:, used], tp_index, tp_size) / input_gain.astype(F32)
     d_normed = scatter_end(kept, last)
@@ -1222,14 +1232,7 @@
         decay = WEIGHT_DECAY if at in large else 0.0
         rate = LEARN_RATE if at in large else LEARN_SMALL
         if at == 1:
-            grads[1], *updated[1] = adam_pair(
-                lambda w, g, m, v: adamw_step(w, g, m, v, WEIGHT_DECAY, LEARN_RATE),
-                grad_gate,
-                grad_x,
-                proj_inner,
-                moments[1],
-                moments[10],
-            )
+            grads[1], *updated[1] = pair
         else:
             updated[at] = adamw_step(
                 weights[at], grads[at], moments[at], moments[9 + at], decay, rate

time: 555 us -> 541 us (0.975)
  local copies, waits for them, and re-layouts: 67 us -> 58.1 us
    unnamed x203 -> x213, local copies, waits for them, and re-layouts: 12 us -> 13.7 us
  transfers between devices with their start and end apart: 46 -> 46, of which waited for: 14 -> 15; matrix products, arithmetic and copies ran while one was open for 33% -> 31% of each run, Pallas kernels for 38% -> 39%
where the time goes in v5:
time: 541 us; the launch traced here: 536 us
  Pallas kernels  211 us (39%)
  other arithmetic  81.3 us (15%)
  waiting for transfers between devices  65.7 us (12%)
  local copies, waits for them, and re-layouts  58.1 us (11%)
  matrix products  53.8 us (10%)
  starting transfers between devices  48.3 us (9%)
  between operations  17 us (3%)
    pallas_call x4, Pallas kernels, row_call(): pl.pallas_call(kernel, grid=(length // rows,), out_shape=tuple((jax.Shape...  73.3 us
    pallas_call x1, Pallas kernels, ssd_backward(): pl.pallas_call(functools.partial(ssd_bwd_kernel, heads), grid=(chunks,),...  53.4 us
    ppermute x30, waiting for transfers between devices, swap(): lax.ppermute(value, 'tp', [(at, at ^ distance) for at in range(size)])  50.6 us
    pallas_call x4, Pallas kernels, d_normed_blocks(): pl.pallas_call(functools.partial(dn_kernel, count, rows), grid_spec=pltpu...  48 us
    dot_general x3, matrix products, contract_rows(): lax.dot_general(left_mat, right_mat, (((0,), (0,)), ((), ())), preferred_...  40.9 us
    ppermute x30, starting transfers between devices, swap(): lax.ppermute(value, 'tp', [(at, at ^ distance) for at in range(size)])  38.5 us
    pallas_call x1, Pallas kernels, ssd_forward(): pl.pallas_call(functools.partial(ssd_fwd_kernel, heads), grid=(chunks,),...  21.3 us
    pallas_call x1, Pallas kernels, adam_pair(): pl.pallas_call(functools.partial(adam_kernel, step), grid=(shard // rows,...  15.5 us
  transfers between devices with their start and end apart: 46, of which 15 were waited for; matrix products, arithmetic and copies ran while one was open for 31% of the time, Pallas kernels for 39%

profile of v5, /device:TPU:0, one launch (start us, length us, event | category | flops | bytes accessed | tf_op | source)
XLA Modules:
  0.0 535.6 jit_solution(9553486144462482171)
XLA Ops:
  12.9 3.0 collective-permute-start.4
  28.2 2.1 collective-permute-done.2
  30.3 2.9 collective-permute-start.3
  34.0 3.6 collective-permute-done.3
  39.1 3.7 broadcast.296.clone
  44.6 14.2 %collective-permute-done.4 = bf16[384,2560]{1,0:T(8,128)(2,1)} collective-permute-done((bf16[384,2560]{1,0:T(8,128)(2,1)S(1)}, bf16[384,2560]{1,0:T(8,128)(2,1)}, u32[]{:S(2)}, u32[]{:S(2)}) %collective-permute-start.4) | collective-permute-done | bytes 1966112 | tf_op jit(solution)/shard_map/ppermute | solution.py:812
  68.9 14.2 %collective-permute-done.5 = bf16[192,2560]{1,0:T(8,128)(2,1)S(1)} collective-permute-done((bf16[192,2560]{1,0:T(8,128)(2,1)S(1)}, bf16[192,2560]{1,0:T(8,128)(2,1)S(1)}, u32[]{:S(2)}, u32[]{:S(2)}) %collective-permute-start.5) | collective-permute-done | bytes 983072 | tf_op jit(solution)/shard_map/ppermute | solution.py:812
  83.1 4.4 collective-permute-done.6
  89.8 3.0 fusion.8
  92.8 3.3 fusion.26
  96.1 3.5 fusion.25
  101.9 6.3 %fusion.33.small_ref = f32[128,1536]{1,0:T(8,128)S(1)} fusion(bf16[1536,2560]{1,0:T(8,128)(2,1)} %fusion.24.left_ref.refs_6_.refs_7_, bf16[2560,1408]{1,0:T(8,128)(2,1)} %all-gather.5.cloned.1.call-done.right_ref.refs_9_), kind=kOutput, calls=%fused_computation.82 | convolution fusion | flops 1006632960 | bytes 9306112 | tf_op jit(solution)/shard_map/dot_general | solution.py:1037
  113.8 15.7 %inner_product.1.raw_ref.halo_ref = f32[1536,1280]{1,0:T(8,128)} custom-call(bf16[1536,2560]{1,0:T(8,128)(2,1)} %fusion.24.left_ref.refs_6_.refs_7_, bf16[2560,1408]{1,0:T(8,128)(2,1)} %all-gather.5.cloned.1.call-done.right_ref.refs_9_), custom_call_target="tpu_custom_call" | custom-call | flops 15399999488 | bytes 47600000 | tf_op jit(solution)/shard_map/inner_product/pallas_call | solution.py:675
  129.5 8.3 %collective-permute-done.7 = bf16[64,1536]{1,0:T(8,128)(2,1)S(1)} collective-permute-done((bf16[64,1536]{1,0:T(8,128)(2,1)S(1)}, bf16[64,1536]{1,0:T(8,128)(2,1)S(1)}, u32[]{:S(2)}, u32[]{:S(2)}) %collective-permute-start.7) | collective-permute-done | bytes 196640 | tf_op jit(solution)/shard_map/ppermute | solution.py:812
  141.8 21.3 %ssd_fwd.1 = (f32[1536,1280]{1,0:T(8,128)}, f32[6,128,1280]{2,1,0:T(8,128)}) custom-call(f32[1536,1280]{1,0:T(8,128)} %inner_product.1.raw_ref.halo_ref, f32[128,1536]{1,0:T(8,128)} %copy-done.16, bf16[256,1536]{1,0:T(8,128)(2,1)} %copy-done.28, f32[1536,384]{1,0:T(8,128)} %pad_maximum_fusion.masks_ref.masks_next_ref, ...), custom_call_target="tpu_custom_call" | custom-call | flops 40699998208 | bytes 125800000 | tf_op jit(solution)/shard_map/ssd_fwd/pallas_call | solution.py:388
  163.1 19.4 %gate_product.1 = (f32[1536,1280]{1,0:T(8,128)}, f32[1536,1280]{1,0:T(8,128)}, f32[8,1536]{1,0:T(8,128)}) custom-call(bf16[1536,2560]{1,0:T(8,128)(2,1)} %fusion.24.left_ref.refs_6_.refs_7_, bf16[2560,1280]{1,0:T(8,128)(2,1)} %bitcast.103, f32[1536,1280]{1,0:T(8,128)} %get-tuple-element.159.mixed_ref.y_ref), custom_call_target="tpu_custom_call" | custom-call | flops 17600000000 | bytes 54400000 | tf_op jit(solution)/shard_map/gate_product/pallas_call | solution.py:675
  194.1 2.2 copy-done.4
  196.3 11.0 %convolution_convert_fusion.2 = bf16[2560,1280]{1,0:T(8,128)(2,1)S(1)} fusion(bf16[1536,2560]{1,0:T(8,128)(2,1)S(1)} %constant_dynamic-update-slice_fusion.grad_ref.left_ref, bf16[1536,1280]{1,0:T(8,128)(2,1)S(1)} %multiply_convert_fusion.left_ref), kind=kOutput, calls=%fused_computation.2 | convolution fusion | flops 10069606400 | bytes 18350080 | tf_op jit(solution)/shard_map/dot_general | solution.py:794
  212.2 4.9 collective-permute-done.16
  217.1 4.4 fusion.2
  221.5 2.5 all-gather.7.cloned.1.call-done.right_ref
  224.0 16.9 %output_product.1 = (bf16[1536,1280]{1,0:T(8,128)(2,1)}, bf16[1536,1280]{1,0:T(8,128)(2,1)}, f32[8,1536]{1,0:T(8,128)}) custom-call(bf16[1536,1280]{1,0:T(8,128)(2,1)} %copy-done.12, bf16[2560,1280]{1,0:T(8,128)(2,1)} %all-gather.7.cloned.1.call-done.right_ref, bf16[1536,2560]{1,0:T(8,128)(2,1)} %copy-done.4), custom_call_target="tpu_custom_call" | custom-call | flops 17600000000 | bytes 54400000 | tf_op jit(solution)/shard_map/output_product/pallas_call | solution.py:675
  241.8 2.4 collective-permute-start.19
  254.1 21.3 %gate_gradient.1 = (f32[1536,1280]{1,0:T(8,128)}, bf16[1536,1280]{1,0:T(8,128)(2,1)}, f32[8,1280]{1,0:T(8,128)}) custom-call(bf16[1536,2560]{1,0:T(8,128)(2,1)} %copy-done.4, bf16[2560,1280]{1,0:T(8,128)(2,1)} %all-gather.7.cloned.1.call-done.right_ref, f32[1536,1280]{1,0:T(8,128)} %get-tuple-element.172.z_ref, ...), custom_call_target="tpu_custom_call" | custom-call | flops 19800000512 | bytes 61200000 | tf_op jit(solution)/shard_map/gate_gradient/pallas_call | solution.py:675
  275.4 14.0 %convolution_convert_fusion.1 = bf16[2560,1280]{1,0:T(8,128)(2,1)S(1)} fusion(bf16[1536,2560]{1,0:T(8,128)(2,1)} %fusion.24.left_ref.refs_6_.refs_7_, bf16[1536,1280]{1,0:T(8,128)(2,1)} %get-tuple-element.174.refs_0_.refs_1_), kind=kOutput, calls=%fused_computation.1 | convolution fusion | flops 10069606400 | bytes 18350080 | tf_op jit(solution)/shard_map/dot_general | solution.py:794
  289.4 3.5 collective-permute-done.21
  292.9 2.6 collective-permute-done.20
  297.2 2.4 add_convert_fusion.3
  301.6 2.6 fusion.1
  307.4 53.4 %ssd_bwd.1 = (bf16[1536,1280]{1,0:T(8,128)(2,1)}, f32[32,1536]{1,0:T(8,128)}, f32[256,1536]{1,0:T(8,128)}, f32[8,1280]{1,0:T(8,128)}, f32[32,128]{1,0:T(8,128)}, /*index=5*/f32[8,1280]{1,0:T(8,128)}) custom-call(f32[1536,1280]{1,0:T(8,128)} %inner_product.1.raw_ref.halo_ref, f32[1536,1280]{1,0:T(8,128)} %inner_product.1.raw_ref.halo_ref, ...), custom_call_target="tpu_custom_call" | custom-call | flops 75900002304 | bytes 234600000 | tf_op jit(solution)/shard_map/ssd_bwd/pallas_call | solution.py:438
  365.9 15.9 %convolution_convert_fusion = bf16[2560,1280]{1,0:T(8,128)(2,1)} fusion(bf16[1536,2560]{1,0:T(8,128)(2,1)} %fusion.24.left_ref.refs_6_.refs_7_, bf16[1536,1280]{1,0:T(8,128)(2,1)} %get-tuple-element.184.refs_2_.refs_3_), kind=kOutput, calls=%fused_computation | convolution fusion | flops 10069606400 | bytes 18350080 | tf_op jit(solution)/shard_map/dot_general | solution.py:794
  383.4 4.0 dynamic-slice_bitcast_fusion
  391.0 12.2 %d_normed.6 = (bf16[768,1280]{1,0:T(8,128)(2,1)}, f32[8,1280]{1,0:T(8,128)}) custom-call(s32[2]{0:T(128)} %get-tuple-element.474.at_ref, bf16[1536,1280]{1,0:T(8,128)(2,1)} %get-tuple-element.174.refs_0_.refs_1_, bf16[1536,1280]{1,0:T(8,128)(2,1)} %get-tuple-element.174.refs_0_.refs_1_, bf16[1536,1280]{1,0:T(8,128)(2,1)} %get-tuple-element.184.refs_2_.refs_3_, ...), custom_call_target="tpu_custom_call" | custom-call | flops 110000000 | bytes 340000 | tf_op jit(solution)/shard_map/d_normed/pallas_call | solution.py:556
  403.3 4.4 fusion
  410.3 12.3 %d_normed.4 = (bf16[768,1280]{1,0:T(8,128)(2,1)}, f32[8,1280]{1,0:T(8,128)}) custom-call(s32[2]{0:T(128)} %get-tuple-element.476.at_ref, bf16[1536,1280]{1,0:T(8,128)(2,1)} %get-tuple-element.174.refs_0_.refs_1_, bf16[1536,1280]{1,0:T(8,128)(2,1)} %get-tuple-element.174.refs_0_.refs_1_, bf16[1536,1280]{1,0:T(8,128)(2,1)} %get-tuple-element.184.refs_2_.refs_3_, ...), custom_call_target="tpu_custom_call" | custom-call | flops 110000000 | bytes 340000 | tf_op jit(solution)/shard_map/d_normed/pallas_call | solution.py:556
  425.1 6.7 %fusion.44 = f32[2560,128]{1,0:T(8,128)} fusion(bf16[1536,2560]{1,0:T(8,128)(2,1)} %fusion.24.left_ref.refs_6_.refs_7_, f32[64,1536]{1,0:T(8,128)S(1)} %copy-done.26, f32[20,1536]{1,0:T(8,128)S(1)} %slice.235), kind=kOutput, calls=%fused_computation.104 | convolution fusion | flops 1008009216 | bytes 9691136 | tf_op jit(solution)/shard_map/dot_general | solution.py:1106
  431.8 3.3 convert_add_fusion.7
  435.1 3.1 convert_add_fusion.8
  439.2 11.7 %d_normed.5 = (bf16[768,1280]{1,0:T(8,128)(2,1)}, f32[8,1280]{1,0:T(8,128)}) custom-call(s32[2]{0:T(128)} %get-tuple-element.475.at_ref, bf16[1536,1280]{1,0:T(8,128)(2,1)} %get-tuple-element.174.refs_0_.refs_1_, bf16[1536,1280]{1,0:T(8,128)(2,1)} %get-tuple-element.174.refs_0_.refs_1_, bf16[1536,1280]{1,0:T(8,128)(2,1)} %get-tuple-element.184.refs_2_.refs_3_, ...), custom_call_target="tpu_custom_call" | custom-call | flops 110000000 | bytes 340000 | tf_op jit(solution)/shard_map/d_normed/pallas_call | solution.py:556
  450.8 2.2 slice.237
  455.2 11.8 %d_normed.7 = (bf16[768,1280]{1,0:T(8,128)(2,1)}, f32[8,1280]{1,0:T(8,128)}) custom-call(s32[2]{0:T(128)} %get-tuple-element.473.at_ref, bf16[1536,1280]{1,0:T(8,128)(2,1)} %get-tuple-element.174.refs_0_.refs_1_, bf16[1536,1280]{1,0:T(8,128)(2,1)} %get-tuple-element.174.refs_0_.refs_1_, bf16[1536,1280]{1,0:T(8,128)(2,1)} %get-tuple-element.184.refs_2_.refs_3_, ...), custom_call_target="tpu_custom_call" | custom-call | flops 110000000 | bytes 340000 | tf_op jit(solution)/shard_map/d_normed/pallas_call | solution.py:556
  468.3 2.2 fusion.31
  472.2 2.4 add_convert_fusion
  477.7 3.3 collective-permute-start.36
  483.0 5.1 fusion.29
  489.5 15.5 %adam_pair.1 = (f32[320,2,1280]{2,1,0:T(2,128)}, bf16[320,2,1280]{2,1,0:T(2,128)(2,1)}, f32[320,2,1280]{2,1,0:T(2,128)}, f32[320,2,1280]{2,1,0:T(2,128)}) custom-call(bf16[320,1280]{1,0:T(8,128)(2,1)} %reduce-scatter.6.cloned.1.call-done.gate_ref, bf16[320,1280]{1,0:T(8,128)(2,1)} %reduce-scatter.8.cloned.1.call-done.inner_ref, ...), custom_call_target="tpu_custom_call" | custom-call | flops 1000 | bytes 1000 | tf_op jit(solution)/shard_map/adam_pair/pallas_call | solution.py:611
  511.8 2.4 convert_add_fusion.6
  518.9 6.0 %fusion.7 = (bf16[384,2560]{1,0:T(8,128)(2,1)}, bf16[384,2560]{1,0:T(8,128)(2,1)}) fusion(bf16[384,2560]{1,0:T(8,128)(2,1)} %param.36, bf16[384,2560]{1,0:T(8,128)(2,1)S(1)} %copy-done.1, f32[384,1280]{1,0:T(8,128)} %copy-done.2, f32[384,1280]{1,0:T(8,128)} %copy-done.3, f32[384]{0:T(512)S(1)} %broadcast_multiply_fusion, f32[2560]{0:T(1024)S(1)} %copy-done.30, ...), kind=kLoop, calls=%fused_computation.25 | loop fusion | flops 13762560 | bytes 15742336 | tf_op jit(solution)/shard_map/convert_element_type | solution.py:1203
  (475 shorter events, 121.2 us)
Async XLA Ops:
  7.2 94.7 %all-gather.5.cloned.1.call-start = ((), (), s32[]{:S(2)}) async-start(), calls=%async_computation.3 | async-start | bytes 8110080 | tf_op jit(solution)/shard_map/all_gather | solution.py:970
  12.8 150.3 %all-gather.9.cloned.1.call-start = ((), (), s32[]{:S(2)}) async-start(), calls=%async_computation.8 | async-start | bytes 7372800 | tf_op jit(solution)/shard_map/all_gather | solution.py:971
  12.9 46.0 %collective-permute-start.4 = (bf16[384,2560]{1,0:T(8,128)(2,1)S(1)}, bf16[384,2560]{1,0:T(8,128)(2,1)}, u32[]{:S(2)}, u32[]{:S(2)}) collective-permute-start(bf16[384,2560]{1,0:T(8,128)(2,1)S(1)} %copy-done), channel_id=1, source_target_pairs={{0,2},{1,3},{2,0},{3,1},{4,6},{5,7},{6,4},{7,5},{8,10},{9,11},{10,... | collective-permute-start | bytes 5898248 | tf_op jit(solution)/shard_map/ppermute | solution.py:812
  15.9 46.0 %collective-permute-start = (bf16[384,2560]{1,0:T(8,128)(2,1)S(1)}, bf16[384,2560]{1,0:T(8,128)(2,1)}, u32[]{:S(2)}, u32[]{:S(2)}) collective-permute-start(bf16[384,2560]{1,0:T(8,128)(2,1)S(1)} %copy-done), channel_id=1, source_target_pairs={{0,1},{1,0},{2,3},{3,2},{4,5},{5,4},{6,7},{7,6},{8,9},{9,8},{10,11... | collective-permute-start | bytes 5898248 | tf_op jit(solution)/shard_map/ppermute | solution.py:812
  17.8 7.8 %collective-permute-start.1 = (bf16[8,1320]{1,0:T(8,128)(2,1)S(1)}, bf16[8,1320]{1,0:T(8,128)(2,1)S(1)}, u32[]{:S(2)}, u32[]{:S(2)}) collective-permute-start(bf16[8,1320]{1,0:T(8,128)(2,1)S(1)} %dynamic_update_slice.53), channel_id=1, source_target_pairs={{0,4},{4,0},{8,12},{12,8},{16,20},{20,16},{24,28},{28,24},{1,5},{5... | collective-permute-start | bytes 63368 | tf_op jit(solution)/shard_map/ppermute | solution.py:890
  17.9 206.1 %all-gather.7.cloned.1.call-start = ((), (), s32[]{:S(2)}) async-start(), calls=%async_computation.4 | async-start | bytes 7372800 | tf_op jit(solution)/shard_map/all_gather | solution.py:1052
  19.9 88.4 %copy-start.36 = (f32[1536]{0:T(1024)}, f32[1536]{0:T(1024)S(1)}, u32[]{:S(2)}) copy-start(f32[1536]{0:T(1024)S(1)} %get-tuple-element.459) | copy-start | bytes 18436
  19.9 88.4 %copy-start.38 = (f32[1536]{0:T(1024)}, f32[1536]{0:T(1024)S(1)}, u32[]{:S(2)}) copy-start(f32[1536]{0:T(1024)S(1)} %get-tuple-element.460) | copy-start | bytes 18436
  25.9 4.4 collective-permute-start.2
  30.3 7.4 %collective-permute-start.3 = (bf16[8,1320]{1,0:T(8,128)(2,1)S(1)}, bf16[8,1320]{1,0:T(8,128)(2,1)S(1)}, u32[]{:S(2)}, u32[]{:S(2)}) collective-permute-start(bf16[8,1320]{1,0:T(8,128)(2,1)S(1)} %add.471), channel_id=1, source_target_pairs={{0,16},{4,20},{8,24},{12,28},{16,0},{20,4},{24,8},{28,12},{1,17},{... | collective-permute-start | bytes 63368 | tf_op jit(solution)/shard_map/ppermute | solution.py:890
  60.1 23.0 %collective-permute-start.5 = (bf16[192,2560]{1,0:T(8,128)(2,1)S(1)}, bf16[192,2560]{1,0:T(8,128)(2,1)S(1)}, u32[]{:S(2)}, u32[]{:S(2)}) collective-permute-start(bf16[192,2560]{1,0:T(8,128)(2,1)S(1)} %slice.266), channel_id=1, source_target_pairs={{0,1},{1,0},{2,3},{3,2},{4,5},{5,4},{6,7},{7,6},{8,9},{9,8},{10,11... | collective-permute-start | bytes 2949128 | tf_op jit(solution)/shard_map/ppermute | solution.py:812
  65.1 22.4 %collective-permute-start.6 = (bf16[192,2560]{1,0:T(8,128)(2,1)S(1)}, bf16[192,2560]{1,0:T(8,128)(2,1)S(1)}, u32[]{:S(2)}, u32[]{:S(2)}) collective-permute-start(bf16[192,2560]{1,0:T(8,128)(2,1)S(1)} %slice.216), channel_id=1, source_target_pairs={{0,2},{1,3},{2,0},{3,1},{4,6},{5,7},{6,4},{7,5},{8,10},{9,11},{10,... | collective-permute-start | bytes 2949128 | tf_op jit(solution)/shard_map/ppermute | solution.py:812
  87.6 95.7 %collective-permute-start.11 = (bf16[384,2560]{1,0:T(8,128)(2,1)S(1)}, bf16[384,2560]{1,0:T(8,128)(2,1)}, u32[]{:S(2)}, u32[]{:S(2)}) collective-permute-start(bf16[384,2560]{1,0:T(8,128)(2,1)S(1)} %copy-done.6), channel_id=1, source_target_pairs={{0,2},{1,3},{2,0},{3,1},{4,6},{5,7},{6,4},{7,5},{8,10},{9,11},{10,... | collective-permute-start | bytes 5898248 | tf_op jit(solution)/shard_map/ppermute | solution.py:812
  89.2 94.1 %collective-permute-start.10 = (bf16[384,2560]{1,0:T(8,128)(2,1)S(1)}, bf16[384,2560]{1,0:T(8,128)(2,1)}, u32[]{:S(2)}, u32[]{:S(2)}) collective-permute-start(bf16[384,2560]{1,0:T(8,128)(2,1)S(1)} %copy-done.6), channel_id=1, source_target_pairs={{0,1},{1,0},{2,3},{3,2},{4,5},{5,4},{6,7},{7,6},{8,9},{9,8},{10,11... | collective-permute-start | bytes 5898248 | tf_op jit(solution)/shard_map/ppermute | solution.py:812
  110.3 27.5 %collective-permute-start.8 = (bf16[64,1536]{1,0:T(8,128)(2,1)S(1)}, bf16[64,1536]{1,0:T(8,128)(2,1)S(1)}, u32[]{:S(2)}, u32[]{:S(2)}) collective-permute-start(bf16[64,1536]{1,0:T(8,128)(2,1)S(1)} %get-tuple-element.435), channel_id=1, source_target_pairs={{0,2},{1,3},{2,0},{3,1},{4,6},{5,7},{6,4},{7,5},{8,10},{9,11},{10,... | collective-permute-start | bytes 589832 | tf_op jit(solution)/shard_map/ppermute | solution.py:812
  110.8 27.0 %collective-permute-start.7 = (bf16[64,1536]{1,0:T(8,128)(2,1)S(1)}, bf16[64,1536]{1,0:T(8,128)(2,1)S(1)}, u32[]{:S(2)}, u32[]{:S(2)}) collective-permute-start(bf16[64,1536]{1,0:T(8,128)(2,1)S(1)} %get-tuple-element.435), channel_id=1, source_target_pairs={{0,1},{1,0},{2,3},{3,2},{4,5},{5,4},{6,7},{7,6},{8,9},{9,8},{10,11... | collective-permute-start | bytes 589832 | tf_op jit(solution)/shard_map/ppermute | solution.py:812
  112.2 27.7 %collective-permute-start.9 = (bf16[64,1536]{1,0:T(8,128)(2,1)S(1)}, bf16[64,1536]{1,0:T(8,128)(2,1)S(1)}, u32[]{:S(2)}, u32[]{:S(2)}) collective-permute-start(bf16[64,1536]{1,0:T(8,128)(2,1)S(1)} %get-tuple-element.435), channel_id=1, source_target_pairs={{0,3},{1,2},{2,1},{3,0},{4,7},{5,6},{6,5},{7,4},{8,11},{9,10},{10,... | collective-permute-start | bytes 589832 | tf_op jit(solution)/shard_map/ppermute | solution.py:812
  139.9 43.4 %collective-permute-start.12 = (bf16[384,2560]{1,0:T(8,128)(2,1)S(1)}, bf16[384,2560]{1,0:T(8,128)(2,1)}, u32[]{:S(2)}, u32[]{:S(2)}) collective-permute-start(bf16[384,2560]{1,0:T(8,128)(2,1)S(1)} %copy-done.6), channel_id=1, source_target_pairs={{0,3},{1,2},{2,1},{3,0},{4,7},{5,6},{6,5},{7,4},{8,11},{9,10},{10,... | collective-permute-start | bytes 5898248 | tf_op jit(solution)/shard_map/ppermute | solution.py:812
  141.5 162.7 %reduce-scatter.4.cloned.1.call-start = ((), (), s32[]{:S(2)}) async-start(), calls=%async_computation.5 | async-start | bytes 4096000 | tf_op jit(solution)/shard_map/reduce_scatter | solution.py:912
  183.3 10.0 %collective-permute-start.15 = (f32[1536]{0:T(1024)S(1)}, f32[1536]{0:T(1024)S(1)}, u32[]{:S(2)}, u32[]{:S(2)}) collective-permute-start(f32[1536]{0:T(1024)S(1)} %slice_reduce_fusion.2), channel_id=1, source_target_pairs={{0,3},{1,2},{2,1},{3,0},{4,7},{5,6},{6,5},{7,4},{8,11},{9,10},{10,... | collective-permute-start | bytes 18440 | tf_op jit(solution)/shard_map/ppermute | solution.py:812
  184.4 8.9 %collective-permute-start.14 = (f32[1536]{0:T(1024)S(1)}, f32[1536]{0:T(1024)S(1)}, u32[]{:S(2)}, u32[]{:S(2)}) collective-permute-start(f32[1536]{0:T(1024)S(1)} %slice_reduce_fusion.2), channel_id=1, source_target_pairs={{0,2},{1,3},{2,0},{3,1},{4,6},{5,7},{6,4},{7,5},{8,10},{9,11},{10,... | collective-permute-start | bytes 18440 | tf_op jit(solution)/shard_map/ppermute | solution.py:812
  186.4 6.9 %collective-permute-start.13 = (f32[1536]{0:T(1024)S(1)}, f32[1536]{0:T(1024)S(1)}, u32[]{:S(2)}, u32[]{:S(2)}) collective-permute-start(f32[1536]{0:T(1024)S(1)} %slice_reduce_fusion.2), channel_id=1, source_target_pairs={{0,1},{1,0},{2,3},{3,2},{4,5},{5,4},{6,7},{7,6},{8,9},{9,8},{10,11... | collective-permute-start | bytes 18440 | tf_op jit(solution)/shard_map/ppermute | solution.py:812
  211.0 6.1 %collective-permute-start.16 = (bf16[4,320,1280]{2,1,0:T(8,128)(2,1)}, bf16[4,320,1280]{2,1,0:T(8,128)(2,1)S(1)}, u32[]{:S(2)}, u32[]{:S(2)}) collective-permute-start(bf16[4,320,1280]{2,1,0:T(8,128)(2,1)} %dynamic-slice_bitcast_fusion.2), channel_id=1, source_target_pairs={{0,4},{4,0},{8,12},{12,8},{16,20},{20,16},{24,28},{28,24},{1,5},{5... | collective-permute-start | bytes 9830408 | tf_op jit(solution)/shard_map/ppermute | solution.py:890
  221.5 161.8 %reduce-scatter.6.cloned.1.call-start = ((), (), s32[]{:S(2)}) async-start(), calls=%async_computation.6 | async-start | bytes 4096000 | tf_op jit(solution)/shard_map/reduce_scatter | solution.py:912
  241.8 11.1 %collective-permute-start.19 = (f32[1536]{0:T(1024)S(1)}, f32[1536]{0:T(1024)S(1)}, u32[]{:S(2)}, u32[]{:S(2)}) collective-permute-start(f32[1536]{0:T(1024)S(1)} %slice_reduce_fusion.1), channel_id=1, source_target_pairs={{0,3},{1,2},{2,1},{3,0},{4,7},{5,6},{6,5},{7,4},{8,11},{9,10},{10,... | collective-permute-start | bytes 18440 | tf_op jit(solution)/shard_map/ppermute | solution.py:812
  244.3 8.6 %collective-permute-start.18 = (f32[1536]{0:T(1024)S(1)}, f32[1536]{0:T(1024)S(1)}, u32[]{:S(2)}, u32[]{:S(2)}) collective-permute-start(f32[1536]{0:T(1024)S(1)} %slice_reduce_fusion.1), channel_id=1, source_target_pairs={{0,2},{1,3},{2,0},{3,1},{4,6},{5,7},{6,4},{7,5},{8,10},{9,11},{10,... | collective-permute-start | bytes 18440 | tf_op jit(solution)/shard_map/ppermute | solution.py:812
  244.8 8.1 %collective-permute-start.17 = (f32[1536]{0:T(1024)S(1)}, f32[1536]{0:T(1024)S(1)}, u32[]{:S(2)}, u32[]{:S(2)}) collective-permute-start(f32[1536]{0:T(1024)S(1)} %slice_reduce_fusion.1), channel_id=1, source_target_pairs={{0,1},{1,0},{2,3},{3,2},{4,5},{5,4},{6,7},{7,6},{8,9},{9,8},{10,11... | collective-permute-start | bytes 18440 | tf_op jit(solution)/shard_map/ppermute | solution.py:812
  248.6 44.3 %collective-permute-start.21 = (bf16[768,1280]{1,0:T(8,128)(2,1)}, bf16[768,1280]{1,0:T(8,128)(2,1)S(1)}, u32[]{:S(2)}, u32[]{:S(2)}) collective-permute-start(bf16[768,1280]{1,0:T(8,128)(2,1)} %pad_maximum_fusion.3), channel_id=1, source_target_pairs={{0,2},{1,3},{2,0},{3,1},{4,6},{5,7},{6,4},{7,5},{8,10},{9,11},{10,... | collective-permute-start | bytes 5898248 | tf_op jit(solution)/shard_map/ppermute | solution.py:812
  251.4 44.1 %collective-permute-start.20 = (bf16[768,1280]{1,0:T(8,128)(2,1)}, bf16[768,1280]{1,0:T(8,128)(2,1)S(1)}, u32[]{:S(2)}, u32[]{:S(2)}) collective-permute-start(bf16[768,1280]{1,0:T(8,128)(2,1)} %pad_maximum_fusion.2), channel_id=1, source_target_pairs={{0,1},{1,0},{2,3},{3,2},{4,5},{5,4},{6,7},{7,6},{8,9},{9,8},{10,11... | collective-permute-start | bytes 5898248 | tf_op jit(solution)/shard_map/ppermute | solution.py:812
  295.7 5.9 %collective-permute-start.22 = (bf16[4,320,1280]{2,1,0:T(8,128)(2,1)S(1)}, bf16[4,320,1280]{2,1,0:T(8,128)(2,1)S(1)}, u32[]{:S(2)}, u32[]{:S(2)}) collective-permute-start(bf16[4,320,1280]{2,1,0:T(8,128)(2,1)S(1)} %dynamic-slice_bitcast_fusion.1), channel_id=1, source_target_pairs={{0,4},{4,0},{8,12},{12,8},{16,20},{20,16},{24,28},{28,24},{1,5},{5... | collective-permute-start | bytes 9830408 | tf_op jit(solution)/shard_map/ppermute | solution.py:890
  304.2 176.7 %reduce-scatter.8.cloned.1.call-start = ((), (), s32[]{:S(2)}) async-start(), calls=%async_computation.7 | async-start | bytes 4096000 | tf_op jit(solution)/shard_map/reduce_scatter | solution.py:912
  305.4 77.1 %collective-permute-start.23 = (bf16[384,1280]{1,0:T(8,128)(2,1)S(1)}, bf16[384,1280]{1,0:T(8,128)(2,1)}, u32[]{:S(2)}, u32[]{:S(2)}) collective-permute-start(bf16[384,1280]{1,0:T(8,128)(2,1)S(1)} %copy-done.27), channel_id=1, source_target_pairs={{0,2},{1,3},{2,0},{3,1},{4,6},{5,7},{6,4},{7,5},{8,10},{9,11},{10,... | collective-permute-start | bytes 2949128 | tf_op jit(solution)/shard_map/ppermute | solution.py:812
  305.9 77.3 %collective-permute-start.24 = (bf16[384,1280]{1,0:T(8,128)(2,1)S(1)}, bf16[384,1280]{1,0:T(8,128)(2,1)}, u32[]{:S(2)}, u32[]{:S(2)}) collective-permute-start(bf16[384,1280]{1,0:T(8,128)(2,1)S(1)} %add_convert_fusion.2), channel_id=1, source_target_pairs={{0,1},{1,0},{2,3},{3,2},{4,5},{5,4},{6,7},{7,6},{8,9},{9,8},{10,11... | collective-permute-start | bytes 2949128 | tf_op jit(solution)/shard_map/ppermute | solution.py:812
  362.3 19.5 %collective-permute-start.27 = (f32[64,1536]{1,0:T(8,128)S(1)}, f32[64,1536]{1,0:T(8,128)S(1)}, u32[]{:S(2)}, u32[]{:S(2)}) collective-permute-start(f32[64,1536]{1,0:T(8,128)S(1)} %get-tuple-element.445), channel_id=1, source_target_pairs={{0,3},{1,2},{2,1},{3,0},{4,7},{5,6},{6,5},{7,4},{8,11},{9,10},{10,... | collective-permute-start | bytes 1179656 | tf_op jit(solution)/shard_map/ppermute | solution.py:812
  363.9 18.4 %collective-permute-start.26 = (f32[64,1536]{1,0:T(8,128)S(1)}, f32[64,1536]{1,0:T(8,128)S(1)}, u32[]{:S(2)}, u32[]{:S(2)}) collective-permute-start(f32[64,1536]{1,0:T(8,128)S(1)} %get-tuple-element.446), channel_id=1, source_target_pairs={{0,2},{1,3},{2,0},{3,1},{4,6},{5,7},{6,4},{7,5},{8,10},{9,11},{10,... | collective-permute-start | bytes 1179656 | tf_op jit(solution)/shard_map/ppermute | solution.py:812
  364.5 18.0 %collective-permute-start.25 = (f32[64,1536]{1,0:T(8,128)S(1)}, f32[64,1536]{1,0:T(8,128)S(1)}, u32[]{:S(2)}, u32[]{:S(2)}) collective-permute-start(f32[64,1536]{1,0:T(8,128)S(1)} %get-tuple-element.447), channel_id=1, source_target_pairs={{0,1},{1,0},{2,3},{3,2},{4,5},{5,4},{6,7},{7,6},{8,9},{9,8},{10,11... | collective-permute-start | bytes 1179656 | tf_op jit(solution)/shard_map/ppermute | solution.py:812
  387.4 15.8 %collective-permute-start.30 = (bf16[4,320,1280]{2,1,0:T(8,128)(2,1)}, bf16[4,320,1280]{2,1,0:T(8,128)(2,1)}, u32[]{:S(2)}, u32[]{:S(2)}) collective-permute-start(bf16[4,320,1280]{2,1,0:T(8,128)(2,1)} %dynamic-slice_bitcast_fusion), channel_id=1, source_target_pairs={{0,4},{4,0},{8,12},{12,8},{16,20},{20,16},{24,28},{28,24},{1,5},{5... | collective-permute-start | bytes 9830408 | tf_op jit(solution)/shard_map/ppermute | solution.py:890
  409.7 45.4 %collective-permute-start.28 = (bf16[768,1280]{1,0:T(8,128)(2,1)}, bf16[768,1280]{1,0:T(8,128)(2,1)S(1)}, u32[]{:S(2)}, u32[]{:S(2)}) collective-permute-start(bf16[768,1280]{1,0:T(8,128)(2,1)} %get-tuple-element.203), channel_id=1, source_target_pairs={{0,1},{1,0},{2,3},{3,2},{4,5},{5,4},{6,7},{7,6},{8,9},{9,8},{10,11... | collective-permute-start | bytes 5898248 | tf_op jit(solution)/shard_map/ppermute | solution.py:812
  422.6 49.4 %collective-permute-start.29 = (bf16[768,1280]{1,0:T(8,128)(2,1)}, bf16[768,1280]{1,0:T(8,128)(2,1)}, u32[]{:S(2)}, u32[]{:S(2)}) collective-permute-start(bf16[768,1280]{1,0:T(8,128)(2,1)} %get-tuple-element.208), channel_id=1, source_target_pairs={{0,2},{1,3},{2,0},{3,1},{4,6},{5,7},{6,4},{7,5},{8,10},{9,11},{10,... | collective-permute-start | bytes 5898248 | tf_op jit(solution)/shard_map/ppermute | solution.py:812
  470.6 4.1 collective-permute-start.33
  476.6 28.5 %collective-permute-start.34 = (f32[320,128]{0,1:T(8,128)}, f32[320,128]{0,1:T(8,128)}, u32[]{:S(2)}, u32[]{:S(2)}) collective-permute-start(f32[320,128]{0,1:T(8,128)} %copy.251), channel_id=1, source_target_pairs={{0,8},{4,12},{8,0},{12,4},{16,24},{20,28},{24,16},{28,20},{1,9},{5... | collective-permute-start | bytes 491528 | tf_op jit(solution)/shard_map/ppermute | solution.py:890
  476.6 28.5 %collective-permute-start.35 = (f32[320,128]{0,1:T(8,128)S(1)}, f32[320,128]{0,1:T(8,128)}, u32[]{:S(2)}, u32[]{:S(2)}) collective-permute-start(f32[320,128]{0,1:T(8,128)S(1)} %copy.252), channel_id=1, source_target_pairs={{0,16},{4,20},{8,24},{12,28},{16,0},{20,4},{24,8},{28,12},{1,17},{... | collective-permute-start | bytes 491528 | tf_op jit(solution)/shard_map/ppermute | solution.py:890
  477.7 27.4 %collective-permute-start.36 = (f32[320,128]{0,1:T(8,128)}, f32[320,128]{0,1:T(8,128)}, u32[]{:S(2)}, u32[]{:S(2)}) collective-permute-start(f32[320,128]{0,1:T(8,128)} %copy.253), channel_id=1, source_target_pairs={{0,24},{4,28},{8,16},{12,20},{16,8},{20,12},{24,0},{28,4},{1,25},{... | collective-permute-start | bytes 491528 | tf_op jit(solution)/shard_map/ppermute | solution.py:890
  481.0 25.5 %collective-permute-start.31 = (bf16[384,1280]{1,0:T(8,128)(2,1)}, bf16[384,1280]{1,0:T(8,128)(2,1)}, u32[]{:S(2)}, u32[]{:S(2)}) collective-permute-start(bf16[384,1280]{1,0:T(8,128)(2,1)} %add_convert_fusion.1), channel_id=1, source_target_pairs={{0,2},{1,3},{2,0},{3,1},{4,6},{5,7},{6,4},{7,5},{8,10},{9,11},{10,... | collective-permute-start | bytes 2949128 | tf_op jit(solution)/shard_map/ppermute | solution.py:812
  481.9 24.5 %collective-permute-start.32 = (bf16[384,1280]{1,0:T(8,128)(2,1)}, bf16[384,1280]{1,0:T(8,128)(2,1)}, u32[]{:S(2)}, u32[]{:S(2)}) collective-permute-start(bf16[384,1280]{1,0:T(8,128)(2,1)} %add_convert_fusion), channel_id=1, source_target_pairs={{0,1},{1,0},{2,3},{3,2},{4,5},{5,4},{6,7},{7,6},{8,9},{9,8},{10,11... | collective-permute-start | bytes 2949128 | tf_op jit(solution)/shard_map/ppermute | solution.py:812
  506.7 20.9 %collective-permute-start.39 = (f32[320]{0:T(512)S(1)}, f32[320]{0:T(512)S(1)}, u32[]{:S(2)}, u32[]{:S(2)}) collective-permute-start(f32[320]{0:T(512)S(1)} %get-tuple-element.456), channel_id=1, source_target_pairs={{0,3},{1,2},{2,1},{3,0},{4,7},{5,6},{6,5},{7,4},{8,11},{9,10},{10,... | collective-permute-start | bytes 3848 | tf_op jit(solution)/shard_map/ppermute | solution.py:812
  508.2 19.3 %collective-permute-start.38 = (f32[320]{0:T(512)S(1)}, f32[320]{0:T(512)S(1)}, u32[]{:S(2)}, u32[]{:S(2)}) collective-permute-start(f32[320]{0:T(512)S(1)} %get-tuple-element.456), channel_id=1, source_target_pairs={{0,2},{1,3},{2,0},{3,1},{4,6},{5,7},{6,4},{7,5},{8,10},{9,11},{10,... | collective-permute-start | bytes 3848 | tf_op jit(solution)/shard_map/ppermute | solution.py:812
  509.2 18.3 %collective-permute-start.37 = (f32[320]{0:T(512)S(1)}, f32[320]{0:T(512)S(1)}, u32[]{:S(2)}, u32[]{:S(2)}) collective-permute-start(f32[320]{0:T(512)S(1)} %get-tuple-element.456), channel_id=1, source_target_pairs={{0,1},{1,0},{2,3},{3,2},{4,5},{5,4},{6,7},{7,6},{8,9},{9,8},{10,11... | collective-permute-start | bytes 3848 | tf_op jit(solution)/shard_map/ppermute | solution.py:812
  (103 other events, 684.6 us)
Sparse Core Ops, SparseCore 0:
  12.9 75.9 all-gather.4
  91.1 65.5 all-gather.8
  158.4 65.5 all-gather.6
  226.7 60.9 reduce-scatter.3
  304.3 60.3 reduce-scatter.5
  407.8 59.7 reduce-scatter.7

commit v6 on v5

--- a/solution.py
+++ b/solution.py
@@ -758,6 +758,71 @@
         ],
     )
 
+
+def added(refs):
+    total = refs[0][...].astype(F32)
+    for ref in refs[1:]:
+        total = total + ref[...].astype(F32)
+    return total
+
+
+def block_out_kernel(count, *refs):
+    left, right = refs[:count], refs[count : 2 * count]
+    block_ref, live_ref, out_ref = refs[2 * count :]
+    half = out_ref.shape[1] // 2
+    live = live_ref[...] > 0.0
+    for at, pieces in ((0, left), (half, right)):
+        cols = slice(at, at + half)
+        total = jnp.where(live, added(pieces), 0.0)
+        out_ref[:, cols] = (block_ref[:, cols].astype(F32) + total).astype(BF16)
+
+
+def d_input_kernel(eps, count, *refs):
+    left, right = refs[:count], refs[count : 2 * count]
+    block_ref, cot_ref, gain_ref, out_ref = refs[2 * count :]
+    model = out_ref.shape[1]
+    half = model // 2
+    rows = block_ref[...].astype(F32)
+    inv = lax.rsqrt(jnp.sum(rows * rows, axis=1, keepdims=True) / model + eps)
+    unit = rows * inv
+    parts = [
+        added(pieces) * gain_ref[0:1, at : at + half]
+        for at, pieces in ((0, left), (half, right))
+    ]
+    mean = (
+        jnp.sum(parts[0] * unit[:, :half], axis=1, keepdims=True)
+        + jnp.sum(parts[1] * unit[:, half:], axis=1, keepdims=True)
+    ) / model
+    for at, scaled in ((0, parts[0]), (half, parts[1])):
+        cols = slice(at, at + half)
+        d_block = inv * (scaled - unit[:, cols] * mean)
+        out_ref[:, cols] = (cot_ref[:, cols].astype(F32) + d_block).astype(BF16)
+
+
+def finish(kernel, name, left, right, ins, length, model, rows=128):
+    half = model // 2
+
+    def piece(first):
+        return pl.BlockSpec((rows, half), lambda m: (m + first // rows, 0))
+
+    pieces = list(left) + list(right)
+    return pl.pallas_call(
+        functools.partial(kernel, len(left)),
+        grid=(length // rows,),
+        out_shape=jax.ShapeDtypeStruct((length, model), BF16),
+        in_specs=[piece(first) for _, first in pieces]
+        + [
+            pl.BlockSpec((rows, array.shape[1]), lambda m: (m, 0))
+            if array.shape[0] == length
+            else full_spec(array.shape)
+            for array in ins
+        ],
+        out_specs=pl.BlockSpec((rows, model), lambda m: (m, 0)),
+        compiler_params=pltpu.CompilerParams(vmem_limit_bytes=VMEM_CAP),
+        cost_estimate=time_like(1e-7),
+        name=name,
+    )(*[array for array, _ in pieces], *ins)
+
 DI = 5120
 STEP = 3
 NORM_EPS = 1e-05
@@ -836,7 +901,7 @@
         if size == 4:
             pair = jnp.concatenate([block(half, 3), block(half, near)], axis=0)
             sent.append(swap(pair, near, size))
-            kept.append((block(half, 3 - near), block(half, 0)))
+            kept.append((block(half, 3 - near), (block(half, 0), 0)))
         else:
             sent.append([swap(block(half, k), k, size) for k in range(1, size)])
             kept.append(block(half, 0))
@@ -845,11 +910,11 @@
 
 def scatter_middle(sent, kept, rows, size):
     if size != 4:
-        return sent, [(one,) for one in kept]
+        return sent, [[(one, 0)] for one in kept]
     passed = [
         (kept[at][0].astype(F32) + sent[at][:rows].astype(F32)).astype(BF16) for at in range(2)
     ]
-    return passed, [(kept[at][1], sent[at][rows:]) for at in range(2)]
+    return passed, [[kept[at][1], (sent[at], rows)] for at in range(2)]
 
 
 def scatter_last(passed, size):
@@ -860,15 +925,9 @@
 
 def scatter_end(own, last):
     each = len(last) // 2
-    totals = []
-    for at in range(2):
-        total = own[at][0].astype(F32)
-        for piece in own[at][1:]:
-            total = total + piece.astype(F32)
-        for piece in last[at * each : (at + 1) * each]:
-            total = total + piece.astype(F32)
-        totals.append(total)
-    return jnp.concatenate(totals, axis=1)
+    return [
+        own[at] + [(piece, 0) for piece in last[at * each : (at + 1) * each]] for at in range(2)
+    ]
 
 
 def row_sum(value, size):
@@ -1152,20 +1211,32 @@
         )
         sent = [swap(left_away, 1, 4), swap(right_away, 2, 4)]
         left_kept, gains_three = d_normed_of([2, 0], 0)
-        mixed_rows = scatter_end(mixed_kept, mixed_last)
-        block_out = (block_f + jnp.where(live_rows, mixed_rows, 0.0)).astype(BF16)
+        block_out = finish(
+            block_out_kernel,
+            "block_out",
+            *scatter_end(mixed_kept, mixed_last),
+            [block_in, live_rows.astype(F32)],
+            own_rows,
+            model,
+        )
         sent[0], d_side_late, side_part, grad_out = tied(sent[0], d_side, side_part, grad_out)
         right_kept, gains_four = d_normed_blocks(
             d_z, d_x, d_side_late, gate_all, x_all, normed, tp_index ^ jnp.array([1, 0]), 1, own_rows
         )
         kept = [
-            (left_kept[:own_rows], left_kept[own_rows:]),
-            (right_kept[:own_rows], right_kept[own_rows:]),
+            (left_kept[:own_rows], (left_kept, own_rows)),
+            (right_kept[:own_rows], (right_kept, own_rows)),
         ]
         gain_sums = jnp.concatenate([gains_one + gains_three, gains_two + gains_four], axis=1)[0]
     else:
-        mixed_rows = scatter_end(mixed_kept, mixed_last)
-        block_out = (block_f + jnp.where(live_rows, mixed_rows, 0.0)).astype(BF16)
+        block_out = finish(
+            block_out_kernel,
+            "block_out",
+            *scatter_end(mixed_kept, mixed_last),
+            [block_in, live_rows.astype(F32)],
+            own_rows,
+            model,
+        )
         left, gains_one = d_normed_of(list(range(tp_size)), 0)
         right, gains_two = d_normed_of(list(range(tp_size)), 1)
         sent = [
@@ -1189,18 +1260,19 @@
         moments[1],
         moments[10],
     )
-    kept, last = tied(kept, last)
     grad_side, pair = side_gradient(
         side_part, d_taps, d_skip, d_heads, grad_conv_state, gain_sums, pair
     )
     grad_side, last[0] = tied(grad_side, last[0])
     grad_input_gain = all_sum(grad_side[:, used], tp_index, tp_size) / input_gain.astype(F32)
-    d_normed = scatter_end(kept, last)
-
-    unit_rows, inv_rms = unit_of(block_in)
-    scaled = d_normed * gain_f[None, :]
-    d_block = inv_rms * (scaled - unit_rows * jnp.mean(scaled * unit_rows, axis=1, keepdims=True))
-    d_input = (cot_f + d_block).astype(BF16)
+    d_input = finish(
+        functools.partial(d_input_kernel, NORM_EPS),
+        "d_input",
+        *scatter_end(kept, last),
+        [block_in, cotangent, gain_f[None, :]],
+        own_rows,
+        model,
+    )
 
     own_extras = grad_side[:, used + 1 : used + 1 + small_cols].reshape(-1)
     grads = (

time: 541 us -> 537 us (level)
  other arithmetic: 81.3 us -> 62.8 us
  Pallas kernels: 211 us -> 224 us
    pallas_call x0 -> x2, Pallas kernels: none -> 13.4 us  [finish(): pl.pallas_call(functools.partial(kernel, len(left)), grid=(length // rows...]
    add x4 -> x0, other arithmetic: 10.3 us -> none  [scatter_end(): total = total + piece.astype(F32)]
    unnamed x213 -> x185, local copies, waits for them, and re-layouts: 13.7 us -> 11.6 us
  transfers between devices with their start and end apart: 46 -> 46, of which waited for: 15 -> 14; matrix products, arithmetic and copies ran while one was open for 31% -> 29% of each run, Pallas kernels for 39% -> 42%
where the time goes in v6:
time: 537 us; the launch traced here: 532 us
  Pallas kernels  224 us (42%)
  waiting for transfers between devices  66.5 us (12%)
  other arithmetic  62.8 us (12%)
  local copies, waits for them, and re-layouts  59.2 us (11%)
  matrix products  53.8 us (10%)
  starting transfers between devices  48.9 us (9%)
  between operations  16.7 us (3%)
    pallas_call x4, Pallas kernels, row_call(): pl.pallas_call(kernel, grid=(length // rows,), out_shape=tuple((jax.Shape...  73.3 us
    pallas_call x1, Pallas kernels, ssd_backward(): pl.pallas_call(functools.partial(ssd_bwd_kernel, heads), grid=(chunks,),...  53.5 us
    ppermute x30, waiting for transfers between devices, swap(): lax.ppermute(value, 'tp', [(at, at ^ distance) for at in range(size)])  51.4 us
    pallas_call x4, Pallas kernels, d_normed_blocks(): pl.pallas_call(functools.partial(dn_kernel, count, rows), grid_spec=pltpu...  47.7 us
    dot_general x3, matrix products, contract_rows(): lax.dot_general(left_mat, right_mat, (((0,), (0,)), ((), ())), preferred_...  41 us
    ppermute x30, starting transfers between devices, swap(): lax.ppermute(value, 'tp', [(at, at ^ distance) for at in range(size)])  38.6 us
    pallas_call x1, Pallas kernels, ssd_forward(): pl.pallas_call(functools.partial(ssd_fwd_kernel, heads), grid=(chunks,),...  21.2 us
    pallas_call x1, Pallas kernels, adam_pair(): pl.pallas_call(functools.partial(adam_kernel, step), grid=(shard // rows,...  15.2 us
  transfers between devices with their start and end apart: 46, of which 14 were waited for; matrix products, arithmetic and copies ran while one was open for 29% of the time, Pallas kernels for 42%

profile of v6, /device:TPU:0, one launch (start us, length us, event | category | flops | bytes accessed | tf_op | source)
XLA Modules:
  0.0 532.3 jit_solution(9717962445674676246)
XLA Ops:
  12.9 3.0 collective-permute-start.4
  27.6 2.1 collective-permute-done.2
  29.8 3.4 collective-permute-start.3
  34.1 3.6 collective-permute-done.3
  39.7 3.7 broadcast.302.clone
  45.2 13.6 %collective-permute-done.4 = bf16[384,2560]{1,0:T(8,128)(2,1)} collective-permute-done((bf16[384,2560]{1,0:T(8,128)(2,1)S(1)}, bf16[384,2560]{1,0:T(8,128)(2,1)}, u32[]{:S(2)}, u32[]{:S(2)}) %collective-permute-start.4) | collective-permute-done | bytes 1966112 | tf_op jit(solution)/shard_map/ppermute | solution.py:877
  67.9 15.2 %collective-permute-done.5 = bf16[192,2560]{1,0:T(8,128)(2,1)S(1)} collective-permute-done((bf16[192,2560]{1,0:T(8,128)(2,1)S(1)}, bf16[192,2560]{1,0:T(8,128)(2,1)S(1)}, u32[]{:S(2)}, u32[]{:S(2)}) %collective-permute-start.5) | collective-permute-done | bytes 983072 | tf_op jit(solution)/shard_map/ppermute | solution.py:877
  83.1 4.3 collective-permute-done.6
  89.8 3.0 fusion.6
  92.8 3.4 fusion.17
  96.1 3.5 fusion.16
  102.0 6.2 %fusion.25.small_ref = f32[128,1536]{1,0:T(8,128)S(1)} fusion(bf16[1536,2560]{1,0:T(8,128)(2,1)} %fusion.15.left_ref.refs_6_.refs_7_, bf16[2560,1408]{1,0:T(8,128)(2,1)} %all-gather.5.cloned.1.call-done.right_ref.refs_9_), kind=kOutput, calls=%fused_computation.66 | convolution fusion | flops 1006632960 | bytes 9306112 | tf_op jit(solution)/shard_map/dot_general | solution.py:1096
  113.8 15.7 %inner_product.1.raw_ref.halo_ref = f32[1536,1280]{1,0:T(8,128)} custom-call(bf16[1536,2560]{1,0:T(8,128)(2,1)} %fusion.15.left_ref.refs_6_.refs_7_, bf16[2560,1408]{1,0:T(8,128)(2,1)} %all-gather.5.cloned.1.call-done.right_ref.refs_9_), custom_call_target="tpu_custom_call" | custom-call | flops 15399999488 | bytes 47600000 | tf_op jit(solution)/shard_map/inner_product/pallas_call | solution.py:675
  129.5 8.4 %collective-permute-done.7 = bf16[64,1536]{1,0:T(8,128)(2,1)S(1)} collective-permute-done((bf16[64,1536]{1,0:T(8,128)(2,1)S(1)}, bf16[64,1536]{1,0:T(8,128)(2,1)S(1)}, u32[]{:S(2)}, u32[]{:S(2)}) %collective-permute-start.7) | collective-permute-done | bytes 196640 | tf_op jit(solution)/shard_map/ppermute | solution.py:877
  137.9 2.0 collective-permute-done.9
  141.8 21.2 %ssd_fwd.1 = (f32[1536,1280]{1,0:T(8,128)}, f32[6,128,1280]{2,1,0:T(8,128)}) custom-call(f32[1536,1280]{1,0:T(8,128)} %inner_product.1.raw_ref.halo_ref, f32[128,1536]{1,0:T(8,128)} %copy-done.16, bf16[256,1536]{1,0:T(8,128)(2,1)} %copy-done.22, f32[1536,384]{1,0:T(8,128)} %pad_maximum_fusion.masks_ref.masks_next_ref, ...), custom_call_target="tpu_custom_call" | custom-call | flops 40699998208 | bytes 125800000 | tf_op jit(solution)/shard_map/ssd_fwd/pallas_call | solution.py:388
  163.0 19.4 %gate_product.1 = (f32[1536,1280]{1,0:T(8,128)}, f32[1536,1280]{1,0:T(8,128)}, f32[8,1536]{1,0:T(8,128)}) custom-call(bf16[1536,2560]{1,0:T(8,128)(2,1)} %fusion.15.left_ref.refs_6_.refs_7_, bf16[2560,1280]{1,0:T(8,128)(2,1)} %bitcast.104, f32[1536,1280]{1,0:T(8,128)} %get-tuple-element.153.mixed_ref.y_ref), custom_call_target="tpu_custom_call" | custom-call | flops 17600000000 | bytes 54400000 | tf_op jit(solution)/shard_map/gate_product/pallas_call | solution.py:675
  184.4 2.0 collective-permute-start.14
  187.6 1.9 constant_dynamic-update-slice_fusion.2
  194.0 2.2 copy-done.1
  196.3 11.0 %convolution_convert_fusion.2 = bf16[2560,1280]{1,0:T(8,128)(2,1)S(1)} fusion(bf16[1536,2560]{1,0:T(8,128)(2,1)S(1)} %constant_dynamic-update-slice_fusion.grad_ref.left_ref, bf16[1536,1280]{1,0:T(8,128)(2,1)S(1)} %multiply_convert_fusion.left_ref), kind=kOutput, calls=%fused_computation.2 | convolution fusion | flops 10069606400 | bytes 18350080 | tf_op jit(solution)/shard_map/dot_general | solution.py:859
  207.3 2.1 dynamic-slice_bitcast_fusion.2
  212.1 4.9 collective-permute-done.16
  217.0 4.4 fusion.2
  221.5 2.4 all-gather.7.cloned.1.call-done.right_ref
  223.9 16.9 %output_product.1 = (bf16[1536,1280]{1,0:T(8,128)(2,1)}, bf16[1536,1280]{1,0:T(8,128)(2,1)}, f32[8,1536]{1,0:T(8,128)}) custom-call(bf16[1536,1280]{1,0:T(8,128)(2,1)} %copy-done.12, bf16[2560,1280]{1,0:T(8,128)(2,1)} %all-gather.7.cloned.1.call-done.right_ref, bf16[1536,2560]{1,0:T(8,128)(2,1)} %copy-done.1), custom_call_target="tpu_custom_call" | custom-call | flops 17600000000 | bytes 54400000 | tf_op jit(solution)/shard_map/output_product/pallas_call | solution.py:675
  241.6 2.4 collective-permute-start.19
  245.2 2.9 constant_dynamic-slice_fusion.8
  256.2 21.3 %gate_gradient.1 = (f32[1536,1280]{1,0:T(8,128)}, bf16[1536,1280]{1,0:T(8,128)(2,1)}, f32[8,1280]{1,0:T(8,128)}) custom-call(bf16[1536,2560]{1,0:T(8,128)(2,1)} %copy-done.1, bf16[2560,1280]{1,0:T(8,128)(2,1)} %all-gather.7.cloned.1.call-done.right_ref, f32[1536,1280]{1,0:T(8,128)} %get-tuple-element.166.z_ref, ...), custom_call_target="tpu_custom_call" | custom-call | flops 19800000512 | bytes 61200000 | tf_op jit(solution)/shard_map/gate_gradient/pallas_call | solution.py:675
  277.5 14.1 %convolution_convert_fusion.1 = bf16[2560,1280]{1,0:T(8,128)(2,1)S(1)} fusion(bf16[1536,2560]{1,0:T(8,128)(2,1)} %fusion.15.left_ref.refs_6_.refs_7_, bf16[1536,1280]{1,0:T(8,128)(2,1)} %get-tuple-element.168.refs_0_.refs_1_), kind=kOutput, calls=%fused_computation.1 | convolution fusion | flops 10069606400 | bytes 18350080 | tf_op jit(solution)/shard_map/dot_general | solution.py:859
  291.6 2.2 collective-permute-done.20.refs_1_
  293.8 4.0 collective-permute-done.21.refs_4_
  303.9 2.6 fusion.1
  309.7 53.5 %ssd_bwd.1 = (bf16[1536,1280]{1,0:T(8,128)(2,1)}, f32[32,1536]{1,0:T(8,128)}, f32[256,1536]{1,0:T(8,128)}, f32[8,1280]{1,0:T(8,128)}, f32[32,128]{1,0:T(8,128)}, /*index=5*/f32[8,1280]{1,0:T(8,128)}) custom-call(f32[1536,1280]{1,0:T(8,128)} %inner_product.1.raw_ref.halo_ref, f32[1536,1280]{1,0:T(8,128)} %inner_product.1.raw_ref.halo_ref, ...), custom_call_target="tpu_custom_call" | custom-call | flops 75900002304 | bytes 234600000 | tf_op jit(solution)/shard_map/ssd_bwd/pallas_call | solution.py:438
  368.3 15.9 %convolution_convert_fusion = bf16[2560,1280]{1,0:T(8,128)(2,1)} fusion(bf16[1536,2560]{1,0:T(8,128)(2,1)} %fusion.15.left_ref.refs_6_.refs_7_, bf16[1536,1280]{1,0:T(8,128)(2,1)} %get-tuple-element.178.refs_2_.refs_3_), kind=kOutput, calls=%fused_computation | convolution fusion | flops 10069606400 | bytes 18350080 | tf_op jit(solution)/shard_map/dot_general | solution.py:859
  385.3 4.0 dynamic-slice_bitcast_fusion
  392.2 12.2 %d_normed.6 = (bf16[768,1280]{1,0:T(8,128)(2,1)}, f32[8,1280]{1,0:T(8,128)}) custom-call(s32[2]{0:T(128)} %get-tuple-element.462.at_ref, bf16[1536,1280]{1,0:T(8,128)(2,1)} %get-tuple-element.168.refs_0_.refs_1_, bf16[1536,1280]{1,0:T(8,128)(2,1)} %get-tuple-element.168.refs_0_.refs_1_, bf16[1536,1280]{1,0:T(8,128)(2,1)} %get-tuple-element.178.refs_2_.refs_3_, ...), custom_call_target="tpu_custom_call" | custom-call | flops 110000000 | bytes 340000 | tf_op jit(solution)/shard_map/d_normed/pallas_call | solution.py:556
  404.4 4.4 fusion
  412.0 11.9 %d_normed.4 = (bf16[768,1280]{1,0:T(8,128)(2,1)}, f32[8,1280]{1,0:T(8,128)}) custom-call(s32[2]{0:T(128)} %get-tuple-element.464.at_ref, bf16[1536,1280]{1,0:T(8,128)(2,1)} %get-tuple-element.168.refs_0_.refs_1_, bf16[1536,1280]{1,0:T(8,128)(2,1)} %get-tuple-element.168.refs_0_.refs_1_, bf16[1536,1280]{1,0:T(8,128)(2,1)} %get-tuple-element.178.refs_2_.refs_3_, ...), custom_call_target="tpu_custom_call" | custom-call | flops 110000000 | bytes 340000 | tf_op jit(solution)/shard_map/d_normed/pallas_call | solution.py:556
  426.2 6.6 %fusion.36 = f32[2560,128]{1,0:T(8,128)} fusion(bf16[1536,2560]{1,0:T(8,128)(2,1)} %fusion.15.left_ref.refs_6_.refs_7_, f32[64,1536]{1,0:T(8,128)S(1)} %fusion.33, f32[20,1536]{1,0:T(8,128)S(1)} %slice.216), kind=kOutput, calls=%fused_computation.88 | convolution fusion | flops 1008009216 | bytes 9691136 | tf_op jit(solution)/shard_map/dot_general | solution.py:1165
  435.1 6.1 %block_out.1 = bf16[384,2560]{1,0:T(8,128)(2,1)} custom-call(bf16[384,1280]{1,0:T(8,128)(2,1)} %get-tuple-element.430.refs_0_, bf16[768,1280]{1,0:T(8,128)(2,1)} %copy-done.5, bf16[384,1280]{1,0:T(8,128)(2,1)} %collective-permute-done.23.refs_2_, bf16[384,1280]{1,0:T(8,128)(2,1)} %get-tuple-element.425.refs_3_, bf16[768,1280]{1,0:T(8,128)(2,1)} %copy-done.6, ...), custom_call_target="tpu_custom_call" | custom-call | flops 110000000 | bytes 340000 | tf_op jit(solution)/shard_map/block_out/pallas_call | solution.py:809
  441.1 11.8 %d_normed.5 = (bf16[768,1280]{1,0:T(8,128)(2,1)}, f32[8,1280]{1,0:T(8,128)}) custom-call(s32[2]{0:T(128)} %get-tuple-element.463.at_ref, bf16[1536,1280]{1,0:T(8,128)(2,1)} %get-tuple-element.168.refs_0_.refs_1_, bf16[1536,1280]{1,0:T(8,128)(2,1)} %get-tuple-element.168.refs_0_.refs_1_, bf16[1536,1280]{1,0:T(8,128)(2,1)} %get-tuple-element.178.refs_2_.refs_3_, ...), custom_call_target="tpu_custom_call" | custom-call | flops 110000000 | bytes 340000 | tf_op jit(solution)/shard_map/d_normed/pallas_call | solution.py:556
  454.3 11.8 %d_normed.7 = (bf16[768,1280]{1,0:T(8,128)(2,1)}, f32[8,1280]{1,0:T(8,128)}) custom-call(s32[2]{0:T(128)} %get-tuple-element.461.at_ref, bf16[1536,1280]{1,0:T(8,128)(2,1)} %get-tuple-element.168.refs_0_.refs_1_, bf16[1536,1280]{1,0:T(8,128)(2,1)} %get-tuple-element.168.refs_0_.refs_1_, bf16[1536,1280]{1,0:T(8,128)(2,1)} %get-tuple-element.178.refs_2_.refs_3_, ...), custom_call_target="tpu_custom_call" | custom-call | flops 110000000 | bytes 340000 | tf_op jit(solution)/shard_map/d_normed/pallas_call | solution.py:556
  467.4 2.2 fusion.23
  480.4 3.0 collective-permute-start.33
  484.5 4.6 fusion.21
  490.9 15.2 %adam_pair.1 = (f32[320,2,1280]{2,1,0:T(2,128)}, bf16[320,2,1280]{2,1,0:T(2,128)(2,1)}, f32[320,2,1280]{2,1,0:T(2,128)}, f32[320,2,1280]{2,1,0:T(2,128)}) custom-call(bf16[320,1280]{1,0:T(8,128)(2,1)} %reduce-scatter.6.cloned.1.call-done.gate_ref, bf16[320,1280]{1,0:T(8,128)(2,1)} %reduce-scatter.8.cloned.1.call-done.inner_ref, ...), custom_call_target="tpu_custom_call" | custom-call | flops 1000 | bytes 1000 | tf_op jit(solution)/shard_map/adam_pair/pallas_call | solution.py:611
  516.9 7.3 %d_input.1 = bf16[384,2560]{1,0:T(8,128)(2,1)} custom-call(bf16[768,1280]{1,0:T(8,128)(2,1)} %get-tuple-element.196.refs_0_, bf16[768,1280]{1,0:T(8,128)(2,1)} %copy-done.7, bf16[384,1280]{1,0:T(8,128)(2,1)} %collective-permute-done.35.refs_2_, bf16[768,1280]{1,0:T(8,128)(2,1)} %get-tuple-element.215.refs_3_, ...), custom_call_target="tpu_custom_call" | custom-call | flops 110000000 | bytes 340000 | tf_op jit(solution)/shard_map/d_input/pallas_call | solution.py:809
  (439 shorter events, 115.8 us)
Async XLA Ops:
  7.2 94.8 %all-gather.5.cloned.1.call-start = ((), (), s32[]{:S(2)}) async-start(), calls=%async_computation.3 | async-start | bytes 8110080 | tf_op jit(solution)/shard_map/all_gather | solution.py:1029
  12.8 150.2 %all-gather.9.cloned.1.call-start = ((), (), s32[]{:S(2)}) async-start(), calls=%async_computation.8 | async-start | bytes 7372800 | tf_op jit(solution)/shard_map/all_gather | solution.py:1030
  12.9 46.0 %collective-permute-start.4 = (bf16[384,2560]{1,0:T(8,128)(2,1)S(1)}, bf16[384,2560]{1,0:T(8,128)(2,1)}, u32[]{:S(2)}, u32[]{:S(2)}) collective-permute-start(bf16[384,2560]{1,0:T(8,128)(2,1)S(1)} %copy-done), channel_id=1, source_target_pairs={{0,2},{1,3},{2,0},{3,1},{4,6},{5,7},{6,4},{7,5},{8,10},{9,11},{10,... | collective-permute-start | bytes 5898248 | tf_op jit(solution)/shard_map/ppermute | solution.py:877
  15.9 46.0 %collective-permute-start = (bf16[384,2560]{1,0:T(8,128)(2,1)S(1)}, bf16[384,2560]{1,0:T(8,128)(2,1)}, u32[]{:S(2)}, u32[]{:S(2)}) collective-permute-start(bf16[384,2560]{1,0:T(8,128)(2,1)S(1)} %copy-done), channel_id=1, source_target_pairs={{0,1},{1,0},{2,3},{3,2},{4,5},{5,4},{6,7},{7,6},{8,9},{9,8},{10,11... | collective-permute-start | bytes 5898248 | tf_op jit(solution)/shard_map/ppermute | solution.py:877
  17.8 7.3 %collective-permute-start.1 = (bf16[8,1320]{1,0:T(8,128)(2,1)S(1)}, bf16[8,1320]{1,0:T(8,128)(2,1)S(1)}, u32[]{:S(2)}, u32[]{:S(2)}) collective-permute-start(bf16[8,1320]{1,0:T(8,128)(2,1)S(1)} %dynamic_update_slice.53), channel_id=1, source_target_pairs={{0,4},{4,0},{8,12},{12,8},{16,20},{20,16},{24,28},{28,24},{1,5},{5... | collective-permute-start | bytes 63368 | tf_op jit(solution)/shard_map/ppermute | solution.py:949
  17.9 206.0 %all-gather.7.cloned.1.call-start = ((), (), s32[]{:S(2)}) async-start(), calls=%async_computation.4 | async-start | bytes 7372800 | tf_op jit(solution)/shard_map/all_gather | solution.py:1111
  19.9 88.4 %copy-start.26 = (f32[1536]{0:T(1024)}, f32[1536]{0:T(1024)S(1)}, u32[]{:S(2)}) copy-start(f32[1536]{0:T(1024)S(1)} %get-tuple-element.447) | copy-start | bytes 18436
  19.9 88.4 %copy-start.28 = (f32[1536]{0:T(1024)}, f32[1536]{0:T(1024)S(1)}, u32[]{:S(2)}) copy-start(f32[1536]{0:T(1024)S(1)} %get-tuple-element.448) | copy-start | bytes 18436
  25.4 4.4 collective-permute-start.2
  29.8 7.9 %collective-permute-start.3 = (bf16[8,1320]{1,0:T(8,128)(2,1)S(1)}, bf16[8,1320]{1,0:T(8,128)(2,1)S(1)}, u32[]{:S(2)}, u32[]{:S(2)}) collective-permute-start(bf16[8,1320]{1,0:T(8,128)(2,1)S(1)} %add.448), channel_id=1, source_target_pairs={{0,16},{4,20},{8,24},{12,28},{16,0},{20,4},{24,8},{28,12},{1,17},{... | collective-permute-start | bytes 63368 | tf_op jit(solution)/shard_map/ppermute | solution.py:949
  60.1 23.0 %collective-permute-start.5 = (bf16[192,2560]{1,0:T(8,128)(2,1)S(1)}, bf16[192,2560]{1,0:T(8,128)(2,1)S(1)}, u32[]{:S(2)}, u32[]{:S(2)}) collective-permute-start(bf16[192,2560]{1,0:T(8,128)(2,1)S(1)} %slice.242), channel_id=1, source_target_pairs={{0,1},{1,0},{2,3},{3,2},{4,5},{5,4},{6,7},{7,6},{8,9},{9,8},{10,11... | collective-permute-start | bytes 2949128 | tf_op jit(solution)/shard_map/ppermute | solution.py:877
  65.1 22.4 %collective-permute-start.6 = (bf16[192,2560]{1,0:T(8,128)(2,1)S(1)}, bf16[192,2560]{1,0:T(8,128)(2,1)S(1)}, u32[]{:S(2)}, u32[]{:S(2)}) collective-permute-start(bf16[192,2560]{1,0:T(8,128)(2,1)S(1)} %slice.198), channel_id=1, source_target_pairs={{0,2},{1,3},{2,0},{3,1},{4,6},{5,7},{6,4},{7,5},{8,10},{9,11},{10,... | collective-permute-start | bytes 2949128 | tf_op jit(solution)/shard_map/ppermute | solution.py:877
  87.6 95.6 %collective-permute-start.11 = (bf16[384,2560]{1,0:T(8,128)(2,1)S(1)}, bf16[384,2560]{1,0:T(8,128)(2,1)}, u32[]{:S(2)}, u32[]{:S(2)}) collective-permute-start(bf16[384,2560]{1,0:T(8,128)(2,1)S(1)} %copy-done.2), channel_id=1, source_target_pairs={{0,2},{1,3},{2,0},{3,1},{4,6},{5,7},{6,4},{7,5},{8,10},{9,11},{10,... | collective-permute-start | bytes 5898248 | tf_op jit(solution)/shard_map/ppermute | solution.py:877
  89.2 94.0 %collective-permute-start.10 = (bf16[384,2560]{1,0:T(8,128)(2,1)S(1)}, bf16[384,2560]{1,0:T(8,128)(2,1)}, u32[]{:S(2)}, u32[]{:S(2)}) collective-permute-start(bf16[384,2560]{1,0:T(8,128)(2,1)S(1)} %copy-done.2), channel_id=1, source_target_pairs={{0,1},{1,0},{2,3},{3,2},{4,5},{5,4},{6,7},{7,6},{8,9},{9,8},{10,11... | collective-permute-start | bytes 5898248 | tf_op jit(solution)/shard_map/ppermute | solution.py:877
  110.3 27.6 %collective-permute-start.8 = (bf16[64,1536]{1,0:T(8,128)(2,1)S(1)}, bf16[64,1536]{1,0:T(8,128)(2,1)S(1)}, u32[]{:S(2)}, u32[]{:S(2)}) collective-permute-start(bf16[64,1536]{1,0:T(8,128)(2,1)S(1)} %get-tuple-element.423), channel_id=1, source_target_pairs={{0,2},{1,3},{2,0},{3,1},{4,6},{5,7},{6,4},{7,5},{8,10},{9,11},{10,... | collective-permute-start | bytes 589832 | tf_op jit(solution)/shard_map/ppermute | solution.py:877
  110.8 27.0 %collective-permute-start.7 = (bf16[64,1536]{1,0:T(8,128)(2,1)S(1)}, bf16[64,1536]{1,0:T(8,128)(2,1)S(1)}, u32[]{:S(2)}, u32[]{:S(2)}) collective-permute-start(bf16[64,1536]{1,0:T(8,128)(2,1)S(1)} %get-tuple-element.423), channel_id=1, source_target_pairs={{0,1},{1,0},{2,3},{3,2},{4,5},{5,4},{6,7},{7,6},{8,9},{9,8},{10,11... | collective-permute-start | bytes 589832 | tf_op jit(solution)/shard_map/ppermute | solution.py:877
  112.1 27.8 %collective-permute-start.9 = (bf16[64,1536]{1,0:T(8,128)(2,1)S(1)}, bf16[64,1536]{1,0:T(8,128)(2,1)S(1)}, u32[]{:S(2)}, u32[]{:S(2)}) collective-permute-start(bf16[64,1536]{1,0:T(8,128)(2,1)S(1)} %get-tuple-element.423), channel_id=1, source_target_pairs={{0,3},{1,2},{2,1},{3,0},{4,7},{5,6},{6,5},{7,4},{8,11},{9,10},{10,... | collective-permute-start | bytes 589832 | tf_op jit(solution)/shard_map/ppermute | solution.py:877
  139.9 43.3 %collective-permute-start.12 = (bf16[384,2560]{1,0:T(8,128)(2,1)S(1)}, bf16[384,2560]{1,0:T(8,128)(2,1)}, u32[]{:S(2)}, u32[]{:S(2)}) collective-permute-start(bf16[384,2560]{1,0:T(8,128)(2,1)S(1)} %copy-done.2), channel_id=1, source_target_pairs={{0,3},{1,2},{2,1},{3,0},{4,7},{5,6},{6,5},{7,4},{8,11},{9,10},{10,... | collective-permute-start | bytes 5898248 | tf_op jit(solution)/shard_map/ppermute | solution.py:877
  141.5 165.0 %reduce-scatter.4.cloned.1.call-start = ((), (), s32[]{:S(2)}) async-start(), calls=%async_computation.5 | async-start | bytes 4096000 | tf_op jit(solution)/shard_map/reduce_scatter | solution.py:971
  183.3 10.0 %collective-permute-start.15 = (f32[1536]{0:T(1024)S(1)}, f32[1536]{0:T(1024)S(1)}, u32[]{:S(2)}, u32[]{:S(2)}) collective-permute-start(f32[1536]{0:T(1024)S(1)} %slice_reduce_fusion.2), channel_id=1, source_target_pairs={{0,3},{1,2},{2,1},{3,0},{4,7},{5,6},{6,5},{7,4},{8,11},{9,10},{10,... | collective-permute-start | bytes 18440 | tf_op jit(solution)/shard_map/ppermute | solution.py:877
  184.4 8.9 %collective-permute-start.14 = (f32[1536]{0:T(1024)S(1)}, f32[1536]{0:T(1024)S(1)}, u32[]{:S(2)}, u32[]{:S(2)}) collective-permute-start(f32[1536]{0:T(1024)S(1)} %slice_reduce_fusion.2), channel_id=1, source_target_pairs={{0,2},{1,3},{2,0},{3,1},{4,6},{5,7},{6,4},{7,5},{8,10},{9,11},{10,... | collective-permute-start | bytes 18440 | tf_op jit(solution)/shard_map/ppermute | solution.py:877
  186.3 6.9 %collective-permute-start.13 = (f32[1536]{0:T(1024)S(1)}, f32[1536]{0:T(1024)S(1)}, u32[]{:S(2)}, u32[]{:S(2)}) collective-permute-start(f32[1536]{0:T(1024)S(1)} %slice_reduce_fusion.2), channel_id=1, source_target_pairs={{0,1},{1,0},{2,3},{3,2},{4,5},{5,4},{6,7},{7,6},{8,9},{9,8},{10,11... | collective-permute-start | bytes 18440 | tf_op jit(solution)/shard_map/ppermute | solution.py:877
  211.0 6.1 %collective-permute-start.16 = (bf16[4,320,1280]{2,1,0:T(8,128)(2,1)}, bf16[4,320,1280]{2,1,0:T(8,128)(2,1)S(1)}, u32[]{:S(2)}, u32[]{:S(2)}) collective-permute-start(bf16[4,320,1280]{2,1,0:T(8,128)(2,1)} %dynamic-slice_bitcast_fusion.2), channel_id=1, source_target_pairs={{0,4},{4,0},{8,12},{12,8},{16,20},{20,16},{24,28},{28,24},{1,5},{5... | collective-permute-start | bytes 9830408 | tf_op jit(solution)/shard_map/ppermute | solution.py:949
  221.5 163.7 %reduce-scatter.6.cloned.1.call-start = ((), (), s32[]{:S(2)}) async-start(), calls=%async_computation.6 | async-start | bytes 4096000 | tf_op jit(solution)/shard_map/reduce_scatter | solution.py:971
  241.6 13.4 %collective-permute-start.19 = (f32[1536]{0:T(1024)S(1)}, f32[1536]{0:T(1024)S(1)}, u32[]{:S(2)}, u32[]{:S(2)}) collective-permute-start(f32[1536]{0:T(1024)S(1)} %slice_reduce_fusion.1), channel_id=1, source_target_pairs={{0,3},{1,2},{2,1},{3,0},{4,7},{5,6},{6,5},{7,4},{8,11},{9,10},{10,... | collective-permute-start | bytes 18440 | tf_op jit(solution)/shard_map/ppermute | solution.py:877
  244.1 10.9 %collective-permute-start.18 = (f32[1536]{0:T(1024)S(1)}, f32[1536]{0:T(1024)S(1)}, u32[]{:S(2)}, u32[]{:S(2)}) collective-permute-start(f32[1536]{0:T(1024)S(1)} %slice_reduce_fusion.1), channel_id=1, source_target_pairs={{0,2},{1,3},{2,0},{3,1},{4,6},{5,7},{6,4},{7,5},{8,10},{9,11},{10,... | collective-permute-start | bytes 18440 | tf_op jit(solution)/shard_map/ppermute | solution.py:877
  244.6 10.4 %collective-permute-start.17 = (f32[1536]{0:T(1024)S(1)}, f32[1536]{0:T(1024)S(1)}, u32[]{:S(2)}, u32[]{:S(2)}) collective-permute-start(f32[1536]{0:T(1024)S(1)} %slice_reduce_fusion.1), channel_id=1, source_target_pairs={{0,1},{1,0},{2,3},{3,2},{4,5},{5,4},{6,7},{7,6},{8,9},{9,8},{10,11... | collective-permute-start | bytes 18440 | tf_op jit(solution)/shard_map/ppermute | solution.py:877
  249.5 44.3 %collective-permute-start.20 = (bf16[768,1280]{1,0:T(8,128)(2,1)}, bf16[768,1280]{1,0:T(8,128)(2,1)S(1)}, u32[]{:S(2)}, u32[]{:S(2)}) collective-permute-start(bf16[768,1280]{1,0:T(8,128)(2,1)} %pad_maximum_fusion.2), channel_id=1, source_target_pairs={{0,1},{1,0},{2,3},{3,2},{4,5},{5,4},{6,7},{7,6},{8,9},{9,8},{10,11... | collective-permute-start | bytes 5898248 | tf_op jit(solution)/shard_map/ppermute | solution.py:877
  253.5 44.3 %collective-permute-start.21 = (bf16[768,1280]{1,0:T(8,128)(2,1)}, bf16[768,1280]{1,0:T(8,128)(2,1)S(1)}, u32[]{:S(2)}, u32[]{:S(2)}) collective-permute-start(bf16[768,1280]{1,0:T(8,128)(2,1)} %pad_maximum_fusion.3), channel_id=1, source_target_pairs={{0,2},{1,3},{2,0},{3,1},{4,6},{5,7},{6,4},{7,5},{8,10},{9,11},{10,... | collective-permute-start | bytes 5898248 | tf_op jit(solution)/shard_map/ppermute | solution.py:877
  298.0 5.9 %collective-permute-start.22 = (bf16[4,320,1280]{2,1,0:T(8,128)(2,1)S(1)}, bf16[4,320,1280]{2,1,0:T(8,128)(2,1)S(1)}, u32[]{:S(2)}, u32[]{:S(2)}) collective-permute-start(bf16[4,320,1280]{2,1,0:T(8,128)(2,1)S(1)} %dynamic-slice_bitcast_fusion.1), channel_id=1, source_target_pairs={{0,4},{4,0},{8,12},{12,8},{16,20},{20,16},{24,28},{28,24},{1,5},{5... | collective-permute-start | bytes 9830408 | tf_op jit(solution)/shard_map/ppermute | solution.py:949
  306.5 176.9 %reduce-scatter.8.cloned.1.call-start = ((), (), s32[]{:S(2)}) async-start(), calls=%async_computation.7 | async-start | bytes 4096000 | tf_op jit(solution)/shard_map/reduce_scatter | solution.py:971
  306.7 77.7 %collective-permute-start.23 = (bf16[384,1280]{1,0:T(8,128)(2,1)S(1)}, bf16[384,1280]{1,0:T(8,128)(2,1)}, u32[]{:S(2)}, u32[]{:S(2)}) collective-permute-start(bf16[384,1280]{1,0:T(8,128)(2,1)S(1)} %add_convert_fusion.3), channel_id=1, source_target_pairs={{0,2},{1,3},{2,0},{3,1},{4,6},{5,7},{6,4},{7,5},{8,10},{9,11},{10,... | collective-permute-start | bytes 2949128 | tf_op jit(solution)/shard_map/ppermute | solution.py:877
  308.3 76.9 %collective-permute-start.24 = (bf16[384,1280]{1,0:T(8,128)(2,1)S(1)}, bf16[384,1280]{1,0:T(8,128)(2,1)}, u32[]{:S(2)}, u32[]{:S(2)}) collective-permute-start(bf16[384,1280]{1,0:T(8,128)(2,1)S(1)} %copy-done.20), channel_id=1, source_target_pairs={{0,1},{1,0},{2,3},{3,2},{4,5},{5,4},{6,7},{7,6},{8,9},{9,8},{10,11... | collective-permute-start | bytes 2949128 | tf_op jit(solution)/shard_map/ppermute | solution.py:877
  364.7 19.5 %collective-permute-start.27 = (f32[64,1536]{1,0:T(8,128)S(1)}, f32[64,1536]{1,0:T(8,128)S(1)}, u32[]{:S(2)}, u32[]{:S(2)}) collective-permute-start(f32[64,1536]{1,0:T(8,128)S(1)} %get-tuple-element.433), channel_id=1, source_target_pairs={{0,3},{1,2},{2,1},{3,0},{4,7},{5,6},{6,5},{7,4},{8,11},{9,10},{10,... | collective-permute-start | bytes 1179656 | tf_op jit(solution)/shard_map/ppermute | solution.py:877
  365.1 19.1 %collective-permute-start.26 = (f32[64,1536]{1,0:T(8,128)S(1)}, f32[64,1536]{1,0:T(8,128)S(1)}, u32[]{:S(2)}, u32[]{:S(2)}) collective-permute-start(f32[64,1536]{1,0:T(8,128)S(1)} %get-tuple-element.434), channel_id=1, source_target_pairs={{0,2},{1,3},{2,0},{3,1},{4,6},{5,7},{6,4},{7,5},{8,10},{9,11},{10,... | collective-permute-start | bytes 1179656 | tf_op jit(solution)/shard_map/ppermute | solution.py:877
  366.8 17.7 %collective-permute-start.25 = (f32[64,1536]{1,0:T(8,128)S(1)}, f32[64,1536]{1,0:T(8,128)S(1)}, u32[]{:S(2)}, u32[]{:S(2)}) collective-permute-start(f32[64,1536]{1,0:T(8,128)S(1)} %get-tuple-element.435), channel_id=1, source_target_pairs={{0,1},{1,0},{2,3},{3,2},{4,5},{5,4},{6,7},{7,6},{8,9},{9,8},{10,11... | collective-permute-start | bytes 1179656 | tf_op jit(solution)/shard_map/ppermute | solution.py:877
  389.3 15.1 %collective-permute-start.29 = (bf16[4,320,1280]{2,1,0:T(8,128)(2,1)}, bf16[4,320,1280]{2,1,0:T(8,128)(2,1)}, u32[]{:S(2)}, u32[]{:S(2)}) collective-permute-start(bf16[4,320,1280]{2,1,0:T(8,128)(2,1)} %dynamic-slice_bitcast_fusion), channel_id=1, source_target_pairs={{0,4},{4,0},{8,12},{12,8},{16,20},{20,16},{24,28},{28,24},{1,5},{5... | collective-permute-start | bytes 9830408 | tf_op jit(solution)/shard_map/ppermute | solution.py:949
  408.8 45.5 %collective-permute-start.28 = (bf16[768,1280]{1,0:T(8,128)(2,1)}, bf16[768,1280]{1,0:T(8,128)(2,1)S(1)}, u32[]{:S(2)}, u32[]{:S(2)}) collective-permute-start(bf16[768,1280]{1,0:T(8,128)(2,1)} %get-tuple-element.197), channel_id=1, source_target_pairs={{0,1},{1,0},{2,3},{3,2},{4,5},{5,4},{6,7},{7,6},{8,9},{9,8},{10,11... | collective-permute-start | bytes 5898248 | tf_op jit(solution)/shard_map/ppermute | solution.py:877
  423.9 47.3 %collective-permute-start.34 = (bf16[768,1280]{1,0:T(8,128)(2,1)}, bf16[768,1280]{1,0:T(8,128)(2,1)}, u32[]{:S(2)}, u32[]{:S(2)}) collective-permute-start(bf16[768,1280]{1,0:T(8,128)(2,1)} %get-tuple-element.216), channel_id=1, source_target_pairs={{0,2},{1,3},{2,0},{3,1},{4,6},{5,7},{6,4},{7,5},{8,10},{9,11},{10,... | collective-permute-start | bytes 5898248 | tf_op jit(solution)/shard_map/ppermute | solution.py:877
  469.7 3.1 collective-permute-start.30
  479.0 27.2 %collective-permute-start.31 = (f32[320,128]{0,1:T(8,128)}, f32[320,128]{0,1:T(8,128)}, u32[]{:S(2)}, u32[]{:S(2)}) collective-permute-start(f32[320,128]{0,1:T(8,128)} %copy.254), channel_id=1, source_target_pairs={{0,8},{4,12},{8,0},{12,4},{16,24},{20,28},{24,16},{28,20},{1,9},{5... | collective-permute-start | bytes 491528 | tf_op jit(solution)/shard_map/ppermute | solution.py:949
  479.0 27.2 %collective-permute-start.32 = (f32[320,128]{0,1:T(8,128)}, f32[320,128]{0,1:T(8,128)}, u32[]{:S(2)}, u32[]{:S(2)}) collective-permute-start(f32[320,128]{0,1:T(8,128)} %copy.255), channel_id=1, source_target_pairs={{0,16},{4,20},{8,24},{12,28},{16,0},{20,4},{24,8},{28,12},{1,17},{... | collective-permute-start | bytes 491528 | tf_op jit(solution)/shard_map/ppermute | solution.py:949
  480.4 25.8 %collective-permute-start.33 = (f32[320,128]{0,1:T(8,128)}, f32[320,128]{0,1:T(8,128)}, u32[]{:S(2)}, u32[]{:S(2)}) collective-permute-start(f32[320,128]{0,1:T(8,128)} %copy.256), channel_id=1, source_target_pairs={{0,24},{4,28},{8,16},{12,20},{16,8},{20,12},{24,0},{28,4},{1,25},{... | collective-permute-start | bytes 491528 | tf_op jit(solution)/shard_map/ppermute | solution.py:949
  483.4 24.0 %collective-permute-start.35 = (bf16[384,1280]{1,0:T(8,128)(2,1)}, bf16[384,1280]{1,0:T(8,128)(2,1)}, u32[]{:S(2)}, u32[]{:S(2)}) collective-permute-start(bf16[384,1280]{1,0:T(8,128)(2,1)} %add_convert_fusion.1), channel_id=1, source_target_pairs={{0,2},{1,3},{2,0},{3,1},{4,6},{5,7},{6,4},{7,5},{8,10},{9,11},{10,... | collective-permute-start | bytes 2949128 | tf_op jit(solution)/shard_map/ppermute | solution.py:877
  490.4 25.5 %collective-permute-start.36 = (bf16[384,1280]{1,0:T(8,128)(2,1)S(1)}, bf16[384,1280]{1,0:T(8,128)(2,1)S(1)}, u32[]{:S(2)}, u32[]{:S(2)}) collective-permute-start(bf16[384,1280]{1,0:T(8,128)(2,1)S(1)} %add_convert_fusion), channel_id=1, source_target_pairs={{0,1},{1,0},{2,3},{3,2},{4,5},{5,4},{6,7},{7,6},{8,9},{9,8},{10,11... | collective-permute-start | bytes 2949128 | tf_op jit(solution)/shard_map/ppermute | solution.py:877
  507.7 16.6 %collective-permute-start.37 = (f32[320]{0:T(512)S(1)}, f32[320]{0:T(512)S(1)}, u32[]{:S(2)}, u32[]{:S(2)}) collective-permute-start(f32[320]{0:T(512)S(1)} %get-tuple-element.444), channel_id=1, source_target_pairs={{0,1},{1,0},{2,3},{3,2},{4,5},{5,4},{6,7},{7,6},{8,9},{9,8},{10,11... | collective-permute-start | bytes 3848 | tf_op jit(solution)/shard_map/ppermute | solution.py:877
  510.8 13.7 %collective-permute-start.39 = (f32[320]{0:T(512)S(1)}, f32[320]{0:T(512)S(1)}, u32[]{:S(2)}, u32[]{:S(2)}) collective-permute-start(f32[320]{0:T(512)S(1)} %get-tuple-element.444), channel_id=1, source_target_pairs={{0,3},{1,2},{2,1},{3,0},{4,7},{5,6},{6,5},{7,4},{8,11},{9,10},{10,... | collective-permute-start | bytes 3848 | tf_op jit(solution)/shard_map/ppermute | solution.py:877
  511.6 12.8 %collective-permute-start.38 = (f32[320]{0:T(512)S(1)}, f32[320]{0:T(512)S(1)}, u32[]{:S(2)}, u32[]{:S(2)}) collective-permute-start(f32[320]{0:T(512)S(1)} %get-tuple-element.444), channel_id=1, source_target_pairs={{0,2},{1,3},{2,0},{3,1},{4,6},{5,7},{6,4},{7,5},{8,10},{9,11},{10,... | collective-permute-start | bytes 3848 | tf_op jit(solution)/shard_map/ppermute | solution.py:877
  (88 other events, 1078.0 us)
Sparse Core Ops, SparseCore 0:
  12.9 75.9 all-gather.4
  91.1 65.5 all-gather.8
  158.3 65.5 all-gather.6
  226.7 60.9 reduce-scatter.3
  306.6 61.0 reduce-scatter.5
  409.0 59.6 reduce-scatter.7
